TPU v7x, 32 devices: a whole 2x2x4 slice. The times are simulated.
32 devices in a mesh: row: 8 (over z, y), col: 4 (over x, core).
Axes of the slice: x: 2, y: 2, z: 4, core: 2. Of those that a mesh axis runs over, the one named last changes fastest.
Arguments:
- rhs: float32 [32768, 256], P(('row', 'col')), may hold values from -6 to 6
- local_mat: bfloat16 [32768, 1024], P(('row', 'col')), may hold values from -1 to 5
- local_inv: bfloat16 [32768, 1024], P(('row', 'col')), may hold values from -1 to 1
- basis_t: bfloat16 [3072, 1024], P(('row', 'col')), may hold values from -0.1875 to 0.1875
- coarse_inv: bfloat16 [3072, 3072], P('col', 'row'), may hold values from -0.109375 to 0.109375
- couple: float32 [32, 4, 128], P(('row', 'col')), may hold values from 0.5 to 2
- margin_rows: int32 [32, 4, 128], P(('row', 'col')), may hold values from 0 to 1023, as said below
Outputs:
- solution: float32 [32768, 256], P(('row', 'col'))
- residual: float32 [32768, 256], P(('row', 'col'))
Inputs may be any that keep to these rules, and one draw needn't show every extreme that they name: `margin_rows`: within each subdomain the 512 listed rows are all different.
All inputs are finite; a program needn't handle non-finite values.
Results may differ from a plain program's by a relative error of at most 0.024.
Values may be sent and summed in bfloat16 or wider, within the bound.
No kernel may reach another device: no remote copies, remote signals or barrier semaphores. Data moves between devices by JAX's collectives and lax.ppermute only.
A program may use at most 64 MiB of HBM per device.

v0:
```python
import jax
import jax.numpy as jnp
from jax import lax
from jax.sharding import PartitionSpec as P

STEPS = 2


def padded(cells, sides, width):
    for axis, dim in sides:
        count = lax.axis_size(axis)
        ends = count - 1
        head = lax.slice_in_dim(cells, 0, width, axis=dim)
        tail = lax.slice_in_dim(cells, cells.shape[dim] - width, cells.shape[dim], axis=dim)
        cells = jnp.concatenate(
            [
                lax.ppermute(tail, axis, [(i, (i + 1) % count) for i in range(ends)]),
                cells,
                lax.ppermute(head, axis, [((i + 1) % count, i) for i in range(ends)]),
            ],
            axis=dim,
        )
    return cells


def per_device(rhs, local_mat, local_inv, basis_t, coarse_inv, couple, margin_rows):
    face_index = margin_rows[0]
    flat_rows = face_index.reshape(-1)
    weights = couple[0]
    columns = rhs.shape[1]

    def neighbour_faces(vector_b):
        face_vals = vector_b[face_index]
        north_south = padded(face_vals[0:2], (("row", 0),), 1)
        west_east = padded(face_vals[2:4], (("col", 0),), 1)
        received = jnp.stack([north_south[0], north_south[3], west_east[0], west_east[3]])
        return received

    def apply_operator(vector):
        vector_b = vector.astype(jnp.bfloat16)
        received = neighbour_faces(vector_b)
        coupling_terms = (weights[:, :, None] * received.astype(jnp.float32)).reshape(-1, columns)
        coupled = jnp.zeros(vector.shape, jnp.float32).at[flat_rows].add(coupling_terms)
        return jnp.dot(local_mat, vector_b, preferred_element_type=jnp.float32) - coupled

    solution = jnp.zeros(rhs.shape, jnp.float32)
    residual = rhs
    for sweep in range(STEPS):
        if sweep > 0:
            residual = rhs - apply_operator(solution)
        rounded = residual.astype(jnp.bfloat16)
        restricted = jnp.dot(basis_t, rounded, preferred_element_type=jnp.float32).astype(
            jnp.bfloat16
        )
        block_rows = restricted.shape[0]
        partial_sum = jnp.dot(
            coarse_inv,
            lax.all_gather(restricted, "col", axis=0, tiled=True),
            preferred_element_type=jnp.float32,
        )
        summed = lax.psum(partial_sum, "row")
        coarse_part = lax.dynamic_slice_in_dim(
            summed, lax.axis_index("row") * block_rows, block_rows, 0
        )
        coarse_b = coarse_part.astype(jnp.bfloat16)
        solution = solution + lax.dot_general(
            basis_t, coarse_b, (((0,), (0,)), ((), ())), preferred_element_type=jnp.float32
        )
        residual = rhs - apply_operator(solution)
        solution = solution + jnp.dot(
            local_inv, residual.astype(jnp.bfloat16), preferred_element_type=jnp.float32
        )
    residual = rhs - apply_operator(solution)
    return (solution, residual)


def solution(mesh):
    placed = (
        P(("row", "col"), None),
        P(("row", "col"), None),
        P(("row", "col"), None),
        P(("row", "col"), None),
        P("col", "row"),
        P(("row", "col"), None, None),
        P(("row", "col"), None, None),
    )
    return jax.shard_map(
        per_device,
        mesh=mesh,
        in_specs=placed,
        out_specs=(P(("row", "col"), None), P(("row", "col"), None)),
        check_vma=False,
    )
```

profile of v0, /device:TPU:0, one launch (start us, length us, event | category | flops | bytes accessed | tf_op | source)
XLA Modules:
  0.0 241.2 jit_solution(8589869174017089495)
XLA Ops:
  1.5 1.6 convolution_convert_fusion
  3.1 6.9 %all_gather.6 = bf16[384,256]{1,0:T(8,128)(2,1)S(1)} all-gather(bf16[96,256]{1,0:T(8,128)(2,1)S(1)} %convolution_convert_fusion), channel_id=1, replica_groups=mesh['row'=8,'col'=4] {'col'}, dimensions={0}, use_global_device_ids=true | all-gather | bytes 245760 | tf_op jit(solution)/shard_map/all_gather | solution.py:58
  9.9 1.5 convolution_bitcast_fusion.5
  11.4 46.6 %all-reduce.2 = bf16[768,256]{0,1:T(8,128)(2,1)} all-reduce(f32[768,256]{0,1:T(8,128)S(1)} %convolution_bitcast_fusion.5), channel_id=1, replica_groups=mesh['row'=8,'col'=4] {'row'}, use_global_device_ids=true, to_apply=%region_0.0 | all-reduce | flops 196608 | bytes 1179648 | tf_op jit(solution)/shard_map/psum | solution.py:61
  60.6 2.0 gather_fusion
  63.2 2.7 %collective-permute-start = (bf16[1,128,256]{2,1,0:T(8,128)(2,1)}, bf16[1,128,256]{2,1,0:T(8,128)(2,1)S(1)}, u32[]{:S(2)}, u32[]{:S(2)}) collective-permute-start(bf16[1,128,256]{2,1,0:T(8,128)(2,1)} %get-tuple-element.20), channel_id=1, source_target_pairs={{0,4},{4,8},{8,12},{12,16},{16,20},{20,24},{24,28},{1,5},{5,9},{9,... | collective-permute-start | bytes 196616 | tf_op jit(solution)/shard_map/ppermute | solution.py:17
  65.9 1.9 collective-permute-start.2
  69.1 1.3 collective-permute-start.3
  70.4 1.6 copy.33
  72.0 2.7 %collective-permute-done.1 = bf16[1,128,256]{2,1,0:T(8,128)(2,1)} collective-permute-done((bf16[1,128,256]{2,1,0:T(8,128)(2,1)S(1)}, bf16[1,128,256]{2,1,0:T(8,128)(2,1)}, u32[]{:S(2)}, u32[]{:S(2)}) %collective-permute-start.1) | collective-permute-done | bytes 65568 | tf_op jit(solution)/shard_map/ppermute | solution.py:19
  74.7 1.6 pad_maximum_fusion
  76.4 4.8 %scatter_custom_fusion = f32[1024,256]{1,0:T(8,128)} fusion(s32[512]{0:T(512)S(1)} %bitcast.127, bf16[512,256]{1,0:T(8,128)(2,1)} %bitcast.119, f32[]{:T(128)} %constant.4.clone.1, f32[512]{0:T(512)S(1)} %bitcast.122), kind=kCustom, calls=%fused_computation.40 | custom fusion | flops 393216 | bytes 1312772 | tf_op jit(solution)/shard_map/scatter-add | solution.py:43
  81.2 2.5 %copy.32 = f32[1024,256]{0,1:T(8,128)} copy(f32[1024,256]{1,0:T(8,128)} %scatter_custom_fusion) | data formatting | bytes 2097152 | tf_op jit(solution)/shard_map/scatter-add | solution.py:43
  83.7 4.8 %convolution_add_fusion.2 = f32[256,1024]{1,0:T(8,128)} fusion(f32[256,1024]{1,0:T(8,128)} %copy-done.2, bf16[1024,1024]{1,0:T(8,128)(2,1)} %param.9, f32[1024,256]{0,1:T(8,128)S(1)} %copy.33, f32[1024,256]{0,1:T(8,128)} %copy.32, bf16[1024,1024]{1,0:T(8,128)(2,1)S(1)} %copy-done), kind=kOutput, calls=%fused_computation.23 | convolution fusion | flops 1075052544 | bytes 8388608 | tf_op jit(solution)/shard_map/dot_general | solution.py:70
  88.5 2.1 convert_bitcast_fusion.1
  90.6 2.0 copy.34
  92.6 3.3 %gather_fusion.1 = bf16[512,256]{1,0:T(8,128)(2,1)} fusion(bf16[1024,256]{1,0:T(8,128)(2,1)} %copy.34, s32[1024]{0:T(1024)S(1)} %pad_clamp_fusion), kind=kCustom, calls=%fused_computation.1 | custom fusion | bytes 526336 | tf_op jit(solution)/shard_map/gather | solution.py:33
  96.9 2.5 %collective-permute-start.4 = (bf16[1,128,256]{2,1,0:T(8,128)(2,1)S(1)}, bf16[1,128,256]{2,1,0:T(8,128)(2,1)S(1)}, u32[]{:S(2)}, u32[]{:S(2)}) collective-permute-start(bf16[1,128,256]{2,1,0:T(8,128)(2,1)S(1)} %get-tuple-element.16), channel_id=1, source_target_pairs={{0,4},{4,8},{8,12},{12,16},{16,20},{20,24},{24,28},{1,5},{5,9},{9,... | collective-permute-start | bytes 196616 | tf_op jit(solution)/shard_map/ppermute | solution.py:17
  99.4 4.4 %collective-permute-start.6 = (bf16[1,128,256]{2,1,0:T(8,128)(2,1)S(1)}, bf16[1,128,256]{2,1,0:T(8,128)(2,1)S(1)}, u32[]{:S(2)}, u32[]{:S(2)}) collective-permute-start(bf16[1,128,256]{2,1,0:T(8,128)(2,1)S(1)} %get-tuple-element.17), channel_id=1, source_target_pairs={{0,1},{1,2},{2,3},{4,5},{5,6},{6,7},{8,9},{9,10},{10,11},{12,13},{... | collective-permute-start | bytes 196616 | tf_op jit(solution)/shard_map/ppermute | solution.py:17
  103.8 1.3 collective-permute-start.5
  105.1 1.3 collective-permute-start.7
  106.4 3.5 %collective-permute-done.5 = bf16[1,128,256]{2,1,0:T(8,128)(2,1)S(1)} collective-permute-done((bf16[1,128,256]{2,1,0:T(8,128)(2,1)S(1)}, bf16[1,128,256]{2,1,0:T(8,128)(2,1)S(1)}, u32[]{:S(2)}, u32[]{:S(2)}) %collective-permute-start.5) | collective-permute-done | bytes 65568 | tf_op jit(solution)/shard_map/ppermute | solution.py:19
  110.7 4.8 %scatter_custom_fusion.1 = f32[1024,256]{1,0:T(8,128)} fusion(s32[512]{0:T(512)S(1)} %bitcast.128, bf16[512,256]{1,0:T(8,128)(2,1)} %bitcast.120, f32[]{:T(128)} %constant.4.clone.1, f32[512]{0:T(512)S(1)} %bitcast.123), kind=kCustom, calls=%fused_computation.38 | custom fusion | flops 393216 | bytes 1312772 | tf_op jit(solution)/shard_map/scatter-add | solution.py:43
  115.5 2.5 %copy.35 = f32[1024,256]{0,1:T(8,128)} copy(f32[1024,256]{1,0:T(8,128)} %scatter_custom_fusion.1) | data formatting | bytes 2097152 | tf_op jit(solution)/shard_map/scatter-add | solution.py:43
  118.1 2.5 %fusion.14 = bf16[96,256]{1,0:T(8,128)(2,1)S(1)} fusion(bf16[96,1024]{1,0:T(8,128)(2,1)S(1)} %copy-done.3, f32[1024,256]{0,1:T(8,128)S(1)} %copy.33, f32[1024,256]{0,1:T(8,128)} %copy.35, bf16[1024,1024]{1,0:T(8,128)(2,1)S(1)} %copy-done, f32[256,1024]{1,0:T(8,128)} %convolution_add_fusion.2), kind=kOutput, calls=%fused_computation.32 | convolution fusion | flops 588275712 | bytes 5488640 | tf_op jit(solution)/shard_map/dot_general | solution.py:52
  120.6 6.0 %all_gather.7 = bf16[384,256]{1,0:T(8,128)(2,1)S(1)} all-gather(bf16[96,256]{1,0:T(8,128)(2,1)S(1)} %fusion.14), channel_id=1, replica_groups=mesh['row'=8,'col'=4] {'col'}, dimensions={0}, use_global_device_ids=true | all-gather | bytes 245760 | tf_op jit(solution)/shard_map/all_gather | solution.py:58
  126.6 2.4 convolution_bitcast_fusion.4
  128.9 49.3 %all-reduce.3 = bf16[768,256]{0,1:T(8,128)(2,1)} all-reduce(f32[768,256]{0,1:T(8,128)} %convolution_bitcast_fusion.4), channel_id=1, replica_groups=mesh['row'=8,'col'=4] {'row'}, use_global_device_ids=true, to_apply=%region_3.0 | all-reduce | flops 196608 | bytes 1179648 | tf_op jit(solution)/shard_map/psum | solution.py:61
  178.2 1.6 convolution_add_fusion
  181.7 2.0 copy.37
  183.8 2.7 %gather_fusion.2 = bf16[512,256]{1,0:T(8,128)(2,1)S(1)} fusion(bf16[1024,256]{1,0:T(8,128)(2,1)} %copy.37, s32[1024]{0:T(1024)S(1)} %pad_clamp_fusion), kind=kCustom, calls=%fused_computation.2 | custom fusion | bytes 526336 | tf_op jit(solution)/shard_map/gather | solution.py:33
  186.5 1.3 collective-permute-start.8
  187.8 1.3 collective-permute-start.10
  189.1 1.3 collective-permute-start.9
  191.7 3.8 %collective-permute-done.9 = bf16[1,128,256]{2,1,0:T(8,128)(2,1)S(1)} collective-permute-done((bf16[1,128,256]{2,1,0:T(8,128)(2,1)S(1)}, bf16[1,128,256]{2,1,0:T(8,128)(2,1)S(1)}, u32[]{:S(2)}, u32[]{:S(2)}) %collective-permute-start.9) | collective-permute-done | bytes 65568 | tf_op jit(solution)/shard_map/ppermute | solution.py:19
  195.5 4.4 %scatter_custom_fusion.2 = f32[1024,256]{1,0:T(8,128)} fusion(s32[512]{0:T(512)S(1)} %bitcast.129, bf16[512,256]{1,0:T(8,128)(2,1)S(1)} %bitcast.121, f32[]{:T(128)} %constant.4.clone.1, f32[512]{0:T(512)S(1)} %bitcast.124), kind=kCustom, calls=%fused_computation.36 | custom fusion | flops 393216 | bytes 1312772 | tf_op jit(solution)/shard_map/scatter-add | solution.py:43
  200.0 2.6 %copy.38 = f32[1024,256]{0,1:T(8,128)} copy(f32[1024,256]{1,0:T(8,128)} %scatter_custom_fusion.2) | data formatting | bytes 2097152 | tf_op jit(solution)/shard_map/scatter-add | solution.py:43
  202.5 5.0 %fusion.38 = (bf16[1024,256]{0,1:T(8,128)(2,1)}, f32[1024,256]{0,1:T(8,128)}) fusion(f32[256,1024]{1,0:T(8,128)} %copy-done.1, bf16[1024,1024]{1,0:T(8,128)(2,1)} %param.9, f32[1024,256]{0,1:T(8,128)S(1)} %copy.33, f32[1024,256]{0,1:T(8,128)} %copy.38, bf16[1024,1024]{1,0:T(8,128)(2,1)S(1)} %copy-done), kind=kOutput, calls=%fused_computation.85 | convolution fusion | flops 1075314688 | bytes 8912896 | tf_op jit(solution)/shard_map/dot_general | solution.py:70
  207.5 2.0 copy.40
  209.5 2.7 %gather_fusion.3 = bf16[512,256]{1,0:T(8,128)(2,1)S(1)} fusion(bf16[1024,256]{1,0:T(8,128)(2,1)} %copy.40, s32[1024]{0:T(1024)S(1)} %pad_clamp_fusion), kind=kCustom, calls=%fused_computation.3 | custom fusion | bytes 526336 | tf_op jit(solution)/shard_map/gather | solution.py:33
  212.9 4.5 %collective-permute-start.12 = (bf16[1,128,256]{2,1,0:T(8,128)(2,1)}, bf16[1,128,256]{2,1,0:T(8,128)(2,1)S(1)}, u32[]{:S(2)}, u32[]{:S(2)}) collective-permute-start(bf16[1,128,256]{2,1,0:T(8,128)(2,1)} %get-tuple-element.8), channel_id=1, source_target_pairs={{0,4},{4,8},{8,12},{12,16},{16,20},{20,24},{24,28},{1,5},{5,9},{9,... | collective-permute-start | bytes 196616 | tf_op jit(solution)/shard_map/ppermute | solution.py:17
  217.4 2.3 collective-permute-start.14
  222.3 2.5 %copy.43 = f32[1024,256]{1,0:T(8,128)} copy(f32[1024,256]{0,1:T(8,128)} %get-tuple-element.25) | data formatting | bytes 2097152
  224.9 2.1 collective-permute-done.13
  228.6 4.4 %scatter_custom_fusion.3 = f32[1024,256]{1,0:T(8,128)} fusion(s32[512]{0:T(512)S(1)} %bitcast.130, bf16[512,256]{1,0:T(8,128)(2,1)S(1)} %bitcast.118, f32[]{:T(128)} %constant.4.clone.1, f32[512]{0:T(512)S(1)} %bitcast.125), kind=kCustom, calls=%fused_computation.34 | custom fusion | flops 393216 | bytes 1312772 | tf_op jit(solution)/shard_map/scatter-add | solution.py:43
  233.0 2.5 %copy.41 = f32[1024,256]{0,1:T(8,128)} copy(f32[1024,256]{1,0:T(8,128)} %scatter_custom_fusion.3) | data formatting | bytes 2097152 | tf_op jit(solution)/shard_map/scatter-add | solution.py:43
  235.5 3.1 %fusion.7 = f32[1024,256]{0,1:T(8,128)} fusion(f32[1024,256]{0,1:T(8,128)S(1)} %copy.33, f32[1024,256]{0,1:T(8,128)} %copy.41, bf16[1024,256]{0,1:T(8,128)(2,1)} %get-tuple-element.24, bf16[1024,1024]{1,0:T(8,128)(2,1)S(1)} %copy-done), kind=kOutput, calls=%fused_computation.20 | convolution fusion | flops 537395200 | bytes 5767168 | tf_op jit(solution)/shard_map/dot_general | solution.py:44
  238.6 2.5 %copy.44 = f32[1024,256]{1,0:T(8,128)} copy(f32[1024,256]{0,1:T(8,128)} %fusion.7) | data formatting | bytes 2097152
  (46 shorter events, 15.0 us)
Async XLA Ops:
  0.6 83.1 %copy-start = (bf16[1024,1024]{1,0:T(8,128)(2,1)S(1)}, bf16[1024,1024]{1,0:T(8,128)(2,1)}, u32[]{:S(2)}) copy-start(bf16[1024,1024]{1,0:T(8,128)(2,1)} %param.8) | copy-start | bytes 6291460
  1.5 56.6 %copy-start.3 = (bf16[96,1024]{1,0:T(8,128)(2,1)S(1)}, bf16[96,1024]{1,0:T(8,128)(2,1)}, u32[]{:S(2)}) copy-start(bf16[96,1024]{1,0:T(8,128)(2,1)} %param.10) | copy-start | bytes 589828
  59.3 1.0 copy-start.2
  60.3 10.0 %copy-start.7 = (s32[1,4,128]{2,1,0:T(4,128)S(1)}, s32[1,4,128]{2,1,0:T(4,128)}, u32[]{:S(2)}) copy-start(s32[1,4,128]{2,1,0:T(4,128)} %param.13) | copy-start | bytes 6148
  62.5 13.8 %copy-start.6 = (f32[1,4,128]{2,1,0:T(4,128)S(1)}, f32[1,4,128]{2,1,0:T(4,128)}, u32[]{:S(2)}) copy-start(f32[1,4,128]{2,1,0:T(4,128)} %param.12) | copy-start | bytes 6148
  63.2 8.8 %collective-permute-start = (bf16[1,128,256]{2,1,0:T(8,128)(2,1)}, bf16[1,128,256]{2,1,0:T(8,128)(2,1)S(1)}, u32[]{:S(2)}, u32[]{:S(2)}) collective-permute-start(bf16[1,128,256]{2,1,0:T(8,128)(2,1)} %get-tuple-element.20), channel_id=1, source_target_pairs={{0,4},{4,8},{8,12},{12,16},{16,20},{20,24},{24,28},{1,5},{5,9},{9,... | collective-permute-start | bytes 196616 | tf_op jit(solution)/shard_map/ppermute | solution.py:17
  65.9 6.1 %collective-permute-start.2 = (bf16[1,128,256]{2,1,0:T(8,128)(2,1)}, bf16[1,128,256]{2,1,0:T(8,128)(2,1)}, u32[]{:S(2)}, u32[]{:S(2)}) collective-permute-start(bf16[1,128,256]{2,1,0:T(8,128)(2,1)} %get-tuple-element.21), channel_id=1, source_target_pairs={{0,1},{1,2},{2,3},{4,5},{5,6},{6,7},{8,9},{9,10},{10,11},{12,13},{... | collective-permute-start | bytes 196616 | tf_op jit(solution)/shard_map/ppermute | solution.py:17
  67.8 6.9 %collective-permute-start.1 = (bf16[1,128,256]{2,1,0:T(8,128)(2,1)S(1)}, bf16[1,128,256]{2,1,0:T(8,128)(2,1)}, u32[]{:S(2)}, u32[]{:S(2)}) collective-permute-start(bf16[1,128,256]{2,1,0:T(8,128)(2,1)S(1)} %get-tuple-element.22), channel_id=1, source_target_pairs={{4,0},{8,4},{12,8},{16,12},{20,16},{24,20},{28,24},{5,1},{9,5},{13... | collective-permute-start | bytes 196616 | tf_op jit(solution)/shard_map/ppermute | solution.py:19
  69.1 5.7 %collective-permute-start.3 = (bf16[1,128,256]{2,1,0:T(8,128)(2,1)S(1)}, bf16[1,128,256]{2,1,0:T(8,128)(2,1)}, u32[]{:S(2)}, u32[]{:S(2)}) collective-permute-start(bf16[1,128,256]{2,1,0:T(8,128)(2,1)S(1)} %get-tuple-element.23), channel_id=1, source_target_pairs={{1,0},{2,1},{3,2},{5,4},{6,5},{7,6},{9,8},{10,9},{11,10},{13,12},{... | collective-permute-start | bytes 196616 | tf_op jit(solution)/shard_map/ppermute | solution.py:19
  96.9 9.5 %collective-permute-start.4 = (bf16[1,128,256]{2,1,0:T(8,128)(2,1)S(1)}, bf16[1,128,256]{2,1,0:T(8,128)(2,1)S(1)}, u32[]{:S(2)}, u32[]{:S(2)}) collective-permute-start(bf16[1,128,256]{2,1,0:T(8,128)(2,1)S(1)} %get-tuple-element.16), channel_id=1, source_target_pairs={{0,4},{4,8},{8,12},{12,16},{16,20},{20,24},{24,28},{1,5},{5,9},{9,... | collective-permute-start | bytes 196616 | tf_op jit(solution)/shard_map/ppermute | solution.py:17
  99.4 7.0 %collective-permute-start.6 = (bf16[1,128,256]{2,1,0:T(8,128)(2,1)S(1)}, bf16[1,128,256]{2,1,0:T(8,128)(2,1)S(1)}, u32[]{:S(2)}, u32[]{:S(2)}) collective-permute-start(bf16[1,128,256]{2,1,0:T(8,128)(2,1)S(1)} %get-tuple-element.17), channel_id=1, source_target_pairs={{0,1},{1,2},{2,3},{4,5},{5,6},{6,7},{8,9},{9,10},{10,11},{12,13},{... | collective-permute-start | bytes 196616 | tf_op jit(solution)/shard_map/ppermute | solution.py:17
  103.8 6.2 %collective-permute-start.5 = (bf16[1,128,256]{2,1,0:T(8,128)(2,1)S(1)}, bf16[1,128,256]{2,1,0:T(8,128)(2,1)S(1)}, u32[]{:S(2)}, u32[]{:S(2)}) collective-permute-start(bf16[1,128,256]{2,1,0:T(8,128)(2,1)S(1)} %get-tuple-element.18), channel_id=1, source_target_pairs={{4,0},{8,4},{12,8},{16,12},{20,16},{24,20},{28,24},{5,1},{9,5},{13... | collective-permute-start | bytes 196616 | tf_op jit(solution)/shard_map/ppermute | solution.py:19
  105.1 4.9 %collective-permute-start.7 = (bf16[1,128,256]{2,1,0:T(8,128)(2,1)S(1)}, bf16[1,128,256]{2,1,0:T(8,128)(2,1)S(1)}, u32[]{:S(2)}, u32[]{:S(2)}) collective-permute-start(bf16[1,128,256]{2,1,0:T(8,128)(2,1)S(1)} %get-tuple-element.19), channel_id=1, source_target_pairs={{1,0},{2,1},{3,2},{5,4},{6,5},{7,6},{9,8},{10,9},{11,10},{13,12},{... | collective-permute-start | bytes 196616 | tf_op jit(solution)/shard_map/ppermute | solution.py:19
  179.9 1.0 copy-start.1
  186.5 5.2 %collective-permute-start.8 = (bf16[1,128,256]{2,1,0:T(8,128)(2,1)S(1)}, bf16[1,128,256]{2,1,0:T(8,128)(2,1)S(1)}, u32[]{:S(2)}, u32[]{:S(2)}) collective-permute-start(bf16[1,128,256]{2,1,0:T(8,128)(2,1)S(1)} %get-tuple-element.12), channel_id=1, source_target_pairs={{0,4},{4,8},{8,12},{12,16},{16,20},{20,24},{24,28},{1,5},{5,9},{9,... | collective-permute-start | bytes 196616 | tf_op jit(solution)/shard_map/ppermute | solution.py:17
  187.8 3.9 %collective-permute-start.10 = (bf16[1,128,256]{2,1,0:T(8,128)(2,1)S(1)}, bf16[1,128,256]{2,1,0:T(8,128)(2,1)S(1)}, u32[]{:S(2)}, u32[]{:S(2)}) collective-permute-start(bf16[1,128,256]{2,1,0:T(8,128)(2,1)S(1)} %get-tuple-element.13), channel_id=1, source_target_pairs={{0,1},{1,2},{2,3},{4,5},{5,6},{6,7},{8,9},{9,10},{10,11},{12,13},{... | collective-permute-start | bytes 196616 | tf_op jit(solution)/shard_map/ppermute | solution.py:17
  189.1 6.4 %collective-permute-start.9 = (bf16[1,128,256]{2,1,0:T(8,128)(2,1)S(1)}, bf16[1,128,256]{2,1,0:T(8,128)(2,1)S(1)}, u32[]{:S(2)}, u32[]{:S(2)}) collective-permute-start(bf16[1,128,256]{2,1,0:T(8,128)(2,1)S(1)} %get-tuple-element.14), channel_id=1, source_target_pairs={{4,0},{8,4},{12,8},{16,12},{20,16},{24,20},{28,24},{5,1},{9,5},{13... | collective-permute-start | bytes 196616 | tf_op jit(solution)/shard_map/ppermute | solution.py:19
  190.4 5.1 %collective-permute-start.11 = (bf16[1,128,256]{2,1,0:T(8,128)(2,1)S(1)}, bf16[1,128,256]{2,1,0:T(8,128)(2,1)S(1)}, u32[]{:S(2)}, u32[]{:S(2)}) collective-permute-start(bf16[1,128,256]{2,1,0:T(8,128)(2,1)S(1)} %get-tuple-element.15), channel_id=1, source_target_pairs={{1,0},{2,1},{3,2},{5,4},{6,5},{7,6},{9,8},{10,9},{11,10},{13,12},{... | collective-permute-start | bytes 196616 | tf_op jit(solution)/shard_map/ppermute | solution.py:19
  212.9 12.0 %collective-permute-start.12 = (bf16[1,128,256]{2,1,0:T(8,128)(2,1)}, bf16[1,128,256]{2,1,0:T(8,128)(2,1)S(1)}, u32[]{:S(2)}, u32[]{:S(2)}) collective-permute-start(bf16[1,128,256]{2,1,0:T(8,128)(2,1)} %get-tuple-element.8), channel_id=1, source_target_pairs={{0,4},{4,8},{8,12},{12,16},{16,20},{20,24},{24,28},{1,5},{5,9},{9,... | collective-permute-start | bytes 196616 | tf_op jit(solution)/shard_map/ppermute | solution.py:17
  217.4 7.5 %collective-permute-start.14 = (bf16[1,128,256]{2,1,0:T(8,128)(2,1)}, bf16[1,128,256]{2,1,0:T(8,128)(2,1)S(1)}, u32[]{:S(2)}, u32[]{:S(2)}) collective-permute-start(bf16[1,128,256]{2,1,0:T(8,128)(2,1)} %get-tuple-element.9), channel_id=1, source_target_pairs={{0,1},{1,2},{2,3},{4,5},{5,6},{6,7},{8,9},{9,10},{10,11},{12,13},{... | collective-permute-start | bytes 196616 | tf_op jit(solution)/shard_map/ppermute | solution.py:17
  219.7 7.3 %collective-permute-start.13 = (bf16[1,128,256]{2,1,0:T(8,128)(2,1)}, bf16[1,128,256]{2,1,0:T(8,128)(2,1)S(1)}, u32[]{:S(2)}, u32[]{:S(2)}) collective-permute-start(bf16[1,128,256]{2,1,0:T(8,128)(2,1)} %get-tuple-element.10), channel_id=1, source_target_pairs={{4,0},{8,4},{12,8},{16,12},{20,16},{24,20},{28,24},{5,1},{9,5},{13... | collective-permute-start | bytes 196616 | tf_op jit(solution)/shard_map/ppermute | solution.py:19
  221.0 6.6 %collective-permute-start.15 = (bf16[1,128,256]{2,1,0:T(8,128)(2,1)S(1)}, bf16[1,128,256]{2,1,0:T(8,128)(2,1)}, u32[]{:S(2)}, u32[]{:S(2)}) collective-permute-start(bf16[1,128,256]{2,1,0:T(8,128)(2,1)S(1)} %get-tuple-element.11), channel_id=1, source_target_pairs={{1,0},{2,1},{3,2},{5,4},{6,5},{7,6},{9,8},{10,9},{11,10},{13,12},{... | collective-permute-start | bytes 196616 | tf_op jit(solution)/shard_map/ppermute | solution.py:19
  224.9 2.1 copy-start.4
  227.0 0.6 copy-start.5
where the time goes:
time: 244 us; the launch traced here: 241 us
  blocking collectives  109 us (45%)
  local copies, waits for them, and re-layouts  38.5 us (16%)
  starting transfers between devices  31.3 us (13%)
  other arithmetic  25.7 us (11%)
  matrix products  23.6 us (10%)
  waiting for transfers between devices  12.2 us (5%)
    psum x2, blocking collectives, per_device(): summed = lax.psum(partial_sum, 'row')  96 us
    ppermute x8, starting transfers between devices, padded(): lax.ppermute(tail, axis, [(i, (i + 1) % count) for i in range(ends)])  20.9 us
    scatter-add x4, other arithmetic, apply_operator(): jnp.zeros(vector.shape, jnp.float32).at[flat_rows].add(coupling_terms)  18.5 us
    all_gather x2, blocking collectives, per_device(): lax.all_gather(restricted, 'col', axis=0, tiled=True)  12.9 us
    ppermute x8, waiting for transfers between devices, padded(): lax.ppermute(head, axis, [((i + 1) % count, i) for i in range(ends)])  12.2 us
    gather x4, local copies, waits for them, and re-layouts, neighbour_faces(): face_vals = vector_b[face_index]  10.6 us
    ppermute x8, starting transfers between devices, padded(): lax.ppermute(head, axis, [((i + 1) % count, i) for i in range(ends)])  10.3 us
    scatter-add x4, local copies, waits for them, and re-layouts, apply_operator(): jnp.zeros(vector.shape, jnp.float32).at[flat_rows].add(coupling_terms)  10.2 us
  transfers between devices with their start and end apart: 16, of which 4 were waited for; matrix products, arithmetic and copies ran while one was open for 2% of the time, Pallas kernels for 0%

commit v1 on v0

v1 whole, which is shorter than its diff:
```python
import functools

import jax
import jax.numpy as jnp
from jax import lax
from jax.experimental import pallas as pl
from jax.experimental.pallas import tpu as pltpu
from jax.sharding import PartitionSpec as P

STEPS = 2
BF = jnp.bfloat16
F32 = jnp.float32
VMEM = pl.BlockSpec(memory_space=pltpu.VMEM)
LIMIT = 24 << 20


def mm(a, b):
    return jnp.dot(a, b, preferred_element_type=F32)


def mm_tn(a, b):
    return lax.dot_general(a, b, (((0,), (0,)), ((), ())), preferred_element_type=F32)


def mm_nt(a, b):
    return lax.dot_general(a, b, (((1,), (1,)), ((), ())), preferred_element_type=F32)


def call(kernel, outs, *args, name, scratch=(), flops=0):
    nbytes = sum(a.size * a.dtype.itemsize for a in args)
    return pl.pallas_call(
        kernel,
        out_shape=[jax.ShapeDtypeStruct(s, d) for s, d in outs],
        in_specs=[VMEM] * len(args),
        out_specs=[VMEM] * len(outs),
        scratch_shapes=list(scratch),
        compiler_params=pltpu.CompilerParams(vmem_limit_bytes=LIMIT),
        cost_estimate=pl.CostEstimate(flops=flops, bytes_accessed=nbytes, transcendentals=0),
        name=name,
    )(*args)


def tiles(rows):
    return 256 if rows % 256 == 0 else rows


def per_device(nr, nc, rhs, local_mat, local_inv, basis_t, coarse_inv, couple, margin_rows):
    nloc, nrhs = rhs.shape
    cpd = basis_t.shape[0]
    ovl = margin_rows.shape[2]
    nf = 4 * ovl
    nz = nr // 2
    both = ("row", "col")

    def pairs(row_parity, col_parity):
        perm = {}
        for r in range(nr):
            for c in range(nc):
                if row_parity is not None:
                    o = r + 1 if r % 2 == row_parity else r - 1
                    other = (o, c) if 0 <= o < nr else (r, c ^ 1)
                else:
                    o = c + 1 if c % 2 == col_parity else c - 1
                    other = (r, o) if 0 <= o < nc else (r ^ 1, c)
                perm[r * nc + c] = other[0] * nc + other[1]
        return sorted(perm.items())

    slot_perms = [pairs(1, None), pairs(None, 1), pairs(0, None), pairs(None, 0)]

    def slot_faces():
        r, c = lax.axis_index("row"), lax.axis_index("col")
        pr, pc = lax.rem(r, 2), lax.rem(c, 2)
        one = lambda ok: jnp.where(ok, 1.0, 0.0).astype(F32)
        return [
            (pr, one((pr == 1) & (r + 1 < nr) | (pr == 0) & (r > 0))),
            (2 + pc, one((pc == 1) & (c + 1 < nc) | (pc == 0) & (c > 0))),
            (1 - pr, one((pr == 1) | (r + 1 < nr))),
            (3 - pc, one((pc == 1) | (c + 1 < nc))),
        ]

    def halo(faces):
        return [lax.ppermute(f, both, p) for f, p in zip(faces, slot_perms)]

    def k_setup(rows_ref, couple_ref, inv_ref, basis_ref, sel_ref, wt_ref, bf_ref, t_ref, m_ref, f_ref):
        for s, (k, ok) in enumerate(slot_faces()):
            row = rows_ref[0, pl.ds(k, 1), :]
            w = couple_ref[0, pl.ds(k, 1), :] * ok
            at = pl.ds(s * ovl, ovl)
            down = lax.broadcasted_iota(jnp.int32, (nloc, ovl), 0)
            wt_ref[:, at] = jnp.where(down == row, jnp.broadcast_to(w, (nloc, ovl)), 0.0).astype(BF)
            idx = jnp.broadcast_to(row.astype(F32), (ovl, ovl)).T
            for j in range(nloc // ovl):
                across = lax.broadcasted_iota(jnp.int32, (ovl, ovl), 1) + j * ovl
                sel_ref[at, pl.ds(j * ovl, ovl)] = jnp.where(idx == across.astype(F32), 1.0, 0.0).astype(BF)
        bf_ref[...] = mm_nt(sel_ref[...], basis_ref[...]).astype(BF)
        t_ref[...] = mm(basis_ref[...], wt_ref[...]).astype(BF)
        step = tiles(nloc)

        @pl.loop(0, nloc // step)
        def _(i):
            at = pl.ds(pl.multiple_of(i * step, step), step)
            m_ref[at, :] = mm(inv_ref[at, :], wt_ref[...]).astype(BF)

        f_ref[...] = mm(sel_ref[...], m_ref[...]).astype(BF)

    sel, wt, bfac, tmat, mmat, fmat = call(
        k_setup,
        [((nf, nloc), BF), ((nloc, nf), BF), ((nf, cpd), BF), ((cpd, nf), BF), ((nloc, nf), BF), ((nf, nf), BF)],
        margin_rows, couple, local_inv, basis_t, name="setup", flops=2 * nloc * nf * (nloc + nf),
    )

    def k_restrict(rhs_ref, basis_ref, out_ref):
        out_ref[...] = mm(basis_ref[...], rhs_ref[...].astype(BF)).astype(BF)

    def k_coarse(*refs):
        blocks, (inv_ref, keep_ref, send_ref, group, prod) = refs[:nc], refs[nc:]
        r, c = lax.axis_index("row"), lax.axis_index("col")
        for i, block in enumerate(blocks):
            group[pl.ds(pl.multiple_of((c ^ i) * cpd, 16), cpd), :] = block[...]
        prod[...] = mm(inv_ref[...], group[...])
        for i in range(nz):
            for ref, m in ((keep_ref, 2 * i), (send_ref, 2 * i + 1)):
                src = pl.ds(pl.multiple_of((r ^ m) * cpd, 8), cpd)
                ref[pl.ds(i * cpd, cpd), :] = prod[src, :].astype(ref.dtype)

    def k_half(keep_ref, recv_ref, own_ref, *sends):
        own_ref[...] = keep_ref[pl.ds(0, cpd), :] + recv_ref[pl.ds(0, cpd), :].astype(F32)
        for i, ref in enumerate(sends):
            at = pl.ds((i + 1) * cpd, cpd)
            ref[...] = (keep_ref[at, :] + recv_ref[at, :].astype(F32)).astype(BF)

    def coarse_parts(restricted):
        blocks = [restricted] + [
            lax.ppermute(restricted, "col", [(i, i ^ k) for i in range(nc)]) for k in range(1, nc)
        ]
        keep, send = call(
            k_coarse, [((nz * cpd, nrhs), F32), ((nz * cpd, nrhs), BF)], *blocks, coarse_inv,
            scratch=[pltpu.VMEM((nc * cpd, nrhs), BF), pltpu.VMEM((nr * cpd, nrhs), F32)],
            name="coarse", flops=2 * nr * cpd * nc * cpd * nrhs,
        )
        recv = lax.ppermute(send, "row", [(i, i ^ 1) for i in range(nr)])
        own, *sends = call(
            k_half, [((cpd, nrhs), F32)] + [((cpd, nrhs), BF)] * (nz - 1), keep, recv, name="half",
        )
        recvs = [
            lax.ppermute(s, "row", [(i, i ^ (2 * (k + 1))) for i in range(nr)]) for k, s in enumerate(sends)
        ]
        return [own] + recvs

    def k_coarse_faces(*refs):
        parts, (bf_ref, y_ref), faces = refs[:nz], refs[nz : nz + 2], refs[nz + 2 :]
        total = parts[0][...]
        for p in parts[1:]:
            total = total + p[...].astype(F32)
        y = total.astype(BF)
        y_ref[...] = y
        for s, ref in enumerate(faces):
            ref[...] = mm(bf_ref[pl.ds(s * ovl, ovl), :], y).astype(BF)

    def coarse_faces(parts):
        y, *faces = call(
            k_coarse_faces, [((cpd, nrhs), BF)] + [((ovl, nrhs), BF)] * 4, *parts, bfac, name="coarse_faces",
        )
        return y, faces

    step = tiles(nloc)

    def row_loop(body):
        @pl.loop(0, nloc // step)
        def _(i):
            body(pl.ds(pl.multiple_of(i * step, step), step))

    def k_local(first, y_ref, basis_ref, base_ref, old_ref, mat_ref, inv_ref, sel_ref, sol_ref, face_ref, vb, wb):
        def corr_tile(at):
            corr = mm_tn(basis_ref[:, at], y_ref[...])
            vb[at, :] = corr.astype(BF)
            sol_ref[at, :] = corr if first else old_ref[at, :] + corr

        for i in range(nloc // step):
            corr_tile(pl.ds(i * step, step))

        def res_tile(at):
            wb[at, :] = (base_ref[at, :] - mm(mat_ref[at, :], vb[...])).astype(BF)

        row_loop(res_tile)

        def sol_tile(at):
            sol = sol_ref[at, :] + mm(inv_ref[at, :], wb[...])
            sol_ref[at, :] = sol
            vb[at, :] = sol.astype(BF)

        row_loop(sol_tile)
        face_ref[...] = mm(sel_ref[...], vb[...])

    def local(y, base, old, first):
        args = (y, basis_t, base) + (() if first else (old,)) + (local_mat, local_inv, sel)
        body = functools.partial(k_local, first)
        if first:
            kernel = lambda a, b, c, *rest: body(a, b, c, None, *rest)
        else:
            kernel = body
        return call(
            kernel, [((nloc, nrhs), F32), ((nf, nrhs), F32)], *args,
            scratch=[pltpu.VMEM((nloc, nrhs), BF)] * 2, name="local", flops=5 * nloc * nloc * nrhs,
        )

    def k_faces(base_ref, f_ref, *refs):
        recvs, faces = refs[:4], refs[4:]
        recv = jnp.concatenate([x[...] for x in recvs], axis=0)
        for s, ref in enumerate(faces):
            at = pl.ds(s * ovl, ovl)
            ref[...] = (base_ref[at, :] + mm(f_ref[at, :], recv)).astype(BF)

    def faces_after(base, recv):
        return call(k_faces, [((ovl, nrhs), BF)] * 4, base, fmat, *recv, name="faces", flops=2 * nf * nf * nrhs)

    def k_advance(restrict, sol_ref, m_ref, rhs_ref, mat_ref, basis_ref, *refs):
        recvs, (new_ref, res_ref), rest = refs[:4], refs[4:6], refs[6:]
        recv, vb = rest[-2:]
        for s, x in enumerate(recvs):
            recv[pl.ds(s * ovl, ovl), :] = x[...]

        def sol_tile(at):
            new = sol_ref[at, :] + mm(m_ref[at, :], recv[...])
            new_ref[at, :] = new
            vb[at, :] = new.astype(BF)

        row_loop(sol_tile)

        def res_tile(at):
            res_ref[at, :] = rhs_ref[at, :] - mm(mat_ref[at, :], vb[...])

        row_loop(res_tile)
        if restrict:
            rest[0][...] = mm(basis_ref[...], res_ref[...].astype(BF))

    def advance(sol, recv, restrict):
        outs = [((nloc, nrhs), F32)] * 2 + ([((cpd, nrhs), F32)] if restrict else [])
        return call(
            functools.partial(k_advance, restrict), outs, sol, mmat, rhs, local_mat, basis_t, *recv,
            scratch=[pltpu.VMEM((nf, nrhs), BF), pltpu.VMEM((nloc, nrhs), BF)],
            name="advance", flops=3 * nloc * nloc * nrhs,
        )

    def k_restrict_recv(base_ref, t_ref, *refs):
        recvs, out_ref = refs[:4], refs[4]
        recv = jnp.concatenate([x[...] for x in recvs], axis=0)
        out_ref[...] = (base_ref[...] + mm(t_ref[...], recv)).astype(BF)

    def k_couple(res_ref, wt_ref, *refs):
        recvs, out_ref, recv = refs[:4], refs[4], refs[5]
        for s, x in enumerate(recvs):
            recv[pl.ds(s * ovl, ovl), :] = x[...]

        def tile(at):
            out_ref[at, :] = res_ref[at, :] + mm(wt_ref[at, :], recv[...])

        row_loop(tile)

    def coupled(res, recv):
        return call(
            k_couple, [((nloc, nrhs), F32)], res, wt, *recv,
            scratch=[pltpu.VMEM((nf, nrhs), BF)], name="couple", flops=2 * nloc * nf * nrhs,
        )[0]

    (restricted,) = call(k_restrict, [((cpd, nrhs), BF)], rhs, basis_t, name="restrict")
    residual, solution = rhs, None
    for sweep in range(STEPS):
        y, faces = coarse_faces(coarse_parts(restricted))
        recv = halo(faces)
        partial, face_base = local(y, residual, solution, sweep == 0)
        recv2 = halo(faces_after(face_base, recv))
        last = sweep == STEPS - 1
        if last:
            solution, res = advance(partial, recv, False)
        else:
            solution, res, restr = advance(partial, recv, True)
            (restricted,) = call(
                k_restrict_recv, [((cpd, nrhs), BF)], restr, tmat, *recv2, name="restrict_recv",
            )
        residual = coupled(res, recv2)
    return (solution, residual)


def solution(mesh):
    nr, nc = mesh.shape["row"], mesh.shape["col"]
    placed = (
        P(("row", "col"), None),
        P(("row", "col"), None),
        P(("row", "col"), None),
        P(("row", "col"), None),
        P("col", "row"),
        P(("row", "col"), None, None),
        P(("row", "col"), None, None),
    )
    return jax.shard_map(
        functools.partial(per_device, nr, nc),
        mesh=mesh,
        in_specs=placed,
        out_specs=(P(("row", "col"), None), P(("row", "col"), None)),
        check_vma=False,
    )
```

time: 244 us -> 80.6 us (0.33); the launches traced: 241 us -> 80.4 us
  blocking collectives: 109 us -> 0 us
  local copies, waits for them, and re-layouts: 38.5 us -> 4.74 us
  other arithmetic: 25.7 us -> 0 us
  matrix products: 23.6 us -> 0 us
  Pallas kernels: 0 us -> 20.2 us
  waiting for transfers between devices: 12.2 us -> 25 us
    psum x2 -> x0, blocking collectives: 96 us -> none  [per_device(): summed = lax.psum(partial_sum, 'row')]
    dot_general x9 -> x0, matrix products: 23.6 us -> none  [the longest x2 9.72 us: per_device(): jnp.dot(local_inv, residual.astype(jnp.bfloat16), preferred_element_type=...]
    pallas_call x0 -> x17, Pallas kernels: none -> 20.2 us  [call(): pl.pallas_call(kernel, out_shape=[jax.ShapeDtypeStruct(s, d) for s, d in...]
    scatter-add x4 -> x0, other arithmetic: 18.5 us -> none  [apply_operator(): jnp.zeros(vector.shape, jnp.float32).at[flat_rows].add(coupling_terms)]
    all_gather x2 -> x0, blocking collectives: 12.9 us -> none  [per_device(): lax.all_gather(restricted, 'col', axis=0, tiled=True)]
    ppermute x16 -> x30, waiting for transfers between devices: 12.2 us -> 25 us  [the longest x2 10.5 us: coarse_parts(): recv = lax.ppermute(send, 'row', [(i, i ^ 1) for i in range(nr)])]
    gather x4 -> x0, local copies, waits for them, and re-layouts: 10.6 us -> none  [neighbour_faces(): face_vals = vector_b[face_index]]
    scatter-add x4 -> x0, local copies, waits for them, and re-layouts: 10.2 us -> none  [apply_operator(): jnp.zeros(vector.shape, jnp.float32).at[flat_rows].add(coupling_terms)]
  transfers between devices with their start and end apart: 16 -> 30, of which waited for: 4 -> 13; matrix products, arithmetic and copies ran while one was open for 2% -> 0% of each run, Pallas kernels for 0% -> 20%
where the time goes in v1:
time: 80.6 us; the launch traced here: 80.4 us
  starting transfers between devices  29.6 us (37%)
  waiting for transfers between devices  25 us (31%)
  Pallas kernels  20.2 us (25%)
  local copies, waits for them, and re-layouts  4.74 us (6%)
  between operations  0.87 us (1%)
    pallas_call x17, Pallas kernels, call(): pl.pallas_call(kernel, out_shape=[jax.ShapeDtypeStruct(s, d) for s, d in...  20.2 us
    ppermute x16, starting transfers between devices, halo(): return [lax.ppermute(f, both, p) for f, p in zip(faces, slot_perms)]  12.6 us
    ppermute x2, waiting for transfers between devices, coarse_parts(): recv = lax.ppermute(send, 'row', [(i, i ^ 1) for i in range(nr)])  10.5 us
    ppermute x6, starting transfers between devices, coarse_parts(): lax.ppermute(s, 'row', [(i, i ^ 2 * (k + 1)) for i in range(nr)])  8.9 us
    ppermute x6, waiting for transfers between devices, coarse_parts(): lax.ppermute(restricted, 'col', [(i, i ^ k) for i in range(nc)])  6.35 us
    ppermute x6, starting transfers between devices, coarse_parts(): lax.ppermute(restricted, 'col', [(i, i ^ k) for i in range(nc)])  5.07 us
    unnamed x20, local copies, waits for them, and re-layouts  4.74 us
    ppermute x6, waiting for transfers between devices, coarse_parts(): lax.ppermute(s, 'row', [(i, i ^ 2 * (k + 1)) for i in range(nr)])  4.56 us
  transfers between devices with their start and end apart: 30, of which 13 were waited for; matrix products, arithmetic and copies ran while one was open for 0% of the time, Pallas kernels for 20%

profile of v1, /device:TPU:0, one launch (start us, length us, event | category | flops | bytes accessed | tf_op | source)
XLA Modules:
  0.0 80.4 jit_solution(16299837124450963373)
XLA Ops:
  0.6 1.2 %copy-done.1 = f32[1024,256]{1,0:T(8,128)S(1)} copy-done((f32[1024,256]{1,0:T(8,128)S(1)}, f32[1024,256]{1,0:T(8,128)}, u32[]{:S(2)}) %copy-start.1) | copy-done | bytes 1048600
  1.9 0.9 %copy-done.4 = bf16[96,1024]{1,0:T(8,128)(2,1)S(1)} copy-done((bf16[96,1024]{1,0:T(8,128)(2,1)S(1)}, bf16[96,1024]{1,0:T(8,128)(2,1)}, u32[]{:S(2)}) %copy-start.4) | copy-done | bytes 196632
  3.0 2.5 %collective-permute-start.2 = (bf16[96,256]{1,0:T(8,128)(2,1)S(1)}, bf16[96,256]{1,0:T(8,128)(2,1)S(1)}, u32[]{:S(2)}, u32[]{:S(2)}) collective-permute-start(bf16[96,256]{1,0:T(8,128)(2,1)S(1)} %restrict.1.refs_0_), channel_id=1, source_target_pairs={{0,3},{1,2},{2,1},{3,0},{4,7},{5,6},{6,5},{7,4},{8,11},{9,10},{10,... | collective-permute-start | bytes 147464 | tf_op jit(solution)/shard_map/ppermute | solution.py:134
  5.5 0.6 collective-permute-start.1
  6.2 1.5 %collective-permute-done.2.refs_3_ = bf16[96,256]{1,0:T(8,128)(2,1)S(1)} collective-permute-done((bf16[96,256]{1,0:T(8,128)(2,1)S(1)}, bf16[96,256]{1,0:T(8,128)(2,1)S(1)}, u32[]{:S(2)}, u32[]{:S(2)}) %collective-permute-start.2) | collective-permute-done | bytes 49184 | tf_op jit(solution)/shard_map/ppermute | solution.py:134
  7.6 2.2 %collective-permute-done.1.refs_2_ = bf16[96,256]{1,0:T(8,128)(2,1)S(1)} collective-permute-done((bf16[96,256]{1,0:T(8,128)(2,1)S(1)}, bf16[96,256]{1,0:T(8,128)(2,1)S(1)}, u32[]{:S(2)}, u32[]{:S(2)}) %collective-permute-start.1) | collective-permute-done | bytes 49184 | tf_op jit(solution)/shard_map/ppermute | solution.py:134
  9.8 1.1 %copy-done.6 = bf16[768,384]{1,0:T(8,128)(2,1)S(1)} copy-done((bf16[768,384]{1,0:T(8,128)(2,1)S(1)}, bf16[768,384]{1,0:T(8,128)(2,1)}, u32[]{:S(2)}) %copy-start.6) | copy-done | bytes 589848
  10.9 0.4 coarse.2
  11.3 1.6 %collective-permute-start.3 = (bf16[384,256]{1,0:T(8,128)(2,1)S(1)}, bf16[384,256]{1,0:T(8,128)(2,1)S(1)}, u32[]{:S(2)}, u32[]{:S(2)}) collective-permute-start(bf16[384,256]{1,0:T(8,128)(2,1)S(1)} %get-tuple-element.48), channel_id=1, source_target_pairs={{0,4},{4,0},{8,12},{12,8},{16,20},{20,16},{24,28},{28,24},{1,5},{5... | collective-permute-start | bytes 589832 | tf_op jit(solution)/shard_map/ppermute | solution.py:141
  12.9 5.1 %collective-permute-done.3.recv_ref = bf16[384,256]{1,0:T(8,128)(2,1)S(1)} collective-permute-done((bf16[384,256]{1,0:T(8,128)(2,1)S(1)}, bf16[384,256]{1,0:T(8,128)(2,1)S(1)}, u32[]{:S(2)}, u32[]{:S(2)}) %collective-permute-start.3) | collective-permute-done | bytes 196640 | tf_op jit(solution)/shard_map/ppermute | solution.py:141
  18.0 1.6 %collective-permute-start.4 = (bf16[96,256]{1,0:T(8,128)(2,1)S(1)}, bf16[96,256]{1,0:T(8,128)(2,1)S(1)}, u32[]{:S(2)}, u32[]{:S(2)}) collective-permute-start(bf16[96,256]{1,0:T(8,128)(2,1)S(1)} %get-tuple-element.50), channel_id=1, source_target_pairs={{0,8},{4,12},{8,0},{12,4},{16,24},{20,28},{24,16},{28,20},{1,9},{5... | collective-permute-start | bytes 147464 | tf_op jit(solution)/shard_map/ppermute | solution.py:146
  19.7 2.6 %collective-permute-start.5 = (bf16[96,256]{1,0:T(8,128)(2,1)S(1)}, bf16[96,256]{1,0:T(8,128)(2,1)S(1)}, u32[]{:S(2)}, u32[]{:S(2)}) collective-permute-start(bf16[96,256]{1,0:T(8,128)(2,1)S(1)} %get-tuple-element.51), channel_id=1, source_target_pairs={{0,16},{4,20},{8,24},{12,28},{16,0},{20,4},{24,8},{28,12},{1,17},{... | collective-permute-start | bytes 147464 | tf_op jit(solution)/shard_map/ppermute | solution.py:146
  22.5 0.8 %copy-done.8 = s32[1,4,128]{2,1,0:T(4,128)S(1)} copy-done((s32[1,4,128]{2,1,0:T(4,128)S(1)}, s32[1,4,128]{2,1,0:T(4,128)}, u32[]{:S(2)}) %copy-start.8) | copy-done | bytes 2072
  23.3 0.7 copy-done.9
  24.0 3.3 %setup.1 = (bf16[512,1024]{1,0:T(8,128)(2,1)S(1)}, bf16[1024,512]{1,0:T(8,128)(2,1)S(1)}, bf16[512,96]{1,0:T(8,128)(2,1)S(1)}, bf16[96,512]{1,0:T(8,128)(2,1)S(1...) custom-call(s32[1,4,128]{2,1,0:T(4,128)S(1)} %copy-done.8, f32[1,4,128]{2,1,0:T(4,128)S(1)} %copy-done.9, ...), custom_call_target="tpu_custom_call" | custom-call | flops 1610612736 | bytes 2297856 | tf_op jit(solution)/shard_map/setup/pallas_call | solution.py:31
  27.4 0.8 %collective-permute-done.6.refs_3_ = bf16[96,256]{1,0:T(8,128)(2,1)S(1)} collective-permute-done((bf16[96,256]{1,0:T(8,128)(2,1)S(1)}, bf16[96,256]{1,0:T(8,128)(2,1)S(1)}, u32[]{:S(2)}, u32[]{:S(2)}) %collective-permute-start.6) | collective-permute-done | bytes 49184 | tf_op jit(solution)/shard_map/ppermute | solution.py:146
  28.2 0.2 coarse_faces.2
  28.5 1.6 %collective-permute-start.8 = (bf16[128,256]{1,0:T(8,128)(2,1)S(1)}, bf16[128,256]{1,0:T(8,128)(2,1)S(1)}, u32[]{:S(2)}, u32[]{:S(2)}) collective-permute-start(bf16[128,256]{1,0:T(8,128)(2,1)S(1)} %get-tuple-element.59), channel_id=1, source_target_pairs={{0,4},{1,2},{2,1},{3,7},{4,0},{5,6},{6,5},{7,3},{8,12},{9,10},{10,... | collective-permute-start | bytes 196616 | tf_op jit(solution)/shard_map/ppermute | solution.py:82
  30.1 0.5 collective-permute-start.9
  30.6 0.9 %collective-permute-start.10 = (bf16[128,256]{1,0:T(8,128)(2,1)S(1)}, bf16[128,256]{1,0:T(8,128)(2,1)S(1)}, u32[]{:S(2)}, u32[]{:S(2)}) collective-permute-start(bf16[128,256]{1,0:T(8,128)(2,1)S(1)} %get-tuple-element.61), channel_id=1, source_target_pairs={{0,1},{1,0},{2,3},{3,2},{4,5},{5,4},{6,7},{7,6},{8,9},{9,8},{10,11... | collective-permute-start | bytes 196616 | tf_op jit(solution)/shard_map/ppermute | solution.py:82
  31.5 3.2 %local.2 = (f32[1024,256]{1,0:T(8,128)S(1)}, f32[512,256]{1,0:T(8,128)S(1)}) custom-call(bf16[96,256]{1,0:T(8,128)(2,1)S(1)} %get-tuple-element.54.a, bf16[96,1024]{1,0:T(8,128)(2,1)S(1)} %copy-done.5, f32[1024,256]{1,0:T(8,128)S(1)} %copy-done.2, bf16[1024,1024]{1,0:T(8,128)(2,1)S(1)} %copy-done, bf16[1024,1024]{1,0:T(8,128)(2,1)S(1)} %copy-done.3, ...), custom_call_target="tpu_custom_call" | custom-call | flops 1342177280 | bytes 6537216 | tf_op jit(solution)/shard_map/local/pallas_call | solution.py:31
  34.8 0.3 faces.2
  35.2 3.7 %collective-permute-start.12 = (bf16[128,256]{1,0:T(8,128)(2,1)S(1)}, bf16[128,256]{1,0:T(8,128)(2,1)S(1)}, u32[]{:S(2)}, u32[]{:S(2)}) collective-permute-start(bf16[128,256]{1,0:T(8,128)(2,1)S(1)} %get-tuple-element.67), channel_id=1, source_target_pairs={{0,4},{1,2},{2,1},{3,7},{4,0},{5,6},{6,5},{7,3},{8,12},{9,10},{10,... | collective-permute-start | bytes 196616 | tf_op jit(solution)/shard_map/ppermute | solution.py:82
  39.0 2.4 %advance.2 = (f32[1024,256]{1,0:T(8,128)S(1)}, f32[1024,256]{1,0:T(8,128)S(1)}, f32[96,256]{1,0:T(8,128)S(1)}) custom-call(f32[1024,256]{1,0:T(8,128)S(1)} %get-tuple-element.56.sol_ref, bf16[1024,512]{1,0:T(8,128)(2,1)S(1)} %get-tuple-element.57.m_ref, f32[1024,256]{1,0:T(8,128)S(1)} %copy-done.2, bf16[1024,1024]{1,0:T(8,128)(2,1)S(1)} %copy-done, ...), custom_call_target="tpu_custom_call" | custom-call | flops 805306368 | bytes 5701632 | tf_op jit(solution)/shard_map/advance/pallas_call | solution.py:31
  41.6 1.6 %collective-permute-done.13.refs_2_ = bf16[128,256]{1,0:T(8,128)(2,1)S(1)} collective-permute-done((bf16[128,256]{1,0:T(8,128)(2,1)S(1)}, bf16[128,256]{1,0:T(8,128)(2,1)S(1)}, u32[]{:S(2)}, u32[]{:S(2)}) %collective-permute-start.13) | collective-permute-done | bytes 65568 | tf_op jit(solution)/shard_map/ppermute | solution.py:82
  43.4 0.3 collective-permute-start.16
  43.8 1.5 %collective-permute-start.15 = (bf16[96,256]{1,0:T(8,128)(2,1)S(1)}, bf16[96,256]{1,0:T(8,128)(2,1)S(1)}, u32[]{:S(2)}, u32[]{:S(2)}) collective-permute-start(bf16[96,256]{1,0:T(8,128)(2,1)S(1)} %restrict_recv.1.refs_0_), channel_id=1, source_target_pairs={{0,1},{1,0},{2,3},{3,2},{4,5},{5,4},{6,7},{7,6},{8,9},{9,8},{10,11... | collective-permute-start | bytes 147464 | tf_op jit(solution)/shard_map/ppermute | solution.py:134
  45.3 1.7 %collective-permute-done.17.refs_3_ = bf16[96,256]{1,0:T(8,128)(2,1)S(1)} collective-permute-done((bf16[96,256]{1,0:T(8,128)(2,1)S(1)}, bf16[96,256]{1,0:T(8,128)(2,1)S(1)}, u32[]{:S(2)}, u32[]{:S(2)}) %collective-permute-start.17) | collective-permute-done | bytes 49184 | tf_op jit(solution)/shard_map/ppermute | solution.py:134
  46.9 1.1 %collective-permute-done.16.refs_2_ = bf16[96,256]{1,0:T(8,128)(2,1)S(1)} collective-permute-done((bf16[96,256]{1,0:T(8,128)(2,1)S(1)}, bf16[96,256]{1,0:T(8,128)(2,1)S(1)}, u32[]{:S(2)}, u32[]{:S(2)}) %collective-permute-start.16) | collective-permute-done | bytes 49184 | tf_op jit(solution)/shard_map/ppermute | solution.py:134
  48.0 0.4 coarse.3
  48.4 1.5 %collective-permute-start.18 = (bf16[384,256]{1,0:T(8,128)(2,1)S(1)}, bf16[384,256]{1,0:T(8,128)(2,1)S(1)}, u32[]{:S(2)}, u32[]{:S(2)}) collective-permute-start(bf16[384,256]{1,0:T(8,128)(2,1)S(1)} %get-tuple-element.71), channel_id=1, source_target_pairs={{0,4},{4,0},{8,12},{12,8},{16,20},{20,16},{24,28},{28,24},{1,5},{5... | collective-permute-start | bytes 589832 | tf_op jit(solution)/shard_map/ppermute | solution.py:141
  49.9 5.4 %collective-permute-done.18.recv_ref = bf16[384,256]{1,0:T(8,128)(2,1)S(1)} collective-permute-done((bf16[384,256]{1,0:T(8,128)(2,1)S(1)}, bf16[384,256]{1,0:T(8,128)(2,1)S(1)}, u32[]{:S(2)}, u32[]{:S(2)}) %collective-permute-start.18) | collective-permute-done | bytes 196640 | tf_op jit(solution)/shard_map/ppermute | solution.py:141
  55.3 1.7 %collective-permute-start.19 = (bf16[96,256]{1,0:T(8,128)(2,1)S(1)}, bf16[96,256]{1,0:T(8,128)(2,1)S(1)}, u32[]{:S(2)}, u32[]{:S(2)}) collective-permute-start(bf16[96,256]{1,0:T(8,128)(2,1)S(1)} %get-tuple-element.73), channel_id=1, source_target_pairs={{0,8},{4,12},{8,0},{12,4},{16,24},{20,28},{24,16},{28,20},{1,9},{5... | collective-permute-start | bytes 147464 | tf_op jit(solution)/shard_map/ppermute | solution.py:146
  57.1 1.5 %collective-permute-start.20 = (bf16[96,256]{1,0:T(8,128)(2,1)S(1)}, bf16[96,256]{1,0:T(8,128)(2,1)S(1)}, u32[]{:S(2)}, u32[]{:S(2)}) collective-permute-start(bf16[96,256]{1,0:T(8,128)(2,1)S(1)} %get-tuple-element.74), channel_id=1, source_target_pairs={{0,16},{4,20},{8,24},{12,28},{16,0},{20,4},{24,8},{28,12},{1,17},{... | collective-permute-start | bytes 147464 | tf_op jit(solution)/shard_map/ppermute | solution.py:146
  58.6 1.2 %collective-permute-start.21 = (bf16[96,256]{1,0:T(8,128)(2,1)S(1)}, bf16[96,256]{1,0:T(8,128)(2,1)S(1)}, u32[]{:S(2)}, u32[]{:S(2)}) collective-permute-start(bf16[96,256]{1,0:T(8,128)(2,1)S(1)} %get-tuple-element.75), channel_id=1, source_target_pairs={{0,24},{4,28},{8,16},{12,20},{16,8},{20,12},{24,0},{28,4},{1,25},{... | collective-permute-start | bytes 147464 | tf_op jit(solution)/shard_map/ppermute | solution.py:146
  59.8 0.9 %couple.2.base_ref = f32[1024,256]{1,0:T(8,128)S(1)} custom-call(f32[1024,256]{1,0:T(8,128)S(1)} %get-tuple-element.77.res_ref, bf16[1024,512]{1,0:T(8,128)(2,1)S(1)} %get-tuple-element.78.wt_ref, bf16[128,256]{1,0:T(8,128)(2,1)S(1)} %collective-permute-done.11.refs_0_, bf16[128,256]{1,0:T(8,128)(2,1)S(1)} %collective-permute-done.12.refs_1_, ...), custom_call_target="tpu_custom_call" | custom-call | flops 268435456 | bytes 2359296 | tf_op jit(solution)/shard_map/couple/pallas_call | solution.py:31
  60.7 2.2 %collective-permute-done.20.refs_2_ = bf16[96,256]{1,0:T(8,128)(2,1)S(1)} collective-permute-done((bf16[96,256]{1,0:T(8,128)(2,1)S(1)}, bf16[96,256]{1,0:T(8,128)(2,1)S(1)}, u32[]{:S(2)}, u32[]{:S(2)}) %collective-permute-start.20) | collective-permute-done | bytes 49184 | tf_op jit(solution)/shard_map/ppermute | solution.py:146
  62.9 1.6 %collective-permute-done.21.refs_3_ = bf16[96,256]{1,0:T(8,128)(2,1)S(1)} collective-permute-done((bf16[96,256]{1,0:T(8,128)(2,1)S(1)}, bf16[96,256]{1,0:T(8,128)(2,1)S(1)}, u32[]{:S(2)}, u32[]{:S(2)}) %collective-permute-start.21) | collective-permute-done | bytes 49184 | tf_op jit(solution)/shard_map/ppermute | solution.py:146
  64.5 0.2 coarse_faces.3
  64.8 1.0 %collective-permute-start.23 = (bf16[128,256]{1,0:T(8,128)(2,1)S(1)}, bf16[128,256]{1,0:T(8,128)(2,1)S(1)}, u32[]{:S(2)}, u32[]{:S(2)}) collective-permute-start(bf16[128,256]{1,0:T(8,128)(2,1)S(1)} %get-tuple-element.82), channel_id=1, source_target_pairs={{0,4},{1,2},{2,1},{3,7},{4,0},{5,6},{6,5},{7,3},{8,12},{9,10},{10,... | collective-permute-start | bytes 196616 | tf_op jit(solution)/shard_map/ppermute | solution.py:82
  65.7 1.1 %collective-permute-start.24 = (bf16[128,256]{1,0:T(8,128)(2,1)S(1)}, bf16[128,256]{1,0:T(8,128)(2,1)S(1)}, u32[]{:S(2)}, u32[]{:S(2)}) collective-permute-start(bf16[128,256]{1,0:T(8,128)(2,1)S(1)} %get-tuple-element.83), channel_id=1, source_target_pairs={{0,4},{1,5},{2,6},{3,7},{4,0},{5,1},{6,2},{7,3},{8,12},{9,13},{10,... | collective-permute-start | bytes 196616 | tf_op jit(solution)/shard_map/ppermute | solution.py:82
  66.9 3.2 %local.3 = (f32[1024,256]{1,0:T(8,128)S(1)}, f32[512,256]{1,0:T(8,128)S(1)}) custom-call(bf16[96,256]{1,0:T(8,128)(2,1)S(1)} %get-tuple-element.76.y_ref, bf16[96,1024]{1,0:T(8,128)(2,1)S(1)} %copy-done.5, f32[1024,256]{1,0:T(8,128)S(1)} %couple.2.base_ref, f32[1024,256]{1,0:T(8,128)S(1)} %get-tuple-element.79.old_ref, bf16[1024,1024]{1,0:T(8,128)(2,1)S(1)} %copy-done, ...), custom_call_target="tpu_custom_call" | custom-call | flops 1342177280 | bytes 7585792 | tf_op jit(solution)/shard_map/local/pallas_call | solution.py:31
  70.1 0.4 collective-permute-done.24.refs_2_
  70.5 0.3 faces.3
  71.0 3.1 %collective-permute-start.27 = (bf16[128,256]{1,0:T(8,128)(2,1)S(1)}, bf16[128,256]{1,0:T(8,128)(2,1)S(1)}, u32[]{:S(2)}, u32[]{:S(2)}) collective-permute-start(bf16[128,256]{1,0:T(8,128)(2,1)S(1)} %get-tuple-element.89), channel_id=1, source_target_pairs={{0,4},{1,2},{2,1},{3,7},{4,0},{5,6},{6,5},{7,3},{8,12},{9,10},{10,... | collective-permute-start | bytes 196616 | tf_op jit(solution)/shard_map/ppermute | solution.py:82
  74.2 2.8 %advance.3 = (f32[1024,256]{1,0:T(8,128)}, f32[1024,256]{1,0:T(8,128)S(1)}) custom-call(f32[1024,256]{1,0:T(8,128)S(1)} %get-tuple-element.80.sol_ref, bf16[1024,512]{1,0:T(8,128)(2,1)S(1)} %get-tuple-element.57.m_ref, f32[1024,256]{1,0:T(8,128)S(1)} %copy-done.2, bf16[1024,1024]{1,0:T(8,128)(2,1)S(1)} %copy-done, bf16[96,1024]{1,0:T(8,128)(2,1)S(1)} %copy-done.5, ...), custom_call_target="tpu_custom_call" | custom-call | flops 805306368 | bytes 5701632 | tf_op jit(solution)/shard_map/advance/pallas_call | solution.py:31
  77.1 1.4 %collective-permute-done.28.refs_2_ = bf16[128,256]{1,0:T(8,128)(2,1)S(1)} collective-permute-done((bf16[128,256]{1,0:T(8,128)(2,1)S(1)}, bf16[128,256]{1,0:T(8,128)(2,1)S(1)}, u32[]{:S(2)}, u32[]{:S(2)}) %collective-permute-start.28) | collective-permute-done | bytes 65568 | tf_op jit(solution)/shard_map/ppermute | solution.py:82
  78.5 1.9 %couple.3 = f32[1024,256]{1,0:T(8,128)} custom-call(f32[1024,256]{1,0:T(8,128)S(1)} %get-tuple-element.86.res_ref, bf16[1024,512]{1,0:T(8,128)(2,1)S(1)} %get-tuple-element.78.wt_ref, bf16[128,256]{1,0:T(8,128)(2,1)S(1)} %collective-permute-done.26.refs_0_, bf16[128,256]{1,0:T(8,128)(2,1)S(1)} %collective-permute-done.27.refs_1_, ...), custom_call_target="tpu_custom_call" | custom-call | flops 268435456 | bytes 2359296 | tf_op jit(solution)/shard_map/couple/pallas_call | solution.py:31
  (49 shorter events, 1.6 us)
Async XLA Ops:
  0.6 1.2 %copy-start.1 = (f32[1024,256]{1,0:T(8,128)S(1)}, f32[1024,256]{1,0:T(8,128)}, u32[]{:S(2)}) copy-start(f32[1024,256]{1,0:T(8,128)} %rhs_ref.5) | copy-start | bytes 3145732
  1.9 0.9 %copy-start.4 = (bf16[96,1024]{1,0:T(8,128)(2,1)S(1)}, bf16[96,1024]{1,0:T(8,128)(2,1)}, u32[]{:S(2)}) copy-start(bf16[96,1024]{1,0:T(8,128)(2,1)} %basis_ref.9) | copy-start | bytes 589828
  2.8 19.7 %copy-start.3 = (bf16[1024,1024]{1,0:T(8,128)(2,1)S(1)}, bf16[1024,1024]{1,0:T(8,128)(2,1)}, u32[]{:S(2)}) copy-start(bf16[1024,1024]{1,0:T(8,128)(2,1)} %inv_ref.3) | copy-start | bytes 6291460
  2.8 19.7 %copy-start.5 = (bf16[96,1024]{1,0:T(8,128)(2,1)S(1)}, bf16[96,1024]{1,0:T(8,128)(2,1)}, u32[]{:S(2)}) copy-start(bf16[96,1024]{1,0:T(8,128)(2,1)} %basis_ref.9) | copy-start | bytes 589828
  3.0 4.6 %collective-permute-start.2 = (bf16[96,256]{1,0:T(8,128)(2,1)S(1)}, bf16[96,256]{1,0:T(8,128)(2,1)S(1)}, u32[]{:S(2)}, u32[]{:S(2)}) collective-permute-start(bf16[96,256]{1,0:T(8,128)(2,1)S(1)} %restrict.1.refs_0_), channel_id=1, source_target_pairs={{0,3},{1,2},{2,1},{3,0},{4,7},{5,6},{6,5},{7,4},{8,11},{9,10},{10,... | collective-permute-start | bytes 147464 | tf_op jit(solution)/shard_map/ppermute | solution.py:134
  5.5 4.3 %collective-permute-start.1 = (bf16[96,256]{1,0:T(8,128)(2,1)S(1)}, bf16[96,256]{1,0:T(8,128)(2,1)S(1)}, u32[]{:S(2)}, u32[]{:S(2)}) collective-permute-start(bf16[96,256]{1,0:T(8,128)(2,1)S(1)} %restrict.1.refs_0_), channel_id=1, source_target_pairs={{0,2},{1,3},{2,0},{3,1},{4,6},{5,7},{6,4},{7,5},{8,10},{9,11},{10,... | collective-permute-start | bytes 147464 | tf_op jit(solution)/shard_map/ppermute | solution.py:134
  6.1 3.7 %collective-permute-start = (bf16[96,256]{1,0:T(8,128)(2,1)S(1)}, bf16[96,256]{1,0:T(8,128)(2,1)S(1)}, u32[]{:S(2)}, u32[]{:S(2)}) collective-permute-start(bf16[96,256]{1,0:T(8,128)(2,1)S(1)} %restrict.1.refs_0_), channel_id=1, source_target_pairs={{0,1},{1,0},{2,3},{3,2},{4,5},{5,4},{6,7},{7,6},{8,9},{9,8},{10,11... | collective-permute-start | bytes 147464 | tf_op jit(solution)/shard_map/ppermute | solution.py:134
  9.8 1.1 %copy-start.6 = (bf16[768,384]{1,0:T(8,128)(2,1)S(1)}, bf16[768,384]{1,0:T(8,128)(2,1)}, u32[]{:S(2)}) copy-start(bf16[768,384]{1,0:T(8,128)(2,1)} %refs_4_.3) | copy-start | bytes 1769476
  11.3 6.7 %collective-permute-start.3 = (bf16[384,256]{1,0:T(8,128)(2,1)S(1)}, bf16[384,256]{1,0:T(8,128)(2,1)S(1)}, u32[]{:S(2)}, u32[]{:S(2)}) collective-permute-start(bf16[384,256]{1,0:T(8,128)(2,1)S(1)} %get-tuple-element.48), channel_id=1, source_target_pairs={{0,4},{4,0},{8,12},{12,8},{16,20},{20,16},{24,28},{28,24},{1,5},{5... | collective-permute-start | bytes 589832 | tf_op jit(solution)/shard_map/ppermute | solution.py:141
  18.0 9.3 %collective-permute-start.4 = (bf16[96,256]{1,0:T(8,128)(2,1)S(1)}, bf16[96,256]{1,0:T(8,128)(2,1)S(1)}, u32[]{:S(2)}, u32[]{:S(2)}) collective-permute-start(bf16[96,256]{1,0:T(8,128)(2,1)S(1)} %get-tuple-element.50), channel_id=1, source_target_pairs={{0,8},{4,12},{8,0},{12,4},{16,24},{20,28},{24,16},{28,20},{1,9},{5... | collective-permute-start | bytes 147464 | tf_op jit(solution)/shard_map/ppermute | solution.py:146
  19.7 7.7 %collective-permute-start.5 = (bf16[96,256]{1,0:T(8,128)(2,1)S(1)}, bf16[96,256]{1,0:T(8,128)(2,1)S(1)}, u32[]{:S(2)}, u32[]{:S(2)}) collective-permute-start(bf16[96,256]{1,0:T(8,128)(2,1)S(1)} %get-tuple-element.51), channel_id=1, source_target_pairs={{0,16},{4,20},{8,24},{12,28},{16,0},{20,4},{24,8},{28,12},{1,17},{... | collective-permute-start | bytes 147464 | tf_op jit(solution)/shard_map/ppermute | solution.py:146
  22.3 9.2 %copy-start = (bf16[1024,1024]{1,0:T(8,128)(2,1)S(1)}, bf16[1024,1024]{1,0:T(8,128)(2,1)}, u32[]{:S(2)}) copy-start(bf16[1024,1024]{1,0:T(8,128)(2,1)} %mat_ref.5) | copy-start | bytes 6291460
  22.3 9.2 %copy-start.2 = (f32[1024,256]{1,0:T(8,128)S(1)}, f32[1024,256]{1,0:T(8,128)}, u32[]{:S(2)}) copy-start(f32[1024,256]{1,0:T(8,128)} %rhs_ref.5) | copy-start | bytes 3145732
  22.3 5.9 %collective-permute-start.6 = (bf16[96,256]{1,0:T(8,128)(2,1)S(1)}, bf16[96,256]{1,0:T(8,128)(2,1)S(1)}, u32[]{:S(2)}, u32[]{:S(2)}) collective-permute-start(bf16[96,256]{1,0:T(8,128)(2,1)S(1)} %get-tuple-element.52), channel_id=1, source_target_pairs={{0,24},{4,28},{8,16},{12,20},{16,8},{20,12},{24,0},{28,4},{1,25},{... | collective-permute-start | bytes 147464 | tf_op jit(solution)/shard_map/ppermute | solution.py:146
  22.5 0.8 %copy-start.8 = (s32[1,4,128]{2,1,0:T(4,128)S(1)}, s32[1,4,128]{2,1,0:T(4,128)}, u32[]{:S(2)}) copy-start(s32[1,4,128]{2,1,0:T(4,128)} %rows_ref.1) | copy-start | bytes 6148
  23.3 0.7 copy-start.9
  28.4 6.4 %collective-permute-start.7 = (bf16[128,256]{1,0:T(8,128)(2,1)S(1)}, bf16[128,256]{1,0:T(8,128)(2,1)S(1)}, u32[]{:S(2)}, u32[]{:S(2)}) collective-permute-start(bf16[128,256]{1,0:T(8,128)(2,1)S(1)} %get-tuple-element.58), channel_id=1, source_target_pairs={{0,1},{1,0},{2,3},{3,2},{4,8},{5,9},{6,10},{7,11},{8,4},{9,5},{10,... | collective-permute-start | bytes 196616 | tf_op jit(solution)/shard_map/ppermute | solution.py:82
  28.5 6.3 %collective-permute-start.8 = (bf16[128,256]{1,0:T(8,128)(2,1)S(1)}, bf16[128,256]{1,0:T(8,128)(2,1)S(1)}, u32[]{:S(2)}, u32[]{:S(2)}) collective-permute-start(bf16[128,256]{1,0:T(8,128)(2,1)S(1)} %get-tuple-element.59), channel_id=1, source_target_pairs={{0,4},{1,2},{2,1},{3,7},{4,0},{5,6},{6,5},{7,3},{8,12},{9,10},{10,... | collective-permute-start | bytes 196616 | tf_op jit(solution)/shard_map/ppermute | solution.py:82
  30.1 4.7 %collective-permute-start.9 = (bf16[128,256]{1,0:T(8,128)(2,1)S(1)}, bf16[128,256]{1,0:T(8,128)(2,1)S(1)}, u32[]{:S(2)}, u32[]{:S(2)}) collective-permute-start(bf16[128,256]{1,0:T(8,128)(2,1)S(1)} %get-tuple-element.60), channel_id=1, source_target_pairs={{0,4},{1,5},{2,6},{3,7},{4,0},{5,1},{6,2},{7,3},{8,12},{9,13},{10,... | collective-permute-start | bytes 196616 | tf_op jit(solution)/shard_map/ppermute | solution.py:82
  30.6 4.2 %collective-permute-start.10 = (bf16[128,256]{1,0:T(8,128)(2,1)S(1)}, bf16[128,256]{1,0:T(8,128)(2,1)S(1)}, u32[]{:S(2)}, u32[]{:S(2)}) collective-permute-start(bf16[128,256]{1,0:T(8,128)(2,1)S(1)} %get-tuple-element.61), channel_id=1, source_target_pairs={{0,1},{1,0},{2,3},{3,2},{4,5},{5,4},{6,7},{7,6},{8,9},{9,8},{10,11... | collective-permute-start | bytes 196616 | tf_op jit(solution)/shard_map/ppermute | solution.py:82
  35.1 6.3 %collective-permute-start.11 = (bf16[128,256]{1,0:T(8,128)(2,1)S(1)}, bf16[128,256]{1,0:T(8,128)(2,1)S(1)}, u32[]{:S(2)}, u32[]{:S(2)}) collective-permute-start(bf16[128,256]{1,0:T(8,128)(2,1)S(1)} %get-tuple-element.66), channel_id=1, source_target_pairs={{0,1},{1,0},{2,3},{3,2},{4,8},{5,9},{6,10},{7,11},{8,4},{9,5},{10,... | collective-permute-start | bytes 196616 | tf_op jit(solution)/shard_map/ppermute | solution.py:82
  35.2 6.4 %collective-permute-start.12 = (bf16[128,256]{1,0:T(8,128)(2,1)S(1)}, bf16[128,256]{1,0:T(8,128)(2,1)S(1)}, u32[]{:S(2)}, u32[]{:S(2)}) collective-permute-start(bf16[128,256]{1,0:T(8,128)(2,1)S(1)} %get-tuple-element.67), channel_id=1, source_target_pairs={{0,4},{1,2},{2,1},{3,7},{4,0},{5,6},{6,5},{7,3},{8,12},{9,10},{10,... | collective-permute-start | bytes 196616 | tf_op jit(solution)/shard_map/ppermute | solution.py:82
  38.9 4.3 %collective-permute-start.13 = (bf16[128,256]{1,0:T(8,128)(2,1)S(1)}, bf16[128,256]{1,0:T(8,128)(2,1)S(1)}, u32[]{:S(2)}, u32[]{:S(2)}) collective-permute-start(bf16[128,256]{1,0:T(8,128)(2,1)S(1)} %get-tuple-element.68), channel_id=1, source_target_pairs={{0,4},{1,5},{2,6},{3,7},{4,0},{5,1},{6,2},{7,3},{8,12},{9,13},{10,... | collective-permute-start | bytes 196616 | tf_op jit(solution)/shard_map/ppermute | solution.py:82
  38.9 4.2 %collective-permute-start.14 = (bf16[128,256]{1,0:T(8,128)(2,1)S(1)}, bf16[128,256]{1,0:T(8,128)(2,1)S(1)}, u32[]{:S(2)}, u32[]{:S(2)}) collective-permute-start(bf16[128,256]{1,0:T(8,128)(2,1)S(1)} %get-tuple-element.69), channel_id=1, source_target_pairs={{0,1},{1,0},{2,3},{3,2},{4,5},{5,4},{6,7},{7,6},{8,9},{9,8},{10,11... | collective-permute-start | bytes 196616 | tf_op jit(solution)/shard_map/ppermute | solution.py:82
  39.0 9.0 %copy-start.7 = (bf16[768,384]{1,0:T(8,128)(2,1)S(1)}, bf16[768,384]{1,0:T(8,128)(2,1)}, u32[]{:S(2)}) copy-start(bf16[768,384]{1,0:T(8,128)(2,1)} %refs_4_.3) | copy-start | bytes 1769476
  43.4 3.6 %collective-permute-start.17 = (bf16[96,256]{1,0:T(8,128)(2,1)S(1)}, bf16[96,256]{1,0:T(8,128)(2,1)S(1)}, u32[]{:S(2)}, u32[]{:S(2)}) collective-permute-start(bf16[96,256]{1,0:T(8,128)(2,1)S(1)} %restrict_recv.1.refs_0_), channel_id=1, source_target_pairs={{0,3},{1,2},{2,1},{3,0},{4,7},{5,6},{6,5},{7,4},{8,11},{9,10},{10,... | collective-permute-start | bytes 147464 | tf_op jit(solution)/shard_map/ppermute | solution.py:134
  43.4 4.6 %collective-permute-start.16 = (bf16[96,256]{1,0:T(8,128)(2,1)S(1)}, bf16[96,256]{1,0:T(8,128)(2,1)S(1)}, u32[]{:S(2)}, u32[]{:S(2)}) collective-permute-start(bf16[96,256]{1,0:T(8,128)(2,1)S(1)} %restrict_recv.1.refs_0_), channel_id=1, source_target_pairs={{0,2},{1,3},{2,0},{3,1},{4,6},{5,7},{6,4},{7,5},{8,10},{9,11},{10,... | collective-permute-start | bytes 147464 | tf_op jit(solution)/shard_map/ppermute | solution.py:134
  43.8 4.2 %collective-permute-start.15 = (bf16[96,256]{1,0:T(8,128)(2,1)S(1)}, bf16[96,256]{1,0:T(8,128)(2,1)S(1)}, u32[]{:S(2)}, u32[]{:S(2)}) collective-permute-start(bf16[96,256]{1,0:T(8,128)(2,1)S(1)} %restrict_recv.1.refs_0_), channel_id=1, source_target_pairs={{0,1},{1,0},{2,3},{3,2},{4,5},{5,4},{6,7},{7,6},{8,9},{9,8},{10,11... | collective-permute-start | bytes 147464 | tf_op jit(solution)/shard_map/ppermute | solution.py:134
  48.4 6.9 %collective-permute-start.18 = (bf16[384,256]{1,0:T(8,128)(2,1)S(1)}, bf16[384,256]{1,0:T(8,128)(2,1)S(1)}, u32[]{:S(2)}, u32[]{:S(2)}) collective-permute-start(bf16[384,256]{1,0:T(8,128)(2,1)S(1)} %get-tuple-element.71), channel_id=1, source_target_pairs={{0,4},{4,0},{8,12},{12,8},{16,20},{20,16},{24,28},{28,24},{1,5},{5... | collective-permute-start | bytes 589832 | tf_op jit(solution)/shard_map/ppermute | solution.py:141
  55.3 5.4 %collective-permute-start.19 = (bf16[96,256]{1,0:T(8,128)(2,1)S(1)}, bf16[96,256]{1,0:T(8,128)(2,1)S(1)}, u32[]{:S(2)}, u32[]{:S(2)}) collective-permute-start(bf16[96,256]{1,0:T(8,128)(2,1)S(1)} %get-tuple-element.73), channel_id=1, source_target_pairs={{0,8},{4,12},{8,0},{12,4},{16,24},{20,28},{24,16},{28,20},{1,9},{5... | collective-permute-start | bytes 147464 | tf_op jit(solution)/shard_map/ppermute | solution.py:146
  57.1 5.8 %collective-permute-start.20 = (bf16[96,256]{1,0:T(8,128)(2,1)S(1)}, bf16[96,256]{1,0:T(8,128)(2,1)S(1)}, u32[]{:S(2)}, u32[]{:S(2)}) collective-permute-start(bf16[96,256]{1,0:T(8,128)(2,1)S(1)} %get-tuple-element.74), channel_id=1, source_target_pairs={{0,16},{4,20},{8,24},{12,28},{16,0},{20,4},{24,8},{28,12},{1,17},{... | collective-permute-start | bytes 147464 | tf_op jit(solution)/shard_map/ppermute | solution.py:146
  58.6 5.9 %collective-permute-start.21 = (bf16[96,256]{1,0:T(8,128)(2,1)S(1)}, bf16[96,256]{1,0:T(8,128)(2,1)S(1)}, u32[]{:S(2)}, u32[]{:S(2)}) collective-permute-start(bf16[96,256]{1,0:T(8,128)(2,1)S(1)} %get-tuple-element.75), channel_id=1, source_target_pairs={{0,24},{4,28},{8,16},{12,20},{16,8},{20,12},{24,0},{28,4},{1,25},{... | collective-permute-start | bytes 147464 | tf_op jit(solution)/shard_map/ppermute | solution.py:146
  64.7 5.4 %collective-permute-start.22 = (bf16[128,256]{1,0:T(8,128)(2,1)S(1)}, bf16[128,256]{1,0:T(8,128)(2,1)S(1)}, u32[]{:S(2)}, u32[]{:S(2)}) collective-permute-start(bf16[128,256]{1,0:T(8,128)(2,1)S(1)} %get-tuple-element.81), channel_id=1, source_target_pairs={{0,1},{1,0},{2,3},{3,2},{4,8},{5,9},{6,10},{7,11},{8,4},{9,5},{10,... | collective-permute-start | bytes 196616 | tf_op jit(solution)/shard_map/ppermute | solution.py:82
  64.8 5.3 %collective-permute-start.23 = (bf16[128,256]{1,0:T(8,128)(2,1)S(1)}, bf16[128,256]{1,0:T(8,128)(2,1)S(1)}, u32[]{:S(2)}, u32[]{:S(2)}) collective-permute-start(bf16[128,256]{1,0:T(8,128)(2,1)S(1)} %get-tuple-element.82), channel_id=1, source_target_pairs={{0,4},{1,2},{2,1},{3,7},{4,0},{5,6},{6,5},{7,3},{8,12},{9,10},{10,... | collective-permute-start | bytes 196616 | tf_op jit(solution)/shard_map/ppermute | solution.py:82
  65.7 4.8 %collective-permute-start.24 = (bf16[128,256]{1,0:T(8,128)(2,1)S(1)}, bf16[128,256]{1,0:T(8,128)(2,1)S(1)}, u32[]{:S(2)}, u32[]{:S(2)}) collective-permute-start(bf16[128,256]{1,0:T(8,128)(2,1)S(1)} %get-tuple-element.83), channel_id=1, source_target_pairs={{0,4},{1,5},{2,6},{3,7},{4,0},{5,1},{6,2},{7,3},{8,12},{9,13},{10,... | collective-permute-start | bytes 196616 | tf_op jit(solution)/shard_map/ppermute | solution.py:82
  66.9 3.6 %collective-permute-start.25 = (bf16[128,256]{1,0:T(8,128)(2,1)S(1)}, bf16[128,256]{1,0:T(8,128)(2,1)S(1)}, u32[]{:S(2)}, u32[]{:S(2)}) collective-permute-start(bf16[128,256]{1,0:T(8,128)(2,1)S(1)} %get-tuple-element.84), channel_id=1, source_target_pairs={{0,1},{1,0},{2,3},{3,2},{4,5},{5,4},{6,7},{7,6},{8,9},{9,8},{10,11... | collective-permute-start | bytes 196616 | tf_op jit(solution)/shard_map/ppermute | solution.py:82
  70.8 6.2 %collective-permute-start.26 = (bf16[128,256]{1,0:T(8,128)(2,1)S(1)}, bf16[128,256]{1,0:T(8,128)(2,1)S(1)}, u32[]{:S(2)}, u32[]{:S(2)}) collective-permute-start(bf16[128,256]{1,0:T(8,128)(2,1)S(1)} %get-tuple-element.88), channel_id=1, source_target_pairs={{0,1},{1,0},{2,3},{3,2},{4,8},{5,9},{6,10},{7,11},{8,4},{9,5},{10,... | collective-permute-start | bytes 196616 | tf_op jit(solution)/shard_map/ppermute | solution.py:82
  71.0 6.0 %collective-permute-start.27 = (bf16[128,256]{1,0:T(8,128)(2,1)S(1)}, bf16[128,256]{1,0:T(8,128)(2,1)S(1)}, u32[]{:S(2)}, u32[]{:S(2)}) collective-permute-start(bf16[128,256]{1,0:T(8,128)(2,1)S(1)} %get-tuple-element.89), channel_id=1, source_target_pairs={{0,4},{1,2},{2,1},{3,7},{4,0},{5,6},{6,5},{7,3},{8,12},{9,10},{10,... | collective-permute-start | bytes 196616 | tf_op jit(solution)/shard_map/ppermute | solution.py:82
  74.2 4.3 %collective-permute-start.28 = (bf16[128,256]{1,0:T(8,128)(2,1)S(1)}, bf16[128,256]{1,0:T(8,128)(2,1)S(1)}, u32[]{:S(2)}, u32[]{:S(2)}) collective-permute-start(bf16[128,256]{1,0:T(8,128)(2,1)S(1)} %get-tuple-element.90), channel_id=1, source_target_pairs={{0,4},{1,5},{2,6},{3,7},{4,0},{5,1},{6,2},{7,3},{8,12},{9,13},{10,... | collective-permute-start | bytes 196616 | tf_op jit(solution)/shard_map/ppermute | solution.py:82
  74.2 4.2 %collective-permute-start.29 = (bf16[128,256]{1,0:T(8,128)(2,1)S(1)}, bf16[128,256]{1,0:T(8,128)(2,1)S(1)}, u32[]{:S(2)}, u32[]{:S(2)}) collective-permute-start(bf16[128,256]{1,0:T(8,128)(2,1)S(1)} %get-tuple-element.91), channel_id=1, source_target_pairs={{0,1},{1,0},{2,3},{3,2},{4,5},{5,4},{6,7},{7,6},{8,9},{9,8},{10,11... | collective-permute-start | bytes 196616 | tf_op jit(solution)/shard_map/ppermute | solution.py:82

commit v2 on v1

v2 whole, which is shorter than its diff:
```python
import functools

import jax
import jax.numpy as jnp
from jax import lax
from jax.experimental import pallas as pl
from jax.experimental.pallas import tpu as pltpu
from jax.sharding import PartitionSpec as P

STEPS = 2
BF = jnp.bfloat16
F32 = jnp.float32
VMEM = pl.BlockSpec(memory_space=pltpu.VMEM)
ANY = pl.BlockSpec(memory_space=pl.ANY)
LIMIT = 24 << 20


def mm(a, b):
    return jnp.dot(a, b, preferred_element_type=F32)


def call(kernel, outs, *args, name, scratch=(), flops=0, hbm_ins=0, hbm_outs=0, tokens=0):
    nbytes = sum(a.size * a.dtype.itemsize for a in args)
    inner = len(args) - hbm_ins - tokens
    return pl.pallas_call(
        kernel,
        out_shape=[jax.ShapeDtypeStruct(s, d) for s, d in outs],
        in_specs=[ANY] * hbm_ins + [VMEM] * inner + [ANY] * tokens,
        out_specs=[ANY] * hbm_outs + [VMEM] * (len(outs) - hbm_outs),
        scratch_shapes=list(scratch),
        compiler_params=pltpu.CompilerParams(vmem_limit_bytes=LIMIT),
        cost_estimate=pl.CostEstimate(flops=flops, bytes_accessed=nbytes, transcendentals=0),
        name=name,
    )(*args)


def tiles(rows):
    return 256 if rows % 256 == 0 else rows


def per_device(nr, nc, rhs, local_mat, local_inv, basis_t, coarse_inv, couple, margin_rows):
    nloc, nrhs = rhs.shape
    cpd = basis_t.shape[0]
    ovl = margin_rows.shape[2]
    nf = 4 * ovl
    nz = nr // 2
    both = ("row", "col")

    step = tiles(nloc)

    def row_loop(body):
        @pl.loop(0, nloc // step)
        def _(i):
            body(pl.ds(pl.multiple_of(i * step, step), step))

    def pairs(row_parity, col_parity):
        perm = {}
        for r in range(nr):
            for c in range(nc):
                if row_parity is not None:
                    o = r + 1 if r % 2 == row_parity else r - 1
                    other = (o, c) if 0 <= o < nr else (r, c ^ 1)
                else:
                    o = c + 1 if c % 2 == col_parity else c - 1
                    other = (r, o) if 0 <= o < nc else (r ^ 1, c)
                perm[r * nc + c] = other[0] * nc + other[1]
        return sorted(perm.items())

    slot_perms = [pairs(1, None), pairs(None, 1), pairs(0, None), pairs(None, 0)]

    def slot_faces():
        r, c = lax.axis_index("row"), lax.axis_index("col")
        pr, pc = lax.rem(r, 2), lax.rem(c, 2)
        one = lambda ok: jnp.where(ok, 1.0, 0.0).astype(F32)
        return [
            (pr, one((pr == 1) & (r + 1 < nr) | (pr == 0) & (r > 0))),
            (2 + pc, one((pc == 1) & (c + 1 < nc) | (pc == 0) & (c > 0))),
            (1 - pr, one((pr == 1) | (r + 1 < nr))),
            (3 - pc, one((pc == 1) | (c + 1 < nc))),
        ]

    def halo(faces):
        return [lax.ppermute(f, both, p) for f, p in zip(faces, slot_perms)]

    def k_select(inv_hbm, table_ref, token, sel_ref, wt_ref, inv_ref, sem):
        load = pltpu.make_async_copy(inv_hbm, inv_ref, sem)
        load.start()
        for s, (k, ok) in enumerate(slot_faces()):
            row = table_ref[pl.ds(k, 1), :].astype(jnp.int32)
            w = table_ref[pl.ds(4 + k, 1), :] * ok
            at = pl.ds(s * ovl, ovl)
            down = lax.broadcasted_iota(jnp.int32, (nloc, ovl), 0)
            wt_ref[:, at] = jnp.where(down == row, jnp.broadcast_to(w, (nloc, ovl)), 0.0).astype(BF)
            idx = jnp.broadcast_to(row.astype(F32), (ovl, ovl)).T
            for j in range(nloc // ovl):
                across = lax.broadcasted_iota(jnp.int32, (ovl, ovl), 1) + j * ovl
                sel_ref[at, pl.ds(j * ovl, ovl)] = jnp.where(idx == across.astype(F32), 1.0, 0.0).astype(BF)
        load.wait()

    def k_products(
        sel_ref, wt_ref, inv_ref, mat_ref, basis_ref, token, bf_ref, t_ref, si_ref, f_ref, bt_ref, lb_ref
    ):
        bt = basis_ref[...].astype(F32).T.astype(BF)
        bt_ref[...] = bt
        bf_ref[...] = mm(sel_ref[...], bt).astype(BF)
        t_ref[...] = mm(basis_ref[...], wt_ref[...]).astype(BF)
        fstep = tiles(nf)

        @pl.loop(0, nf // fstep)
        def _(i):
            at = pl.ds(pl.multiple_of(i * fstep, fstep), fstep)
            si_ref[at, :] = mm(sel_ref[at, :], inv_ref[...]).astype(BF)
            f_ref[at, :] = mm(si_ref[at, :], wt_ref[...]).astype(BF)

        def tile(at):
            lb_ref[at, :] = mm(mat_ref[at, :], bt_ref[...]).astype(BF)

        row_loop(tile)

    def k_coarse(*refs):
        blocks, (inv_ref, keep_ref, send_ref, group, prod) = refs[:nc], refs[nc:]
        r, c = lax.axis_index("row"), lax.axis_index("col")
        for i, block in enumerate(blocks):
            group[pl.ds(pl.multiple_of((c ^ i) * cpd, 16), cpd), :] = block[...]
        prod[...] = mm(inv_ref[...], group[...])
        for i in range(nz):
            for ref, m in ((keep_ref, 2 * i), (send_ref, 2 * i + 1)):
                src = pl.ds(pl.multiple_of((r ^ m) * cpd, 8), cpd)
                ref[pl.ds(i * cpd, cpd), :] = prod[src, :].astype(ref.dtype)

    def k_half(keep_ref, recv_ref, token, own_ref, *sends):
        own_ref[...] = keep_ref[pl.ds(0, cpd), :] + recv_ref[pl.ds(0, cpd), :].astype(F32)
        for i, ref in enumerate(sends):
            at = pl.ds((i + 1) * cpd, cpd)
            ref[...] = (keep_ref[at, :] + recv_ref[at, :].astype(F32)).astype(BF)

    def coarse_send(restricted, inv):
        blocks = [restricted] + [
            lax.ppermute(restricted, "col", [(i, i ^ k) for i in range(nc)]) for k in range(1, nc)
        ]
        keep, send = call(
            k_coarse, [((nz * cpd, nrhs), F32), ((nz * cpd, nrhs), BF)], *blocks, inv,
            scratch=[pltpu.VMEM((nc * cpd, nrhs), BF), pltpu.VMEM((nr * cpd, nrhs), F32)],
            name="coarse", flops=2 * nr * cpd * nc * cpd * nrhs,
        )
        return keep, lax.ppermute(send, "row", [(i, i ^ 1) for i in range(nr)])

    def coarse_recv(keep, recv, token):
        own, *sends = call(
            k_half, [((cpd, nrhs), F32)] + [((cpd, nrhs), BF)] * (nz - 1), keep, recv, token,
            tokens=1, name="half",
        )
        recvs = [
            lax.ppermute(s, "row", [(i, i ^ (2 * (k + 1))) for i in range(nr)]) for k, s in enumerate(sends)
        ]
        return [own] + recvs

    def k_coarse_faces(*refs):
        parts, (bf_ref, y_ref), faces = refs[:nz], refs[nz : nz + 2], refs[nz + 2 :]
        total = parts[0][...]
        for p in parts[1:]:
            total = total + p[...].astype(F32)
        y = total.astype(BF)
        y_ref[...] = y
        for s, ref in enumerate(faces):
            ref[...] = mm(bf_ref[pl.ds(s * ovl, ovl), :], y).astype(BF)

    def coarse_faces(parts):
        y, *faces = call(
            k_coarse_faces, [((cpd, nrhs), BF)] + [((ovl, nrhs), BF)] * 4, *parts, bfac, name="coarse_faces",
        )
        return y, faces

    def k_local(y_ref, base_ref, lb_ref, si_ref, bf_ref, *refs):
        olds, face_ref, wb = refs[:-2], refs[-2], refs[-1]
        y = y_ref[...]

        def tile(at):
            wb[at, :] = (base_ref[at, :] - mm(lb_ref[at, :], y)).astype(BF)

        row_loop(tile)
        for s in range(4):
            at = pl.ds(s * ovl, ovl)
            face = mm(bf_ref[at, :], y) + mm(si_ref[at, :], wb[...])
            face_ref[at, :] = face + olds[s][...].astype(F32) if olds else face

    def local(y, base, olds):
        (face,) = call(
            k_local, [((nf, nrhs), F32)], y, base, lbmat, simat, bfac, *olds,
            scratch=[pltpu.VMEM((nloc, nrhs), BF)], name="local", flops=2 * nf * nloc * nrhs,
        )
        return face

    def k_faces(base_ref, f_ref, *refs):
        recvs, faces = refs[:4], refs[4:]
        recv = jnp.concatenate([x[...] for x in recvs], axis=0)
        for s, ref in enumerate(faces):
            at = pl.ds(s * ovl, ovl)
            ref[...] = (base_ref[at, :] + mm(f_ref[at, :], recv)).astype(BF)

    def faces_after(base, recv):
        return call(k_faces, [((ovl, nrhs), BF)] * 4, base, fmat, *recv, name="faces", flops=2 * nf * nf * nrhs)

    def k_advance(first, last, *refs):
        y_ref, base_ref, lb_ref, bt_ref, wt_ref, inv_ref, mat_ref, rhs_ref, basis_ref = refs[:9]
        recvs, refs = refs[9:13], refs[13:]
        old_ref, refs = (None, refs) if first else (refs[0], refs[1:])
        out_ref, res_ref = refs[:2]
        if last:
            wb, vb, recv, new_ref, sem = refs[2:]
        else:
            restr_ref, wb, vb, recv = refs[2:]
            new_ref = out_ref
        y = y_ref[...]
        for s, x in enumerate(recvs):
            recv[pl.ds(s * ovl, ovl), :] = x[...]

        def base_tile(at):
            wb[at, :] = (base_ref[at, :] - mm(lb_ref[at, :], y) + mm(wt_ref[at, :], recv[...])).astype(BF)

        row_loop(base_tile)

        def sol_tile(at):
            new = mm(bt_ref[at, :], y) + mm(inv_ref[at, :], wb[...])
            if not first:
                new = new + old_ref[at, :]
            new_ref[at, :] = new
            vb[at, :] = new.astype(BF)

        row_loop(sol_tile)
        if last:
            store = pltpu.make_async_copy(new_ref, out_ref, sem)
            store.start()

        def res_tile(at):
            res_ref[at, :] = rhs_ref[at, :] - mm(mat_ref[at, :], vb[...])

        row_loop(res_tile)
        if last:
            store.wait()
        else:
            restr_ref[...] = mm(basis_ref[...], res_ref[...].astype(BF))

    def advance(y, base, recv, old, last):
        first = old is None
        outs = [((nloc, nrhs), F32)] * 2 + ([] if last else [((cpd, nrhs), F32)])
        extra = [pltpu.VMEM((nloc, nrhs), F32), pltpu.SemaphoreType.DMA] if last else []
        return call(
            functools.partial(k_advance, first, last), outs,
            y, base, lbmat, btmat, wt, local_inv, local_mat, rhs, basis_t, *recv, *([] if first else [old]),
            scratch=[pltpu.VMEM((nloc, nrhs), BF)] * 2 + [pltpu.VMEM((nf, nrhs), BF)] + extra,
            hbm_outs=1 if last else 0, name="advance", flops=5 * nloc * nloc * nrhs,
        )

    def k_restrict_recv(base_ref, t_ref, *refs):
        recvs, out_ref = refs[:4], refs[4]
        recv = jnp.concatenate([x[...] for x in recvs], axis=0)
        out_ref[...] = (base_ref[...] + mm(t_ref[...], recv)).astype(BF)

    def k_couple(res_ref, wt_ref, *refs):
        recvs, out_ref, recv = refs[:4], refs[4], refs[5]
        for s, x in enumerate(recvs):
            recv[pl.ds(s * ovl, ovl), :] = x[...]

        def tile(at):
            out_ref[at, :] = res_ref[at, :] + mm(wt_ref[at, :], recv[...])

        row_loop(tile)

    def k_couple_last(res_ref, wt_ref, *refs):
        recvs, (out_ref, recv, buf, sems) = refs[:4], refs[4:]
        for s, x in enumerate(recvs):
            recv[pl.ds(s * ovl, ovl), :] = x[...]
        copies = []
        for i in range(nloc // step):
            at = pl.ds(i * step, step)
            buf[at, :] = res_ref[at, :] + mm(wt_ref[at, :], recv[...])
            copies.append(pltpu.make_async_copy(buf.at[at, :], out_ref.at[at, :], sems.at[i]))
            copies[-1].start()
        for copy in copies:
            copy.wait()

    def coupled(res, recv, last):
        extra = [pltpu.VMEM((nloc, nrhs), F32), pltpu.SemaphoreType.DMA((nloc // step,))] if last else []
        return call(
            k_couple_last if last else k_couple, [((nloc, nrhs), F32)], res, wt, *recv,
            scratch=[pltpu.VMEM((nf, nrhs), BF)] + extra, hbm_outs=1 if last else 0,
            name="couple", flops=2 * nloc * nf * nrhs,
        )[0]

    restricted = mm(basis_t, rhs.astype(BF)).astype(BF)
    table = jnp.concatenate([margin_rows[0].astype(F32), couple[0]], axis=0)
    sel, wt, inv_here = call(
        k_select, [((nf, nloc), BF), ((nloc, nf), BF), (coarse_inv.shape, BF)],
        coarse_inv, table, restricted, hbm_ins=1, tokens=1, name="select",
        scratch=[pltpu.SemaphoreType.DMA],
    )
    keep, recv = coarse_send(restricted, inv_here)
    bfac, tmat, simat, fmat, btmat, lbmat = call(
        k_products,
        [((nf, cpd), BF), ((cpd, nf), BF), ((nf, nloc), BF), ((nf, nf), BF), ((nloc, cpd), BF), ((nloc, cpd), BF)],
        sel, wt, local_inv, local_mat, basis_t, keep, tokens=1,
        name="products", flops=2 * nf * nloc * (nloc + nf + 3 * cpd),
    )
    token = tmat
    residual, solution, sent = rhs, None, []
    for sweep in range(STEPS):
        y, faces = coarse_faces(coarse_recv(keep, recv, token))
        recv = halo(faces)
        sent = faces_after(local(y, residual, sent), recv)
        recv2 = halo(sent)
        last = sweep == STEPS - 1
        new = advance(y, residual, recv, solution, last)
        solution, res = new[:2]
        if not last:
            (restricted,) = call(
                k_restrict_recv, [((cpd, nrhs), BF)], new[2], tmat, *recv2, name="restrict_recv",
            )
            keep, recv = coarse_send(restricted, inv_here)
        residual = coupled(res, recv2, last)
        token = residual
    return (solution, residual)


def solution(mesh):
    nr, nc = mesh.shape["row"], mesh.shape["col"]
    placed = (
        P(("row", "col"), None),
        P(("row", "col"), None),
        P(("row", "col"), None),
        P(("row", "col"), None),
        P("col", "row"),
        P(("row", "col"), None, None),
        P(("row", "col"), None, None),
    )
    return jax.shard_map(
        functools.partial(per_device, nr, nc),
        mesh=mesh,
        in_specs=placed,
        out_specs=(P(("row", "col"), None), P(("row", "col"), None)),
        check_vma=False,
    )
```

time: 80.6 us -> 77.7 us (0.964)
  waiting for transfers between devices: 25 us -> 21.3 us
  local copies, waits for them, and re-layouts: 4.74 us -> 2.67 us
  matrix products: 0 us -> 1.69 us
  other arithmetic: 0 us -> 1.37 us
  Pallas kernels: 20.2 us -> 18.9 us
  starting transfers between devices: 29.6 us -> 30.6 us
    ppermute x14, waiting for transfers between devices: 21.4 us -> 16.3 us  [the longest x6 9.12 us: coarse_recv(): lax.ppermute(s, 'row', [(i, i ^ 2 * (k + 1)) for i in range(nr)])]
    unnamed x20 -> x12, local copies, waits for them, and re-layouts: 4.74 us -> 2.67 us
    dot_general x0 -> x1, matrix products: none -> 1.69 us  [mm(): return jnp.dot(a, b, preferred_element_type=F32)]
    ppermute x16, waiting for transfers between devices: 3.56 us -> 5.02 us  [halo(): return [lax.ppermute(f, both, p) for f, p in zip(faces, slot_perms)]]
    pallas_call x17, Pallas kernels: 20.2 us -> 18.9 us  [call(): pl.pallas_call(kernel, out_shape=[jax.ShapeDtypeStruct(s, d) for s, d in...]
    ppermute x16, starting transfers between devices: 12.6 us -> 13.4 us  [halo(): return [lax.ppermute(f, both, p) for f, p in zip(faces, slot_perms)]]
  transfers between devices with their start and end apart: 30 -> 30, of which waited for: 13 -> 16; matrix products, arithmetic and copies ran while one was open for 0% -> 2% of each run, Pallas kernels for 20% -> 20%
where the time goes in v2:
time: 77.7 us; the launch traced here: 77.5 us
  starting transfers between devices  30.6 us (39%)
  waiting for transfers between devices  21.3 us (27%)
  Pallas kernels  18.9 us (24%)
  local copies, waits for them, and re-layouts  2.67 us (3%)
  matrix products  1.69 us (2%)
  other arithmetic  1.37 us (2%)
  between operations  0.87 us (1%)
    pallas_call x17, Pallas kernels, call(): pl.pallas_call(kernel, out_shape=[jax.ShapeDtypeStruct(s, d) for s, d in...  18.9 us
    ppermute x16, starting transfers between devices, halo(): return [lax.ppermute(f, both, p) for f, p in zip(faces, slot_perms)]  13.4 us
    ppermute x6, waiting for transfers between devices, coarse_recv(): lax.ppermute(s, 'row', [(i, i ^ 2 * (k + 1)) for i in range(nr)])  9.12 us
    ppermute x6, starting transfers between devices, coarse_recv(): lax.ppermute(s, 'row', [(i, i ^ 2 * (k + 1)) for i in range(nr)])  8.9 us
    ppermute x6, starting transfers between devices, coarse_send(): lax.ppermute(restricted, 'col', [(i, i ^ k) for i in range(nc)])  5.08 us
    ppermute x16, waiting for transfers between devices, halo(): return [lax.ppermute(f, both, p) for f, p in zip(faces, slot_perms)]  5.02 us
    ppermute x6, waiting for transfers between devices, coarse_send(): lax.ppermute(restricted, 'col', [(i, i ^ k) for i in range(nc)])  3.58 us
    ppermute x2, waiting for transfers between devices, coarse_send(): return (keep, lax.ppermute(send, 'row', [(i, i ^ 1) for i in range(nr)]))  3.57 us
  transfers between devices with their start and end apart: 30, of which 16 were waited for; matrix products, arithmetic and copies ran while one was open for 2% of the time, Pallas kernels for 20%

profile of v2, /device:TPU:0, one launch (start us, length us, event | category | flops | bytes accessed | tf_op | source)
XLA Modules:
  0.0 77.5 jit_solution(3170667113829911919)
XLA Ops:
  0.6 1.7 %convolution_convert_fusion.token.refs_0_ = bf16[96,256]{1,0:T(8,128)(2,1)S(1)} fusion(bf16[96,1024]{1,0:T(8,128)(2,1)} %refs_8_.3, f32[1024,256]{1,0:T(8,128)} %refs_7_.3), kind=kOutput, calls=%fused_computation | convolution fusion | flops 50618368 | bytes 1294336 | tf_op jit(solution)/shard_map/dot_general | solution.py:19
  2.3 2.5 %collective-permute-start.2 = (bf16[96,256]{1,0:T(8,128)(2,1)S(1)}, bf16[96,256]{1,0:T(8,128)(2,1)S(1)}, u32[]{:S(2)}, u32[]{:S(2)}) collective-permute-start(bf16[96,256]{1,0:T(8,128)(2,1)S(1)} %convolution_convert_fusion.token.refs_0_), channel_id=1, source_target_pairs={{0,3},{1,2},{2,1},{3,0},{4,7},{5,6},{6,5},{7,4},{8,11},{9,10},{10,... | collective-permute-start | bytes 147464 | tf_op jit(solution)/shard_map/ppermute | solution.py:139
  4.8 0.6 collective-permute-start.1
  5.5 0.7 convert_bitcast_fusion
  6.2 0.7 pad_maximum_fusion.table_ref
  6.9 1.1 %copy-done.5 = bf16[768,384]{1,0:T(8,128)(2,1)S(1)} copy-done((bf16[768,384]{1,0:T(8,128)(2,1)S(1)}, bf16[768,384]{1,0:T(8,128)(2,1)}, u32[]{:S(2)}) %copy-start.5) | copy-done | bytes 589848
  7.9 0.9 %select.1 = (bf16[512,1024]{1,0:T(8,128)(2,1)S(1)}, bf16[1024,512]{1,0:T(8,128)(2,1)S(1)}, bf16[768,384]{1,0:T(8,128)(2,1)S(1)}) custom-call(bf16[768,384]{1,0:T(8,128)(2,1)S(1)} %copy-done.5, f32[8,128]{1,0:T(8,128)S(1)} %pad_maximum_fusion.table_ref, bf16[96,256]{1,0:T(8,128)(2,1)S(1)} %convolution_convert_fusion.token.refs_0_), custom_call_target="tpu_custom_call" | custom-call | bytes 643072 | tf_op jit(solution)/shard_map/select/pallas_call | solution.py:25
  8.8 0.3 collective-permute-done.1.refs_2_
  9.1 0.4 coarse.2
  9.6 1.6 %collective-permute-start.3 = (bf16[384,256]{1,0:T(8,128)(2,1)S(1)}, bf16[384,256]{1,0:T(8,128)(2,1)S(1)}, u32[]{:S(2)}, u32[]{:S(2)}) collective-permute-start(bf16[384,256]{1,0:T(8,128)(2,1)S(1)} %get-tuple-element.48), channel_id=1, source_target_pairs={{0,4},{4,0},{8,12},{12,8},{16,20},{20,16},{24,28},{28,24},{1,5},{5... | collective-permute-start | bytes 589832 | tf_op jit(solution)/shard_map/ppermute | solution.py:146
  11.2 1.6 %copy-done.2 = bf16[1024,1024]{1,0:T(8,128)(2,1)S(1)} copy-done((bf16[1024,1024]{1,0:T(8,128)(2,1)S(1)}, bf16[1024,1024]{1,0:T(8,128)(2,1)}, u32[]{:S(2)}) %copy-start.2) | copy-done | bytes 2097176
  12.8 3.8 %products.1 = (bf16[512,96]{1,0:T(8,128)(2,1)S(1)}, bf16[96,512]{1,0:T(8,128)(2,1)S(1)}, bf16[512,1024]{1,0:T(8,128)(2,1)S(1)}, bf16[512,512]{1,0:T(8,128)(2,1)S...) custom-call(bf16[512,1024]{1,0:T(8,128)(2,1)S(1)} %get-tuple-element.49.sel_ref, ...), custom_call_target="tpu_custom_call" | custom-call | flops 1912602624 | bytes 6881280 | tf_op jit(solution)/shard_map/products/pallas_call | solution.py:25
  16.7 1.6 %collective-permute-start.4 = (bf16[96,256]{1,0:T(8,128)(2,1)S(1)}, bf16[96,256]{1,0:T(8,128)(2,1)S(1)}, u32[]{:S(2)}, u32[]{:S(2)}) collective-permute-start(bf16[96,256]{1,0:T(8,128)(2,1)S(1)} %get-tuple-element.53), channel_id=1, source_target_pairs={{0,8},{4,12},{8,0},{12,4},{16,24},{20,28},{24,16},{28,20},{1,9},{5... | collective-permute-start | bytes 147464 | tf_op jit(solution)/shard_map/ppermute | solution.py:154
  18.3 2.6 %collective-permute-start.5 = (bf16[96,256]{1,0:T(8,128)(2,1)S(1)}, bf16[96,256]{1,0:T(8,128)(2,1)S(1)}, u32[]{:S(2)}, u32[]{:S(2)}) collective-permute-start(bf16[96,256]{1,0:T(8,128)(2,1)S(1)} %get-tuple-element.54), channel_id=1, source_target_pairs={{0,16},{4,20},{8,24},{12,28},{16,0},{20,4},{24,8},{28,12},{1,17},{... | collective-permute-start | bytes 147464 | tf_op jit(solution)/shard_map/ppermute | solution.py:154
  21.1 3.1 %collective-permute-done.5.refs_2_ = bf16[96,256]{1,0:T(8,128)(2,1)S(1)} collective-permute-done((bf16[96,256]{1,0:T(8,128)(2,1)S(1)}, bf16[96,256]{1,0:T(8,128)(2,1)S(1)}, u32[]{:S(2)}, u32[]{:S(2)}) %collective-permute-start.5) | collective-permute-done | bytes 49184 | tf_op jit(solution)/shard_map/ppermute | solution.py:154
  24.2 2.6 %collective-permute-done.6.refs_3_ = bf16[96,256]{1,0:T(8,128)(2,1)S(1)} collective-permute-done((bf16[96,256]{1,0:T(8,128)(2,1)S(1)}, bf16[96,256]{1,0:T(8,128)(2,1)S(1)}, u32[]{:S(2)}, u32[]{:S(2)}) %collective-permute-start.6) | collective-permute-done | bytes 49184 | tf_op jit(solution)/shard_map/ppermute | solution.py:154
  27.1 1.5 %collective-permute-start.8 = (bf16[128,256]{1,0:T(8,128)(2,1)S(1)}, bf16[128,256]{1,0:T(8,128)(2,1)S(1)}, u32[]{:S(2)}, u32[]{:S(2)}) collective-permute-start(bf16[128,256]{1,0:T(8,128)(2,1)S(1)} %get-tuple-element.61), channel_id=1, source_target_pairs={{0,4},{1,2},{2,1},{3,7},{4,0},{5,6},{6,5},{7,3},{8,12},{9,10},{10,... | collective-permute-start | bytes 196616 | tf_op jit(solution)/shard_map/ppermute | solution.py:83
  28.7 0.6 collective-permute-start.9
  29.2 0.7 collective-permute-start.10
  29.9 1.2 %local.2.base_ref = f32[512,256]{1,0:T(8,128)S(1)} custom-call(bf16[96,256]{1,0:T(8,128)(2,1)S(1)} %get-tuple-element.57.refs_0_.y_ref, f32[1024,256]{1,0:T(8,128)S(1)} %copy-done, bf16[1024,96]{1,0:T(8,128)(2,1)S(1)} %get-tuple-element.58.refs_2_.lb_ref, bf16[512,1024]{1,0:T(8,128)(2,1)S(1)} %get-tuple-element.65.si_ref, ...), custom_call_target="tpu_custom_call" | custom-call | flops 268435456 | bytes 2441216 | tf_op jit(solution)/shard_map/local/pallas_call | solution.py:25
  31.1 0.5 collective-permute-done.8.refs_10_.refs_1_
  31.6 1.3 %collective-permute-done.9.refs_11_.refs_2_ = bf16[128,256]{1,0:T(8,128)(2,1)S(1)} collective-permute-done((bf16[128,256]{1,0:T(8,128)(2,1)S(1)}, bf16[128,256]{1,0:T(8,128)(2,1)S(1)}, u32[]{:S(2)}, u32[]{:S(2)}) %collective-permute-start.9) | collective-permute-done | bytes 65568 | tf_op jit(solution)/shard_map/ppermute | solution.py:83
  32.9 0.3 faces.2
  33.3 4.2 %collective-permute-start.12 = (bf16[128,256]{1,0:T(8,128)(2,1)S(1)}, bf16[128,256]{1,0:T(8,128)(2,1)S(1)}, u32[]{:S(2)}, u32[]{:S(2)}) collective-permute-start(bf16[128,256]{1,0:T(8,128)(2,1)S(1)} %get-tuple-element.68.refs_1_), channel_id=1, source_target_pairs={{0,4},{1,2},{2,1},{3,7},{4,0},{5,6},{6,5},{7,3},{8,12},{9,10},{10,... | collective-permute-start | bytes 196616 | tf_op jit(solution)/shard_map/ppermute | solution.py:83
  37.6 3.9 %advance.2 = (f32[1024,256]{1,0:T(8,128)S(1)}, f32[1024,256]{1,0:T(8,128)S(1)}, f32[96,256]{1,0:T(8,128)S(1)}) custom-call(bf16[96,256]{1,0:T(8,128)(2,1)S(1)} %get-tuple-element.57.refs_0_.y_ref, f32[1024,256]{1,0:T(8,128)S(1)} %copy-done, bf16[1024,96]{1,0:T(8,128)(2,1)S(1)} %get-tuple-element.58.refs_2_.lb_ref, ...), custom_call_target="tpu_custom_call" | custom-call | flops 1342177280 | bytes 8241152 | tf_op jit(solution)/shard_map/advance/pallas_call | solution.py:25
  41.5 0.4 collective-permute-done.13.refs_2_
  42.0 1.1 %collective-permute-start.17 = (bf16[96,256]{1,0:T(8,128)(2,1)S(1)}, bf16[96,256]{1,0:T(8,128)(2,1)S(1)}, u32[]{:S(2)}, u32[]{:S(2)}) collective-permute-start(bf16[96,256]{1,0:T(8,128)(2,1)S(1)} %restrict_recv.1.refs_0_), channel_id=1, source_target_pairs={{0,3},{1,2},{2,1},{3,0},{4,7},{5,6},{6,5},{7,4},{8,11},{9,10},{10,... | collective-permute-start | bytes 147464 | tf_op jit(solution)/shard_map/ppermute | solution.py:139
  43.1 0.8 collective-permute-start.16
  44.0 1.8 %collective-permute-done.17.refs_3_ = bf16[96,256]{1,0:T(8,128)(2,1)S(1)} collective-permute-done((bf16[96,256]{1,0:T(8,128)(2,1)S(1)}, bf16[96,256]{1,0:T(8,128)(2,1)S(1)}, u32[]{:S(2)}, u32[]{:S(2)}) %collective-permute-start.17) | collective-permute-done | bytes 49184 | tf_op jit(solution)/shard_map/ppermute | solution.py:139
  45.8 1.4 %collective-permute-done.16.refs_2_ = bf16[96,256]{1,0:T(8,128)(2,1)S(1)} collective-permute-done((bf16[96,256]{1,0:T(8,128)(2,1)S(1)}, bf16[96,256]{1,0:T(8,128)(2,1)S(1)}, u32[]{:S(2)}, u32[]{:S(2)}) %collective-permute-start.16) | collective-permute-done | bytes 49184 | tf_op jit(solution)/shard_map/ppermute | solution.py:139
  47.2 0.4 coarse.3
  47.7 1.7 %collective-permute-start.18 = (bf16[384,256]{1,0:T(8,128)(2,1)S(1)}, bf16[384,256]{1,0:T(8,128)(2,1)S(1)}, u32[]{:S(2)}, u32[]{:S(2)}) collective-permute-start(bf16[384,256]{1,0:T(8,128)(2,1)S(1)} %get-tuple-element.72), channel_id=1, source_target_pairs={{0,4},{4,0},{8,12},{12,8},{16,20},{20,16},{24,28},{28,24},{1,5},{5... | collective-permute-start | bytes 589832 | tf_op jit(solution)/shard_map/ppermute | solution.py:146
  49.4 0.9 %couple.2.token.refs_1_.base_ref = f32[1024,256]{1,0:T(8,128)S(1)} custom-call(f32[1024,256]{1,0:T(8,128)S(1)} %get-tuple-element.73.res_ref, bf16[1024,512]{1,0:T(8,128)(2,1)S(1)} %get-tuple-element.50.wt_ref.refs_4_, bf16[128,256]{1,0:T(8,128)(2,1)S(1)} %collective-permute-done.11.refs_0_, bf16[128,256]{1,0:T(8,128)(2,1)S(1)} %collective-permute-done.12.refs_1_, ...), custom_call_target="tpu_custom_call" | custom-call | flops 268435456 | bytes 2359296 | tf_op jit(solution)/shard_map/couple/pallas_call | solution.py:25
  50.3 3.5 %collective-permute-done.18.recv_ref = bf16[384,256]{1,0:T(8,128)(2,1)S(1)} collective-permute-done((bf16[384,256]{1,0:T(8,128)(2,1)S(1)}, bf16[384,256]{1,0:T(8,128)(2,1)S(1)}, u32[]{:S(2)}, u32[]{:S(2)}) %collective-permute-start.18) | collective-permute-done | bytes 196640 | tf_op jit(solution)/shard_map/ppermute | solution.py:146
  53.8 1.7 %collective-permute-start.19 = (bf16[96,256]{1,0:T(8,128)(2,1)S(1)}, bf16[96,256]{1,0:T(8,128)(2,1)S(1)}, u32[]{:S(2)}, u32[]{:S(2)}) collective-permute-start(bf16[96,256]{1,0:T(8,128)(2,1)S(1)} %get-tuple-element.75), channel_id=1, source_target_pairs={{0,8},{4,12},{8,0},{12,4},{16,24},{20,28},{24,16},{28,20},{1,9},{5... | collective-permute-start | bytes 147464 | tf_op jit(solution)/shard_map/ppermute | solution.py:154
  55.7 2.6 %collective-permute-start.21 = (bf16[96,256]{1,0:T(8,128)(2,1)S(1)}, bf16[96,256]{1,0:T(8,128)(2,1)S(1)}, u32[]{:S(2)}, u32[]{:S(2)}) collective-permute-start(bf16[96,256]{1,0:T(8,128)(2,1)S(1)} %get-tuple-element.77), channel_id=1, source_target_pairs={{0,24},{4,28},{8,16},{12,20},{16,8},{20,12},{24,0},{28,4},{1,25},{... | collective-permute-start | bytes 147464 | tf_op jit(solution)/shard_map/ppermute | solution.py:154
  58.5 2.4 %collective-permute-done.20.refs_2_ = bf16[96,256]{1,0:T(8,128)(2,1)S(1)} collective-permute-done((bf16[96,256]{1,0:T(8,128)(2,1)S(1)}, bf16[96,256]{1,0:T(8,128)(2,1)S(1)}, u32[]{:S(2)}, u32[]{:S(2)}) %collective-permute-start.20) | collective-permute-done | bytes 49184 | tf_op jit(solution)/shard_map/ppermute | solution.py:154
  60.9 0.8 %collective-permute-done.21.refs_3_ = bf16[96,256]{1,0:T(8,128)(2,1)S(1)} collective-permute-done((bf16[96,256]{1,0:T(8,128)(2,1)S(1)}, bf16[96,256]{1,0:T(8,128)(2,1)S(1)}, u32[]{:S(2)}, u32[]{:S(2)}) %collective-permute-start.21) | collective-permute-done | bytes 49184 | tf_op jit(solution)/shard_map/ppermute | solution.py:154
  62.0 2.2 %collective-permute-start.23 = (bf16[128,256]{1,0:T(8,128)(2,1)S(1)}, bf16[128,256]{1,0:T(8,128)(2,1)S(1)}, u32[]{:S(2)}, u32[]{:S(2)}) collective-permute-start(bf16[128,256]{1,0:T(8,128)(2,1)S(1)} %get-tuple-element.80), channel_id=1, source_target_pairs={{0,4},{1,2},{2,1},{3,7},{4,0},{5,6},{6,5},{7,3},{8,12},{9,10},{10,... | collective-permute-start | bytes 196616 | tf_op jit(solution)/shard_map/ppermute | solution.py:83
  64.3 0.8 %collective-permute-start.25 = (bf16[128,256]{1,0:T(8,128)(2,1)S(1)}, bf16[128,256]{1,0:T(8,128)(2,1)S(1)}, u32[]{:S(2)}, u32[]{:S(2)}) collective-permute-start(bf16[128,256]{1,0:T(8,128)(2,1)S(1)} %get-tuple-element.82), channel_id=1, source_target_pairs={{0,1},{1,0},{2,3},{3,2},{4,5},{5,4},{6,7},{7,6},{8,9},{9,8},{10,11... | collective-permute-start | bytes 196616 | tf_op jit(solution)/shard_map/ppermute | solution.py:83
  65.1 1.2 %local.3.base_ref = f32[512,256]{1,0:T(8,128)S(1)} custom-call(bf16[96,256]{1,0:T(8,128)(2,1)S(1)} %get-tuple-element.78.refs_0_.y_ref, f32[1024,256]{1,0:T(8,128)S(1)} %couple.2.token.refs_1_.base_ref, bf16[1024,96]{1,0:T(8,128)(2,1)S(1)} %get-tuple-element.58.refs_2_.lb_ref, bf16[512,1024]{1,0:T(8,128)(2,1)S(1)} %get-tuple-element.65.si_ref, ...), custom_call_target="tpu_custom_call" | custom-call | flops 268435456 | bytes 2703360 | tf_op jit(solution)/shard_map/local/pallas_call | solution.py:25
  66.3 0.7 collective-permute-done.23.refs_10_.refs_1_
  67.0 1.5 %collective-permute-done.24.refs_11_.refs_2_ = bf16[128,256]{1,0:T(8,128)(2,1)S(1)} collective-permute-done((bf16[128,256]{1,0:T(8,128)(2,1)S(1)}, bf16[128,256]{1,0:T(8,128)(2,1)S(1)}, u32[]{:S(2)}, u32[]{:S(2)}) %collective-permute-start.24) | collective-permute-done | bytes 65568 | tf_op jit(solution)/shard_map/ppermute | solution.py:83
  68.5 0.3 faces.3
  68.9 3.0 %collective-permute-start.27 = (bf16[128,256]{1,0:T(8,128)(2,1)S(1)}, bf16[128,256]{1,0:T(8,128)(2,1)S(1)}, u32[]{:S(2)}, u32[]{:S(2)}) collective-permute-start(bf16[128,256]{1,0:T(8,128)(2,1)S(1)} %get-tuple-element.87), channel_id=1, source_target_pairs={{0,4},{1,2},{2,1},{3,7},{4,0},{5,6},{6,5},{7,3},{8,12},{9,10},{10,... | collective-permute-start | bytes 196616 | tf_op jit(solution)/shard_map/ppermute | solution.py:83
  71.9 3.6 %advance.3 = (f32[1024,256]{1,0:T(8,128)}, f32[1024,256]{1,0:T(8,128)S(1)}) custom-call(bf16[96,256]{1,0:T(8,128)(2,1)S(1)} %get-tuple-element.78.refs_0_.y_ref, f32[1024,256]{1,0:T(8,128)S(1)} %couple.2.token.refs_1_.base_ref, bf16[1024,96]{1,0:T(8,128)(2,1)S(1)} %get-tuple-element.58.refs_2_.lb_ref, bf16[1024,96]{1,0:T(8,128)(2,1)S(1)} %get-tuple-element.59.refs_3_, ...), custom_call_target="tpu_custom_call" | custom-call | flops 1342177280 | bytes 9289728 | tf_op jit(solution)/shard_map/advance/pallas_call | solution.py:25
  75.6 0.6 collective-permute-done.28.refs_2_
  76.2 1.3 %couple.3 = f32[1024,256]{1,0:T(8,128)} custom-call(f32[1024,256]{1,0:T(8,128)S(1)} %get-tuple-element.85.res_ref, bf16[1024,512]{1,0:T(8,128)(2,1)S(1)} %get-tuple-element.50.wt_ref.refs_4_, bf16[128,256]{1,0:T(8,128)(2,1)S(1)} %collective-permute-done.26.refs_0_, bf16[128,256]{1,0:T(8,128)(2,1)S(1)} %collective-permute-done.27.refs_1_, ...), custom_call_target="tpu_custom_call" | custom-call | flops 268435456 | bytes 2359296 | tf_op jit(solution)/shard_map/couple/pallas_call | solution.py:25
  (44 shorter events, 2.0 us)
Async XLA Ops:
  0.6 10.5 %copy-start.4 = (bf16[96,1024]{1,0:T(8,128)(2,1)S(1)}, bf16[96,1024]{1,0:T(8,128)(2,1)}, u32[]{:S(2)}) copy-start(bf16[96,1024]{1,0:T(8,128)(2,1)} %refs_8_.3) | copy-start | bytes 589828
  0.6 10.5 %copy-start.1 = (bf16[1024,1024]{1,0:T(8,128)(2,1)S(1)}, bf16[1024,1024]{1,0:T(8,128)(2,1)}, u32[]{:S(2)}) copy-start(bf16[1024,1024]{1,0:T(8,128)(2,1)} %refs_5_.3) | copy-start | bytes 6291460
  2.3 6.5 %collective-permute-start.2 = (bf16[96,256]{1,0:T(8,128)(2,1)S(1)}, bf16[96,256]{1,0:T(8,128)(2,1)S(1)}, u32[]{:S(2)}, u32[]{:S(2)}) collective-permute-start(bf16[96,256]{1,0:T(8,128)(2,1)S(1)} %convolution_convert_fusion.token.refs_0_), channel_id=1, source_target_pairs={{0,3},{1,2},{2,1},{3,0},{4,7},{5,6},{6,5},{7,4},{8,11},{9,10},{10,... | collective-permute-start | bytes 147464 | tf_op jit(solution)/shard_map/ppermute | solution.py:139
  4.8 4.3 %collective-permute-start.1 = (bf16[96,256]{1,0:T(8,128)(2,1)S(1)}, bf16[96,256]{1,0:T(8,128)(2,1)S(1)}, u32[]{:S(2)}, u32[]{:S(2)}) collective-permute-start(bf16[96,256]{1,0:T(8,128)(2,1)S(1)} %convolution_convert_fusion.token.refs_0_), channel_id=1, source_target_pairs={{0,2},{1,3},{2,0},{3,1},{4,6},{5,7},{6,4},{7,5},{8,10},{9,11},{10,... | collective-permute-start | bytes 147464 | tf_op jit(solution)/shard_map/ppermute | solution.py:139
  5.5 3.7 %collective-permute-start = (bf16[96,256]{1,0:T(8,128)(2,1)S(1)}, bf16[96,256]{1,0:T(8,128)(2,1)S(1)}, u32[]{:S(2)}, u32[]{:S(2)}) collective-permute-start(bf16[96,256]{1,0:T(8,128)(2,1)S(1)} %convolution_convert_fusion.token.refs_0_), channel_id=1, source_target_pairs={{0,1},{1,0},{2,3},{3,2},{4,5},{5,4},{6,7},{7,6},{8,9},{9,8},{10,11... | collective-permute-start | bytes 147464 | tf_op jit(solution)/shard_map/ppermute | solution.py:139
  6.9 1.1 %copy-start.5 = (bf16[768,384]{1,0:T(8,128)(2,1)S(1)}, bf16[768,384]{1,0:T(8,128)(2,1)}, u32[]{:S(2)}) copy-start(bf16[768,384]{1,0:T(8,128)(2,1)} %inv_hbm.1) | copy-start | bytes 1769476
  9.6 7.1 %collective-permute-start.3 = (bf16[384,256]{1,0:T(8,128)(2,1)S(1)}, bf16[384,256]{1,0:T(8,128)(2,1)S(1)}, u32[]{:S(2)}, u32[]{:S(2)}) collective-permute-start(bf16[384,256]{1,0:T(8,128)(2,1)S(1)} %get-tuple-element.48), channel_id=1, source_target_pairs={{0,4},{4,0},{8,12},{12,8},{16,20},{20,16},{24,28},{28,24},{1,5},{5... | collective-permute-start | bytes 589832 | tf_op jit(solution)/shard_map/ppermute | solution.py:146
  11.2 1.6 %copy-start.2 = (bf16[1024,1024]{1,0:T(8,128)(2,1)S(1)}, bf16[1024,1024]{1,0:T(8,128)(2,1)}, u32[]{:S(2)}) copy-start(bf16[1024,1024]{1,0:T(8,128)(2,1)} %refs_6_.3) | copy-start | bytes 6291460
  12.8 17.1 %copy-start = (f32[1024,256]{1,0:T(8,128)S(1)}, f32[1024,256]{1,0:T(8,128)}, u32[]{:S(2)}) copy-start(f32[1024,256]{1,0:T(8,128)} %refs_7_.3) | copy-start | bytes 3145732
  16.7 4.5 %collective-permute-start.4 = (bf16[96,256]{1,0:T(8,128)(2,1)S(1)}, bf16[96,256]{1,0:T(8,128)(2,1)S(1)}, u32[]{:S(2)}, u32[]{:S(2)}) collective-permute-start(bf16[96,256]{1,0:T(8,128)(2,1)S(1)} %get-tuple-element.53), channel_id=1, source_target_pairs={{0,8},{4,12},{8,0},{12,4},{16,24},{20,28},{24,16},{28,20},{1,9},{5... | collective-permute-start | bytes 147464 | tf_op jit(solution)/shard_map/ppermute | solution.py:154
  18.3 5.9 %collective-permute-start.5 = (bf16[96,256]{1,0:T(8,128)(2,1)S(1)}, bf16[96,256]{1,0:T(8,128)(2,1)S(1)}, u32[]{:S(2)}, u32[]{:S(2)}) collective-permute-start(bf16[96,256]{1,0:T(8,128)(2,1)S(1)} %get-tuple-element.54), channel_id=1, source_target_pairs={{0,16},{4,20},{8,24},{12,28},{16,0},{20,4},{24,8},{28,12},{1,17},{... | collective-permute-start | bytes 147464 | tf_op jit(solution)/shard_map/ppermute | solution.py:154
  20.9 5.9 %collective-permute-start.6 = (bf16[96,256]{1,0:T(8,128)(2,1)S(1)}, bf16[96,256]{1,0:T(8,128)(2,1)S(1)}, u32[]{:S(2)}, u32[]{:S(2)}) collective-permute-start(bf16[96,256]{1,0:T(8,128)(2,1)S(1)} %get-tuple-element.55), channel_id=1, source_target_pairs={{0,24},{4,28},{8,16},{12,20},{16,8},{20,12},{24,0},{28,4},{1,25},{... | collective-permute-start | bytes 147464 | tf_op jit(solution)/shard_map/ppermute | solution.py:154
  27.1 4.0 %collective-permute-start.7 = (bf16[128,256]{1,0:T(8,128)(2,1)S(1)}, bf16[128,256]{1,0:T(8,128)(2,1)S(1)}, u32[]{:S(2)}, u32[]{:S(2)}) collective-permute-start(bf16[128,256]{1,0:T(8,128)(2,1)S(1)} %get-tuple-element.60), channel_id=1, source_target_pairs={{0,1},{1,0},{2,3},{3,2},{4,8},{5,9},{6,10},{7,11},{8,4},{9,5},{10,... | collective-permute-start | bytes 196616 | tf_op jit(solution)/shard_map/ppermute | solution.py:83
  27.1 4.5 %collective-permute-start.8 = (bf16[128,256]{1,0:T(8,128)(2,1)S(1)}, bf16[128,256]{1,0:T(8,128)(2,1)S(1)}, u32[]{:S(2)}, u32[]{:S(2)}) collective-permute-start(bf16[128,256]{1,0:T(8,128)(2,1)S(1)} %get-tuple-element.61), channel_id=1, source_target_pairs={{0,4},{1,2},{2,1},{3,7},{4,0},{5,6},{6,5},{7,3},{8,12},{9,10},{10,... | collective-permute-start | bytes 196616 | tf_op jit(solution)/shard_map/ppermute | solution.py:83
  28.7 4.3 %collective-permute-start.9 = (bf16[128,256]{1,0:T(8,128)(2,1)S(1)}, bf16[128,256]{1,0:T(8,128)(2,1)S(1)}, u32[]{:S(2)}, u32[]{:S(2)}) collective-permute-start(bf16[128,256]{1,0:T(8,128)(2,1)S(1)} %get-tuple-element.62), channel_id=1, source_target_pairs={{0,4},{1,5},{2,6},{3,7},{4,0},{5,1},{6,2},{7,3},{8,12},{9,13},{10,... | collective-permute-start | bytes 196616 | tf_op jit(solution)/shard_map/ppermute | solution.py:83
  29.2 3.7 %collective-permute-start.10 = (bf16[128,256]{1,0:T(8,128)(2,1)S(1)}, bf16[128,256]{1,0:T(8,128)(2,1)S(1)}, u32[]{:S(2)}, u32[]{:S(2)}) collective-permute-start(bf16[128,256]{1,0:T(8,128)(2,1)S(1)} %get-tuple-element.63), channel_id=1, source_target_pairs={{0,1},{1,0},{2,3},{3,2},{4,5},{5,4},{6,7},{7,6},{8,9},{9,8},{10,11... | collective-permute-start | bytes 196616 | tf_op jit(solution)/shard_map/ppermute | solution.py:83
  29.9 7.7 %copy-start.3 = (bf16[1024,1024]{1,0:T(8,128)(2,1)S(1)}, bf16[1024,1024]{1,0:T(8,128)(2,1)}, u32[]{:S(2)}) copy-start(bf16[1024,1024]{1,0:T(8,128)(2,1)} %refs_6_.3) | copy-start | bytes 6291460
  33.3 8.2 %collective-permute-start.11 = (bf16[128,256]{1,0:T(8,128)(2,1)S(1)}, bf16[128,256]{1,0:T(8,128)(2,1)S(1)}, u32[]{:S(2)}, u32[]{:S(2)}) collective-permute-start(bf16[128,256]{1,0:T(8,128)(2,1)S(1)} %get-tuple-element.67.refs_0_), channel_id=1, source_target_pairs={{0,1},{1,0},{2,3},{3,2},{4,8},{5,9},{6,10},{7,11},{8,4},{9,5},{10,... | collective-permute-start | bytes 196616 | tf_op jit(solution)/shard_map/ppermute | solution.py:83
  33.3 8.1 %collective-permute-start.12 = (bf16[128,256]{1,0:T(8,128)(2,1)S(1)}, bf16[128,256]{1,0:T(8,128)(2,1)S(1)}, u32[]{:S(2)}, u32[]{:S(2)}) collective-permute-start(bf16[128,256]{1,0:T(8,128)(2,1)S(1)} %get-tuple-element.68.refs_1_), channel_id=1, source_target_pairs={{0,4},{1,2},{2,1},{3,7},{4,0},{5,6},{6,5},{7,3},{8,12},{9,10},{10,... | collective-permute-start | bytes 196616 | tf_op jit(solution)/shard_map/ppermute | solution.py:83
  37.6 4.3 %collective-permute-start.13 = (bf16[128,256]{1,0:T(8,128)(2,1)S(1)}, bf16[128,256]{1,0:T(8,128)(2,1)S(1)}, u32[]{:S(2)}, u32[]{:S(2)}) collective-permute-start(bf16[128,256]{1,0:T(8,128)(2,1)S(1)} %get-tuple-element.69.refs_2_), channel_id=1, source_target_pairs={{0,4},{1,5},{2,6},{3,7},{4,0},{5,1},{6,2},{7,3},{8,12},{9,13},{10,... | collective-permute-start | bytes 196616 | tf_op jit(solution)/shard_map/ppermute | solution.py:83
  37.6 4.2 %collective-permute-start.14 = (bf16[128,256]{1,0:T(8,128)(2,1)S(1)}, bf16[128,256]{1,0:T(8,128)(2,1)S(1)}, u32[]{:S(2)}, u32[]{:S(2)}) collective-permute-start(bf16[128,256]{1,0:T(8,128)(2,1)S(1)} %get-tuple-element.70.refs_3_), channel_id=1, source_target_pairs={{0,1},{1,0},{2,3},{3,2},{4,5},{5,4},{6,7},{7,6},{8,9},{9,8},{10,11... | collective-permute-start | bytes 196616 | tf_op jit(solution)/shard_map/ppermute | solution.py:83
  42.0 3.8 %collective-permute-start.17 = (bf16[96,256]{1,0:T(8,128)(2,1)S(1)}, bf16[96,256]{1,0:T(8,128)(2,1)S(1)}, u32[]{:S(2)}, u32[]{:S(2)}) collective-permute-start(bf16[96,256]{1,0:T(8,128)(2,1)S(1)} %restrict_recv.1.refs_0_), channel_id=1, source_target_pairs={{0,3},{1,2},{2,1},{3,0},{4,7},{5,6},{6,5},{7,4},{8,11},{9,10},{10,... | collective-permute-start | bytes 147464 | tf_op jit(solution)/shard_map/ppermute | solution.py:139
  43.1 4.1 %collective-permute-start.16 = (bf16[96,256]{1,0:T(8,128)(2,1)S(1)}, bf16[96,256]{1,0:T(8,128)(2,1)S(1)}, u32[]{:S(2)}, u32[]{:S(2)}) collective-permute-start(bf16[96,256]{1,0:T(8,128)(2,1)S(1)} %restrict_recv.1.refs_0_), channel_id=1, source_target_pairs={{0,2},{1,3},{2,0},{3,1},{4,6},{5,7},{6,4},{7,5},{8,10},{9,11},{10,... | collective-permute-start | bytes 147464 | tf_op jit(solution)/shard_map/ppermute | solution.py:139
  43.9 3.3 %collective-permute-start.15 = (bf16[96,256]{1,0:T(8,128)(2,1)S(1)}, bf16[96,256]{1,0:T(8,128)(2,1)S(1)}, u32[]{:S(2)}, u32[]{:S(2)}) collective-permute-start(bf16[96,256]{1,0:T(8,128)(2,1)S(1)} %restrict_recv.1.refs_0_), channel_id=1, source_target_pairs={{0,1},{1,0},{2,3},{3,2},{4,5},{5,4},{6,7},{7,6},{8,9},{9,8},{10,11... | collective-permute-start | bytes 147464 | tf_op jit(solution)/shard_map/ppermute | solution.py:139
  47.7 6.1 %collective-permute-start.18 = (bf16[384,256]{1,0:T(8,128)(2,1)S(1)}, bf16[384,256]{1,0:T(8,128)(2,1)S(1)}, u32[]{:S(2)}, u32[]{:S(2)}) collective-permute-start(bf16[384,256]{1,0:T(8,128)(2,1)S(1)} %get-tuple-element.72), channel_id=1, source_target_pairs={{0,4},{4,0},{8,12},{12,8},{16,20},{20,16},{24,28},{28,24},{1,5},{5... | collective-permute-start | bytes 589832 | tf_op jit(solution)/shard_map/ppermute | solution.py:146
  53.8 4.7 %collective-permute-start.19 = (bf16[96,256]{1,0:T(8,128)(2,1)S(1)}, bf16[96,256]{1,0:T(8,128)(2,1)S(1)}, u32[]{:S(2)}, u32[]{:S(2)}) collective-permute-start(bf16[96,256]{1,0:T(8,128)(2,1)S(1)} %get-tuple-element.75), channel_id=1, source_target_pairs={{0,8},{4,12},{8,0},{12,4},{16,24},{20,28},{24,16},{28,20},{1,9},{5... | collective-permute-start | bytes 147464 | tf_op jit(solution)/shard_map/ppermute | solution.py:154
  55.5 5.4 %collective-permute-start.20 = (bf16[96,256]{1,0:T(8,128)(2,1)S(1)}, bf16[96,256]{1,0:T(8,128)(2,1)S(1)}, u32[]{:S(2)}, u32[]{:S(2)}) collective-permute-start(bf16[96,256]{1,0:T(8,128)(2,1)S(1)} %get-tuple-element.76), channel_id=1, source_target_pairs={{0,16},{4,20},{8,24},{12,28},{16,0},{20,4},{24,8},{28,12},{1,17},{... | collective-permute-start | bytes 147464 | tf_op jit(solution)/shard_map/ppermute | solution.py:154
  55.7 6.0 %collective-permute-start.21 = (bf16[96,256]{1,0:T(8,128)(2,1)S(1)}, bf16[96,256]{1,0:T(8,128)(2,1)S(1)}, u32[]{:S(2)}, u32[]{:S(2)}) collective-permute-start(bf16[96,256]{1,0:T(8,128)(2,1)S(1)} %get-tuple-element.77), channel_id=1, source_target_pairs={{0,24},{4,28},{8,16},{12,20},{16,8},{20,12},{24,0},{28,4},{1,25},{... | collective-permute-start | bytes 147464 | tf_op jit(solution)/shard_map/ppermute | solution.py:154
  61.9 4.3 %collective-permute-start.22 = (bf16[128,256]{1,0:T(8,128)(2,1)S(1)}, bf16[128,256]{1,0:T(8,128)(2,1)S(1)}, u32[]{:S(2)}, u32[]{:S(2)}) collective-permute-start(bf16[128,256]{1,0:T(8,128)(2,1)S(1)} %get-tuple-element.79), channel_id=1, source_target_pairs={{0,1},{1,0},{2,3},{3,2},{4,8},{5,9},{6,10},{7,11},{8,4},{9,5},{10,... | collective-permute-start | bytes 196616 | tf_op jit(solution)/shard_map/ppermute | solution.py:83
  62.0 5.0 %collective-permute-start.23 = (bf16[128,256]{1,0:T(8,128)(2,1)S(1)}, bf16[128,256]{1,0:T(8,128)(2,1)S(1)}, u32[]{:S(2)}, u32[]{:S(2)}) collective-permute-start(bf16[128,256]{1,0:T(8,128)(2,1)S(1)} %get-tuple-element.80), channel_id=1, source_target_pairs={{0,4},{1,2},{2,1},{3,7},{4,0},{5,6},{6,5},{7,3},{8,12},{9,10},{10,... | collective-permute-start | bytes 196616 | tf_op jit(solution)/shard_map/ppermute | solution.py:83
  64.3 4.3 %collective-permute-start.24 = (bf16[128,256]{1,0:T(8,128)(2,1)S(1)}, bf16[128,256]{1,0:T(8,128)(2,1)S(1)}, u32[]{:S(2)}, u32[]{:S(2)}) collective-permute-start(bf16[128,256]{1,0:T(8,128)(2,1)S(1)} %get-tuple-element.81), channel_id=1, source_target_pairs={{0,4},{1,5},{2,6},{3,7},{4,0},{5,1},{6,2},{7,3},{8,12},{9,13},{10,... | collective-permute-start | bytes 196616 | tf_op jit(solution)/shard_map/ppermute | solution.py:83
  64.3 4.2 %collective-permute-start.25 = (bf16[128,256]{1,0:T(8,128)(2,1)S(1)}, bf16[128,256]{1,0:T(8,128)(2,1)S(1)}, u32[]{:S(2)}, u32[]{:S(2)}) collective-permute-start(bf16[128,256]{1,0:T(8,128)(2,1)S(1)} %get-tuple-element.82), channel_id=1, source_target_pairs={{0,1},{1,0},{2,3},{3,2},{4,5},{5,4},{6,7},{7,6},{8,9},{9,8},{10,11... | collective-permute-start | bytes 196616 | tf_op jit(solution)/shard_map/ppermute | solution.py:83
  68.8 6.8 %collective-permute-start.26 = (bf16[128,256]{1,0:T(8,128)(2,1)S(1)}, bf16[128,256]{1,0:T(8,128)(2,1)S(1)}, u32[]{:S(2)}, u32[]{:S(2)}) collective-permute-start(bf16[128,256]{1,0:T(8,128)(2,1)S(1)} %get-tuple-element.86), channel_id=1, source_target_pairs={{0,1},{1,0},{2,3},{3,2},{4,8},{5,9},{6,10},{7,11},{8,4},{9,5},{10,... | collective-permute-start | bytes 196616 | tf_op jit(solution)/shard_map/ppermute | solution.py:83
  68.9 6.7 %collective-permute-start.27 = (bf16[128,256]{1,0:T(8,128)(2,1)S(1)}, bf16[128,256]{1,0:T(8,128)(2,1)S(1)}, u32[]{:S(2)}, u32[]{:S(2)}) collective-permute-start(bf16[128,256]{1,0:T(8,128)(2,1)S(1)} %get-tuple-element.87), channel_id=1, source_target_pairs={{0,4},{1,2},{2,1},{3,7},{4,0},{5,6},{6,5},{7,3},{8,12},{9,10},{10,... | collective-permute-start | bytes 196616 | tf_op jit(solution)/shard_map/ppermute | solution.py:83
  71.9 4.3 %collective-permute-start.28 = (bf16[128,256]{1,0:T(8,128)(2,1)S(1)}, bf16[128,256]{1,0:T(8,128)(2,1)S(1)}, u32[]{:S(2)}, u32[]{:S(2)}) collective-permute-start(bf16[128,256]{1,0:T(8,128)(2,1)S(1)} %get-tuple-element.88), channel_id=1, source_target_pairs={{0,4},{1,5},{2,6},{3,7},{4,0},{5,1},{6,2},{7,3},{8,12},{9,13},{10,... | collective-permute-start | bytes 196616 | tf_op jit(solution)/shard_map/ppermute | solution.py:83
  71.9 4.2 %collective-permute-start.29 = (bf16[128,256]{1,0:T(8,128)(2,1)S(1)}, bf16[128,256]{1,0:T(8,128)(2,1)S(1)}, u32[]{:S(2)}, u32[]{:S(2)}) collective-permute-start(bf16[128,256]{1,0:T(8,128)(2,1)S(1)} %get-tuple-element.89), channel_id=1, source_target_pairs={{0,1},{1,0},{2,3},{3,2},{4,5},{5,4},{6,7},{7,6},{8,9},{9,8},{10,11... | collective-permute-start | bytes 196616 | tf_op jit(solution)/shard_map/ppermute | solution.py:83

commit v3 on v2

--- a/solution.py
+++ b/solution.py
@@ -34,8 +34,8 @@
     )(*args)
 
 
-def tiles(rows):
-    return 256 if rows % 256 == 0 else rows
+def tiles(rows, most=512):
+    return most if rows % most == 0 else rows
 
 
 def per_device(nr, nc, rhs, local_mat, local_inv, basis_t, coarse_inv, couple, margin_rows):
@@ -46,7 +46,7 @@
     nz = nr // 2
     both = ("row", "col")
 
-    step = tiles(nloc)
+    step, last_step = tiles(nloc), tiles(nloc, 256)
 
     def row_loop(body):
         @pl.loop(0, nloc // step)
@@ -62,7 +62,7 @@
                     other = (o, c) if 0 <= o < nr else (r, c ^ 1)
                 else:
                     o = c + 1 if c % 2 == col_parity else c - 1
-                    other = (r, o) if 0 <= o < nc else (r ^ 1, c)
+                    other = (r, o) if 0 <= o < nc else (r, nc - 1 - c)
                 perm[r * nc + c] = other[0] * nc + other[1]
         return sorted(perm.items())
 
@@ -272,8 +272,8 @@
         for s, x in enumerate(recvs):
             recv[pl.ds(s * ovl, ovl), :] = x[...]
         copies = []
-        for i in range(nloc // step):
-            at = pl.ds(i * step, step)
+        for i in range(nloc // last_step):
+            at = pl.ds(i * last_step, last_step)
             buf[at, :] = res_ref[at, :] + mm(wt_ref[at, :], recv[...])
             copies.append(pltpu.make_async_copy(buf.at[at, :], out_ref.at[at, :], sems.at[i]))
             copies[-1].start()
@@ -281,7 +281,7 @@
             copy.wait()
 
     def coupled(res, recv, last):
-        extra = [pltpu.VMEM((nloc, nrhs), F32), pltpu.SemaphoreType.DMA((nloc // step,))] if last else []
+        extra = [pltpu.VMEM((nloc, nrhs), F32), pltpu.SemaphoreType.DMA((nloc // last_step,))] if last else []
         return call(
             k_couple_last if last else k_couple, [((nloc, nrhs), F32)], res, wt, *recv,
             scratch=[pltpu.VMEM((nf, nrhs), BF)] + extra, hbm_outs=1 if last else 0,

time: 77.7 us -> 75.2 us (0.968)
  Pallas kernels: 18.9 us -> 15.6 us
    pallas_call x17, Pallas kernels: 18.9 us -> 15.6 us  [call(): pl.pallas_call(kernel, out_shape=[jax.ShapeDtypeStruct(s, d) for s, d in...]
    ppermute x2, waiting for transfers between devices: 3.57 us -> 5.42 us  [coarse_send(): return (keep, lax.ppermute(send, 'row', [(i, i ^ 1) for i in range(nr)]))]
    ppermute x16, waiting for transfers between devices: 5.02 us -> 3.68 us  [halo(): return [lax.ppermute(f, both, p) for f, p in zip(faces, slot_perms)]]
    ppermute x16, starting transfers between devices: 13.4 us -> 14.3 us  [halo(): return [lax.ppermute(f, both, p) for f, p in zip(faces, slot_perms)]]
  transfers between devices with their start and end apart: 30 -> 30, of which waited for: 16 -> 12; matrix products, arithmetic and copies ran while one was open for 2% -> 2% of each run, Pallas kernels for 20% -> 16%
where the time goes in v3:
time: 75.2 us; the launch traced here: 75 us
  starting transfers between devices  31.2 us (41%)
  waiting for transfers between devices  21.5 us (29%)
  Pallas kernels  15.6 us (21%)
  local copies, waits for them, and re-layouts  2.67 us (4%)
  matrix products  1.69 us (2%)
  other arithmetic  1.37 us (2%)
  between operations  0.9 us (1%)
    pallas_call x17, Pallas kernels, call(): pl.pallas_call(kernel, out_shape=[jax.ShapeDtypeStruct(s, d) for s, d in...  15.6 us
    ppermute x16, starting transfers between devices, halo(): return [lax.ppermute(f, both, p) for f, p in zip(faces, slot_perms)]  14.3 us
    ppermute x6, starting transfers between devices, coarse_recv(): lax.ppermute(s, 'row', [(i, i ^ 2 * (k + 1)) for i in range(nr)])  8.9 us
    ppermute x6, waiting for transfers between devices, coarse_recv(): lax.ppermute(s, 'row', [(i, i ^ 2 * (k + 1)) for i in range(nr)])  8.82 us
    ppermute x2, waiting for transfers between devices, coarse_send(): return (keep, lax.ppermute(send, 'row', [(i, i ^ 1) for i in range(nr)]))  5.42 us
    ppermute x6, starting transfers between devices, coarse_send(): lax.ppermute(restricted, 'col', [(i, i ^ k) for i in range(nc)])  5.08 us
    ppermute x16, waiting for transfers between devices, halo(): return [lax.ppermute(f, both, p) for f, p in zip(faces, slot_perms)]  3.68 us
    ppermute x6, waiting for transfers between devices, coarse_send(): lax.ppermute(restricted, 'col', [(i, i ^ k) for i in range(nc)])  3.54 us
  transfers between devices with their start and end apart: 30, of which 12 were waited for; matrix products, arithmetic and copies ran while one was open for 2% of the time, Pallas kernels for 16%

profile of v3, /device:TPU:0, one launch (start us, length us, event | category | flops | bytes accessed | tf_op | source)
XLA Modules:
  0.0 75.0 jit_solution(3291999791667177615)
XLA Ops:
  0.6 1.7 %convolution_convert_fusion.token.refs_0_ = bf16[96,256]{1,0:T(8,128)(2,1)S(1)} fusion(bf16[96,1024]{1,0:T(8,128)(2,1)} %refs_8_.3, f32[1024,256]{1,0:T(8,128)} %refs_7_.3), kind=kOutput, calls=%fused_computation | convolution fusion | flops 50618368 | bytes 1294336 | tf_op jit(solution)/shard_map/dot_general | solution.py:19
  2.3 2.5 %collective-permute-start.2 = (bf16[96,256]{1,0:T(8,128)(2,1)S(1)}, bf16[96,256]{1,0:T(8,128)(2,1)S(1)}, u32[]{:S(2)}, u32[]{:S(2)}) collective-permute-start(bf16[96,256]{1,0:T(8,128)(2,1)S(1)} %convolution_convert_fusion.token.refs_0_), channel_id=1, source_target_pairs={{0,3},{1,2},{2,1},{3,0},{4,7},{5,6},{6,5},{7,4},{8,11},{9,10},{10,... | collective-permute-start | bytes 147464 | tf_op jit(solution)/shard_map/ppermute | solution.py:139
  4.8 0.6 collective-permute-start.1
  5.5 0.7 convert_bitcast_fusion
  6.2 0.7 pad_maximum_fusion.table_ref
  6.9 1.1 %copy-done.5 = bf16[768,384]{1,0:T(8,128)(2,1)S(1)} copy-done((bf16[768,384]{1,0:T(8,128)(2,1)S(1)}, bf16[768,384]{1,0:T(8,128)(2,1)}, u32[]{:S(2)}) %copy-start.5) | copy-done | bytes 589848
  7.9 0.9 %select.1 = (bf16[512,1024]{1,0:T(8,128)(2,1)S(1)}, bf16[1024,512]{1,0:T(8,128)(2,1)S(1)}, bf16[768,384]{1,0:T(8,128)(2,1)S(1)}) custom-call(bf16[768,384]{1,0:T(8,128)(2,1)S(1)} %copy-done.5, f32[8,128]{1,0:T(8,128)S(1)} %pad_maximum_fusion.table_ref, bf16[96,256]{1,0:T(8,128)(2,1)S(1)} %convolution_convert_fusion.token.refs_0_), custom_call_target="tpu_custom_call" | custom-call | bytes 643072 | tf_op jit(solution)/shard_map/select/pallas_call | solution.py:25
  9.1 0.4 coarse.2
  9.6 1.6 %collective-permute-start.3 = (bf16[384,256]{1,0:T(8,128)(2,1)S(1)}, bf16[384,256]{1,0:T(8,128)(2,1)S(1)}, u32[]{:S(2)}, u32[]{:S(2)}) collective-permute-start(bf16[384,256]{1,0:T(8,128)(2,1)S(1)} %get-tuple-element.48), channel_id=1, source_target_pairs={{0,4},{4,0},{8,12},{12,8},{16,20},{20,16},{24,28},{28,24},{1,5},{5... | collective-permute-start | bytes 589832 | tf_op jit(solution)/shard_map/ppermute | solution.py:146
  11.2 1.6 %copy-done.2 = bf16[1024,1024]{1,0:T(8,128)(2,1)S(1)} copy-done((bf16[1024,1024]{1,0:T(8,128)(2,1)S(1)}, bf16[1024,1024]{1,0:T(8,128)(2,1)}, u32[]{:S(2)}) %copy-start.2) | copy-done | bytes 2097176
  12.8 3.2 %products.1 = (bf16[512,96]{1,0:T(8,128)(2,1)S(1)}, bf16[96,512]{1,0:T(8,128)(2,1)S(1)}, bf16[512,1024]{1,0:T(8,128)(2,1)S(1)}, bf16[512,512]{1,0:T(8,128)(2,1)S...) custom-call(bf16[512,1024]{1,0:T(8,128)(2,1)S(1)} %get-tuple-element.49.sel_ref, ...), custom_call_target="tpu_custom_call" | custom-call | flops 1912602624 | bytes 6881280 | tf_op jit(solution)/shard_map/products/pallas_call | solution.py:25
  16.0 0.7 collective-permute-done.3.recv_ref
  16.7 1.6 %collective-permute-start.4 = (bf16[96,256]{1,0:T(8,128)(2,1)S(1)}, bf16[96,256]{1,0:T(8,128)(2,1)S(1)}, u32[]{:S(2)}, u32[]{:S(2)}) collective-permute-start(bf16[96,256]{1,0:T(8,128)(2,1)S(1)} %get-tuple-element.53), channel_id=1, source_target_pairs={{0,8},{4,12},{8,0},{12,4},{16,24},{20,28},{24,16},{28,20},{1,9},{5... | collective-permute-start | bytes 147464 | tf_op jit(solution)/shard_map/ppermute | solution.py:154
  18.3 2.6 %collective-permute-start.5 = (bf16[96,256]{1,0:T(8,128)(2,1)S(1)}, bf16[96,256]{1,0:T(8,128)(2,1)S(1)}, u32[]{:S(2)}, u32[]{:S(2)}) collective-permute-start(bf16[96,256]{1,0:T(8,128)(2,1)S(1)} %get-tuple-element.54), channel_id=1, source_target_pairs={{0,16},{4,20},{8,24},{12,28},{16,0},{20,4},{24,8},{28,12},{1,17},{... | collective-permute-start | bytes 147464 | tf_op jit(solution)/shard_map/ppermute | solution.py:154
  21.1 2.7 %collective-permute-done.5.refs_2_ = bf16[96,256]{1,0:T(8,128)(2,1)S(1)} collective-permute-done((bf16[96,256]{1,0:T(8,128)(2,1)S(1)}, bf16[96,256]{1,0:T(8,128)(2,1)S(1)}, u32[]{:S(2)}, u32[]{:S(2)}) %collective-permute-start.5) | collective-permute-done | bytes 49184 | tf_op jit(solution)/shard_map/ppermute | solution.py:154
  23.8 3.0 %collective-permute-done.6.refs_3_ = bf16[96,256]{1,0:T(8,128)(2,1)S(1)} collective-permute-done((bf16[96,256]{1,0:T(8,128)(2,1)S(1)}, bf16[96,256]{1,0:T(8,128)(2,1)S(1)}, u32[]{:S(2)}, u32[]{:S(2)}) %collective-permute-start.6) | collective-permute-done | bytes 49184 | tf_op jit(solution)/shard_map/ppermute | solution.py:154
  27.1 1.5 %collective-permute-start.8 = (bf16[128,256]{1,0:T(8,128)(2,1)S(1)}, bf16[128,256]{1,0:T(8,128)(2,1)S(1)}, u32[]{:S(2)}, u32[]{:S(2)}) collective-permute-start(bf16[128,256]{1,0:T(8,128)(2,1)S(1)} %get-tuple-element.61), channel_id=1, source_target_pairs={{0,3},{1,2},{2,1},{3,0},{4,7},{5,6},{6,5},{7,4},{8,11},{9,10},{10,... | collective-permute-start | bytes 196616 | tf_op jit(solution)/shard_map/ppermute | solution.py:83
  28.8 1.1 %collective-permute-start.10 = (bf16[128,256]{1,0:T(8,128)(2,1)S(1)}, bf16[128,256]{1,0:T(8,128)(2,1)S(1)}, u32[]{:S(2)}, u32[]{:S(2)}) collective-permute-start(bf16[128,256]{1,0:T(8,128)(2,1)S(1)} %get-tuple-element.63), channel_id=1, source_target_pairs={{0,1},{1,0},{2,3},{3,2},{4,5},{5,4},{6,7},{7,6},{8,9},{9,8},{10,11... | collective-permute-start | bytes 196616 | tf_op jit(solution)/shard_map/ppermute | solution.py:83
  29.9 0.9 %local.2.base_ref = f32[512,256]{1,0:T(8,128)S(1)} custom-call(bf16[96,256]{1,0:T(8,128)(2,1)S(1)} %get-tuple-element.57.refs_0_.y_ref, f32[1024,256]{1,0:T(8,128)S(1)} %copy-done, bf16[1024,96]{1,0:T(8,128)(2,1)S(1)} %get-tuple-element.58.refs_2_.lb_ref, bf16[512,1024]{1,0:T(8,128)(2,1)S(1)} %get-tuple-element.65.si_ref, ...), custom_call_target="tpu_custom_call" | custom-call | flops 268435456 | bytes 2441216 | tf_op jit(solution)/shard_map/local/pallas_call | solution.py:25
  31.0 1.9 %collective-permute-done.9.refs_11_.refs_2_ = bf16[128,256]{1,0:T(8,128)(2,1)S(1)} collective-permute-done((bf16[128,256]{1,0:T(8,128)(2,1)S(1)}, bf16[128,256]{1,0:T(8,128)(2,1)S(1)}, u32[]{:S(2)}, u32[]{:S(2)}) %collective-permute-start.9) | collective-permute-done | bytes 65568 | tf_op jit(solution)/shard_map/ppermute | solution.py:83
  32.9 0.3 faces.2
  33.3 0.7 collective-permute-start.12
  34.0 3.2 %collective-permute-start.13 = (bf16[128,256]{1,0:T(8,128)(2,1)S(1)}, bf16[128,256]{1,0:T(8,128)(2,1)S(1)}, u32[]{:S(2)}, u32[]{:S(2)}) collective-permute-start(bf16[128,256]{1,0:T(8,128)(2,1)S(1)} %get-tuple-element.69.refs_2_), channel_id=1, source_target_pairs={{0,4},{1,5},{2,6},{3,7},{4,0},{5,1},{6,2},{7,3},{8,12},{9,13},{10,... | collective-permute-start | bytes 196616 | tf_op jit(solution)/shard_map/ppermute | solution.py:83
  37.3 0.6 collective-permute-start.14
  37.9 2.9 %advance.2 = (f32[1024,256]{1,0:T(8,128)S(1)}, f32[1024,256]{1,0:T(8,128)S(1)}, f32[96,256]{1,0:T(8,128)S(1)}) custom-call(bf16[96,256]{1,0:T(8,128)(2,1)S(1)} %get-tuple-element.57.refs_0_.y_ref, f32[1024,256]{1,0:T(8,128)S(1)} %copy-done, bf16[1024,96]{1,0:T(8,128)(2,1)S(1)} %get-tuple-element.58.refs_2_.lb_ref, ...), custom_call_target="tpu_custom_call" | custom-call | flops 1342177280 | bytes 8241152 | tf_op jit(solution)/shard_map/advance/pallas_call | solution.py:25
  41.0 0.3 collective-permute-start.17
  41.3 1.4 %collective-permute-start.16 = (bf16[96,256]{1,0:T(8,128)(2,1)S(1)}, bf16[96,256]{1,0:T(8,128)(2,1)S(1)}, u32[]{:S(2)}, u32[]{:S(2)}) collective-permute-start(bf16[96,256]{1,0:T(8,128)(2,1)S(1)} %restrict_recv.1.refs_0_), channel_id=1, source_target_pairs={{0,2},{1,3},{2,0},{3,1},{4,6},{5,7},{6,4},{7,5},{8,10},{9,11},{10,... | collective-permute-start | bytes 147464 | tf_op jit(solution)/shard_map/ppermute | solution.py:139
  42.9 2.0 %collective-permute-done.17.refs_3_ = bf16[96,256]{1,0:T(8,128)(2,1)S(1)} collective-permute-done((bf16[96,256]{1,0:T(8,128)(2,1)S(1)}, bf16[96,256]{1,0:T(8,128)(2,1)S(1)}, u32[]{:S(2)}, u32[]{:S(2)}) %collective-permute-start.17) | collective-permute-done | bytes 49184 | tf_op jit(solution)/shard_map/ppermute | solution.py:139
  44.9 1.2 %collective-permute-done.16.refs_2_ = bf16[96,256]{1,0:T(8,128)(2,1)S(1)} collective-permute-done((bf16[96,256]{1,0:T(8,128)(2,1)S(1)}, bf16[96,256]{1,0:T(8,128)(2,1)S(1)}, u32[]{:S(2)}, u32[]{:S(2)}) %collective-permute-start.16) | collective-permute-done | bytes 49184 | tf_op jit(solution)/shard_map/ppermute | solution.py:139
  46.1 0.4 coarse.3
  46.6 1.4 %collective-permute-start.18 = (bf16[384,256]{1,0:T(8,128)(2,1)S(1)}, bf16[384,256]{1,0:T(8,128)(2,1)S(1)}, u32[]{:S(2)}, u32[]{:S(2)}) collective-permute-start(bf16[384,256]{1,0:T(8,128)(2,1)S(1)} %get-tuple-element.72), channel_id=1, source_target_pairs={{0,4},{4,0},{8,12},{12,8},{16,20},{20,16},{24,28},{28,24},{1,5},{5... | collective-permute-start | bytes 589832 | tf_op jit(solution)/shard_map/ppermute | solution.py:146
  48.0 0.6 couple.2.token.refs_1_.base_ref
  48.6 4.7 %collective-permute-done.18.recv_ref = bf16[384,256]{1,0:T(8,128)(2,1)S(1)} collective-permute-done((bf16[384,256]{1,0:T(8,128)(2,1)S(1)}, bf16[384,256]{1,0:T(8,128)(2,1)S(1)}, u32[]{:S(2)}, u32[]{:S(2)}) %collective-permute-start.18) | collective-permute-done | bytes 196640 | tf_op jit(solution)/shard_map/ppermute | solution.py:146
  53.4 0.8 %collective-permute-start.19 = (bf16[96,256]{1,0:T(8,128)(2,1)S(1)}, bf16[96,256]{1,0:T(8,128)(2,1)S(1)}, u32[]{:S(2)}, u32[]{:S(2)}) collective-permute-start(bf16[96,256]{1,0:T(8,128)(2,1)S(1)} %get-tuple-element.75), channel_id=1, source_target_pairs={{0,8},{4,12},{8,0},{12,4},{16,24},{20,28},{24,16},{28,20},{1,9},{5... | collective-permute-start | bytes 147464 | tf_op jit(solution)/shard_map/ppermute | solution.py:154
  54.2 0.9 %collective-permute-start.20 = (bf16[96,256]{1,0:T(8,128)(2,1)S(1)}, bf16[96,256]{1,0:T(8,128)(2,1)S(1)}, u32[]{:S(2)}, u32[]{:S(2)}) collective-permute-start(bf16[96,256]{1,0:T(8,128)(2,1)S(1)} %get-tuple-element.76), channel_id=1, source_target_pairs={{0,16},{4,20},{8,24},{12,28},{16,0},{20,4},{24,8},{28,12},{1,17},{... | collective-permute-start | bytes 147464 | tf_op jit(solution)/shard_map/ppermute | solution.py:154
  55.1 2.8 %collective-permute-start.21 = (bf16[96,256]{1,0:T(8,128)(2,1)S(1)}, bf16[96,256]{1,0:T(8,128)(2,1)S(1)}, u32[]{:S(2)}, u32[]{:S(2)}) collective-permute-start(bf16[96,256]{1,0:T(8,128)(2,1)S(1)} %get-tuple-element.77), channel_id=1, source_target_pairs={{0,24},{4,28},{8,16},{12,20},{16,8},{20,12},{24,0},{28,4},{1,25},{... | collective-permute-start | bytes 147464 | tf_op jit(solution)/shard_map/ppermute | solution.py:154
  57.9 1.5 %collective-permute-done.20.refs_2_ = bf16[96,256]{1,0:T(8,128)(2,1)S(1)} collective-permute-done((bf16[96,256]{1,0:T(8,128)(2,1)S(1)}, bf16[96,256]{1,0:T(8,128)(2,1)S(1)}, u32[]{:S(2)}, u32[]{:S(2)}) %collective-permute-start.20) | collective-permute-done | bytes 49184 | tf_op jit(solution)/shard_map/ppermute | solution.py:154
  59.3 1.7 %collective-permute-done.21.refs_3_ = bf16[96,256]{1,0:T(8,128)(2,1)S(1)} collective-permute-done((bf16[96,256]{1,0:T(8,128)(2,1)S(1)}, bf16[96,256]{1,0:T(8,128)(2,1)S(1)}, u32[]{:S(2)}, u32[]{:S(2)}) %collective-permute-start.21) | collective-permute-done | bytes 49184 | tf_op jit(solution)/shard_map/ppermute | solution.py:154
  61.3 1.0 %collective-permute-start.23 = (bf16[128,256]{1,0:T(8,128)(2,1)S(1)}, bf16[128,256]{1,0:T(8,128)(2,1)S(1)}, u32[]{:S(2)}, u32[]{:S(2)}) collective-permute-start(bf16[128,256]{1,0:T(8,128)(2,1)S(1)} %get-tuple-element.80), channel_id=1, source_target_pairs={{0,3},{1,2},{2,1},{3,0},{4,7},{5,6},{6,5},{7,4},{8,11},{9,10},{10,... | collective-permute-start | bytes 196616 | tf_op jit(solution)/shard_map/ppermute | solution.py:83
  62.3 0.5 collective-permute-start.24
  62.8 1.4 %collective-permute-start.25 = (bf16[128,256]{1,0:T(8,128)(2,1)S(1)}, bf16[128,256]{1,0:T(8,128)(2,1)S(1)}, u32[]{:S(2)}, u32[]{:S(2)}) collective-permute-start(bf16[128,256]{1,0:T(8,128)(2,1)S(1)} %get-tuple-element.82), channel_id=1, source_target_pairs={{0,1},{1,0},{2,3},{3,2},{4,5},{5,4},{6,7},{7,6},{8,9},{9,8},{10,11... | collective-permute-start | bytes 196616 | tf_op jit(solution)/shard_map/ppermute | solution.py:83
  64.2 0.9 %local.3.base_ref = f32[512,256]{1,0:T(8,128)S(1)} custom-call(bf16[96,256]{1,0:T(8,128)(2,1)S(1)} %get-tuple-element.78.refs_0_.y_ref, f32[1024,256]{1,0:T(8,128)S(1)} %couple.2.token.refs_1_.base_ref, bf16[1024,96]{1,0:T(8,128)(2,1)S(1)} %get-tuple-element.58.refs_2_.lb_ref, bf16[512,1024]{1,0:T(8,128)(2,1)S(1)} %get-tuple-element.65.si_ref, ...), custom_call_target="tpu_custom_call" | custom-call | flops 268435456 | bytes 2703360 | tf_op jit(solution)/shard_map/local/pallas_call | solution.py:25
  65.1 1.6 %collective-permute-done.24.refs_11_.refs_2_ = bf16[128,256]{1,0:T(8,128)(2,1)S(1)} collective-permute-done((bf16[128,256]{1,0:T(8,128)(2,1)S(1)}, bf16[128,256]{1,0:T(8,128)(2,1)S(1)}, u32[]{:S(2)}, u32[]{:S(2)}) %collective-permute-start.24) | collective-permute-done | bytes 65568 | tf_op jit(solution)/shard_map/ppermute | solution.py:83
  67.1 1.1 %collective-permute-start.27 = (bf16[128,256]{1,0:T(8,128)(2,1)S(1)}, bf16[128,256]{1,0:T(8,128)(2,1)S(1)}, u32[]{:S(2)}, u32[]{:S(2)}) collective-permute-start(bf16[128,256]{1,0:T(8,128)(2,1)S(1)} %get-tuple-element.87), channel_id=1, source_target_pairs={{0,3},{1,2},{2,1},{3,0},{4,7},{5,6},{6,5},{7,4},{8,11},{9,10},{10,... | collective-permute-start | bytes 196616 | tf_op jit(solution)/shard_map/ppermute | solution.py:83
  68.2 2.3 %collective-permute-start.28 = (bf16[128,256]{1,0:T(8,128)(2,1)S(1)}, bf16[128,256]{1,0:T(8,128)(2,1)S(1)}, u32[]{:S(2)}, u32[]{:S(2)}) collective-permute-start(bf16[128,256]{1,0:T(8,128)(2,1)S(1)} %get-tuple-element.88), channel_id=1, source_target_pairs={{0,4},{1,5},{2,6},{3,7},{4,0},{5,1},{6,2},{7,3},{8,12},{9,13},{10,... | collective-permute-start | bytes 196616 | tf_op jit(solution)/shard_map/ppermute | solution.py:83
  70.5 0.4 collective-permute-start.29
  70.9 2.7 %advance.3 = (f32[1024,256]{1,0:T(8,128)}, f32[1024,256]{1,0:T(8,128)S(1)}) custom-call(bf16[96,256]{1,0:T(8,128)(2,1)S(1)} %get-tuple-element.78.refs_0_.y_ref, f32[1024,256]{1,0:T(8,128)S(1)} %couple.2.token.refs_1_.base_ref, bf16[1024,96]{1,0:T(8,128)(2,1)S(1)} %get-tuple-element.58.refs_2_.lb_ref, bf16[1024,96]{1,0:T(8,128)(2,1)S(1)} %get-tuple-element.59.refs_3_, ...), custom_call_target="tpu_custom_call" | custom-call | flops 1342177280 | bytes 9289728 | tf_op jit(solution)/shard_map/advance/pallas_call | solution.py:25
  73.7 1.3 %couple.3 = f32[1024,256]{1,0:T(8,128)} custom-call(f32[1024,256]{1,0:T(8,128)S(1)} %get-tuple-element.85.res_ref, bf16[1024,512]{1,0:T(8,128)(2,1)S(1)} %get-tuple-element.50.wt_ref.refs_4_, bf16[128,256]{1,0:T(8,128)(2,1)S(1)} %collective-permute-done.26.refs_0_, bf16[128,256]{1,0:T(8,128)(2,1)S(1)} %collective-permute-done.27.refs_1_, ...), custom_call_target="tpu_custom_call" | custom-call | flops 268435456 | bytes 2359296 | tf_op jit(solution)/shard_map/couple/pallas_call | solution.py:25
  (44 shorter events, 2.4 us)
Async XLA Ops:
  0.6 10.5 %copy-start.4 = (bf16[96,1024]{1,0:T(8,128)(2,1)S(1)}, bf16[96,1024]{1,0:T(8,128)(2,1)}, u32[]{:S(2)}) copy-start(bf16[96,1024]{1,0:T(8,128)(2,1)} %refs_8_.3) | copy-start | bytes 589828
  0.6 10.5 %copy-start.1 = (bf16[1024,1024]{1,0:T(8,128)(2,1)S(1)}, bf16[1024,1024]{1,0:T(8,128)(2,1)}, u32[]{:S(2)}) copy-start(bf16[1024,1024]{1,0:T(8,128)(2,1)} %refs_5_.3) | copy-start | bytes 6291460
  2.3 6.5 %collective-permute-start.2 = (bf16[96,256]{1,0:T(8,128)(2,1)S(1)}, bf16[96,256]{1,0:T(8,128)(2,1)S(1)}, u32[]{:S(2)}, u32[]{:S(2)}) collective-permute-start(bf16[96,256]{1,0:T(8,128)(2,1)S(1)} %convolution_convert_fusion.token.refs_0_), channel_id=1, source_target_pairs={{0,3},{1,2},{2,1},{3,0},{4,7},{5,6},{6,5},{7,4},{8,11},{9,10},{10,... | collective-permute-start | bytes 147464 | tf_op jit(solution)/shard_map/ppermute | solution.py:139
  4.8 4.3 %collective-permute-start.1 = (bf16[96,256]{1,0:T(8,128)(2,1)S(1)}, bf16[96,256]{1,0:T(8,128)(2,1)S(1)}, u32[]{:S(2)}, u32[]{:S(2)}) collective-permute-start(bf16[96,256]{1,0:T(8,128)(2,1)S(1)} %convolution_convert_fusion.token.refs_0_), channel_id=1, source_target_pairs={{0,2},{1,3},{2,0},{3,1},{4,6},{5,7},{6,4},{7,5},{8,10},{9,11},{10,... | collective-permute-start | bytes 147464 | tf_op jit(solution)/shard_map/ppermute | solution.py:139
  5.5 3.7 %collective-permute-start = (bf16[96,256]{1,0:T(8,128)(2,1)S(1)}, bf16[96,256]{1,0:T(8,128)(2,1)S(1)}, u32[]{:S(2)}, u32[]{:S(2)}) collective-permute-start(bf16[96,256]{1,0:T(8,128)(2,1)S(1)} %convolution_convert_fusion.token.refs_0_), channel_id=1, source_target_pairs={{0,1},{1,0},{2,3},{3,2},{4,5},{5,4},{6,7},{7,6},{8,9},{9,8},{10,11... | collective-permute-start | bytes 147464 | tf_op jit(solution)/shard_map/ppermute | solution.py:139
  6.9 1.1 %copy-start.5 = (bf16[768,384]{1,0:T(8,128)(2,1)S(1)}, bf16[768,384]{1,0:T(8,128)(2,1)}, u32[]{:S(2)}) copy-start(bf16[768,384]{1,0:T(8,128)(2,1)} %inv_hbm.1) | copy-start | bytes 1769476
  9.6 7.1 %collective-permute-start.3 = (bf16[384,256]{1,0:T(8,128)(2,1)S(1)}, bf16[384,256]{1,0:T(8,128)(2,1)S(1)}, u32[]{:S(2)}, u32[]{:S(2)}) collective-permute-start(bf16[384,256]{1,0:T(8,128)(2,1)S(1)} %get-tuple-element.48), channel_id=1, source_target_pairs={{0,4},{4,0},{8,12},{12,8},{16,20},{20,16},{24,28},{28,24},{1,5},{5... | collective-permute-start | bytes 589832 | tf_op jit(solution)/shard_map/ppermute | solution.py:146
  11.2 1.6 %copy-start.2 = (bf16[1024,1024]{1,0:T(8,128)(2,1)S(1)}, bf16[1024,1024]{1,0:T(8,128)(2,1)}, u32[]{:S(2)}) copy-start(bf16[1024,1024]{1,0:T(8,128)(2,1)} %refs_6_.3) | copy-start | bytes 6291460
  12.8 17.1 %copy-start = (f32[1024,256]{1,0:T(8,128)S(1)}, f32[1024,256]{1,0:T(8,128)}, u32[]{:S(2)}) copy-start(f32[1024,256]{1,0:T(8,128)} %refs_7_.3) | copy-start | bytes 3145732
  16.7 4.5 %collective-permute-start.4 = (bf16[96,256]{1,0:T(8,128)(2,1)S(1)}, bf16[96,256]{1,0:T(8,128)(2,1)S(1)}, u32[]{:S(2)}, u32[]{:S(2)}) collective-permute-start(bf16[96,256]{1,0:T(8,128)(2,1)S(1)} %get-tuple-element.53), channel_id=1, source_target_pairs={{0,8},{4,12},{8,0},{12,4},{16,24},{20,28},{24,16},{28,20},{1,9},{5... | collective-permute-start | bytes 147464 | tf_op jit(solution)/shard_map/ppermute | solution.py:154
  18.3 5.5 %collective-permute-start.5 = (bf16[96,256]{1,0:T(8,128)(2,1)S(1)}, bf16[96,256]{1,0:T(8,128)(2,1)S(1)}, u32[]{:S(2)}, u32[]{:S(2)}) collective-permute-start(bf16[96,256]{1,0:T(8,128)(2,1)S(1)} %get-tuple-element.54), channel_id=1, source_target_pairs={{0,16},{4,20},{8,24},{12,28},{16,0},{20,4},{24,8},{28,12},{1,17},{... | collective-permute-start | bytes 147464 | tf_op jit(solution)/shard_map/ppermute | solution.py:154
  20.9 5.9 %collective-permute-start.6 = (bf16[96,256]{1,0:T(8,128)(2,1)S(1)}, bf16[96,256]{1,0:T(8,128)(2,1)S(1)}, u32[]{:S(2)}, u32[]{:S(2)}) collective-permute-start(bf16[96,256]{1,0:T(8,128)(2,1)S(1)} %get-tuple-element.55), channel_id=1, source_target_pairs={{0,24},{4,28},{8,16},{12,20},{16,8},{20,12},{24,0},{28,4},{1,25},{... | collective-permute-start | bytes 147464 | tf_op jit(solution)/shard_map/ppermute | solution.py:154
  27.1 3.8 %collective-permute-start.7 = (bf16[128,256]{1,0:T(8,128)(2,1)S(1)}, bf16[128,256]{1,0:T(8,128)(2,1)S(1)}, u32[]{:S(2)}, u32[]{:S(2)}) collective-permute-start(bf16[128,256]{1,0:T(8,128)(2,1)S(1)} %get-tuple-element.60), channel_id=1, source_target_pairs={{0,1},{1,0},{2,3},{3,2},{4,8},{5,9},{6,10},{7,11},{8,4},{9,5},{10,... | collective-permute-start | bytes 196616 | tf_op jit(solution)/shard_map/ppermute | solution.py:83
  27.1 3.8 %collective-permute-start.8 = (bf16[128,256]{1,0:T(8,128)(2,1)S(1)}, bf16[128,256]{1,0:T(8,128)(2,1)S(1)}, u32[]{:S(2)}, u32[]{:S(2)}) collective-permute-start(bf16[128,256]{1,0:T(8,128)(2,1)S(1)} %get-tuple-element.61), channel_id=1, source_target_pairs={{0,3},{1,2},{2,1},{3,0},{4,7},{5,6},{6,5},{7,4},{8,11},{9,10},{10,... | collective-permute-start | bytes 196616 | tf_op jit(solution)/shard_map/ppermute | solution.py:83
  28.6 4.3 %collective-permute-start.9 = (bf16[128,256]{1,0:T(8,128)(2,1)S(1)}, bf16[128,256]{1,0:T(8,128)(2,1)S(1)}, u32[]{:S(2)}, u32[]{:S(2)}) collective-permute-start(bf16[128,256]{1,0:T(8,128)(2,1)S(1)} %get-tuple-element.62), channel_id=1, source_target_pairs={{0,4},{1,5},{2,6},{3,7},{4,0},{5,1},{6,2},{7,3},{8,12},{9,13},{10,... | collective-permute-start | bytes 196616 | tf_op jit(solution)/shard_map/ppermute | solution.py:83
  28.8 4.2 %collective-permute-start.10 = (bf16[128,256]{1,0:T(8,128)(2,1)S(1)}, bf16[128,256]{1,0:T(8,128)(2,1)S(1)}, u32[]{:S(2)}, u32[]{:S(2)}) collective-permute-start(bf16[128,256]{1,0:T(8,128)(2,1)S(1)} %get-tuple-element.63), channel_id=1, source_target_pairs={{0,1},{1,0},{2,3},{3,2},{4,5},{5,4},{6,7},{7,6},{8,9},{9,8},{10,11... | collective-permute-start | bytes 196616 | tf_op jit(solution)/shard_map/ppermute | solution.py:83
  29.9 8.0 %copy-start.3 = (bf16[1024,1024]{1,0:T(8,128)(2,1)S(1)}, bf16[1024,1024]{1,0:T(8,128)(2,1)}, u32[]{:S(2)}) copy-start(bf16[1024,1024]{1,0:T(8,128)(2,1)} %refs_6_.3) | copy-start | bytes 6291460
  33.2 7.5 %collective-permute-start.11 = (bf16[128,256]{1,0:T(8,128)(2,1)S(1)}, bf16[128,256]{1,0:T(8,128)(2,1)S(1)}, u32[]{:S(2)}, u32[]{:S(2)}) collective-permute-start(bf16[128,256]{1,0:T(8,128)(2,1)S(1)} %get-tuple-element.67.refs_0_), channel_id=1, source_target_pairs={{0,1},{1,0},{2,3},{3,2},{4,8},{5,9},{6,10},{7,11},{8,4},{9,5},{10,... | collective-permute-start | bytes 196616 | tf_op jit(solution)/shard_map/ppermute | solution.py:83
  33.3 7.5 %collective-permute-start.12 = (bf16[128,256]{1,0:T(8,128)(2,1)S(1)}, bf16[128,256]{1,0:T(8,128)(2,1)S(1)}, u32[]{:S(2)}, u32[]{:S(2)}) collective-permute-start(bf16[128,256]{1,0:T(8,128)(2,1)S(1)} %get-tuple-element.68.refs_1_), channel_id=1, source_target_pairs={{0,3},{1,2},{2,1},{3,0},{4,7},{5,6},{6,5},{7,4},{8,11},{9,10},{10,... | collective-permute-start | bytes 196616 | tf_op jit(solution)/shard_map/ppermute | solution.py:83
  34.0 6.7 %collective-permute-start.13 = (bf16[128,256]{1,0:T(8,128)(2,1)S(1)}, bf16[128,256]{1,0:T(8,128)(2,1)S(1)}, u32[]{:S(2)}, u32[]{:S(2)}) collective-permute-start(bf16[128,256]{1,0:T(8,128)(2,1)S(1)} %get-tuple-element.69.refs_2_), channel_id=1, source_target_pairs={{0,4},{1,5},{2,6},{3,7},{4,0},{5,1},{6,2},{7,3},{8,12},{9,13},{10,... | collective-permute-start | bytes 196616 | tf_op jit(solution)/shard_map/ppermute | solution.py:83
  37.3 3.5 %collective-permute-start.14 = (bf16[128,256]{1,0:T(8,128)(2,1)S(1)}, bf16[128,256]{1,0:T(8,128)(2,1)S(1)}, u32[]{:S(2)}, u32[]{:S(2)}) collective-permute-start(bf16[128,256]{1,0:T(8,128)(2,1)S(1)} %get-tuple-element.70.refs_3_), channel_id=1, source_target_pairs={{0,1},{1,0},{2,3},{3,2},{4,5},{5,4},{6,7},{7,6},{8,9},{9,8},{10,11... | collective-permute-start | bytes 196616 | tf_op jit(solution)/shard_map/ppermute | solution.py:83
  41.0 3.9 %collective-permute-start.17 = (bf16[96,256]{1,0:T(8,128)(2,1)S(1)}, bf16[96,256]{1,0:T(8,128)(2,1)S(1)}, u32[]{:S(2)}, u32[]{:S(2)}) collective-permute-start(bf16[96,256]{1,0:T(8,128)(2,1)S(1)} %restrict_recv.1.refs_0_), channel_id=1, source_target_pairs={{0,3},{1,2},{2,1},{3,0},{4,7},{5,6},{6,5},{7,4},{8,11},{9,10},{10,... | collective-permute-start | bytes 147464 | tf_op jit(solution)/shard_map/ppermute | solution.py:139
  41.3 4.8 %collective-permute-start.16 = (bf16[96,256]{1,0:T(8,128)(2,1)S(1)}, bf16[96,256]{1,0:T(8,128)(2,1)S(1)}, u32[]{:S(2)}, u32[]{:S(2)}) collective-permute-start(bf16[96,256]{1,0:T(8,128)(2,1)S(1)} %restrict_recv.1.refs_0_), channel_id=1, source_target_pairs={{0,2},{1,3},{2,0},{3,1},{4,6},{5,7},{6,4},{7,5},{8,10},{9,11},{10,... | collective-permute-start | bytes 147464 | tf_op jit(solution)/shard_map/ppermute | solution.py:139
  42.7 3.5 %collective-permute-start.15 = (bf16[96,256]{1,0:T(8,128)(2,1)S(1)}, bf16[96,256]{1,0:T(8,128)(2,1)S(1)}, u32[]{:S(2)}, u32[]{:S(2)}) collective-permute-start(bf16[96,256]{1,0:T(8,128)(2,1)S(1)} %restrict_recv.1.refs_0_), channel_id=1, source_target_pairs={{0,1},{1,0},{2,3},{3,2},{4,5},{5,4},{6,7},{7,6},{8,9},{9,8},{10,11... | collective-permute-start | bytes 147464 | tf_op jit(solution)/shard_map/ppermute | solution.py:139
  46.6 6.8 %collective-permute-start.18 = (bf16[384,256]{1,0:T(8,128)(2,1)S(1)}, bf16[384,256]{1,0:T(8,128)(2,1)S(1)}, u32[]{:S(2)}, u32[]{:S(2)}) collective-permute-start(bf16[384,256]{1,0:T(8,128)(2,1)S(1)} %get-tuple-element.72), channel_id=1, source_target_pairs={{0,4},{4,0},{8,12},{12,8},{16,20},{20,16},{24,28},{28,24},{1,5},{5... | collective-permute-start | bytes 589832 | tf_op jit(solution)/shard_map/ppermute | solution.py:146
  53.4 4.5 %collective-permute-start.19 = (bf16[96,256]{1,0:T(8,128)(2,1)S(1)}, bf16[96,256]{1,0:T(8,128)(2,1)S(1)}, u32[]{:S(2)}, u32[]{:S(2)}) collective-permute-start(bf16[96,256]{1,0:T(8,128)(2,1)S(1)} %get-tuple-element.75), channel_id=1, source_target_pairs={{0,8},{4,12},{8,0},{12,4},{16,24},{20,28},{24,16},{28,20},{1,9},{5... | collective-permute-start | bytes 147464 | tf_op jit(solution)/shard_map/ppermute | solution.py:154
  54.2 5.1 %collective-permute-start.20 = (bf16[96,256]{1,0:T(8,128)(2,1)S(1)}, bf16[96,256]{1,0:T(8,128)(2,1)S(1)}, u32[]{:S(2)}, u32[]{:S(2)}) collective-permute-start(bf16[96,256]{1,0:T(8,128)(2,1)S(1)} %get-tuple-element.76), channel_id=1, source_target_pairs={{0,16},{4,20},{8,24},{12,28},{16,0},{20,4},{24,8},{28,12},{1,17},{... | collective-permute-start | bytes 147464 | tf_op jit(solution)/shard_map/ppermute | solution.py:154
  55.1 5.9 %collective-permute-start.21 = (bf16[96,256]{1,0:T(8,128)(2,1)S(1)}, bf16[96,256]{1,0:T(8,128)(2,1)S(1)}, u32[]{:S(2)}, u32[]{:S(2)}) collective-permute-start(bf16[96,256]{1,0:T(8,128)(2,1)S(1)} %get-tuple-element.77), channel_id=1, source_target_pairs={{0,24},{4,28},{8,16},{12,20},{16,8},{20,12},{24,0},{28,4},{1,25},{... | collective-permute-start | bytes 147464 | tf_op jit(solution)/shard_map/ppermute | solution.py:154
  61.2 3.9 %collective-permute-start.22 = (bf16[128,256]{1,0:T(8,128)(2,1)S(1)}, bf16[128,256]{1,0:T(8,128)(2,1)S(1)}, u32[]{:S(2)}, u32[]{:S(2)}) collective-permute-start(bf16[128,256]{1,0:T(8,128)(2,1)S(1)} %get-tuple-element.79), channel_id=1, source_target_pairs={{0,1},{1,0},{2,3},{3,2},{4,8},{5,9},{6,10},{7,11},{8,4},{9,5},{10,... | collective-permute-start | bytes 196616 | tf_op jit(solution)/shard_map/ppermute | solution.py:83
  61.3 3.8 %collective-permute-start.23 = (bf16[128,256]{1,0:T(8,128)(2,1)S(1)}, bf16[128,256]{1,0:T(8,128)(2,1)S(1)}, u32[]{:S(2)}, u32[]{:S(2)}) collective-permute-start(bf16[128,256]{1,0:T(8,128)(2,1)S(1)} %get-tuple-element.80), channel_id=1, source_target_pairs={{0,3},{1,2},{2,1},{3,0},{4,7},{5,6},{6,5},{7,4},{8,11},{9,10},{10,... | collective-permute-start | bytes 196616 | tf_op jit(solution)/shard_map/ppermute | solution.py:83
  62.3 4.4 %collective-permute-start.24 = (bf16[128,256]{1,0:T(8,128)(2,1)S(1)}, bf16[128,256]{1,0:T(8,128)(2,1)S(1)}, u32[]{:S(2)}, u32[]{:S(2)}) collective-permute-start(bf16[128,256]{1,0:T(8,128)(2,1)S(1)} %get-tuple-element.81), channel_id=1, source_target_pairs={{0,4},{1,5},{2,6},{3,7},{4,0},{5,1},{6,2},{7,3},{8,12},{9,13},{10,... | collective-permute-start | bytes 196616 | tf_op jit(solution)/shard_map/ppermute | solution.py:83
  62.8 3.9 %collective-permute-start.25 = (bf16[128,256]{1,0:T(8,128)(2,1)S(1)}, bf16[128,256]{1,0:T(8,128)(2,1)S(1)}, u32[]{:S(2)}, u32[]{:S(2)}) collective-permute-start(bf16[128,256]{1,0:T(8,128)(2,1)S(1)} %get-tuple-element.82), channel_id=1, source_target_pairs={{0,1},{1,0},{2,3},{3,2},{4,5},{5,4},{6,7},{7,6},{8,9},{9,8},{10,11... | collective-permute-start | bytes 196616 | tf_op jit(solution)/shard_map/ppermute | solution.py:83
  67.0 6.6 %collective-permute-start.26 = (bf16[128,256]{1,0:T(8,128)(2,1)S(1)}, bf16[128,256]{1,0:T(8,128)(2,1)S(1)}, u32[]{:S(2)}, u32[]{:S(2)}) collective-permute-start(bf16[128,256]{1,0:T(8,128)(2,1)S(1)} %get-tuple-element.86), channel_id=1, source_target_pairs={{0,1},{1,0},{2,3},{3,2},{4,8},{5,9},{6,10},{7,11},{8,4},{9,5},{10,... | collective-permute-start | bytes 196616 | tf_op jit(solution)/shard_map/ppermute | solution.py:83
  67.1 6.5 %collective-permute-start.27 = (bf16[128,256]{1,0:T(8,128)(2,1)S(1)}, bf16[128,256]{1,0:T(8,128)(2,1)S(1)}, u32[]{:S(2)}, u32[]{:S(2)}) collective-permute-start(bf16[128,256]{1,0:T(8,128)(2,1)S(1)} %get-tuple-element.87), channel_id=1, source_target_pairs={{0,3},{1,2},{2,1},{3,0},{4,7},{5,6},{6,5},{7,4},{8,11},{9,10},{10,... | collective-permute-start | bytes 196616 | tf_op jit(solution)/shard_map/ppermute | solution.py:83
  68.2 5.5 %collective-permute-start.28 = (bf16[128,256]{1,0:T(8,128)(2,1)S(1)}, bf16[128,256]{1,0:T(8,128)(2,1)S(1)}, u32[]{:S(2)}, u32[]{:S(2)}) collective-permute-start(bf16[128,256]{1,0:T(8,128)(2,1)S(1)} %get-tuple-element.88), channel_id=1, source_target_pairs={{0,4},{1,5},{2,6},{3,7},{4,0},{5,1},{6,2},{7,3},{8,12},{9,13},{10,... | collective-permute-start | bytes 196616 | tf_op jit(solution)/shard_map/ppermute | solution.py:83
  70.5 3.2 %collective-permute-start.29 = (bf16[128,256]{1,0:T(8,128)(2,1)S(1)}, bf16[128,256]{1,0:T(8,128)(2,1)S(1)}, u32[]{:S(2)}, u32[]{:S(2)}) collective-permute-start(bf16[128,256]{1,0:T(8,128)(2,1)S(1)} %get-tuple-element.89), channel_id=1, source_target_pairs={{0,1},{1,0},{2,3},{3,2},{4,5},{5,4},{6,7},{7,6},{8,9},{9,8},{10,11... | collective-permute-start | bytes 196616 | tf_op jit(solution)/shard_map/ppermute | solution.py:83

commit v4 on v3

--- a/solution.py
+++ b/solution.py
@@ -82,9 +82,7 @@
     def halo(faces):
         return [lax.ppermute(f, both, p) for f, p in zip(faces, slot_perms)]
 
-    def k_select(inv_hbm, table_ref, token, sel_ref, wt_ref, inv_ref, sem):
-        load = pltpu.make_async_copy(inv_hbm, inv_ref, sem)
-        load.start()
+    def k_select(table_ref, token, sel_ref, wt_ref):
         for s, (k, ok) in enumerate(slot_faces()):
             row = table_ref[pl.ds(k, 1), :].astype(jnp.int32)
             w = table_ref[pl.ds(4 + k, 1), :] * ok
@@ -95,11 +93,8 @@
             for j in range(nloc // ovl):
                 across = lax.broadcasted_iota(jnp.int32, (ovl, ovl), 1) + j * ovl
                 sel_ref[at, pl.ds(j * ovl, ovl)] = jnp.where(idx == across.astype(F32), 1.0, 0.0).astype(BF)
-        load.wait()
-
-    def k_products(
-        sel_ref, wt_ref, inv_ref, mat_ref, basis_ref, token, bf_ref, t_ref, si_ref, f_ref, bt_ref, lb_ref
-    ):
+
+    def k_products(sel_ref, wt_ref, inv_ref, basis_ref, bf_ref, t_ref, si_ref, f_ref, bt_ref):
         bt = basis_ref[...].astype(F32).T.astype(BF)
         bt_ref[...] = bt
         bf_ref[...] = mm(sel_ref[...], bt).astype(BF)
@@ -112,21 +107,31 @@
             si_ref[at, :] = mm(sel_ref[at, :], inv_ref[...]).astype(BF)
             f_ref[at, :] = mm(si_ref[at, :], wt_ref[...]).astype(BF)
 
+    def k_mat_basis(mat_ref, bt_ref, token, lb_ref):
         def tile(at):
             lb_ref[at, :] = mm(mat_ref[at, :], bt_ref[...]).astype(BF)
 
         row_loop(tile)
 
-    def k_coarse(*refs):
-        blocks, (inv_ref, keep_ref, send_ref, group, prod) = refs[:nc], refs[nc:]
-        r, c = lax.axis_index("row"), lax.axis_index("col")
+    half = nz * cpd
+
+    def k_hold(inv_ref, token, same_ref, cross_ref):
+        r = lax.axis_index("row")
+        for i in range(nz):
+            at = pl.ds(i * cpd, cpd)
+            same_ref[at, :] = inv_ref[pl.ds(pl.multiple_of((r ^ (2 * i)) * cpd, 16), cpd), :]
+            cross_ref[at, :] = inv_ref[pl.ds(pl.multiple_of((r ^ (2 * i + 1)) * cpd, 16), cpd), :]
+
+    def place(group, blocks):
+        c = lax.axis_index("col")
         for i, block in enumerate(blocks):
             group[pl.ds(pl.multiple_of((c ^ i) * cpd, 16), cpd), :] = block[...]
-        prod[...] = mm(inv_ref[...], group[...])
-        for i in range(nz):
-            for ref, m in ((keep_ref, 2 * i), (send_ref, 2 * i + 1)):
-                src = pl.ds(pl.multiple_of((r ^ m) * cpd, 8), cpd)
-                ref[pl.ds(i * cpd, cpd), :] = prod[src, :].astype(ref.dtype)
+
+    def k_coarse(*refs):
+        blocks, (same_ref, cross_ref, keep_ref, send_ref, group) = refs[:nc], refs[nc:]
+        place(group, blocks)
+        send_ref[...] = mm(cross_ref[...], group[...]).astype(BF)
+        keep_ref[...] = mm(same_ref[...], group[...])
 
     def k_half(keep_ref, recv_ref, token, own_ref, *sends):
         own_ref[...] = keep_ref[pl.ds(0, cpd), :] + recv_ref[pl.ds(0, cpd), :].astype(F32)
@@ -134,26 +139,30 @@
             at = pl.ds((i + 1) * cpd, cpd)
             ref[...] = (keep_ref[at, :] + recv_ref[at, :].astype(F32)).astype(BF)
 
-    def coarse_send(restricted, inv):
-        blocks = [restricted] + [
-            lax.ppermute(restricted, "col", [(i, i ^ k) for i in range(nc)]) for k in range(1, nc)
-        ]
-        keep, send = call(
-            k_coarse, [((nz * cpd, nrhs), F32), ((nz * cpd, nrhs), BF)], *blocks, inv,
-            scratch=[pltpu.VMEM((nc * cpd, nrhs), BF), pltpu.VMEM((nr * cpd, nrhs), F32)],
-            name="coarse", flops=2 * nr * cpd * nc * cpd * nrhs,
-        )
-        return keep, lax.ppermute(send, "row", [(i, i ^ 1) for i in range(nr)])
-
-    def coarse_recv(keep, recv, token):
-        own, *sends = call(
-            k_half, [((cpd, nrhs), F32)] + [((cpd, nrhs), BF)] * (nz - 1), keep, recv, token,
-            tokens=1, name="half",
-        )
-        recvs = [
+    def k_coarse_pair(*refs):
+        mine, theirs, refs = refs[:nc], refs[nc : 2 * nc], refs[2 * nc :]
+        same_ref, other_ref, token, own_ref = refs[:4]
+        sends, (group, group_other) = refs[4:-2], refs[-2:]
+        place(group, mine)
+        place(group_other, theirs)
+        for i, ref in enumerate((own_ref,) + tuple(sends)):
+            at = pl.ds(i * cpd, cpd)
+            ref[...] = (mm(same_ref[at, :], group[...]) + mm(other_ref[at, :], group_other[...])).astype(ref.dtype)
+
+    def over_col(block):
+        return [block] + [
+            lax.ppermute(block, "col", [(i, i ^ k) for i in range(nc)]) for k in reversed(range(1, nc))
+        ][::-1]
+
+    def over_pair(value):
+        return lax.ppermute(value, "row", [(i, i ^ 1) for i in range(nr)])
+
+    def reduce_rows(own, sends):
+        return [own] + [
             lax.ppermute(s, "row", [(i, i ^ (2 * (k + 1))) for i in range(nr)]) for k, s in enumerate(sends)
         ]
-        return [own] + recvs
+
+    own_and_sends = [((cpd, nrhs), F32)] + [((cpd, nrhs), BF)] * (nz - 1)
 
     def k_coarse_faces(*refs):
         parts, (bf_ref, y_ref), faces = refs[:nz], refs[nz : nz + 2], refs[nz + 2 :]
@@ -289,36 +298,48 @@
         )[0]
 
     restricted = mm(basis_t, rhs.astype(BF)).astype(BF)
+    blocks = over_col(restricted)
+    same, cross = call(
+        k_hold, [((half, coarse_inv.shape[1]), BF)] * 2, coarse_inv, restricted, tokens=1, name="hold",
+    )
+    keep, send = call(
+        k_coarse, [((half, nrhs), F32), ((half, nrhs), BF)], *blocks, same, cross,
+        scratch=[pltpu.VMEM((nc * cpd, nrhs), BF)], name="coarse", flops=4 * half * nc * cpd * nrhs,
+    )
+    arrived = over_pair(send)
+    other = over_pair(cross)
     table = jnp.concatenate([margin_rows[0].astype(F32), couple[0]], axis=0)
-    sel, wt, inv_here = call(
-        k_select, [((nf, nloc), BF), ((nloc, nf), BF), (coarse_inv.shape, BF)],
-        coarse_inv, table, restricted, hbm_ins=1, tokens=1, name="select",
-        scratch=[pltpu.SemaphoreType.DMA],
-    )
-    keep, recv = coarse_send(restricted, inv_here)
-    bfac, tmat, simat, fmat, btmat, lbmat = call(
+    sel, wt = call(k_select, [((nf, nloc), BF), ((nloc, nf), BF)], table, keep, tokens=1, name="select")
+    bfac, tmat, simat, fmat, btmat = call(
         k_products,
-        [((nf, cpd), BF), ((cpd, nf), BF), ((nf, nloc), BF), ((nf, nf), BF), ((nloc, cpd), BF), ((nloc, cpd), BF)],
-        sel, wt, local_inv, local_mat, basis_t, keep, tokens=1,
-        name="products", flops=2 * nf * nloc * (nloc + nf + 3 * cpd),
-    )
-    token = tmat
+        [((nf, cpd), BF), ((cpd, nf), BF), ((nf, nloc), BF), ((nf, nf), BF), ((nloc, cpd), BF)],
+        sel, wt, local_inv, basis_t, name="products", flops=2 * nf * nloc * (nloc + nf + 2 * cpd),
+    )
+    own, *sends = call(k_half, own_and_sends, keep, arrived, tmat, tokens=1, name="half")
+    (lbmat,) = call(
+        k_mat_basis, [((nloc, cpd), BF)], local_mat, btmat, own, tokens=1,
+        name="mat_basis", flops=2 * nloc * nloc * cpd,
+    )
     residual, solution, sent = rhs, None, []
     for sweep in range(STEPS):
-        y, faces = coarse_faces(coarse_recv(keep, recv, token))
+        y, faces = coarse_faces(reduce_rows(own, sends))
         recv = halo(faces)
         sent = faces_after(local(y, residual, sent), recv)
         recv2 = halo(sent)
         last = sweep == STEPS - 1
         new = advance(y, residual, recv, solution, last)
         solution, res = new[:2]
+        residual = coupled(res, recv2, last)
         if not last:
             (restricted,) = call(
                 k_restrict_recv, [((cpd, nrhs), BF)], new[2], tmat, *recv2, name="restrict_recv",
             )
-            keep, recv = coarse_send(restricted, inv_here)
-        residual = coupled(res, recv2, last)
-        token = residual
+            across = over_pair(restricted)
+            own, *sends = call(
+                k_coarse_pair, own_and_sends, *over_col(restricted), *over_col(across), same, other, residual,
+                scratch=[pltpu.VMEM((nc * cpd, nrhs), BF)] * 2, tokens=1,
+                name="coarse_pair", flops=4 * half * nc * cpd * nrhs,
+            )
     return (solution, residual)
 
 

time: 75.2 us -> 72.7 us (0.967)
  waiting for transfers between devices: 21.5 us -> 17.3 us
  starting transfers between devices: 31.2 us -> 34.6 us
  local copies, waits for them, and re-layouts: 2.67 us -> 1.08 us
    ppermute x14 -> x18, waiting for transfers between devices: 17.8 us -> 14.5 us  [the longest x6 7.68 us: reduce_rows(): lax.ppermute(s, 'row', [(i, i ^ 2 * (k + 1)) for i in range(nr)])]
    ppermute x14 -> x18, starting transfers between devices: 17 us -> 19.6 us  [the longest x6 8.9 us: reduce_rows(): lax.ppermute(s, 'row', [(i, i ^ 2 * (k + 1)) for i in range(nr)])]
    unnamed x12 -> x10, local copies, waits for them, and re-layouts: 2.67 us -> 1.08 us
    ppermute x16, waiting for transfers between devices: 3.68 us -> 2.81 us  [halo(): return [lax.ppermute(f, both, p) for f, p in zip(faces, slot_perms)]]
    pallas_call x17 -> x18, Pallas kernels: 15.6 us -> 15.5 us  [call(): pl.pallas_call(kernel, out_shape=[jax.ShapeDtypeStruct(s, d) for s, d in...]
  transfers between devices with their start and end apart: 30 -> 34, of which waited for: 12 -> 11; matrix products, arithmetic and copies ran while one was open for 2% -> 2% of each run, Pallas kernels for 16% -> 18%
where the time goes in v4:
time: 72.7 us; the launch traced here: 72.5 us
  starting transfers between devices  34.6 us (48%)
  waiting for transfers between devices  17.3 us (24%)
  Pallas kernels  15.5 us (21%)
  matrix products  1.69 us (2%)
  other arithmetic  1.37 us (2%)
  local copies, waits for them, and re-layouts  1.08 us (1%)
  between operations  0.97 us (1%)
    pallas_call x18, Pallas kernels, call(): pl.pallas_call(kernel, out_shape=[jax.ShapeDtypeStruct(s, d) for s, d in...  15.5 us
    ppermute x16, starting transfers between devices, halo(): return [lax.ppermute(f, both, p) for f, p in zip(faces, slot_perms)]  15 us
    ppermute x6, starting transfers between devices, reduce_rows(): lax.ppermute(s, 'row', [(i, i ^ 2 * (k + 1)) for i in range(nr)])  8.9 us
    ppermute x6, waiting for transfers between devices, reduce_rows(): lax.ppermute(s, 'row', [(i, i ^ 2 * (k + 1)) for i in range(nr)])  7.68 us
    ppermute x9, starting transfers between devices, over_col(): lax.ppermute(block, 'col', [(i, i ^ k) for i in range(nc)])  6.47 us
    ppermute x9, waiting for transfers between devices, over_col(): lax.ppermute(block, 'col', [(i, i ^ k) for i in range(nc)])  4.31 us
    ppermute x3, starting transfers between devices, over_pair(): return lax.ppermute(value, 'row', [(i, i ^ 1) for i in range(nr)])  4.25 us
    ppermute x16, waiting for transfers between devices, halo(): return [lax.ppermute(f, both, p) for f, p in zip(faces, slot_perms)]  2.81 us
  transfers between devices with their start and end apart: 34, of which 11 were waited for; matrix products, arithmetic and copies ran while one was open for 2% of the time, Pallas kernels for 18%

profile of v4, /device:TPU:0, one launch (start us, length us, event | category | flops | bytes accessed | tf_op | source)
XLA Modules:
  0.0 72.5 jit_solution(11498603753750800447)
XLA Ops:
  0.6 1.7 %convolution_convert_fusion.token.refs_0_ = bf16[96,256]{1,0:T(8,128)(2,1)S(1)} fusion(bf16[96,1024]{1,0:T(8,128)(2,1)} %refs_8_.3, f32[1024,256]{1,0:T(8,128)} %refs_7_.3), kind=kOutput, calls=%fused_computation | convolution fusion | flops 50618368 | bytes 1294336 | tf_op jit(solution)/shard_map/dot_general | solution.py:19
  2.3 2.5 %collective-permute-start.2 = (bf16[96,256]{1,0:T(8,128)(2,1)S(1)}, bf16[96,256]{1,0:T(8,128)(2,1)S(1)}, u32[]{:S(2)}, u32[]{:S(2)}) collective-permute-start(bf16[96,256]{1,0:T(8,128)(2,1)S(1)} %convolution_convert_fusion.token.refs_0_), channel_id=1, source_target_pairs={{0,3},{1,2},{2,1},{3,0},{4,7},{5,6},{6,5},{7,4},{8,11},{9,10},{10,... | collective-permute-start | bytes 147464 | tf_op jit(solution)/shard_map/ppermute | solution.py:154
  4.8 0.6 collective-permute-start.1
  5.5 0.7 convert_bitcast_fusion
  6.2 1.1 %copy-done.4 = bf16[768,384]{1,0:T(8,128)(2,1)S(1)} copy-done((bf16[768,384]{1,0:T(8,128)(2,1)S(1)}, bf16[768,384]{1,0:T(8,128)(2,1)}, u32[]{:S(2)}) %copy-start.4) | copy-done | bytes 589848
  7.3 1.8 %collective-permute-done.1.refs_2_ = bf16[96,256]{1,0:T(8,128)(2,1)S(1)} collective-permute-done((bf16[96,256]{1,0:T(8,128)(2,1)S(1)}, bf16[96,256]{1,0:T(8,128)(2,1)S(1)}, u32[]{:S(2)}, u32[]{:S(2)}) %collective-permute-start.1) | collective-permute-done | bytes 49184 | tf_op jit(solution)/shard_map/ppermute | solution.py:154
  9.5 1.6 %collective-permute-start.3 = (bf16[384,256]{1,0:T(8,128)(2,1)S(1)}, bf16[384,256]{1,0:T(8,128)(2,1)S(1)}, u32[]{:S(2)}, u32[]{:S(2)}) collective-permute-start(bf16[384,256]{1,0:T(8,128)(2,1)S(1)} %get-tuple-element.47), channel_id=1, source_target_pairs={{0,4},{4,0},{8,12},{12,8},{16,20},{20,16},{24,28},{28,24},{1,5},{5... | collective-permute-start | bytes 589832 | tf_op jit(solution)/shard_map/ppermute | solution.py:158
  11.1 0.7 pad_maximum_fusion.table_ref
  11.8 0.8 %select.1 = (bf16[512,1024]{1,0:T(8,128)(2,1)S(1)}, bf16[1024,512]{1,0:T(8,128)(2,1)S(1)}) custom-call(f32[8,128]{1,0:T(8,128)S(1)} %pad_maximum_fusion.table_ref, f32[384,256]{1,0:T(8,128)S(1)} %get-tuple-element.46.token.keep_ref), custom_call_target="tpu_custom_call" | custom-call | bytes 397312 | tf_op jit(solution)/shard_map/select/pallas_call | solution.py:25
  12.6 2.3 %products.1 = (bf16[512,96]{1,0:T(8,128)(2,1)S(1)}, bf16[96,512]{1,0:T(8,128)(2,1)S(1)}, bf16[512,1024]{1,0:T(8,128)(2,1)S(1)}, bf16[512,512]{1,0:T(8,128)(2,1)S(1)}, bf16[1024,96]{1,0:T(8,128)(2,1)S(1)}) custom-call(bf16[512,1024]{1,0:T(8,128)(2,1)S(1)} %get-tuple-element.48.sel_ref, bf16[1024,512]{1,0:T(8,128)(2,1)S(1)} %get-tuple-element.49.wt_ref.refs_4_, ...), custom_call_target="tpu_custom_call" | custom-call | flops 1811939328 | bytes 4390912 | tf_op jit(solution)/shard_map/products/pallas_call | solution.py:25
  14.9 1.3 %collective-permute-done.3.recv_ref = bf16[384,256]{1,0:T(8,128)(2,1)S(1)} collective-permute-done((bf16[384,256]{1,0:T(8,128)(2,1)S(1)}, bf16[384,256]{1,0:T(8,128)(2,1)S(1)}, u32[]{:S(2)}, u32[]{:S(2)}) %collective-permute-start.3) | collective-permute-done | bytes 196640 | tf_op jit(solution)/shard_map/ppermute | solution.py:158
  16.3 1.6 %collective-permute-start.4 = (bf16[96,256]{1,0:T(8,128)(2,1)S(1)}, bf16[96,256]{1,0:T(8,128)(2,1)S(1)}, u32[]{:S(2)}, u32[]{:S(2)}) collective-permute-start(bf16[96,256]{1,0:T(8,128)(2,1)S(1)} %get-tuple-element.52), channel_id=1, source_target_pairs={{0,8},{4,12},{8,0},{12,4},{16,24},{20,28},{24,16},{28,20},{1,9},{5... | collective-permute-start | bytes 147464 | tf_op jit(solution)/shard_map/ppermute | solution.py:162
  17.9 2.6 %collective-permute-start.5 = (bf16[96,256]{1,0:T(8,128)(2,1)S(1)}, bf16[96,256]{1,0:T(8,128)(2,1)S(1)}, u32[]{:S(2)}, u32[]{:S(2)}) collective-permute-start(bf16[96,256]{1,0:T(8,128)(2,1)S(1)} %get-tuple-element.53), channel_id=1, source_target_pairs={{0,16},{4,20},{8,24},{12,28},{16,0},{20,4},{24,8},{28,12},{1,17},{... | collective-permute-start | bytes 147464 | tf_op jit(solution)/shard_map/ppermute | solution.py:162
  20.7 1.5 %collective-permute-start.22 = (bf16[384,384]{1,0:T(8,128)(2,1)S(1)}, bf16[384,384]{1,0:T(8,128)(2,1)S(1)}, u32[]{:S(2)}, u32[]{:S(2)}) collective-permute-start(bf16[384,384]{1,0:T(8,128)(2,1)S(1)} %get-tuple-element.45.refs_5_), channel_id=1, source_target_pairs={{0,4},{4,0},{8,12},{12,8},{16,20},{20,16},{24,28},{28,24},{1,5},{5... | collective-permute-start | bytes 884744 | tf_op jit(solution)/shard_map/ppermute | solution.py:158
  22.2 1.7 %collective-permute-done.5.refs_2_ = bf16[96,256]{1,0:T(8,128)(2,1)S(1)} collective-permute-done((bf16[96,256]{1,0:T(8,128)(2,1)S(1)}, bf16[96,256]{1,0:T(8,128)(2,1)S(1)}, u32[]{:S(2)}, u32[]{:S(2)}) %collective-permute-start.5) | collective-permute-done | bytes 49184 | tf_op jit(solution)/shard_map/ppermute | solution.py:162
  24.0 2.5 %collective-permute-done.6.refs_3_ = bf16[96,256]{1,0:T(8,128)(2,1)S(1)} collective-permute-done((bf16[96,256]{1,0:T(8,128)(2,1)S(1)}, bf16[96,256]{1,0:T(8,128)(2,1)S(1)}, u32[]{:S(2)}, u32[]{:S(2)}) %collective-permute-start.6) | collective-permute-done | bytes 49184 | tf_op jit(solution)/shard_map/ppermute | solution.py:162
  26.8 1.7 %collective-permute-start.8 = (bf16[128,256]{1,0:T(8,128)(2,1)S(1)}, bf16[128,256]{1,0:T(8,128)(2,1)S(1)}, u32[]{:S(2)}, u32[]{:S(2)}) collective-permute-start(bf16[128,256]{1,0:T(8,128)(2,1)S(1)} %get-tuple-element.59), channel_id=1, source_target_pairs={{0,3},{1,2},{2,1},{3,0},{4,7},{5,6},{6,5},{7,4},{8,11},{9,10},{10,... | collective-permute-start | bytes 196616 | tf_op jit(solution)/shard_map/ppermute | solution.py:83
  28.5 1.2 %collective-permute-start.10 = (bf16[128,256]{1,0:T(8,128)(2,1)S(1)}, bf16[128,256]{1,0:T(8,128)(2,1)S(1)}, u32[]{:S(2)}, u32[]{:S(2)}) collective-permute-start(bf16[128,256]{1,0:T(8,128)(2,1)S(1)} %get-tuple-element.61), channel_id=1, source_target_pairs={{0,1},{1,0},{2,3},{3,2},{4,5},{5,4},{6,7},{7,6},{8,9},{9,8},{10,11... | collective-permute-start | bytes 196616 | tf_op jit(solution)/shard_map/ppermute | solution.py:83
  29.7 0.9 %mat_basis.1.refs_2_.lb_ref = bf16[1024,96]{1,0:T(8,128)(2,1)S(1)} custom-call(bf16[1024,1024]{1,0:T(8,128)(2,1)S(1)} %copy-done.1, bf16[1024,96]{1,0:T(8,128)(2,1)S(1)} %get-tuple-element.57.bt_ref.refs_3_, f32[96,256]{1,0:T(8,128)S(1)} %get-tuple-element.51.refs_0_.token), custom_call_target="tpu_custom_call" | custom-call | flops 201326592 | bytes 2392064 | tf_op jit(solution)/shard_map/mat_basis/pallas_call | solution.py:25
  30.6 0.9 %local.2.base_ref = f32[512,256]{1,0:T(8,128)S(1)} custom-call(bf16[96,256]{1,0:T(8,128)(2,1)S(1)} %get-tuple-element.56.refs_0_.y_ref, f32[1024,256]{1,0:T(8,128)S(1)} %copy-done, bf16[1024,96]{1,0:T(8,128)(2,1)S(1)} %mat_basis.1.refs_2_.lb_ref, bf16[512,1024]{1,0:T(8,128)(2,1)S(1)} %get-tuple-element.63.si_ref, ...), custom_call_target="tpu_custom_call" | custom-call | flops 268435456 | bytes 2441216 | tf_op jit(solution)/shard_map/local/pallas_call | solution.py:25
  31.6 1.2 %collective-permute-done.9.refs_11_.refs_2_ = bf16[128,256]{1,0:T(8,128)(2,1)S(1)} collective-permute-done((bf16[128,256]{1,0:T(8,128)(2,1)S(1)}, bf16[128,256]{1,0:T(8,128)(2,1)S(1)}, u32[]{:S(2)}, u32[]{:S(2)}) %collective-permute-start.9) | collective-permute-done | bytes 65568 | tf_op jit(solution)/shard_map/ppermute | solution.py:83
  33.2 0.5 collective-permute-start.12
  33.7 2.9 %collective-permute-start.13 = (bf16[128,256]{1,0:T(8,128)(2,1)S(1)}, bf16[128,256]{1,0:T(8,128)(2,1)S(1)}, u32[]{:S(2)}, u32[]{:S(2)}) collective-permute-start(bf16[128,256]{1,0:T(8,128)(2,1)S(1)} %get-tuple-element.67.refs_2_), channel_id=1, source_target_pairs={{0,4},{1,5},{2,6},{3,7},{4,0},{5,1},{6,2},{7,3},{8,12},{9,13},{10,... | collective-permute-start | bytes 196616 | tf_op jit(solution)/shard_map/ppermute | solution.py:83
  36.6 0.8 %collective-permute-start.14 = (bf16[128,256]{1,0:T(8,128)(2,1)S(1)}, bf16[128,256]{1,0:T(8,128)(2,1)S(1)}, u32[]{:S(2)}, u32[]{:S(2)}) collective-permute-start(bf16[128,256]{1,0:T(8,128)(2,1)S(1)} %get-tuple-element.68.refs_3_), channel_id=1, source_target_pairs={{0,1},{1,0},{2,3},{3,2},{4,5},{5,4},{6,7},{7,6},{8,9},{9,8},{10,11... | collective-permute-start | bytes 196616 | tf_op jit(solution)/shard_map/ppermute | solution.py:83
  37.5 2.9 %advance.2 = (f32[1024,256]{1,0:T(8,128)S(1)}, f32[1024,256]{1,0:T(8,128)S(1)}, f32[96,256]{1,0:T(8,128)S(1)}) custom-call(bf16[96,256]{1,0:T(8,128)(2,1)S(1)} %get-tuple-element.56.refs_0_.y_ref, f32[1024,256]{1,0:T(8,128)S(1)} %copy-done, bf16[1024,96]{1,0:T(8,128)(2,1)S(1)} %mat_basis.1.refs_2_.lb_ref, ...), custom_call_target="tpu_custom_call" | custom-call | flops 1342177280 | bytes 8241152 | tf_op jit(solution)/shard_map/advance/pallas_call | solution.py:25
  40.6 1.1 %collective-permute-start.18 = (bf16[96,256]{1,0:T(8,128)(2,1)S(1)}, bf16[96,256]{1,0:T(8,128)(2,1)S(1)}, u32[]{:S(2)}, u32[]{:S(2)}) collective-permute-start(bf16[96,256]{1,0:T(8,128)(2,1)S(1)} %restrict_recv.1.refs_0_), channel_id=1, source_target_pairs={{0,4},{4,0},{8,12},{12,8},{16,20},{20,16},{24,28},{28,24},{1,5},{5... | collective-permute-start | bytes 147464 | tf_op jit(solution)/shard_map/ppermute | solution.py:158
  41.7 1.5 %collective-permute-start.16 = (bf16[96,256]{1,0:T(8,128)(2,1)S(1)}, bf16[96,256]{1,0:T(8,128)(2,1)S(1)}, u32[]{:S(2)}, u32[]{:S(2)}) collective-permute-start(bf16[96,256]{1,0:T(8,128)(2,1)S(1)} %restrict_recv.1.refs_0_), channel_id=1, source_target_pairs={{0,2},{1,3},{2,0},{3,1},{4,6},{5,7},{6,4},{7,5},{8,10},{9,11},{10,... | collective-permute-start | bytes 147464 | tf_op jit(solution)/shard_map/ppermute | solution.py:154
  43.6 1.2 %collective-permute-done.18.refs_4_ = bf16[96,256]{1,0:T(8,128)(2,1)S(1)} collective-permute-done((bf16[96,256]{1,0:T(8,128)(2,1)S(1)}, bf16[96,256]{1,0:T(8,128)(2,1)S(1)}, u32[]{:S(2)}, u32[]{:S(2)}) %collective-permute-start.18) | collective-permute-done | bytes 49184 | tf_op jit(solution)/shard_map/ppermute | solution.py:158
  44.7 0.6 collective-permute-start.20
  45.3 0.4 collective-permute-done.17.refs_3_
  45.7 0.9 %collective-permute-start.19 = (bf16[96,256]{1,0:T(8,128)(2,1)S(1)}, bf16[96,256]{1,0:T(8,128)(2,1)S(1)}, u32[]{:S(2)}, u32[]{:S(2)}) collective-permute-start(bf16[96,256]{1,0:T(8,128)(2,1)S(1)} %collective-permute-done.18.refs_4_), channel_id=1, source_target_pairs={{0,1},{1,0},{2,3},{3,2},{4,5},{5,4},{6,7},{7,6},{8,9},{9,8},{10,11... | collective-permute-start | bytes 147464 | tf_op jit(solution)/shard_map/ppermute | solution.py:154
  46.6 0.6 couple.2.refs_10_.refs_1_.base_ref
  47.2 1.0 %collective-permute-done.21.refs_7_ = bf16[96,256]{1,0:T(8,128)(2,1)S(1)} collective-permute-done((bf16[96,256]{1,0:T(8,128)(2,1)S(1)}, bf16[96,256]{1,0:T(8,128)(2,1)S(1)}, u32[]{:S(2)}, u32[]{:S(2)}) %collective-permute-start.21) | collective-permute-done | bytes 49184 | tf_op jit(solution)/shard_map/ppermute | solution.py:154
  48.2 1.1 %collective-permute-done.20.refs_6_ = bf16[96,256]{1,0:T(8,128)(2,1)S(1)} collective-permute-done((bf16[96,256]{1,0:T(8,128)(2,1)S(1)}, bf16[96,256]{1,0:T(8,128)(2,1)S(1)}, u32[]{:S(2)}, u32[]{:S(2)}) %collective-permute-start.20) | collective-permute-done | bytes 49184 | tf_op jit(solution)/shard_map/ppermute | solution.py:154
  49.3 0.4 coarse_pair.1
  49.7 0.9 %collective-permute-start.23 = (bf16[96,256]{1,0:T(8,128)(2,1)S(1)}, bf16[96,256]{1,0:T(8,128)(2,1)S(1)}, u32[]{:S(2)}, u32[]{:S(2)}) collective-permute-start(bf16[96,256]{1,0:T(8,128)(2,1)S(1)} %get-tuple-element.71), channel_id=1, source_target_pairs={{0,8},{4,12},{8,0},{12,4},{16,24},{20,28},{24,16},{28,20},{1,9},{5... | collective-permute-start | bytes 147464 | tf_op jit(solution)/shard_map/ppermute | solution.py:162
  50.6 0.9 %collective-permute-start.24 = (bf16[96,256]{1,0:T(8,128)(2,1)S(1)}, bf16[96,256]{1,0:T(8,128)(2,1)S(1)}, u32[]{:S(2)}, u32[]{:S(2)}) collective-permute-start(bf16[96,256]{1,0:T(8,128)(2,1)S(1)} %get-tuple-element.72), channel_id=1, source_target_pairs={{0,16},{4,20},{8,24},{12,28},{16,0},{20,4},{24,8},{28,12},{1,17},{... | collective-permute-start | bytes 147464 | tf_op jit(solution)/shard_map/ppermute | solution.py:162
  51.5 2.7 %collective-permute-start.25 = (bf16[96,256]{1,0:T(8,128)(2,1)S(1)}, bf16[96,256]{1,0:T(8,128)(2,1)S(1)}, u32[]{:S(2)}, u32[]{:S(2)}) collective-permute-start(bf16[96,256]{1,0:T(8,128)(2,1)S(1)} %get-tuple-element.73), channel_id=1, source_target_pairs={{0,24},{4,28},{8,16},{12,20},{16,8},{20,12},{24,0},{28,4},{1,25},{... | collective-permute-start | bytes 147464 | tf_op jit(solution)/shard_map/ppermute | solution.py:162
  54.2 3.4 %collective-permute-done.24.refs_2_ = bf16[96,256]{1,0:T(8,128)(2,1)S(1)} collective-permute-done((bf16[96,256]{1,0:T(8,128)(2,1)S(1)}, bf16[96,256]{1,0:T(8,128)(2,1)S(1)}, u32[]{:S(2)}, u32[]{:S(2)}) %collective-permute-start.24) | collective-permute-done | bytes 49184 | tf_op jit(solution)/shard_map/ppermute | solution.py:162
  57.9 1.2 %collective-permute-start.27 = (bf16[128,256]{1,0:T(8,128)(2,1)S(1)}, bf16[128,256]{1,0:T(8,128)(2,1)S(1)}, u32[]{:S(2)}, u32[]{:S(2)}) collective-permute-start(bf16[128,256]{1,0:T(8,128)(2,1)S(1)} %get-tuple-element.76), channel_id=1, source_target_pairs={{0,3},{1,2},{2,1},{3,0},{4,7},{5,6},{6,5},{7,4},{8,11},{9,10},{10,... | collective-permute-start | bytes 196616 | tf_op jit(solution)/shard_map/ppermute | solution.py:83
  59.2 1.3 %collective-permute-start.28 = (bf16[128,256]{1,0:T(8,128)(2,1)S(1)}, bf16[128,256]{1,0:T(8,128)(2,1)S(1)}, u32[]{:S(2)}, u32[]{:S(2)}) collective-permute-start(bf16[128,256]{1,0:T(8,128)(2,1)S(1)} %get-tuple-element.77), channel_id=1, source_target_pairs={{0,4},{1,5},{2,6},{3,7},{4,0},{5,1},{6,2},{7,3},{8,12},{9,13},{10,... | collective-permute-start | bytes 196616 | tf_op jit(solution)/shard_map/ppermute | solution.py:83
  60.5 0.9 %collective-permute-start.29 = (bf16[128,256]{1,0:T(8,128)(2,1)S(1)}, bf16[128,256]{1,0:T(8,128)(2,1)S(1)}, u32[]{:S(2)}, u32[]{:S(2)}) collective-permute-start(bf16[128,256]{1,0:T(8,128)(2,1)S(1)} %get-tuple-element.78), channel_id=1, source_target_pairs={{0,1},{1,0},{2,3},{3,2},{4,5},{5,4},{6,7},{7,6},{8,9},{9,8},{10,11... | collective-permute-start | bytes 196616 | tf_op jit(solution)/shard_map/ppermute | solution.py:83
  61.4 0.9 %local.3.base_ref = f32[512,256]{1,0:T(8,128)S(1)} custom-call(bf16[96,256]{1,0:T(8,128)(2,1)S(1)} %get-tuple-element.74.refs_0_.y_ref, f32[1024,256]{1,0:T(8,128)S(1)} %couple.2.refs_10_.refs_1_.base_ref, bf16[1024,96]{1,0:T(8,128)(2,1)S(1)} %mat_basis.1.refs_2_.lb_ref, bf16[512,1024]{1,0:T(8,128)(2,1)S(1)} %get-tuple-element.63.si_ref, ...), custom_call_target="tpu_custom_call" | custom-call | flops 268435456 | bytes 2703360 | tf_op jit(solution)/shard_map/local/pallas_call | solution.py:25
  62.4 1.6 %collective-permute-done.28.refs_11_.refs_2_ = bf16[128,256]{1,0:T(8,128)(2,1)S(1)} collective-permute-done((bf16[128,256]{1,0:T(8,128)(2,1)S(1)}, bf16[128,256]{1,0:T(8,128)(2,1)S(1)}, u32[]{:S(2)}, u32[]{:S(2)}) %collective-permute-start.28) | collective-permute-done | bytes 65568 | tf_op jit(solution)/shard_map/ppermute | solution.py:83
  64.4 1.0 %collective-permute-start.31 = (bf16[128,256]{1,0:T(8,128)(2,1)S(1)}, bf16[128,256]{1,0:T(8,128)(2,1)S(1)}, u32[]{:S(2)}, u32[]{:S(2)}) collective-permute-start(bf16[128,256]{1,0:T(8,128)(2,1)S(1)} %get-tuple-element.83), channel_id=1, source_target_pairs={{0,3},{1,2},{2,1},{3,0},{4,7},{5,6},{6,5},{7,4},{8,11},{9,10},{10,... | collective-permute-start | bytes 196616 | tf_op jit(solution)/shard_map/ppermute | solution.py:83
  65.4 2.6 %collective-permute-start.32 = (bf16[128,256]{1,0:T(8,128)(2,1)S(1)}, bf16[128,256]{1,0:T(8,128)(2,1)S(1)}, u32[]{:S(2)}, u32[]{:S(2)}) collective-permute-start(bf16[128,256]{1,0:T(8,128)(2,1)S(1)} %get-tuple-element.84), channel_id=1, source_target_pairs={{0,4},{1,5},{2,6},{3,7},{4,0},{5,1},{6,2},{7,3},{8,12},{9,13},{10,... | collective-permute-start | bytes 196616 | tf_op jit(solution)/shard_map/ppermute | solution.py:83
  68.4 2.7 %advance.3 = (f32[1024,256]{1,0:T(8,128)}, f32[1024,256]{1,0:T(8,128)S(1)}) custom-call(bf16[96,256]{1,0:T(8,128)(2,1)S(1)} %get-tuple-element.74.refs_0_.y_ref, f32[1024,256]{1,0:T(8,128)S(1)} %couple.2.refs_10_.refs_1_.base_ref, bf16[1024,96]{1,0:T(8,128)(2,1)S(1)} %mat_basis.1.refs_2_.lb_ref, bf16[1024,96]{1,0:T(8,128)(2,1)S(1)} %get-tuple-element.57.bt_ref.refs_3_, ...), custom_call_target="tpu_custom_call" | custom-call | flops 1342177280 | bytes 9289728 | tf_op jit(solution)/shard_map/advance/pallas_call | solution.py:25
  71.1 1.3 %couple.3 = f32[1024,256]{1,0:T(8,128)} custom-call(f32[1024,256]{1,0:T(8,128)S(1)} %get-tuple-element.81.res_ref, bf16[1024,512]{1,0:T(8,128)(2,1)S(1)} %get-tuple-element.49.wt_ref.refs_4_, bf16[128,256]{1,0:T(8,128)(2,1)S(1)} %collective-permute-done.30.refs_0_, bf16[128,256]{1,0:T(8,128)(2,1)S(1)} %collective-permute-done.31.refs_1_, ...), custom_call_target="tpu_custom_call" | custom-call | flops 268435456 | bytes 2359296 | tf_op jit(solution)/shard_map/couple/pallas_call | solution.py:25
  (51 shorter events, 3.1 us)
Async XLA Ops:
  0.6 11.9 %copy-start.3 = (bf16[96,1024]{1,0:T(8,128)(2,1)S(1)}, bf16[96,1024]{1,0:T(8,128)(2,1)}, u32[]{:S(2)}) copy-start(bf16[96,1024]{1,0:T(8,128)(2,1)} %refs_8_.3) | copy-start | bytes 589828
  0.6 11.9 %copy-start.2 = (bf16[1024,1024]{1,0:T(8,128)(2,1)S(1)}, bf16[1024,1024]{1,0:T(8,128)(2,1)}, u32[]{:S(2)}) copy-start(bf16[1024,1024]{1,0:T(8,128)(2,1)} %refs_5_.3) | copy-start | bytes 6291460
  2.3 5.0 %collective-permute-start.2 = (bf16[96,256]{1,0:T(8,128)(2,1)S(1)}, bf16[96,256]{1,0:T(8,128)(2,1)S(1)}, u32[]{:S(2)}, u32[]{:S(2)}) collective-permute-start(bf16[96,256]{1,0:T(8,128)(2,1)S(1)} %convolution_convert_fusion.token.refs_0_), channel_id=1, source_target_pairs={{0,3},{1,2},{2,1},{3,0},{4,7},{5,6},{6,5},{7,4},{8,11},{9,10},{10,... | collective-permute-start | bytes 147464 | tf_op jit(solution)/shard_map/ppermute | solution.py:154
  4.8 4.3 %collective-permute-start.1 = (bf16[96,256]{1,0:T(8,128)(2,1)S(1)}, bf16[96,256]{1,0:T(8,128)(2,1)S(1)}, u32[]{:S(2)}, u32[]{:S(2)}) collective-permute-start(bf16[96,256]{1,0:T(8,128)(2,1)S(1)} %convolution_convert_fusion.token.refs_0_), channel_id=1, source_target_pairs={{0,2},{1,3},{2,0},{3,1},{4,6},{5,7},{6,4},{7,5},{8,10},{9,11},{10,... | collective-permute-start | bytes 147464 | tf_op jit(solution)/shard_map/ppermute | solution.py:154
  5.5 3.7 %collective-permute-start = (bf16[96,256]{1,0:T(8,128)(2,1)S(1)}, bf16[96,256]{1,0:T(8,128)(2,1)S(1)}, u32[]{:S(2)}, u32[]{:S(2)}) collective-permute-start(bf16[96,256]{1,0:T(8,128)(2,1)S(1)} %convolution_convert_fusion.token.refs_0_), channel_id=1, source_target_pairs={{0,1},{1,0},{2,3},{3,2},{4,5},{5,4},{6,7},{7,6},{8,9},{9,8},{10,11... | collective-permute-start | bytes 147464 | tf_op jit(solution)/shard_map/ppermute | solution.py:154
  6.2 1.1 %copy-start.4 = (bf16[768,384]{1,0:T(8,128)(2,1)S(1)}, bf16[768,384]{1,0:T(8,128)(2,1)}, u32[]{:S(2)}) copy-start(bf16[768,384]{1,0:T(8,128)(2,1)} %inv_ref.2) | copy-start | bytes 1769476
  9.5 6.7 %collective-permute-start.3 = (bf16[384,256]{1,0:T(8,128)(2,1)S(1)}, bf16[384,256]{1,0:T(8,128)(2,1)S(1)}, u32[]{:S(2)}, u32[]{:S(2)}) collective-permute-start(bf16[384,256]{1,0:T(8,128)(2,1)S(1)} %get-tuple-element.47), channel_id=1, source_target_pairs={{0,4},{4,0},{8,12},{12,8},{16,20},{20,16},{24,28},{28,24},{1,5},{5... | collective-permute-start | bytes 589832 | tf_op jit(solution)/shard_map/ppermute | solution.py:158
  12.6 17.1 %copy-start.1 = (bf16[1024,1024]{1,0:T(8,128)(2,1)S(1)}, bf16[1024,1024]{1,0:T(8,128)(2,1)}, u32[]{:S(2)}) copy-start(bf16[1024,1024]{1,0:T(8,128)(2,1)} %refs_6_.3) | copy-start | bytes 6291460
  14.9 15.7 %copy-start = (f32[1024,256]{1,0:T(8,128)S(1)}, f32[1024,256]{1,0:T(8,128)}, u32[]{:S(2)}) copy-start(f32[1024,256]{1,0:T(8,128)} %refs_7_.3) | copy-start | bytes 3145732
  16.3 6.0 %collective-permute-start.4 = (bf16[96,256]{1,0:T(8,128)(2,1)S(1)}, bf16[96,256]{1,0:T(8,128)(2,1)S(1)}, u32[]{:S(2)}, u32[]{:S(2)}) collective-permute-start(bf16[96,256]{1,0:T(8,128)(2,1)S(1)} %get-tuple-element.52), channel_id=1, source_target_pairs={{0,8},{4,12},{8,0},{12,4},{16,24},{20,28},{24,16},{28,20},{1,9},{5... | collective-permute-start | bytes 147464 | tf_op jit(solution)/shard_map/ppermute | solution.py:162
  17.9 6.0 %collective-permute-start.5 = (bf16[96,256]{1,0:T(8,128)(2,1)S(1)}, bf16[96,256]{1,0:T(8,128)(2,1)S(1)}, u32[]{:S(2)}, u32[]{:S(2)}) collective-permute-start(bf16[96,256]{1,0:T(8,128)(2,1)S(1)} %get-tuple-element.53), channel_id=1, source_target_pairs={{0,16},{4,20},{8,24},{12,28},{16,0},{20,4},{24,8},{28,12},{1,17},{... | collective-permute-start | bytes 147464 | tf_op jit(solution)/shard_map/ppermute | solution.py:162
  20.5 6.0 %collective-permute-start.6 = (bf16[96,256]{1,0:T(8,128)(2,1)S(1)}, bf16[96,256]{1,0:T(8,128)(2,1)S(1)}, u32[]{:S(2)}, u32[]{:S(2)}) collective-permute-start(bf16[96,256]{1,0:T(8,128)(2,1)S(1)} %get-tuple-element.54), channel_id=1, source_target_pairs={{0,24},{4,28},{8,16},{12,20},{16,8},{20,12},{24,0},{28,4},{1,25},{... | collective-permute-start | bytes 147464 | tf_op jit(solution)/shard_map/ppermute | solution.py:162
  20.7 24.0 %collective-permute-start.22 = (bf16[384,384]{1,0:T(8,128)(2,1)S(1)}, bf16[384,384]{1,0:T(8,128)(2,1)S(1)}, u32[]{:S(2)}, u32[]{:S(2)}) collective-permute-start(bf16[384,384]{1,0:T(8,128)(2,1)S(1)} %get-tuple-element.45.refs_5_), channel_id=1, source_target_pairs={{0,4},{4,0},{8,12},{12,8},{16,20},{20,16},{24,28},{28,24},{1,5},{5... | collective-permute-start | bytes 884744 | tf_op jit(solution)/shard_map/ppermute | solution.py:158
  26.7 4.8 %collective-permute-start.7 = (bf16[128,256]{1,0:T(8,128)(2,1)S(1)}, bf16[128,256]{1,0:T(8,128)(2,1)S(1)}, u32[]{:S(2)}, u32[]{:S(2)}) collective-permute-start(bf16[128,256]{1,0:T(8,128)(2,1)S(1)} %get-tuple-element.58), channel_id=1, source_target_pairs={{0,1},{1,0},{2,3},{3,2},{4,8},{5,9},{6,10},{7,11},{8,4},{9,5},{10,... | collective-permute-start | bytes 196616 | tf_op jit(solution)/shard_map/ppermute | solution.py:83
  26.8 4.8 %collective-permute-start.8 = (bf16[128,256]{1,0:T(8,128)(2,1)S(1)}, bf16[128,256]{1,0:T(8,128)(2,1)S(1)}, u32[]{:S(2)}, u32[]{:S(2)}) collective-permute-start(bf16[128,256]{1,0:T(8,128)(2,1)S(1)} %get-tuple-element.59), channel_id=1, source_target_pairs={{0,3},{1,2},{2,1},{3,0},{4,7},{5,6},{6,5},{7,4},{8,11},{9,10},{10,... | collective-permute-start | bytes 196616 | tf_op jit(solution)/shard_map/ppermute | solution.py:83
  28.5 4.3 %collective-permute-start.9 = (bf16[128,256]{1,0:T(8,128)(2,1)S(1)}, bf16[128,256]{1,0:T(8,128)(2,1)S(1)}, u32[]{:S(2)}, u32[]{:S(2)}) collective-permute-start(bf16[128,256]{1,0:T(8,128)(2,1)S(1)} %get-tuple-element.60), channel_id=1, source_target_pairs={{0,4},{1,5},{2,6},{3,7},{4,0},{5,1},{6,2},{7,3},{8,12},{9,13},{10,... | collective-permute-start | bytes 196616 | tf_op jit(solution)/shard_map/ppermute | solution.py:83
  28.5 4.3 %collective-permute-start.10 = (bf16[128,256]{1,0:T(8,128)(2,1)S(1)}, bf16[128,256]{1,0:T(8,128)(2,1)S(1)}, u32[]{:S(2)}, u32[]{:S(2)}) collective-permute-start(bf16[128,256]{1,0:T(8,128)(2,1)S(1)} %get-tuple-element.61), channel_id=1, source_target_pairs={{0,1},{1,0},{2,3},{3,2},{4,5},{5,4},{6,7},{7,6},{8,9},{9,8},{10,11... | collective-permute-start | bytes 196616 | tf_op jit(solution)/shard_map/ppermute | solution.py:83
  33.1 7.2 %collective-permute-start.11 = (bf16[128,256]{1,0:T(8,128)(2,1)S(1)}, bf16[128,256]{1,0:T(8,128)(2,1)S(1)}, u32[]{:S(2)}, u32[]{:S(2)}) collective-permute-start(bf16[128,256]{1,0:T(8,128)(2,1)S(1)} %get-tuple-element.65.refs_0_), channel_id=1, source_target_pairs={{0,1},{1,0},{2,3},{3,2},{4,8},{5,9},{6,10},{7,11},{8,4},{9,5},{10,... | collective-permute-start | bytes 196616 | tf_op jit(solution)/shard_map/ppermute | solution.py:83
  33.2 7.2 %collective-permute-start.12 = (bf16[128,256]{1,0:T(8,128)(2,1)S(1)}, bf16[128,256]{1,0:T(8,128)(2,1)S(1)}, u32[]{:S(2)}, u32[]{:S(2)}) collective-permute-start(bf16[128,256]{1,0:T(8,128)(2,1)S(1)} %get-tuple-element.66.refs_1_), channel_id=1, source_target_pairs={{0,3},{1,2},{2,1},{3,0},{4,7},{5,6},{6,5},{7,4},{8,11},{9,10},{10,... | collective-permute-start | bytes 196616 | tf_op jit(solution)/shard_map/ppermute | solution.py:83
  33.7 6.7 %collective-permute-start.13 = (bf16[128,256]{1,0:T(8,128)(2,1)S(1)}, bf16[128,256]{1,0:T(8,128)(2,1)S(1)}, u32[]{:S(2)}, u32[]{:S(2)}) collective-permute-start(bf16[128,256]{1,0:T(8,128)(2,1)S(1)} %get-tuple-element.67.refs_2_), channel_id=1, source_target_pairs={{0,4},{1,5},{2,6},{3,7},{4,0},{5,1},{6,2},{7,3},{8,12},{9,13},{10,... | collective-permute-start | bytes 196616 | tf_op jit(solution)/shard_map/ppermute | solution.py:83
  36.6 3.7 %collective-permute-start.14 = (bf16[128,256]{1,0:T(8,128)(2,1)S(1)}, bf16[128,256]{1,0:T(8,128)(2,1)S(1)}, u32[]{:S(2)}, u32[]{:S(2)}) collective-permute-start(bf16[128,256]{1,0:T(8,128)(2,1)S(1)} %get-tuple-element.68.refs_3_), channel_id=1, source_target_pairs={{0,1},{1,0},{2,3},{3,2},{4,5},{5,4},{6,7},{7,6},{8,9},{9,8},{10,11... | collective-permute-start | bytes 196616 | tf_op jit(solution)/shard_map/ppermute | solution.py:83
  40.6 4.2 %collective-permute-start.18 = (bf16[96,256]{1,0:T(8,128)(2,1)S(1)}, bf16[96,256]{1,0:T(8,128)(2,1)S(1)}, u32[]{:S(2)}, u32[]{:S(2)}) collective-permute-start(bf16[96,256]{1,0:T(8,128)(2,1)S(1)} %restrict_recv.1.refs_0_), channel_id=1, source_target_pairs={{0,4},{4,0},{8,12},{12,8},{16,20},{20,16},{24,28},{28,24},{1,5},{5... | collective-permute-start | bytes 147464 | tf_op jit(solution)/shard_map/ppermute | solution.py:158
  41.7 4.0 %collective-permute-start.17 = (bf16[96,256]{1,0:T(8,128)(2,1)S(1)}, bf16[96,256]{1,0:T(8,128)(2,1)S(1)}, u32[]{:S(2)}, u32[]{:S(2)}) collective-permute-start(bf16[96,256]{1,0:T(8,128)(2,1)S(1)} %restrict_recv.1.refs_0_), channel_id=1, source_target_pairs={{0,3},{1,2},{2,1},{3,0},{4,7},{5,6},{6,5},{7,4},{8,11},{9,10},{10,... | collective-permute-start | bytes 147464 | tf_op jit(solution)/shard_map/ppermute | solution.py:154
  41.7 5.5 %collective-permute-start.16 = (bf16[96,256]{1,0:T(8,128)(2,1)S(1)}, bf16[96,256]{1,0:T(8,128)(2,1)S(1)}, u32[]{:S(2)}, u32[]{:S(2)}) collective-permute-start(bf16[96,256]{1,0:T(8,128)(2,1)S(1)} %restrict_recv.1.refs_0_), channel_id=1, source_target_pairs={{0,2},{1,3},{2,0},{3,1},{4,6},{5,7},{6,4},{7,5},{8,10},{9,11},{10,... | collective-permute-start | bytes 147464 | tf_op jit(solution)/shard_map/ppermute | solution.py:154
  43.2 4.1 %collective-permute-start.15 = (bf16[96,256]{1,0:T(8,128)(2,1)S(1)}, bf16[96,256]{1,0:T(8,128)(2,1)S(1)}, u32[]{:S(2)}, u32[]{:S(2)}) collective-permute-start(bf16[96,256]{1,0:T(8,128)(2,1)S(1)} %restrict_recv.1.refs_0_), channel_id=1, source_target_pairs={{0,1},{1,0},{2,3},{3,2},{4,5},{5,4},{6,7},{7,6},{8,9},{9,8},{10,11... | collective-permute-start | bytes 147464 | tf_op jit(solution)/shard_map/ppermute | solution.py:154
  44.7 3.5 %collective-permute-start.21 = (bf16[96,256]{1,0:T(8,128)(2,1)S(1)}, bf16[96,256]{1,0:T(8,128)(2,1)S(1)}, u32[]{:S(2)}, u32[]{:S(2)}) collective-permute-start(bf16[96,256]{1,0:T(8,128)(2,1)S(1)} %collective-permute-done.18.refs_4_), channel_id=1, source_target_pairs={{0,3},{1,2},{2,1},{3,0},{4,7},{5,6},{6,5},{7,4},{8,11},{9,10},{10,... | collective-permute-start | bytes 147464 | tf_op jit(solution)/shard_map/ppermute | solution.py:154
  44.7 4.6 %collective-permute-start.20 = (bf16[96,256]{1,0:T(8,128)(2,1)S(1)}, bf16[96,256]{1,0:T(8,128)(2,1)S(1)}, u32[]{:S(2)}, u32[]{:S(2)}) collective-permute-start(bf16[96,256]{1,0:T(8,128)(2,1)S(1)} %collective-permute-done.18.refs_4_), channel_id=1, source_target_pairs={{0,2},{1,3},{2,0},{3,1},{4,6},{5,7},{6,4},{7,5},{8,10},{9,11},{10,... | collective-permute-start | bytes 147464 | tf_op jit(solution)/shard_map/ppermute | solution.py:154
  45.7 3.6 %collective-permute-start.19 = (bf16[96,256]{1,0:T(8,128)(2,1)S(1)}, bf16[96,256]{1,0:T(8,128)(2,1)S(1)}, u32[]{:S(2)}, u32[]{:S(2)}) collective-permute-start(bf16[96,256]{1,0:T(8,128)(2,1)S(1)} %collective-permute-done.18.refs_4_), channel_id=1, source_target_pairs={{0,1},{1,0},{2,3},{3,2},{4,5},{5,4},{6,7},{7,6},{8,9},{9,8},{10,11... | collective-permute-start | bytes 147464 | tf_op jit(solution)/shard_map/ppermute | solution.py:154
  49.7 4.5 %collective-permute-start.23 = (bf16[96,256]{1,0:T(8,128)(2,1)S(1)}, bf16[96,256]{1,0:T(8,128)(2,1)S(1)}, u32[]{:S(2)}, u32[]{:S(2)}) collective-permute-start(bf16[96,256]{1,0:T(8,128)(2,1)S(1)} %get-tuple-element.71), channel_id=1, source_target_pairs={{0,8},{4,12},{8,0},{12,4},{16,24},{20,28},{24,16},{28,20},{1,9},{5... | collective-permute-start | bytes 147464 | tf_op jit(solution)/shard_map/ppermute | solution.py:162
  50.6 7.0 %collective-permute-start.24 = (bf16[96,256]{1,0:T(8,128)(2,1)S(1)}, bf16[96,256]{1,0:T(8,128)(2,1)S(1)}, u32[]{:S(2)}, u32[]{:S(2)}) collective-permute-start(bf16[96,256]{1,0:T(8,128)(2,1)S(1)} %get-tuple-element.72), channel_id=1, source_target_pairs={{0,16},{4,20},{8,24},{12,28},{16,0},{20,4},{24,8},{28,12},{1,17},{... | collective-permute-start | bytes 147464 | tf_op jit(solution)/shard_map/ppermute | solution.py:162
  51.5 6.1 %collective-permute-start.25 = (bf16[96,256]{1,0:T(8,128)(2,1)S(1)}, bf16[96,256]{1,0:T(8,128)(2,1)S(1)}, u32[]{:S(2)}, u32[]{:S(2)}) collective-permute-start(bf16[96,256]{1,0:T(8,128)(2,1)S(1)} %get-tuple-element.73), channel_id=1, source_target_pairs={{0,24},{4,28},{8,16},{12,20},{16,8},{20,12},{24,0},{28,4},{1,25},{... | collective-permute-start | bytes 147464 | tf_op jit(solution)/shard_map/ppermute | solution.py:162
  57.9 4.5 %collective-permute-start.26 = (bf16[128,256]{1,0:T(8,128)(2,1)S(1)}, bf16[128,256]{1,0:T(8,128)(2,1)S(1)}, u32[]{:S(2)}, u32[]{:S(2)}) collective-permute-start(bf16[128,256]{1,0:T(8,128)(2,1)S(1)} %get-tuple-element.75), channel_id=1, source_target_pairs={{0,1},{1,0},{2,3},{3,2},{4,8},{5,9},{6,10},{7,11},{8,4},{9,5},{10,... | collective-permute-start | bytes 196616 | tf_op jit(solution)/shard_map/ppermute | solution.py:83
  57.9 4.4 %collective-permute-start.27 = (bf16[128,256]{1,0:T(8,128)(2,1)S(1)}, bf16[128,256]{1,0:T(8,128)(2,1)S(1)}, u32[]{:S(2)}, u32[]{:S(2)}) collective-permute-start(bf16[128,256]{1,0:T(8,128)(2,1)S(1)} %get-tuple-element.76), channel_id=1, source_target_pairs={{0,3},{1,2},{2,1},{3,0},{4,7},{5,6},{6,5},{7,4},{8,11},{9,10},{10,... | collective-permute-start | bytes 196616 | tf_op jit(solution)/shard_map/ppermute | solution.py:83
  59.2 4.8 %collective-permute-start.28 = (bf16[128,256]{1,0:T(8,128)(2,1)S(1)}, bf16[128,256]{1,0:T(8,128)(2,1)S(1)}, u32[]{:S(2)}, u32[]{:S(2)}) collective-permute-start(bf16[128,256]{1,0:T(8,128)(2,1)S(1)} %get-tuple-element.77), channel_id=1, source_target_pairs={{0,4},{1,5},{2,6},{3,7},{4,0},{5,1},{6,2},{7,3},{8,12},{9,13},{10,... | collective-permute-start | bytes 196616 | tf_op jit(solution)/shard_map/ppermute | solution.py:83
  60.5 3.5 %collective-permute-start.29 = (bf16[128,256]{1,0:T(8,128)(2,1)S(1)}, bf16[128,256]{1,0:T(8,128)(2,1)S(1)}, u32[]{:S(2)}, u32[]{:S(2)}) collective-permute-start(bf16[128,256]{1,0:T(8,128)(2,1)S(1)} %get-tuple-element.78), channel_id=1, source_target_pairs={{0,1},{1,0},{2,3},{3,2},{4,5},{5,4},{6,7},{7,6},{8,9},{9,8},{10,11... | collective-permute-start | bytes 196616 | tf_op jit(solution)/shard_map/ppermute | solution.py:83
  64.3 6.8 %collective-permute-start.30 = (bf16[128,256]{1,0:T(8,128)(2,1)S(1)}, bf16[128,256]{1,0:T(8,128)(2,1)S(1)}, u32[]{:S(2)}, u32[]{:S(2)}) collective-permute-start(bf16[128,256]{1,0:T(8,128)(2,1)S(1)} %get-tuple-element.82), channel_id=1, source_target_pairs={{0,1},{1,0},{2,3},{3,2},{4,8},{5,9},{6,10},{7,11},{8,4},{9,5},{10,... | collective-permute-start | bytes 196616 | tf_op jit(solution)/shard_map/ppermute | solution.py:83
  64.4 6.8 %collective-permute-start.31 = (bf16[128,256]{1,0:T(8,128)(2,1)S(1)}, bf16[128,256]{1,0:T(8,128)(2,1)S(1)}, u32[]{:S(2)}, u32[]{:S(2)}) collective-permute-start(bf16[128,256]{1,0:T(8,128)(2,1)S(1)} %get-tuple-element.83), channel_id=1, source_target_pairs={{0,3},{1,2},{2,1},{3,0},{4,7},{5,6},{6,5},{7,4},{8,11},{9,10},{10,... | collective-permute-start | bytes 196616 | tf_op jit(solution)/shard_map/ppermute | solution.py:83
  65.4 5.8 %collective-permute-start.32 = (bf16[128,256]{1,0:T(8,128)(2,1)S(1)}, bf16[128,256]{1,0:T(8,128)(2,1)S(1)}, u32[]{:S(2)}, u32[]{:S(2)}) collective-permute-start(bf16[128,256]{1,0:T(8,128)(2,1)S(1)} %get-tuple-element.84), channel_id=1, source_target_pairs={{0,4},{1,5},{2,6},{3,7},{4,0},{5,1},{6,2},{7,3},{8,12},{9,13},{10,... | collective-permute-start | bytes 196616 | tf_op jit(solution)/shard_map/ppermute | solution.py:83
  68.0 3.2 %collective-permute-start.33 = (bf16[128,256]{1,0:T(8,128)(2,1)S(1)}, bf16[128,256]{1,0:T(8,128)(2,1)S(1)}, u32[]{:S(2)}, u32[]{:S(2)}) collective-permute-start(bf16[128,256]{1,0:T(8,128)(2,1)S(1)} %get-tuple-element.85), channel_id=1, source_target_pairs={{0,1},{1,0},{2,3},{3,2},{4,5},{5,4},{6,7},{7,6},{8,9},{9,8},{10,11... | collective-permute-start | bytes 196616 | tf_op jit(solution)/shard_map/ppermute | solution.py:83

commit v5 on v4

--- a/solution.py
+++ b/solution.py
@@ -7,6 +7,7 @@
 from jax.experimental.pallas import tpu as pltpu
 from jax.sharding import PartitionSpec as P
 
+
 STEPS = 2
 BF = jnp.bfloat16
 F32 = jnp.float32
@@ -19,7 +20,7 @@
     return jnp.dot(a, b, preferred_element_type=F32)
 
 
-def call(kernel, outs, *args, name, scratch=(), flops=0, hbm_ins=0, hbm_outs=0, tokens=0):
+def call(kernel, outs, *args, scratch=(), flops=0, hbm_ins=0, hbm_outs=0, tokens=0):
     nbytes = sum(a.size * a.dtype.itemsize for a in args)
     inner = len(args) - hbm_ins - tokens
     return pl.pallas_call(
@@ -30,7 +31,6 @@
         scratch_shapes=list(scratch),
         compiler_params=pltpu.CompilerParams(vmem_limit_bytes=LIMIT),
         cost_estimate=pl.CostEstimate(flops=flops, bytes_accessed=nbytes, transcendentals=0),
-        name=name,
     )(*args)
 
 
@@ -94,7 +94,7 @@
                 across = lax.broadcasted_iota(jnp.int32, (ovl, ovl), 1) + j * ovl
                 sel_ref[at, pl.ds(j * ovl, ovl)] = jnp.where(idx == across.astype(F32), 1.0, 0.0).astype(BF)
 
-    def k_products(sel_ref, wt_ref, inv_ref, basis_ref, bf_ref, t_ref, si_ref, f_ref, bt_ref):
+    def k_products(sel_ref, wt_ref, inv_ref, basis_ref, token, bf_ref, t_ref, si_ref, f_ref, bt_ref):
         bt = basis_ref[...].astype(F32).T.astype(BF)
         bt_ref[...] = bt
         bf_ref[...] = mm(sel_ref[...], bt).astype(BF)
@@ -115,8 +115,12 @@
 
     half = nz * cpd
 
-    def k_hold(inv_ref, token, same_ref, cross_ref):
+    def k_lead(out_ref):
+        out_ref[...] = jnp.zeros_like(out_ref)
+
+    def k_hold(inv_ref, block_ref, token, same_ref, cross_ref, out_ref):
         r = lax.axis_index("row")
+        out_ref[...] = block_ref[...]
         for i in range(nz):
             at = pl.ds(i * cpd, cpd)
             same_ref[at, :] = inv_ref[pl.ds(pl.multiple_of((r ^ (2 * i)) * cpd, 16), cpd), :]
@@ -127,21 +131,9 @@
         for i, block in enumerate(blocks):
             group[pl.ds(pl.multiple_of((c ^ i) * cpd, 16), cpd), :] = block[...]
 
-    def k_coarse(*refs):
-        blocks, (same_ref, cross_ref, keep_ref, send_ref, group) = refs[:nc], refs[nc:]
-        place(group, blocks)
-        send_ref[...] = mm(cross_ref[...], group[...]).astype(BF)
-        keep_ref[...] = mm(same_ref[...], group[...])
-
-    def k_half(keep_ref, recv_ref, token, own_ref, *sends):
-        own_ref[...] = keep_ref[pl.ds(0, cpd), :] + recv_ref[pl.ds(0, cpd), :].astype(F32)
-        for i, ref in enumerate(sends):
-            at = pl.ds((i + 1) * cpd, cpd)
-            ref[...] = (keep_ref[at, :] + recv_ref[at, :].astype(F32)).astype(BF)
-
     def k_coarse_pair(*refs):
         mine, theirs, refs = refs[:nc], refs[nc : 2 * nc], refs[2 * nc :]
-        same_ref, other_ref, token, own_ref = refs[:4]
+        same_ref, other_ref, _, own_ref = refs[:4]
         sends, (group, group_other) = refs[4:-2], refs[-2:]
         place(group, mine)
         place(group_other, theirs)
@@ -175,9 +167,7 @@
             ref[...] = mm(bf_ref[pl.ds(s * ovl, ovl), :], y).astype(BF)
 
     def coarse_faces(parts):
-        y, *faces = call(
-            k_coarse_faces, [((cpd, nrhs), BF)] + [((ovl, nrhs), BF)] * 4, *parts, bfac, name="coarse_faces",
-        )
+        y, *faces = call(k_coarse_faces, [((cpd, nrhs), BF)] + [((ovl, nrhs), BF)] * 4, *parts, bfac)
         return y, faces
 
     def k_local(y_ref, base_ref, lb_ref, si_ref, bf_ref, *refs):
@@ -196,7 +186,7 @@
     def local(y, base, olds):
         (face,) = call(
             k_local, [((nf, nrhs), F32)], y, base, lbmat, simat, bfac, *olds,
-            scratch=[pltpu.VMEM((nloc, nrhs), BF)], name="local", flops=2 * nf * nloc * nrhs,
+            scratch=[pltpu.VMEM((nloc, nrhs), BF)], flops=2 * nf * nloc * nrhs,
         )
         return face
 
@@ -208,7 +198,7 @@
             ref[...] = (base_ref[at, :] + mm(f_ref[at, :], recv)).astype(BF)
 
     def faces_after(base, recv):
-        return call(k_faces, [((ovl, nrhs), BF)] * 4, base, fmat, *recv, name="faces", flops=2 * nf * nf * nrhs)
+        return call(k_faces, [((ovl, nrhs), BF)] * 4, base, fmat, *recv, flops=2 * nf * nf * nrhs)
 
     def k_advance(first, last, *refs):
         y_ref, base_ref, lb_ref, bt_ref, wt_ref, inv_ref, mat_ref, rhs_ref, basis_ref = refs[:9]
@@ -258,7 +248,7 @@
             functools.partial(k_advance, first, last), outs,
             y, base, lbmat, btmat, wt, local_inv, local_mat, rhs, basis_t, *recv, *([] if first else [old]),
             scratch=[pltpu.VMEM((nloc, nrhs), BF)] * 2 + [pltpu.VMEM((nf, nrhs), BF)] + extra,
-            hbm_outs=1 if last else 0, name="advance", flops=5 * nloc * nloc * nrhs,
+            hbm_outs=1 if last else 0, flops=5 * nloc * nloc * nrhs,
         )
 
     def k_restrict_recv(base_ref, t_ref, *refs):
@@ -294,31 +284,36 @@
         return call(
             k_couple_last if last else k_couple, [((nloc, nrhs), F32)], res, wt, *recv,
             scratch=[pltpu.VMEM((nf, nrhs), BF)] + extra, hbm_outs=1 if last else 0,
-            name="couple", flops=2 * nloc * nf * nrhs,
+            flops=2 * nloc * nf * nrhs,
         )[0]
 
+    def coarse_pair(mine, across, token):
+        return call(
+            k_coarse_pair, own_and_sends, *mine, *over_col(across), same, other, token,
+            scratch=[pltpu.VMEM((nc * cpd, nrhs), BF)] * 2, tokens=1,
+            flops=4 * half * nc * cpd * nrhs,
+        )
+
+    (lead,) = call(k_lead, [((8, 128), F32)], flops=8 * nloc * nloc * nrhs)
     restricted = mm(basis_t, rhs.astype(BF)).astype(BF)
-    blocks = over_col(restricted)
-    same, cross = call(
-        k_hold, [((half, coarse_inv.shape[1]), BF)] * 2, coarse_inv, restricted, tokens=1, name="hold",
-    )
-    keep, send = call(
-        k_coarse, [((half, nrhs), F32), ((half, nrhs), BF)], *blocks, same, cross,
-        scratch=[pltpu.VMEM((nc * cpd, nrhs), BF)], name="coarse", flops=4 * half * nc * cpd * nrhs,
-    )
-    arrived = over_pair(send)
+    same, cross, restricted = call(
+        k_hold, [((half, coarse_inv.shape[1]), BF)] * 2 + [((cpd, nrhs), BF)], coarse_inv, restricted, lead,
+        tokens=1,
+    )
+    across = over_pair(restricted)
     other = over_pair(cross)
+    mine = over_col(restricted)
     table = jnp.concatenate([margin_rows[0].astype(F32), couple[0]], axis=0)
-    sel, wt = call(k_select, [((nf, nloc), BF), ((nloc, nf), BF)], table, keep, tokens=1, name="select")
+    sel, wt = call(k_select, [((nf, nloc), BF), ((nloc, nf), BF)], table, restricted, tokens=1)
+    own, *sends = coarse_pair(mine, across, wt)
     bfac, tmat, simat, fmat, btmat = call(
         k_products,
         [((nf, cpd), BF), ((cpd, nf), BF), ((nf, nloc), BF), ((nf, nf), BF), ((nloc, cpd), BF)],
-        sel, wt, local_inv, basis_t, name="products", flops=2 * nf * nloc * (nloc + nf + 2 * cpd),
-    )
-    own, *sends = call(k_half, own_and_sends, keep, arrived, tmat, tokens=1, name="half")
+        sel, wt, local_inv, basis_t, own, tokens=1, flops=2 * nf * nloc * (nloc + nf + 2 * cpd),
+    )
     (lbmat,) = call(
         k_mat_basis, [((nloc, cpd), BF)], local_mat, btmat, own, tokens=1,
-        name="mat_basis", flops=2 * nloc * nloc * cpd,
+        flops=2 * nloc * nloc * cpd,
     )
     residual, solution, sent = rhs, None, []
     for sweep in range(STEPS):
@@ -331,15 +326,8 @@
         solution, res = new[:2]
         residual = coupled(res, recv2, last)
         if not last:
-            (restricted,) = call(
-                k_restrict_recv, [((cpd, nrhs), BF)], new[2], tmat, *recv2, name="restrict_recv",
-            )
-            across = over_pair(restricted)
-            own, *sends = call(
-                k_coarse_pair, own_and_sends, *over_col(restricted), *over_col(across), same, other, residual,
-                scratch=[pltpu.VMEM((nc * cpd, nrhs), BF)] * 2, tokens=1,
-                name="coarse_pair", flops=4 * half * nc * cpd * nrhs,
-            )
+            (restricted,) = call(k_restrict_recv, [((cpd, nrhs), BF)], new[2], tmat, *recv2)
+            own, *sends = coarse_pair(over_col(restricted), over_pair(restricted), residual)
     return (solution, residual)
 
 

time: 72.7 us -> 72.2 us (level)
  waiting for transfers between devices: 17.3 us -> 19.9 us
  matrix products: 1.69 us -> 0.22 us
  other arithmetic: 1.37 us -> 0.01 us
    ppermute x16, starting transfers between devices: 15 us -> 12.8 us  [halo(): return [lax.ppermute(f, both, p) for f, p in zip(faces, slot_perms)]]
    dot_general x1, matrix products: 1.69 us -> 0.22 us  [mm(): return jnp.dot(a, b, preferred_element_type=F32)]
    ppermute x3, waiting for transfers between devices: 2.45 us -> 3.68 us  [over_pair(): return lax.ppermute(value, 'row', [(i, i ^ 1) for i in range(nr)])]
    ppermute x9 -> x12, starting transfers between devices: 6.47 us -> 7.66 us  [over_col(): lax.ppermute(block, 'col', [(i, i ^ k) for i in range(nc)])]
    ppermute x16, waiting for transfers between devices: 2.81 us -> 3.96 us  [halo(): return [lax.ppermute(f, both, p) for f, p in zip(faces, slot_perms)]]
    ppermute x9 -> x12, waiting for transfers between devices: 4.31 us -> 5.15 us  [over_col(): lax.ppermute(block, 'col', [(i, i ^ k) for i in range(nc)])]
  transfers between devices with their start and end apart: 34 -> 37, of which waited for: 11 -> 13; matrix products, arithmetic and copies ran while one was open for 2% -> 0% of each run, Pallas kernels for 18% -> 17%
where the time goes in v5:
time: 72.2 us; the launch traced here: 72 us
  starting transfers between devices  34.1 us (47%)
  waiting for transfers between devices  19.9 us (28%)
  Pallas kernels  15.5 us (21%)
  local copies, waits for them, and re-layouts  1.3 us (2%)
  between operations  0.99 us (1%)
    pallas_call x18, Pallas kernels, call(): pl.pallas_call(kernel, out_shape=[jax.ShapeDtypeStruct(s, d) for s, d in...  15.5 us
    ppermute x16, starting transfers between devices, halo(): return [lax.ppermute(f, both, p) for f, p in zip(faces, slot_perms)]  12.8 us
    ppermute x6, starting transfers between devices, reduce_rows(): lax.ppermute(s, 'row', [(i, i ^ 2 * (k + 1)) for i in range(nr)])  8.9 us
    ppermute x12, starting transfers between devices, over_col(): lax.ppermute(block, 'col', [(i, i ^ k) for i in range(nc)])  7.66 us
    ppermute x6, waiting for transfers between devices, reduce_rows(): lax.ppermute(s, 'row', [(i, i ^ 2 * (k + 1)) for i in range(nr)])  7.1 us
    ppermute x12, waiting for transfers between devices, over_col(): lax.ppermute(block, 'col', [(i, i ^ k) for i in range(nc)])  5.15 us
    ppermute x3, starting transfers between devices, over_pair(): return lax.ppermute(value, 'row', [(i, i ^ 1) for i in range(nr)])  4.75 us
    ppermute x16, waiting for transfers between devices, halo(): return [lax.ppermute(f, both, p) for f, p in zip(faces, slot_perms)]  3.96 us
  transfers between devices with their start and end apart: 37, of which 13 were waited for; matrix products, arithmetic and copies ran while one was open for 0% of the time, Pallas kernels for 17%

profile of v5, /device:TPU:0, one launch (start us, length us, event | category | flops | bytes accessed | tf_op | source)
XLA Modules:
  0.0 72.0 jit_solution(17445582226476969015)
XLA Ops:
  0.7 0.9 %copy-done.3 = bf16[96,1024]{1,0:T(8,128)(2,1)S(1)} copy-done((bf16[96,1024]{1,0:T(8,128)(2,1)S(1)}, bf16[96,1024]{1,0:T(8,128)(2,1)}, u32[]{:S(2)}) %copy-start.3) | copy-done | bytes 196632
  1.6 0.4 copy-done
  2.3 3.1 %collective-permute-start.3 = (bf16[96,256]{1,0:T(8,128)(2,1)S(1)}, bf16[96,256]{1,0:T(8,128)(2,1)S(1)}, u32[]{:S(2)}, u32[]{:S(2)}) collective-permute-start(bf16[96,256]{1,0:T(8,128)(2,1)S(1)} %get-tuple-element.43.token.refs_0_), channel_id=1, source_target_pairs={{0,4},{4,0},{8,12},{12,8},{16,20},{20,16},{24,28},{28,24},{1,5},{5... | collective-permute-start | bytes 147464 | tf_op jit(solution)/shard_map/ppermute | solution.py:150
  5.3 0.7 collective-permute-start.2
  6.0 0.8 %collective-permute-start.1 = (bf16[96,256]{1,0:T(8,128)(2,1)S(1)}, bf16[96,256]{1,0:T(8,128)(2,1)S(1)}, u32[]{:S(2)}, u32[]{:S(2)}) collective-permute-start(bf16[96,256]{1,0:T(8,128)(2,1)S(1)} %get-tuple-element.43.token.refs_0_), channel_id=1, source_target_pairs={{0,2},{1,3},{2,0},{3,1},{4,6},{5,7},{6,4},{7,5},{8,10},{9,11},{10,... | collective-permute-start | bytes 147464 | tf_op jit(solution)/shard_map/ppermute | solution.py:146
  7.5 1.1 %collective-permute-start.6 = (bf16[96,256]{1,0:T(8,128)(2,1)S(1)}, bf16[96,256]{1,0:T(8,128)(2,1)S(1)}, u32[]{:S(2)}, u32[]{:S(2)}) collective-permute-start(bf16[96,256]{1,0:T(8,128)(2,1)S(1)} %collective-permute-done.3.refs_4_), channel_id=1, source_target_pairs={{0,3},{1,2},{2,1},{3,0},{4,7},{5,6},{6,5},{7,4},{8,11},{9,10},{10,... | collective-permute-start | bytes 147464 | tf_op jit(solution)/shard_map/ppermute | solution.py:146
  8.6 0.7 %collective-permute-done.2.refs_3_ = bf16[96,256]{1,0:T(8,128)(2,1)S(1)} collective-permute-done((bf16[96,256]{1,0:T(8,128)(2,1)S(1)}, bf16[96,256]{1,0:T(8,128)(2,1)S(1)}, u32[]{:S(2)}, u32[]{:S(2)}) %collective-permute-start.2) | collective-permute-done | bytes 49184 | tf_op jit(solution)/shard_map/ppermute | solution.py:146
  9.3 1.5 %collective-permute-start.5 = (bf16[96,256]{1,0:T(8,128)(2,1)S(1)}, bf16[96,256]{1,0:T(8,128)(2,1)S(1)}, u32[]{:S(2)}, u32[]{:S(2)}) collective-permute-start(bf16[96,256]{1,0:T(8,128)(2,1)S(1)} %collective-permute-done.3.refs_4_), channel_id=1, source_target_pairs={{0,2},{1,3},{2,0},{3,1},{4,6},{5,7},{6,4},{7,5},{8,10},{9,11},{10,... | collective-permute-start | bytes 147464 | tf_op jit(solution)/shard_map/ppermute | solution.py:146
  10.8 0.8 %shard_map.88 = (bf16[512,1024]{1,0:T(8,128)(2,1)S(1)}, bf16[1024,512]{1,0:T(8,128)(2,1)S(1)}) custom-call(f32[8,128]{1,0:T(8,128)S(1)} %pad_maximum_fusion.table_ref, bf16[96,256]{1,0:T(8,128)(2,1)S(1)} %get-tuple-element.43.token.refs_0_), custom_call_target="tpu_custom_call" | custom-call | bytes 53248 | tf_op jit(solution)/shard_map/pallas_call | solution.py:26
  11.6 1.8 %collective-permute-done.5.refs_6_ = bf16[96,256]{1,0:T(8,128)(2,1)S(1)} collective-permute-done((bf16[96,256]{1,0:T(8,128)(2,1)S(1)}, bf16[96,256]{1,0:T(8,128)(2,1)S(1)}, u32[]{:S(2)}, u32[]{:S(2)}) %collective-permute-start.5) | collective-permute-done | bytes 49184 | tf_op jit(solution)/shard_map/ppermute | solution.py:146
  13.4 2.8 %collective-permute-done.7.refs_9_ = bf16[384,384]{1,0:T(8,128)(2,1)S(1)} collective-permute-done((bf16[384,384]{1,0:T(8,128)(2,1)S(1)}, bf16[384,384]{1,0:T(8,128)(2,1)S(1)}, u32[]{:S(2)}, u32[]{:S(2)}) %collective-permute-start.7) | collective-permute-done | bytes 294944 | tf_op jit(solution)/shard_map/ppermute | solution.py:150
  16.3 0.4 shard_map.89
  16.7 1.6 %collective-permute-start.8 = (bf16[96,256]{1,0:T(8,128)(2,1)S(1)}, bf16[96,256]{1,0:T(8,128)(2,1)S(1)}, u32[]{:S(2)}, u32[]{:S(2)}) collective-permute-start(bf16[96,256]{1,0:T(8,128)(2,1)S(1)} %get-tuple-element.48), channel_id=1, source_target_pairs={{0,8},{4,12},{8,0},{12,4},{16,24},{20,28},{24,16},{28,20},{1,9},{5... | collective-permute-start | bytes 147464 | tf_op jit(solution)/shard_map/ppermute | solution.py:154
  18.4 2.6 %collective-permute-start.9 = (bf16[96,256]{1,0:T(8,128)(2,1)S(1)}, bf16[96,256]{1,0:T(8,128)(2,1)S(1)}, u32[]{:S(2)}, u32[]{:S(2)}) collective-permute-start(bf16[96,256]{1,0:T(8,128)(2,1)S(1)} %get-tuple-element.49), channel_id=1, source_target_pairs={{0,16},{4,20},{8,24},{12,28},{16,0},{20,4},{24,8},{28,12},{1,17},{... | collective-permute-start | bytes 147464 | tf_op jit(solution)/shard_map/ppermute | solution.py:154
  21.2 2.3 %shard_map.90 = (bf16[512,96]{1,0:T(8,128)(2,1)S(1)}, bf16[96,512]{1,0:T(8,128)(2,1)S(1)}, bf16[512,1024]{1,0:T(8,128)(2,1)S(1)}, bf16[512,512]{1,0:T(8,128)(2,1)S(1)}, bf16[1024,96]{1,0:T(8,128)(2,1)S(1)}) custom-call(bf16[512,1024]{1,0:T(8,128)(2,1)S(1)} %get-tuple-element.51.sel_ref, bf16[1024,512]{1,0:T(8,128)(2,1)S(1)} %get-tuple-element.46.refs_10_.wt_ref.refs_4_, ...), custom_call_target="tpu_custom_call" | custom-call | flops 1811939328 | bytes 4489216 | tf_op jit(solution)/shard_map/pallas_call | solution.py:26
  23.9 3.1 %collective-permute-done.10.refs_3_ = bf16[96,256]{1,0:T(8,128)(2,1)S(1)} collective-permute-done((bf16[96,256]{1,0:T(8,128)(2,1)S(1)}, bf16[96,256]{1,0:T(8,128)(2,1)S(1)}, u32[]{:S(2)}, u32[]{:S(2)}) %collective-permute-start.10) | collective-permute-done | bytes 49184 | tf_op jit(solution)/shard_map/ppermute | solution.py:154
  27.3 1.6 %collective-permute-start.12 = (bf16[128,256]{1,0:T(8,128)(2,1)S(1)}, bf16[128,256]{1,0:T(8,128)(2,1)S(1)}, u32[]{:S(2)}, u32[]{:S(2)}) collective-permute-start(bf16[128,256]{1,0:T(8,128)(2,1)S(1)} %get-tuple-element.56), channel_id=1, source_target_pairs={{0,3},{1,2},{2,1},{3,0},{4,7},{5,6},{6,5},{7,4},{8,11},{9,10},{10,... | collective-permute-start | bytes 196616 | tf_op jit(solution)/shard_map/ppermute | solution.py:83
  28.9 0.9 %shard_map.92.refs_2_.lb_ref = bf16[1024,96]{1,0:T(8,128)(2,1)S(1)} custom-call(bf16[1024,1024]{1,0:T(8,128)(2,1)S(1)} %copy-done.1, bf16[1024,96]{1,0:T(8,128)(2,1)S(1)} %get-tuple-element.54.bt_ref.refs_3_, f32[96,256]{1,0:T(8,128)S(1)} %get-tuple-element.47.token.refs_0_), custom_call_target="tpu_custom_call" | custom-call | flops 201326592 | bytes 2392064 | tf_op jit(solution)/shard_map/pallas_call | solution.py:26
  29.8 0.9 %shard_map.94.base_ref = f32[512,256]{1,0:T(8,128)S(1)} custom-call(bf16[96,256]{1,0:T(8,128)(2,1)S(1)} %get-tuple-element.53.refs_0_.y_ref, f32[1024,256]{1,0:T(8,128)S(1)} %copy-done, bf16[1024,96]{1,0:T(8,128)(2,1)S(1)} %shard_map.92.refs_2_.lb_ref, bf16[512,1024]{1,0:T(8,128)(2,1)S(1)} %get-tuple-element.61.si_ref, ...), custom_call_target="tpu_custom_call" | custom-call | flops 268435456 | bytes 2441216 | tf_op jit(solution)/shard_map/pallas_call | solution.py:26
  31.1 2.0 %collective-permute-done.13.refs_11_.refs_2_ = bf16[128,256]{1,0:T(8,128)(2,1)S(1)} collective-permute-done((bf16[128,256]{1,0:T(8,128)(2,1)S(1)}, bf16[128,256]{1,0:T(8,128)(2,1)S(1)}, u32[]{:S(2)}, u32[]{:S(2)}) %collective-permute-start.13) | collective-permute-done | bytes 65568 | tf_op jit(solution)/shard_map/ppermute | solution.py:83
  33.5 0.7 collective-permute-start.16
  34.2 2.1 %collective-permute-start.17 = (bf16[128,256]{1,0:T(8,128)(2,1)S(1)}, bf16[128,256]{1,0:T(8,128)(2,1)S(1)}, u32[]{:S(2)}, u32[]{:S(2)}) collective-permute-start(bf16[128,256]{1,0:T(8,128)(2,1)S(1)} %get-tuple-element.65.refs_2_), channel_id=1, source_target_pairs={{0,4},{1,5},{2,6},{3,7},{4,0},{5,1},{6,2},{7,3},{8,12},{9,13},{10,... | collective-permute-start | bytes 196616 | tf_op jit(solution)/shard_map/ppermute | solution.py:83
  36.3 0.6 collective-permute-start.18
  36.9 2.9 %shard_map.93 = (f32[1024,256]{1,0:T(8,128)S(1)}, f32[1024,256]{1,0:T(8,128)S(1)}, f32[96,256]{1,0:T(8,128)S(1)}) custom-call(bf16[96,256]{1,0:T(8,128)(2,1)S(1)} %get-tuple-element.53.refs_0_.y_ref, f32[1024,256]{1,0:T(8,128)S(1)} %copy-done, bf16[1024,96]{1,0:T(8,128)(2,1)S(1)} %shard_map.92.refs_2_.lb_ref, ...), custom_call_target="tpu_custom_call" | custom-call | flops 1342177280 | bytes 8241152 | tf_op jit(solution)/shard_map/pallas_call | solution.py:26
  40.0 1.4 %collective-permute-start.22 = (bf16[96,256]{1,0:T(8,128)(2,1)S(1)}, bf16[96,256]{1,0:T(8,128)(2,1)S(1)}, u32[]{:S(2)}, u32[]{:S(2)}) collective-permute-start(bf16[96,256]{1,0:T(8,128)(2,1)S(1)} %shard_map.96.refs_0_), channel_id=1, source_target_pairs={{0,4},{4,0},{8,12},{12,8},{16,20},{20,16},{24,28},{28,24},{1,5},{5... | collective-permute-start | bytes 147464 | tf_op jit(solution)/shard_map/ppermute | solution.py:150
  41.4 1.4 %collective-permute-start.20 = (bf16[96,256]{1,0:T(8,128)(2,1)S(1)}, bf16[96,256]{1,0:T(8,128)(2,1)S(1)}, u32[]{:S(2)}, u32[]{:S(2)}) collective-permute-start(bf16[96,256]{1,0:T(8,128)(2,1)S(1)} %shard_map.96.refs_0_), channel_id=1, source_target_pairs={{0,2},{1,3},{2,0},{3,1},{4,6},{5,7},{6,4},{7,5},{8,10},{9,11},{10,... | collective-permute-start | bytes 147464 | tf_op jit(solution)/shard_map/ppermute | solution.py:146
  42.8 0.5 collective-permute-start.19
  43.3 0.9 %collective-permute-done.22.refs_4_ = bf16[96,256]{1,0:T(8,128)(2,1)S(1)} collective-permute-done((bf16[96,256]{1,0:T(8,128)(2,1)S(1)}, bf16[96,256]{1,0:T(8,128)(2,1)S(1)}, u32[]{:S(2)}, u32[]{:S(2)}) %collective-permute-start.22) | collective-permute-done | bytes 49184 | tf_op jit(solution)/shard_map/ppermute | solution.py:150
  44.2 0.8 %collective-permute-start.24 = (bf16[96,256]{1,0:T(8,128)(2,1)S(1)}, bf16[96,256]{1,0:T(8,128)(2,1)S(1)}, u32[]{:S(2)}, u32[]{:S(2)}) collective-permute-start(bf16[96,256]{1,0:T(8,128)(2,1)S(1)} %collective-permute-done.22.refs_4_), channel_id=1, source_target_pairs={{0,2},{1,3},{2,0},{3,1},{4,6},{5,7},{6,4},{7,5},{8,10},{9,11},{10,... | collective-permute-start | bytes 147464 | tf_op jit(solution)/shard_map/ppermute | solution.py:146
  44.9 0.5 collective-permute-done.21.refs_3_
  45.5 0.5 collective-permute-start.23
  46.0 0.6 shard_map.97.refs_10_.refs_1_.base_ref
  46.7 1.0 %collective-permute-done.25.refs_7_ = bf16[96,256]{1,0:T(8,128)(2,1)S(1)} collective-permute-done((bf16[96,256]{1,0:T(8,128)(2,1)S(1)}, bf16[96,256]{1,0:T(8,128)(2,1)S(1)}, u32[]{:S(2)}, u32[]{:S(2)}) %collective-permute-start.25) | collective-permute-done | bytes 49184 | tf_op jit(solution)/shard_map/ppermute | solution.py:146
  47.7 1.1 %collective-permute-done.24.refs_6_ = bf16[96,256]{1,0:T(8,128)(2,1)S(1)} collective-permute-done((bf16[96,256]{1,0:T(8,128)(2,1)S(1)}, bf16[96,256]{1,0:T(8,128)(2,1)S(1)}, u32[]{:S(2)}, u32[]{:S(2)}) %collective-permute-start.24) | collective-permute-done | bytes 49184 | tf_op jit(solution)/shard_map/ppermute | solution.py:146
  48.7 0.4 shard_map.98
  49.2 1.1 %collective-permute-start.26 = (bf16[96,256]{1,0:T(8,128)(2,1)S(1)}, bf16[96,256]{1,0:T(8,128)(2,1)S(1)}, u32[]{:S(2)}, u32[]{:S(2)}) collective-permute-start(bf16[96,256]{1,0:T(8,128)(2,1)S(1)} %get-tuple-element.69), channel_id=1, source_target_pairs={{0,8},{4,12},{8,0},{12,4},{16,24},{20,28},{24,16},{28,20},{1,9},{5... | collective-permute-start | bytes 147464 | tf_op jit(solution)/shard_map/ppermute | solution.py:154
  50.2 1.1 %collective-permute-start.27 = (bf16[96,256]{1,0:T(8,128)(2,1)S(1)}, bf16[96,256]{1,0:T(8,128)(2,1)S(1)}, u32[]{:S(2)}, u32[]{:S(2)}) collective-permute-start(bf16[96,256]{1,0:T(8,128)(2,1)S(1)} %get-tuple-element.70), channel_id=1, source_target_pairs={{0,16},{4,20},{8,24},{12,28},{16,0},{20,4},{24,8},{28,12},{1,17},{... | collective-permute-start | bytes 147464 | tf_op jit(solution)/shard_map/ppermute | solution.py:154
  51.3 2.3 %collective-permute-start.28 = (bf16[96,256]{1,0:T(8,128)(2,1)S(1)}, bf16[96,256]{1,0:T(8,128)(2,1)S(1)}, u32[]{:S(2)}, u32[]{:S(2)}) collective-permute-start(bf16[96,256]{1,0:T(8,128)(2,1)S(1)} %get-tuple-element.71), channel_id=1, source_target_pairs={{0,24},{4,28},{8,16},{12,20},{16,8},{20,12},{24,0},{28,4},{1,25},{... | collective-permute-start | bytes 147464 | tf_op jit(solution)/shard_map/ppermute | solution.py:154
  53.6 3.6 %collective-permute-done.27.refs_2_ = bf16[96,256]{1,0:T(8,128)(2,1)S(1)} collective-permute-done((bf16[96,256]{1,0:T(8,128)(2,1)S(1)}, bf16[96,256]{1,0:T(8,128)(2,1)S(1)}, u32[]{:S(2)}, u32[]{:S(2)}) %collective-permute-start.27) | collective-permute-done | bytes 49184 | tf_op jit(solution)/shard_map/ppermute | solution.py:154
  57.6 1.2 %collective-permute-start.30 = (bf16[128,256]{1,0:T(8,128)(2,1)S(1)}, bf16[128,256]{1,0:T(8,128)(2,1)S(1)}, u32[]{:S(2)}, u32[]{:S(2)}) collective-permute-start(bf16[128,256]{1,0:T(8,128)(2,1)S(1)} %get-tuple-element.74), channel_id=1, source_target_pairs={{0,3},{1,2},{2,1},{3,0},{4,7},{5,6},{6,5},{7,4},{8,11},{9,10},{10,... | collective-permute-start | bytes 196616 | tf_op jit(solution)/shard_map/ppermute | solution.py:83
  58.8 1.3 %collective-permute-start.31 = (bf16[128,256]{1,0:T(8,128)(2,1)S(1)}, bf16[128,256]{1,0:T(8,128)(2,1)S(1)}, u32[]{:S(2)}, u32[]{:S(2)}) collective-permute-start(bf16[128,256]{1,0:T(8,128)(2,1)S(1)} %get-tuple-element.75), channel_id=1, source_target_pairs={{0,4},{1,5},{2,6},{3,7},{4,0},{5,1},{6,2},{7,3},{8,12},{9,13},{10,... | collective-permute-start | bytes 196616 | tf_op jit(solution)/shard_map/ppermute | solution.py:83
  60.1 0.9 %collective-permute-start.32 = (bf16[128,256]{1,0:T(8,128)(2,1)S(1)}, bf16[128,256]{1,0:T(8,128)(2,1)S(1)}, u32[]{:S(2)}, u32[]{:S(2)}) collective-permute-start(bf16[128,256]{1,0:T(8,128)(2,1)S(1)} %get-tuple-element.76), channel_id=1, source_target_pairs={{0,1},{1,0},{2,3},{3,2},{4,5},{5,4},{6,7},{7,6},{8,9},{9,8},{10,11... | collective-permute-start | bytes 196616 | tf_op jit(solution)/shard_map/ppermute | solution.py:83
  61.0 0.9 %shard_map.101.base_ref = f32[512,256]{1,0:T(8,128)S(1)} custom-call(bf16[96,256]{1,0:T(8,128)(2,1)S(1)} %get-tuple-element.72.refs_0_.y_ref, f32[1024,256]{1,0:T(8,128)S(1)} %shard_map.97.refs_10_.refs_1_.base_ref, bf16[1024,96]{1,0:T(8,128)(2,1)S(1)} %shard_map.92.refs_2_.lb_ref, bf16[512,1024]{1,0:T(8,128)(2,1)S(1)} %get-tuple-element.61.si_ref, ...), custom_call_target="tpu_custom_call" | custom-call | flops 268435456 | bytes 2703360 | tf_op jit(solution)/shard_map/pallas_call | solution.py:26
  62.0 1.6 %collective-permute-done.31.refs_11_.refs_2_ = bf16[128,256]{1,0:T(8,128)(2,1)S(1)} collective-permute-done((bf16[128,256]{1,0:T(8,128)(2,1)S(1)}, bf16[128,256]{1,0:T(8,128)(2,1)S(1)}, u32[]{:S(2)}, u32[]{:S(2)}) %collective-permute-start.31) | collective-permute-done | bytes 65568 | tf_op jit(solution)/shard_map/ppermute | solution.py:83
  64.0 1.0 %collective-permute-start.34 = (bf16[128,256]{1,0:T(8,128)(2,1)S(1)}, bf16[128,256]{1,0:T(8,128)(2,1)S(1)}, u32[]{:S(2)}, u32[]{:S(2)}) collective-permute-start(bf16[128,256]{1,0:T(8,128)(2,1)S(1)} %get-tuple-element.81), channel_id=1, source_target_pairs={{0,3},{1,2},{2,1},{3,0},{4,7},{5,6},{6,5},{7,4},{8,11},{9,10},{10,... | collective-permute-start | bytes 196616 | tf_op jit(solution)/shard_map/ppermute | solution.py:83
  65.0 2.6 %collective-permute-start.35 = (bf16[128,256]{1,0:T(8,128)(2,1)S(1)}, bf16[128,256]{1,0:T(8,128)(2,1)S(1)}, u32[]{:S(2)}, u32[]{:S(2)}) collective-permute-start(bf16[128,256]{1,0:T(8,128)(2,1)S(1)} %get-tuple-element.82), channel_id=1, source_target_pairs={{0,4},{1,5},{2,6},{3,7},{4,0},{5,1},{6,2},{7,3},{8,12},{9,13},{10,... | collective-permute-start | bytes 196616 | tf_op jit(solution)/shard_map/ppermute | solution.py:83
  68.0 2.7 %shard_map.100 = (f32[1024,256]{1,0:T(8,128)}, f32[1024,256]{1,0:T(8,128)S(1)}) custom-call(bf16[96,256]{1,0:T(8,128)(2,1)S(1)} %get-tuple-element.72.refs_0_.y_ref, f32[1024,256]{1,0:T(8,128)S(1)} %shard_map.97.refs_10_.refs_1_.base_ref, bf16[1024,96]{1,0:T(8,128)(2,1)S(1)} %shard_map.92.refs_2_.lb_ref, ...), custom_call_target="tpu_custom_call" | custom-call | flops 1342177280 | bytes 9289728 | tf_op jit(solution)/shard_map/pallas_call | solution.py:26
  70.7 1.3 %shard_map.103 = f32[1024,256]{1,0:T(8,128)} custom-call(f32[1024,256]{1,0:T(8,128)S(1)} %get-tuple-element.79.res_ref, bf16[1024,512]{1,0:T(8,128)(2,1)S(1)} %get-tuple-element.46.refs_10_.wt_ref.refs_4_, bf16[128,256]{1,0:T(8,128)(2,1)S(1)} %collective-permute-done.33.refs_0_, bf16[128,256]{1,0:T(8,128)(2,1)S(1)} %collective-permute-done.34.refs_1_, ...), custom_call_target="tpu_custom_call" | custom-call | flops 268435456 | bytes 2359296 | tf_op jit(solution)/shard_map/pallas_call | solution.py:26
  (61 shorter events, 4.0 us)
Async XLA Ops:
  0.6 0.9 %copy-start.3 = (bf16[96,1024]{1,0:T(8,128)(2,1)S(1)}, bf16[96,1024]{1,0:T(8,128)(2,1)}, u32[]{:S(2)}) copy-start(bf16[96,1024]{1,0:T(8,128)(2,1)} %refs_8_.3) | copy-start | bytes 589828
  0.6 1.3 %copy-start = (f32[1024,256]{1,0:T(8,128)S(1)}, f32[1024,256]{1,0:T(8,128)}, u32[]{:S(2)}) copy-start(f32[1024,256]{1,0:T(8,128)} %refs_7_.3) | copy-start | bytes 3145732
  0.7 1.6 %copy-start.4 = (bf16[768,384]{1,0:T(8,128)(2,1)S(1)}, bf16[768,384]{1,0:T(8,128)(2,1)}, u32[]{:S(2)}) copy-start(bf16[768,384]{1,0:T(8,128)(2,1)} %inv_ref.2) | copy-start | bytes 1769476
  0.7 6.8 %copy-start.5 = (s32[1,4,128]{2,1,0:T(4,128)S(1)}, s32[1,4,128]{2,1,0:T(4,128)}, u32[]{:S(2)}) copy-start(s32[1,4,128]{2,1,0:T(4,128)} %param.13) | copy-start | bytes 6148
  0.7 10.2 %copy-start.6 = (f32[1,4,128]{2,1,0:T(4,128)S(1)}, f32[1,4,128]{2,1,0:T(4,128)}, u32[]{:S(2)}) copy-start(f32[1,4,128]{2,1,0:T(4,128)} %param.12) | copy-start | bytes 6148
  2.0 19.2 %copy-start.2 = (bf16[1024,1024]{1,0:T(8,128)(2,1)S(1)}, bf16[1024,1024]{1,0:T(8,128)(2,1)}, u32[]{:S(2)}) copy-start(bf16[1024,1024]{1,0:T(8,128)(2,1)} %refs_5_.3) | copy-start | bytes 6291460
  2.3 5.2 %collective-permute-start.3 = (bf16[96,256]{1,0:T(8,128)(2,1)S(1)}, bf16[96,256]{1,0:T(8,128)(2,1)S(1)}, u32[]{:S(2)}, u32[]{:S(2)}) collective-permute-start(bf16[96,256]{1,0:T(8,128)(2,1)S(1)} %get-tuple-element.43.token.refs_0_), channel_id=1, source_target_pairs={{0,4},{4,0},{8,12},{12,8},{16,20},{20,16},{24,28},{28,24},{1,5},{5... | collective-permute-start | bytes 147464 | tf_op jit(solution)/shard_map/ppermute | solution.py:150
  5.3 4.0 %collective-permute-start.2 = (bf16[96,256]{1,0:T(8,128)(2,1)S(1)}, bf16[96,256]{1,0:T(8,128)(2,1)S(1)}, u32[]{:S(2)}, u32[]{:S(2)}) collective-permute-start(bf16[96,256]{1,0:T(8,128)(2,1)S(1)} %get-tuple-element.43.token.refs_0_), channel_id=1, source_target_pairs={{0,3},{1,2},{2,1},{3,0},{4,7},{5,6},{6,5},{7,4},{8,11},{9,10},{10,... | collective-permute-start | bytes 147464 | tf_op jit(solution)/shard_map/ppermute | solution.py:146
  6.0 4.8 %collective-permute-start.1 = (bf16[96,256]{1,0:T(8,128)(2,1)S(1)}, bf16[96,256]{1,0:T(8,128)(2,1)S(1)}, u32[]{:S(2)}, u32[]{:S(2)}) collective-permute-start(bf16[96,256]{1,0:T(8,128)(2,1)S(1)} %get-tuple-element.43.token.refs_0_), channel_id=1, source_target_pairs={{0,2},{1,3},{2,0},{3,1},{4,6},{5,7},{6,4},{7,5},{8,10},{9,11},{10,... | collective-permute-start | bytes 147464 | tf_op jit(solution)/shard_map/ppermute | solution.py:146
  6.8 4.8 %collective-permute-start = (bf16[96,256]{1,0:T(8,128)(2,1)S(1)}, bf16[96,256]{1,0:T(8,128)(2,1)S(1)}, u32[]{:S(2)}, u32[]{:S(2)}) collective-permute-start(bf16[96,256]{1,0:T(8,128)(2,1)S(1)} %get-tuple-element.43.token.refs_0_), channel_id=1, source_target_pairs={{0,1},{1,0},{2,3},{3,2},{4,5},{5,4},{6,7},{7,6},{8,9},{9,8},{10,11... | collective-permute-start | bytes 147464 | tf_op jit(solution)/shard_map/ppermute | solution.py:146
  7.2 9.1 %collective-permute-start.7 = (bf16[384,384]{1,0:T(8,128)(2,1)S(1)}, bf16[384,384]{1,0:T(8,128)(2,1)S(1)}, u32[]{:S(2)}, u32[]{:S(2)}) collective-permute-start(bf16[384,384]{1,0:T(8,128)(2,1)S(1)} %get-tuple-element.45), channel_id=1, source_target_pairs={{0,4},{4,0},{8,12},{12,8},{16,20},{20,16},{24,28},{28,24},{1,5},{5... | collective-permute-start | bytes 884744 | tf_op jit(solution)/shard_map/ppermute | solution.py:150
  7.5 4.2 %collective-permute-start.6 = (bf16[96,256]{1,0:T(8,128)(2,1)S(1)}, bf16[96,256]{1,0:T(8,128)(2,1)S(1)}, u32[]{:S(2)}, u32[]{:S(2)}) collective-permute-start(bf16[96,256]{1,0:T(8,128)(2,1)S(1)} %collective-permute-done.3.refs_4_), channel_id=1, source_target_pairs={{0,3},{1,2},{2,1},{3,0},{4,7},{5,6},{6,5},{7,4},{8,11},{9,10},{10,... | collective-permute-start | bytes 147464 | tf_op jit(solution)/shard_map/ppermute | solution.py:146
  9.3 4.1 %collective-permute-start.5 = (bf16[96,256]{1,0:T(8,128)(2,1)S(1)}, bf16[96,256]{1,0:T(8,128)(2,1)S(1)}, u32[]{:S(2)}, u32[]{:S(2)}) collective-permute-start(bf16[96,256]{1,0:T(8,128)(2,1)S(1)} %collective-permute-done.3.refs_4_), channel_id=1, source_target_pairs={{0,2},{1,3},{2,0},{3,1},{4,6},{5,7},{6,4},{7,5},{8,10},{9,11},{10,... | collective-permute-start | bytes 147464 | tf_op jit(solution)/shard_map/ppermute | solution.py:146
  10.8 2.6 %collective-permute-start.4 = (bf16[96,256]{1,0:T(8,128)(2,1)S(1)}, bf16[96,256]{1,0:T(8,128)(2,1)S(1)}, u32[]{:S(2)}, u32[]{:S(2)}) collective-permute-start(bf16[96,256]{1,0:T(8,128)(2,1)S(1)} %collective-permute-done.3.refs_4_), channel_id=1, source_target_pairs={{0,1},{1,0},{2,3},{3,2},{4,5},{5,4},{6,7},{7,6},{8,9},{9,8},{10,11... | collective-permute-start | bytes 147464 | tf_op jit(solution)/shard_map/ppermute | solution.py:146
  16.7 6.8 %collective-permute-start.8 = (bf16[96,256]{1,0:T(8,128)(2,1)S(1)}, bf16[96,256]{1,0:T(8,128)(2,1)S(1)}, u32[]{:S(2)}, u32[]{:S(2)}) collective-permute-start(bf16[96,256]{1,0:T(8,128)(2,1)S(1)} %get-tuple-element.48), channel_id=1, source_target_pairs={{0,8},{4,12},{8,0},{12,4},{16,24},{20,28},{24,16},{28,20},{1,9},{5... | collective-permute-start | bytes 147464 | tf_op jit(solution)/shard_map/ppermute | solution.py:154
  18.4 5.5 %collective-permute-start.9 = (bf16[96,256]{1,0:T(8,128)(2,1)S(1)}, bf16[96,256]{1,0:T(8,128)(2,1)S(1)}, u32[]{:S(2)}, u32[]{:S(2)}) collective-permute-start(bf16[96,256]{1,0:T(8,128)(2,1)S(1)} %get-tuple-element.49), channel_id=1, source_target_pairs={{0,16},{4,20},{8,24},{12,28},{16,0},{20,4},{24,8},{28,12},{1,17},{... | collective-permute-start | bytes 147464 | tf_op jit(solution)/shard_map/ppermute | solution.py:154
  20.9 6.0 %collective-permute-start.10 = (bf16[96,256]{1,0:T(8,128)(2,1)S(1)}, bf16[96,256]{1,0:T(8,128)(2,1)S(1)}, u32[]{:S(2)}, u32[]{:S(2)}) collective-permute-start(bf16[96,256]{1,0:T(8,128)(2,1)S(1)} %get-tuple-element.50), channel_id=1, source_target_pairs={{0,24},{4,28},{8,16},{12,20},{16,8},{20,12},{24,0},{28,4},{1,25},{... | collective-permute-start | bytes 147464 | tf_op jit(solution)/shard_map/ppermute | solution.py:154
  21.2 7.8 %copy-start.1 = (bf16[1024,1024]{1,0:T(8,128)(2,1)S(1)}, bf16[1024,1024]{1,0:T(8,128)(2,1)}, u32[]{:S(2)}) copy-start(bf16[1024,1024]{1,0:T(8,128)(2,1)} %refs_6_.3) | copy-start | bytes 6291460
  27.2 3.6 %collective-permute-start.11 = (bf16[128,256]{1,0:T(8,128)(2,1)S(1)}, bf16[128,256]{1,0:T(8,128)(2,1)S(1)}, u32[]{:S(2)}, u32[]{:S(2)}) collective-permute-start(bf16[128,256]{1,0:T(8,128)(2,1)S(1)} %get-tuple-element.55), channel_id=1, source_target_pairs={{0,1},{1,0},{2,3},{3,2},{4,8},{5,9},{6,10},{7,11},{8,4},{9,5},{10,... | collective-permute-start | bytes 196616 | tf_op jit(solution)/shard_map/ppermute | solution.py:83
  27.3 3.8 %collective-permute-start.12 = (bf16[128,256]{1,0:T(8,128)(2,1)S(1)}, bf16[128,256]{1,0:T(8,128)(2,1)S(1)}, u32[]{:S(2)}, u32[]{:S(2)}) collective-permute-start(bf16[128,256]{1,0:T(8,128)(2,1)S(1)} %get-tuple-element.56), channel_id=1, source_target_pairs={{0,3},{1,2},{2,1},{3,0},{4,7},{5,6},{6,5},{7,4},{8,11},{9,10},{10,... | collective-permute-start | bytes 196616 | tf_op jit(solution)/shard_map/ppermute | solution.py:83
  28.8 4.3 %collective-permute-start.13 = (bf16[128,256]{1,0:T(8,128)(2,1)S(1)}, bf16[128,256]{1,0:T(8,128)(2,1)S(1)}, u32[]{:S(2)}, u32[]{:S(2)}) collective-permute-start(bf16[128,256]{1,0:T(8,128)(2,1)S(1)} %get-tuple-element.57), channel_id=1, source_target_pairs={{0,4},{1,5},{2,6},{3,7},{4,0},{5,1},{6,2},{7,3},{8,12},{9,13},{10,... | collective-permute-start | bytes 196616 | tf_op jit(solution)/shard_map/ppermute | solution.py:83
  28.8 4.3 %collective-permute-start.14 = (bf16[128,256]{1,0:T(8,128)(2,1)S(1)}, bf16[128,256]{1,0:T(8,128)(2,1)S(1)}, u32[]{:S(2)}, u32[]{:S(2)}) collective-permute-start(bf16[128,256]{1,0:T(8,128)(2,1)S(1)} %get-tuple-element.58), channel_id=1, source_target_pairs={{0,1},{1,0},{2,3},{3,2},{4,5},{5,4},{6,7},{7,6},{8,9},{9,8},{10,11... | collective-permute-start | bytes 196616 | tf_op jit(solution)/shard_map/ppermute | solution.py:83
  33.4 6.3 %collective-permute-start.15 = (bf16[128,256]{1,0:T(8,128)(2,1)S(1)}, bf16[128,256]{1,0:T(8,128)(2,1)S(1)}, u32[]{:S(2)}, u32[]{:S(2)}) collective-permute-start(bf16[128,256]{1,0:T(8,128)(2,1)S(1)} %get-tuple-element.63.refs_0_), channel_id=1, source_target_pairs={{0,1},{1,0},{2,3},{3,2},{4,8},{5,9},{6,10},{7,11},{8,4},{9,5},{10,... | collective-permute-start | bytes 196616 | tf_op jit(solution)/shard_map/ppermute | solution.py:83
  33.5 6.3 %collective-permute-start.16 = (bf16[128,256]{1,0:T(8,128)(2,1)S(1)}, bf16[128,256]{1,0:T(8,128)(2,1)S(1)}, u32[]{:S(2)}, u32[]{:S(2)}) collective-permute-start(bf16[128,256]{1,0:T(8,128)(2,1)S(1)} %get-tuple-element.64.refs_1_), channel_id=1, source_target_pairs={{0,3},{1,2},{2,1},{3,0},{4,7},{5,6},{6,5},{7,4},{8,11},{9,10},{10,... | collective-permute-start | bytes 196616 | tf_op jit(solution)/shard_map/ppermute | solution.py:83
  34.2 5.6 %collective-permute-start.17 = (bf16[128,256]{1,0:T(8,128)(2,1)S(1)}, bf16[128,256]{1,0:T(8,128)(2,1)S(1)}, u32[]{:S(2)}, u32[]{:S(2)}) collective-permute-start(bf16[128,256]{1,0:T(8,128)(2,1)S(1)} %get-tuple-element.65.refs_2_), channel_id=1, source_target_pairs={{0,4},{1,5},{2,6},{3,7},{4,0},{5,1},{6,2},{7,3},{8,12},{9,13},{10,... | collective-permute-start | bytes 196616 | tf_op jit(solution)/shard_map/ppermute | solution.py:83
  36.3 3.5 %collective-permute-start.18 = (bf16[128,256]{1,0:T(8,128)(2,1)S(1)}, bf16[128,256]{1,0:T(8,128)(2,1)S(1)}, u32[]{:S(2)}, u32[]{:S(2)}) collective-permute-start(bf16[128,256]{1,0:T(8,128)(2,1)S(1)} %get-tuple-element.66.refs_3_), channel_id=1, source_target_pairs={{0,1},{1,0},{2,3},{3,2},{4,5},{5,4},{6,7},{7,6},{8,9},{9,8},{10,11... | collective-permute-start | bytes 196616 | tf_op jit(solution)/shard_map/ppermute | solution.py:83
  40.0 4.2 %collective-permute-start.22 = (bf16[96,256]{1,0:T(8,128)(2,1)S(1)}, bf16[96,256]{1,0:T(8,128)(2,1)S(1)}, u32[]{:S(2)}, u32[]{:S(2)}) collective-permute-start(bf16[96,256]{1,0:T(8,128)(2,1)S(1)} %shard_map.96.refs_0_), channel_id=1, source_target_pairs={{0,4},{4,0},{8,12},{12,8},{16,20},{20,16},{24,28},{28,24},{1,5},{5... | collective-permute-start | bytes 147464 | tf_op jit(solution)/shard_map/ppermute | solution.py:150
  41.4 4.0 %collective-permute-start.21 = (bf16[96,256]{1,0:T(8,128)(2,1)S(1)}, bf16[96,256]{1,0:T(8,128)(2,1)S(1)}, u32[]{:S(2)}, u32[]{:S(2)}) collective-permute-start(bf16[96,256]{1,0:T(8,128)(2,1)S(1)} %shard_map.96.refs_0_), channel_id=1, source_target_pairs={{0,3},{1,2},{2,1},{3,0},{4,7},{5,6},{6,5},{7,4},{8,11},{9,10},{10,... | collective-permute-start | bytes 147464 | tf_op jit(solution)/shard_map/ppermute | solution.py:146
  41.4 5.2 %collective-permute-start.20 = (bf16[96,256]{1,0:T(8,128)(2,1)S(1)}, bf16[96,256]{1,0:T(8,128)(2,1)S(1)}, u32[]{:S(2)}, u32[]{:S(2)}) collective-permute-start(bf16[96,256]{1,0:T(8,128)(2,1)S(1)} %shard_map.96.refs_0_), channel_id=1, source_target_pairs={{0,2},{1,3},{2,0},{3,1},{4,6},{5,7},{6,4},{7,5},{8,10},{9,11},{10,... | collective-permute-start | bytes 147464 | tf_op jit(solution)/shard_map/ppermute | solution.py:146
  42.8 3.9 %collective-permute-start.19 = (bf16[96,256]{1,0:T(8,128)(2,1)S(1)}, bf16[96,256]{1,0:T(8,128)(2,1)S(1)}, u32[]{:S(2)}, u32[]{:S(2)}) collective-permute-start(bf16[96,256]{1,0:T(8,128)(2,1)S(1)} %shard_map.96.refs_0_), channel_id=1, source_target_pairs={{0,1},{1,0},{2,3},{3,2},{4,5},{5,4},{6,7},{7,6},{8,9},{9,8},{10,11... | collective-permute-start | bytes 147464 | tf_op jit(solution)/shard_map/ppermute | solution.py:146
  44.2 3.5 %collective-permute-start.25 = (bf16[96,256]{1,0:T(8,128)(2,1)S(1)}, bf16[96,256]{1,0:T(8,128)(2,1)S(1)}, u32[]{:S(2)}, u32[]{:S(2)}) collective-permute-start(bf16[96,256]{1,0:T(8,128)(2,1)S(1)} %collective-permute-done.22.refs_4_), channel_id=1, source_target_pairs={{0,3},{1,2},{2,1},{3,0},{4,7},{5,6},{6,5},{7,4},{8,11},{9,10},{10,... | collective-permute-start | bytes 147464 | tf_op jit(solution)/shard_map/ppermute | solution.py:146
  44.2 4.6 %collective-permute-start.24 = (bf16[96,256]{1,0:T(8,128)(2,1)S(1)}, bf16[96,256]{1,0:T(8,128)(2,1)S(1)}, u32[]{:S(2)}, u32[]{:S(2)}) collective-permute-start(bf16[96,256]{1,0:T(8,128)(2,1)S(1)} %collective-permute-done.22.refs_4_), channel_id=1, source_target_pairs={{0,2},{1,3},{2,0},{3,1},{4,6},{5,7},{6,4},{7,5},{8,10},{9,11},{10,... | collective-permute-start | bytes 147464 | tf_op jit(solution)/shard_map/ppermute | solution.py:146
  45.5 3.2 %collective-permute-start.23 = (bf16[96,256]{1,0:T(8,128)(2,1)S(1)}, bf16[96,256]{1,0:T(8,128)(2,1)S(1)}, u32[]{:S(2)}, u32[]{:S(2)}) collective-permute-start(bf16[96,256]{1,0:T(8,128)(2,1)S(1)} %collective-permute-done.22.refs_4_), channel_id=1, source_target_pairs={{0,1},{1,0},{2,3},{3,2},{4,5},{5,4},{6,7},{7,6},{8,9},{9,8},{10,11... | collective-permute-start | bytes 147464 | tf_op jit(solution)/shard_map/ppermute | solution.py:146
  49.2 4.5 %collective-permute-start.26 = (bf16[96,256]{1,0:T(8,128)(2,1)S(1)}, bf16[96,256]{1,0:T(8,128)(2,1)S(1)}, u32[]{:S(2)}, u32[]{:S(2)}) collective-permute-start(bf16[96,256]{1,0:T(8,128)(2,1)S(1)} %get-tuple-element.69), channel_id=1, source_target_pairs={{0,8},{4,12},{8,0},{12,4},{16,24},{20,28},{24,16},{28,20},{1,9},{5... | collective-permute-start | bytes 147464 | tf_op jit(solution)/shard_map/ppermute | solution.py:154
  50.2 7.0 %collective-permute-start.27 = (bf16[96,256]{1,0:T(8,128)(2,1)S(1)}, bf16[96,256]{1,0:T(8,128)(2,1)S(1)}, u32[]{:S(2)}, u32[]{:S(2)}) collective-permute-start(bf16[96,256]{1,0:T(8,128)(2,1)S(1)} %get-tuple-element.70), channel_id=1, source_target_pairs={{0,16},{4,20},{8,24},{12,28},{16,0},{20,4},{24,8},{28,12},{1,17},{... | collective-permute-start | bytes 147464 | tf_op jit(solution)/shard_map/ppermute | solution.py:154
  51.3 5.9 %collective-permute-start.28 = (bf16[96,256]{1,0:T(8,128)(2,1)S(1)}, bf16[96,256]{1,0:T(8,128)(2,1)S(1)}, u32[]{:S(2)}, u32[]{:S(2)}) collective-permute-start(bf16[96,256]{1,0:T(8,128)(2,1)S(1)} %get-tuple-element.71), channel_id=1, source_target_pairs={{0,24},{4,28},{8,16},{12,20},{16,8},{20,12},{24,0},{28,4},{1,25},{... | collective-permute-start | bytes 147464 | tf_op jit(solution)/shard_map/ppermute | solution.py:154
  57.5 4.5 %collective-permute-start.29 = (bf16[128,256]{1,0:T(8,128)(2,1)S(1)}, bf16[128,256]{1,0:T(8,128)(2,1)S(1)}, u32[]{:S(2)}, u32[]{:S(2)}) collective-permute-start(bf16[128,256]{1,0:T(8,128)(2,1)S(1)} %get-tuple-element.73), channel_id=1, source_target_pairs={{0,1},{1,0},{2,3},{3,2},{4,8},{5,9},{6,10},{7,11},{8,4},{9,5},{10,... | collective-permute-start | bytes 196616 | tf_op jit(solution)/shard_map/ppermute | solution.py:83
  57.6 4.4 %collective-permute-start.30 = (bf16[128,256]{1,0:T(8,128)(2,1)S(1)}, bf16[128,256]{1,0:T(8,128)(2,1)S(1)}, u32[]{:S(2)}, u32[]{:S(2)}) collective-permute-start(bf16[128,256]{1,0:T(8,128)(2,1)S(1)} %get-tuple-element.74), channel_id=1, source_target_pairs={{0,3},{1,2},{2,1},{3,0},{4,7},{5,6},{6,5},{7,4},{8,11},{9,10},{10,... | collective-permute-start | bytes 196616 | tf_op jit(solution)/shard_map/ppermute | solution.py:83
  58.8 4.8 %collective-permute-start.31 = (bf16[128,256]{1,0:T(8,128)(2,1)S(1)}, bf16[128,256]{1,0:T(8,128)(2,1)S(1)}, u32[]{:S(2)}, u32[]{:S(2)}) collective-permute-start(bf16[128,256]{1,0:T(8,128)(2,1)S(1)} %get-tuple-element.75), channel_id=1, source_target_pairs={{0,4},{1,5},{2,6},{3,7},{4,0},{5,1},{6,2},{7,3},{8,12},{9,13},{10,... | collective-permute-start | bytes 196616 | tf_op jit(solution)/shard_map/ppermute | solution.py:83
  60.1 3.5 %collective-permute-start.32 = (bf16[128,256]{1,0:T(8,128)(2,1)S(1)}, bf16[128,256]{1,0:T(8,128)(2,1)S(1)}, u32[]{:S(2)}, u32[]{:S(2)}) collective-permute-start(bf16[128,256]{1,0:T(8,128)(2,1)S(1)} %get-tuple-element.76), channel_id=1, source_target_pairs={{0,1},{1,0},{2,3},{3,2},{4,5},{5,4},{6,7},{7,6},{8,9},{9,8},{10,11... | collective-permute-start | bytes 196616 | tf_op jit(solution)/shard_map/ppermute | solution.py:83
  63.9 6.8 %collective-permute-start.33 = (bf16[128,256]{1,0:T(8,128)(2,1)S(1)}, bf16[128,256]{1,0:T(8,128)(2,1)S(1)}, u32[]{:S(2)}, u32[]{:S(2)}) collective-permute-start(bf16[128,256]{1,0:T(8,128)(2,1)S(1)} %get-tuple-element.80), channel_id=1, source_target_pairs={{0,1},{1,0},{2,3},{3,2},{4,8},{5,9},{6,10},{7,11},{8,4},{9,5},{10,... | collective-permute-start | bytes 196616 | tf_op jit(solution)/shard_map/ppermute | solution.py:83
  64.0 6.7 %collective-permute-start.34 = (bf16[128,256]{1,0:T(8,128)(2,1)S(1)}, bf16[128,256]{1,0:T(8,128)(2,1)S(1)}, u32[]{:S(2)}, u32[]{:S(2)}) collective-permute-start(bf16[128,256]{1,0:T(8,128)(2,1)S(1)} %get-tuple-element.81), channel_id=1, source_target_pairs={{0,3},{1,2},{2,1},{3,0},{4,7},{5,6},{6,5},{7,4},{8,11},{9,10},{10,... | collective-permute-start | bytes 196616 | tf_op jit(solution)/shard_map/ppermute | solution.py:83
  65.0 5.7 %collective-permute-start.35 = (bf16[128,256]{1,0:T(8,128)(2,1)S(1)}, bf16[128,256]{1,0:T(8,128)(2,1)S(1)}, u32[]{:S(2)}, u32[]{:S(2)}) collective-permute-start(bf16[128,256]{1,0:T(8,128)(2,1)S(1)} %get-tuple-element.82), channel_id=1, source_target_pairs={{0,4},{1,5},{2,6},{3,7},{4,0},{5,1},{6,2},{7,3},{8,12},{9,13},{10,... | collective-permute-start | bytes 196616 | tf_op jit(solution)/shard_map/ppermute | solution.py:83
  67.6 3.2 %collective-permute-start.36 = (bf16[128,256]{1,0:T(8,128)(2,1)S(1)}, bf16[128,256]{1,0:T(8,128)(2,1)S(1)}, u32[]{:S(2)}, u32[]{:S(2)}) collective-permute-start(bf16[128,256]{1,0:T(8,128)(2,1)S(1)} %get-tuple-element.83), channel_id=1, source_target_pairs={{0,1},{1,0},{2,3},{3,2},{4,5},{5,4},{6,7},{7,6},{8,9},{9,8},{10,11... | collective-permute-start | bytes 196616 | tf_op jit(solution)/shard_map/ppermute | solution.py:83

commit v6 on v5

--- a/solution.py
+++ b/solution.py
@@ -80,9 +80,13 @@
         ]
 
     def halo(faces):
-        return [lax.ppermute(f, both, p) for f, p in zip(faces, slot_perms)]
-
-    def k_select(table_ref, token, sel_ref, wt_ref):
+        out = []
+        for f, p in zip(faces, slot_perms):
+            out.append(lax.ppermute(f, both, p))
+        return out
+
+    def k_select(table_ref, basis_ref, token, sel_ref, wt_ref, bt_ref):
+        bt_ref[...] = basis_ref[...].astype(F32).T.astype(BF)
         for s, (k, ok) in enumerate(slot_faces()):
             row = table_ref[pl.ds(k, 1), :].astype(jnp.int32)
             w = table_ref[pl.ds(4 + k, 1), :] * ok
@@ -94,11 +98,8 @@
                 across = lax.broadcasted_iota(jnp.int32, (ovl, ovl), 1) + j * ovl
                 sel_ref[at, pl.ds(j * ovl, ovl)] = jnp.where(idx == across.astype(F32), 1.0, 0.0).astype(BF)
 
-    def k_products(sel_ref, wt_ref, inv_ref, basis_ref, token, bf_ref, t_ref, si_ref, f_ref, bt_ref):
-        bt = basis_ref[...].astype(F32).T.astype(BF)
-        bt_ref[...] = bt
-        bf_ref[...] = mm(sel_ref[...], bt).astype(BF)
-        t_ref[...] = mm(basis_ref[...], wt_ref[...]).astype(BF)
+    def k_products(sel_ref, wt_ref, inv_ref, bt_ref, token, bf_ref, si_ref, f_ref):
+        bf_ref[...] = mm(sel_ref[...], bt_ref[...]).astype(BF)
         fstep = tiles(nf)
 
         @pl.loop(0, nf // fstep)
@@ -112,6 +113,11 @@
             lb_ref[at, :] = mm(mat_ref[at, :], bt_ref[...]).astype(BF)
 
         row_loop(tile)
+
+    def k_restrictors(basis_ref, mat_ref, wt_ref, rhs_ref, token, z_ref, t_ref, brhs_ref):
+        z_ref[...] = mm(basis_ref[...], mat_ref[...]).astype(BF)
+        t_ref[...] = mm(basis_ref[...], wt_ref[...]).astype(BF)
+        brhs_ref[...] = mm(basis_ref[...], rhs_ref[...].astype(BF))
 
     half = nz * cpd
 
@@ -150,9 +156,10 @@
         return lax.ppermute(value, "row", [(i, i ^ 1) for i in range(nr)])
 
     def reduce_rows(own, sends):
-        return [own] + [
-            lax.ppermute(s, "row", [(i, i ^ (2 * (k + 1))) for i in range(nr)]) for k, s in enumerate(sends)
-        ]
+        out = [own]
+        for k, block in enumerate(sends):
+            out.append(lax.ppermute(block, "row", [(i, i ^ (2 * (k + 1))) for i in range(nr)]))
+        return out
 
     own_and_sends = [((cpd, nrhs), F32)] + [((cpd, nrhs), BF)] * (nz - 1)
 
@@ -201,15 +208,11 @@
         return call(k_faces, [((ovl, nrhs), BF)] * 4, base, fmat, *recv, flops=2 * nf * nf * nrhs)
 
     def k_advance(first, last, *refs):
-        y_ref, base_ref, lb_ref, bt_ref, wt_ref, inv_ref, mat_ref, rhs_ref, basis_ref = refs[:9]
-        recvs, refs = refs[9:13], refs[13:]
+        y_ref, base_ref, lb_ref, bt_ref, wt_ref, inv_ref, left_ref, right_ref = refs[:8]
+        recvs, refs = refs[8:12], refs[12:]
         old_ref, refs = (None, refs) if first else (refs[0], refs[1:])
-        out_ref, res_ref = refs[:2]
-        if last:
-            wb, vb, recv, new_ref, sem = refs[2:]
-        else:
-            restr_ref, wb, vb, recv = refs[2:]
-            new_ref = out_ref
+        out_ref, res_ref, wb, vb, recv = refs[:5]
+        new_ref, sem = refs[5:] if last else (out_ref, None)
         y = y_ref[...]
         for s, x in enumerate(recvs):
             recv[pl.ds(s * ovl, ovl), :] = x[...]
@@ -231,22 +234,21 @@
             store = pltpu.make_async_copy(new_ref, out_ref, sem)
             store.start()
 
-        def res_tile(at):
-            res_ref[at, :] = rhs_ref[at, :] - mm(mat_ref[at, :], vb[...])
-
-        row_loop(res_tile)
-        if last:
+            def res_tile(at):
+                res_ref[at, :] = left_ref[at, :] - mm(right_ref[at, :], vb[...])
+
+            row_loop(res_tile)
             store.wait()
         else:
-            restr_ref[...] = mm(basis_ref[...], res_ref[...].astype(BF))
-
-    def advance(y, base, recv, old, last):
+            res_ref[...] = left_ref[...] - mm(right_ref[...], vb[...])
+
+    def advance(y, base, recv, old, last, left, right):
         first = old is None
-        outs = [((nloc, nrhs), F32)] * 2 + ([] if last else [((cpd, nrhs), F32)])
+        outs = [((nloc, nrhs), F32), (left.shape, F32)]
         extra = [pltpu.VMEM((nloc, nrhs), F32), pltpu.SemaphoreType.DMA] if last else []
         return call(
             functools.partial(k_advance, first, last), outs,
-            y, base, lbmat, btmat, wt, local_inv, local_mat, rhs, basis_t, *recv, *([] if first else [old]),
+            y, base, lbmat, btmat, wt, local_inv, left, right, *recv, *([] if first else [old]),
             scratch=[pltpu.VMEM((nloc, nrhs), BF)] * 2 + [pltpu.VMEM((nf, nrhs), BF)] + extra,
             hbm_outs=1 if last else 0, flops=5 * nloc * nloc * nrhs,
         )
@@ -256,15 +258,23 @@
         recv = jnp.concatenate([x[...] for x in recvs], axis=0)
         out_ref[...] = (base_ref[...] + mm(t_ref[...], recv)).astype(BF)
 
-    def k_couple(res_ref, wt_ref, *refs):
-        recvs, out_ref, recv = refs[:4], refs[4], refs[5]
+    def k_residual(sol_ref, mat_ref, rhs_ref, wt_ref, *refs):
+        recvs, out_ref, recv, vb = refs[:4], refs[4], refs[5], refs[6]
         for s, x in enumerate(recvs):
             recv[pl.ds(s * ovl, ovl), :] = x[...]
+        vb[...] = sol_ref[...].astype(BF)
 
         def tile(at):
-            out_ref[at, :] = res_ref[at, :] + mm(wt_ref[at, :], recv[...])
+            out_ref[at, :] = rhs_ref[at, :] - mm(mat_ref[at, :], vb[...]) + mm(wt_ref[at, :], recv[...])
 
         row_loop(tile)
+
+    def residual_of(sol, recv):
+        return call(
+            k_residual, [((nloc, nrhs), F32)], sol, local_mat, rhs, wt, *recv,
+            scratch=[pltpu.VMEM((nf, nrhs), BF), pltpu.VMEM((nloc, nrhs), BF)],
+            flops=2 * nloc * (nloc + nf) * nrhs,
+        )[0]
 
     def k_couple_last(res_ref, wt_ref, *refs):
         recvs, (out_ref, recv, buf, sems) = refs[:4], refs[4:]
@@ -279,12 +289,14 @@
         for copy in copies:
             copy.wait()
 
-    def coupled(res, recv, last):
-        extra = [pltpu.VMEM((nloc, nrhs), F32), pltpu.SemaphoreType.DMA((nloc // last_step,))] if last else []
+    def coupled(res, recv):
         return call(
-            k_couple_last if last else k_couple, [((nloc, nrhs), F32)], res, wt, *recv,
-            scratch=[pltpu.VMEM((nf, nrhs), BF)] + extra, hbm_outs=1 if last else 0,
-            flops=2 * nloc * nf * nrhs,
+            k_couple_last, [((nloc, nrhs), F32)], res, wt, *recv,
+            scratch=[
+                pltpu.VMEM((nf, nrhs), BF), pltpu.VMEM((nloc, nrhs), F32),
+                pltpu.SemaphoreType.DMA((nloc // last_step,)),
+            ],
+            hbm_outs=1, flops=2 * nloc * nf * nrhs,
         )[0]
 
     def coarse_pair(mine, across, token):
@@ -304,29 +316,37 @@
     other = over_pair(cross)
     mine = over_col(restricted)
     table = jnp.concatenate([margin_rows[0].astype(F32), couple[0]], axis=0)
-    sel, wt = call(k_select, [((nf, nloc), BF), ((nloc, nf), BF)], table, restricted, tokens=1)
-    own, *sends = coarse_pair(mine, across, wt)
-    bfac, tmat, simat, fmat, btmat = call(
-        k_products,
-        [((nf, cpd), BF), ((cpd, nf), BF), ((nf, nloc), BF), ((nf, nf), BF), ((nloc, cpd), BF)],
-        sel, wt, local_inv, basis_t, own, tokens=1, flops=2 * nf * nloc * (nloc + nf + 2 * cpd),
+    sel, wt, btmat = call(
+        k_select, [((nf, nloc), BF), ((nloc, nf), BF), ((nloc, cpd), BF)], table, basis_t, restricted,
+        tokens=1,
     )
     (lbmat,) = call(
-        k_mat_basis, [((nloc, cpd), BF)], local_mat, btmat, own, tokens=1,
+        k_mat_basis, [((nloc, cpd), BF)], local_mat, btmat, wt, tokens=1,
         flops=2 * nloc * nloc * cpd,
+    )
+    own, *sends = coarse_pair(mine, across, lbmat)
+    bfac, simat, fmat = call(
+        k_products, [((nf, cpd), BF), ((nf, nloc), BF), ((nf, nf), BF)],
+        sel, wt, local_inv, btmat, own, tokens=1, flops=2 * nf * nloc * (nloc + nf + cpd),
     )
     residual, solution, sent = rhs, None, []
     for sweep in range(STEPS):
         y, faces = coarse_faces(reduce_rows(own, sends))
         recv = halo(faces)
+        if sweep == 0:
+            zmat, tmat, brhs = call(
+                k_restrictors, [((cpd, nloc), BF), ((cpd, nf), BF), ((cpd, nrhs), F32)],
+                basis_t, local_mat, wt, rhs, y, tokens=1, flops=2 * cpd * nloc * (nloc + nf + nrhs),
+            )
         sent = faces_after(local(y, residual, sent), recv)
         recv2 = halo(sent)
-        last = sweep == STEPS - 1
-        new = advance(y, residual, recv, solution, last)
-        solution, res = new[:2]
-        residual = coupled(res, recv2, last)
-        if not last:
-            (restricted,) = call(k_restrict_recv, [((cpd, nrhs), BF)], new[2], tmat, *recv2)
+        if sweep == STEPS - 1:
+            solution, res = advance(y, residual, recv, solution, True, rhs, local_mat)
+            residual = coupled(res, recv2)
+        else:
+            solution, restr = advance(y, residual, recv, solution, False, brhs, zmat)
+            (restricted,) = call(k_restrict_recv, [((cpd, nrhs), BF)], restr, tmat, *recv2)
+            residual = residual_of(solution, recv2)
             own, *sends = coarse_pair(over_col(restricted), over_pair(restricted), residual)
     return (solution, residual)
 

time: 72.2 us -> 72.7 us (level)
  starting transfers between devices: 34.1 us -> 38.8 us
  waiting for transfers between devices: 19.9 us -> 15.4 us
    ppermute x22, starting transfers between devices: 21.7 us -> 25.4 us  [the longest x16 16.4 us: halo(): out.append(lax.ppermute(f, both, p))]
    ppermute x22, waiting for transfers between devices: 11.1 us -> 8.55 us  [the longest x6 6.41 us: reduce_rows(): lax.ppermute(block, 'row', [(i, i ^ 2 * (k + 1)) for i in range(nr)])]
    ppermute x12, waiting for transfers between devices: 5.15 us -> 3.04 us  [over_col(): lax.ppermute(block, 'col', [(i, i ^ k) for i in range(nc)])]
    pallas_call x18 -> x19, Pallas kernels: 15.5 us -> 15.8 us  [call(): pl.pallas_call(kernel, out_shape=[jax.ShapeDtypeStruct(s, d) for s, d in...]
  transfers between devices with their start and end apart: 37 -> 37, of which waited for: 13 -> 12; matrix products, arithmetic and copies ran while one was open for 0% -> 0% of each run, Pallas kernels for 17% -> 17%
where the time goes in v6:
time: 72.7 us; the launch traced here: 72.6 us
  starting transfers between devices  38.8 us (53%)
  Pallas kernels  15.8 us (22%)
  waiting for transfers between devices  15.4 us (21%)
  local copies, waits for them, and re-layouts  1.31 us (2%)
  between operations  1.03 us (1%)
    ppermute x16, starting transfers between devices, halo(): out.append(lax.ppermute(f, both, p))  16.4 us
    pallas_call x19, Pallas kernels, call(): pl.pallas_call(kernel, out_shape=[jax.ShapeDtypeStruct(s, d) for s, d in...  15.8 us
    ppermute x6, starting transfers between devices, reduce_rows(): lax.ppermute(block, 'row', [(i, i ^ 2 * (k + 1)) for i in range(nr)])  9.02 us
    ppermute x12, starting transfers between devices, over_col(): lax.ppermute(block, 'col', [(i, i ^ k) for i in range(nc)])  8.27 us
    ppermute x6, waiting for transfers between devices, reduce_rows(): lax.ppermute(block, 'row', [(i, i ^ 2 * (k + 1)) for i in range(nr)])  6.41 us
    ppermute x3, starting transfers between devices, over_pair(): return lax.ppermute(value, 'row', [(i, i ^ 1) for i in range(nr)])  5.14 us
    ppermute x3, waiting for transfers between devices, over_pair(): return lax.ppermute(value, 'row', [(i, i ^ 1) for i in range(nr)])  3.83 us
    ppermute x12, waiting for transfers between devices, over_col(): lax.ppermute(block, 'col', [(i, i ^ k) for i in range(nc)])  3.04 us
  transfers between devices with their start and end apart: 37, of which 12 were waited for; matrix products, arithmetic and copies ran while one was open for 0% of the time, Pallas kernels for 17%

profile of v6, /device:TPU:0, one launch (start us, length us, event | category | flops | bytes accessed | tf_op | source)
XLA Modules:
  0.0 72.6 jit_solution(2037260755770915662)
XLA Ops:
  0.7 0.9 %copy-done.3 = bf16[96,1024]{1,0:T(8,128)(2,1)S(1)} copy-done((bf16[96,1024]{1,0:T(8,128)(2,1)S(1)}, bf16[96,1024]{1,0:T(8,128)(2,1)}, u32[]{:S(2)}) %copy-start.3) | copy-done | bytes 196632
  2.3 3.1 %collective-permute-start.3 = (bf16[96,256]{1,0:T(8,128)(2,1)S(1)}, bf16[96,256]{1,0:T(8,128)(2,1)S(1)}, u32[]{:S(2)}, u32[]{:S(2)}) collective-permute-start(bf16[96,256]{1,0:T(8,128)(2,1)S(1)} %get-tuple-element.44.token.refs_0_), channel_id=1, source_target_pairs={{0,4},{4,0},{8,12},{12,8},{16,20},{20,16},{24,28},{28,24},{1,5},{5... | collective-permute-start | bytes 147464 | tf_op jit(solution)/shard_map/ppermute | solution.py:156
  5.3 1.5 %collective-permute-start.1 = (bf16[96,256]{1,0:T(8,128)(2,1)S(1)}, bf16[96,256]{1,0:T(8,128)(2,1)S(1)}, u32[]{:S(2)}, u32[]{:S(2)}) collective-permute-start(bf16[96,256]{1,0:T(8,128)(2,1)S(1)} %get-tuple-element.44.token.refs_0_), channel_id=1, source_target_pairs={{0,2},{1,3},{2,0},{3,1},{4,6},{5,7},{6,4},{7,5},{8,10},{9,11},{10,... | collective-permute-start | bytes 147464 | tf_op jit(solution)/shard_map/ppermute | solution.py:152
  7.6 1.8 %collective-permute-start.5 = (bf16[96,256]{1,0:T(8,128)(2,1)S(1)}, bf16[96,256]{1,0:T(8,128)(2,1)S(1)}, u32[]{:S(2)}, u32[]{:S(2)}) collective-permute-start(bf16[96,256]{1,0:T(8,128)(2,1)S(1)} %collective-permute-done.3.refs_4_), channel_id=1, source_target_pairs={{0,2},{1,3},{2,0},{3,1},{4,6},{5,7},{6,4},{7,5},{8,10},{9,11},{10,... | collective-permute-start | bytes 147464 | tf_op jit(solution)/shard_map/ppermute | solution.py:152
  9.5 0.7 %collective-permute-start.6 = (bf16[96,256]{1,0:T(8,128)(2,1)S(1)}, bf16[96,256]{1,0:T(8,128)(2,1)S(1)}, u32[]{:S(2)}, u32[]{:S(2)}) collective-permute-start(bf16[96,256]{1,0:T(8,128)(2,1)S(1)} %collective-permute-done.3.refs_4_), channel_id=1, source_target_pairs={{0,3},{1,2},{2,1},{3,0},{4,7},{5,6},{6,5},{7,4},{8,11},{9,10},{10,... | collective-permute-start | bytes 147464 | tf_op jit(solution)/shard_map/ppermute | solution.py:152
  10.3 0.8 %shard_map.88 = (bf16[512,1024]{1,0:T(8,128)(2,1)S(1)}, bf16[1024,512]{1,0:T(8,128)(2,1)S(1)}, bf16[1024,96]{1,0:T(8,128)(2,1)S(1)}) custom-call(f32[8,128]{1,0:T(8,128)S(1)} %pad_maximum_fusion.table_ref, bf16[96,1024]{1,0:T(8,128)(2,1)S(1)} %copy-done.3, bf16[96,256]{1,0:T(8,128)(2,1)S(1)} %get-tuple-element.44.token.refs_0_), custom_call_target="tpu_custom_call" | custom-call | bytes 249856 | tf_op jit(solution)/shard_map/pallas_call | solution.py:26
  11.1 0.9 %shard_map.89.refs_10_.refs_2_.lb_ref = bf16[1024,96]{1,0:T(8,128)(2,1)S(1)} custom-call(bf16[1024,1024]{1,0:T(8,128)(2,1)S(1)} %copy-done.1, bf16[1024,96]{1,0:T(8,128)(2,1)S(1)} %get-tuple-element.47.bt_ref.refs_3_, bf16[1024,512]{1,0:T(8,128)(2,1)S(1)} %get-tuple-element.48.token.wt_ref.refs_4_), custom_call_target="tpu_custom_call" | custom-call | flops 201326592 | bytes 3342336 | tf_op jit(solution)/shard_map/pallas_call | solution.py:26
  12.0 1.0 %collective-permute-done.6.refs_7_ = bf16[96,256]{1,0:T(8,128)(2,1)S(1)} collective-permute-done((bf16[96,256]{1,0:T(8,128)(2,1)S(1)}, bf16[96,256]{1,0:T(8,128)(2,1)S(1)}, u32[]{:S(2)}, u32[]{:S(2)}) %collective-permute-start.6) | collective-permute-done | bytes 49184 | tf_op jit(solution)/shard_map/ppermute | solution.py:152
  13.0 3.4 %collective-permute-done.7.refs_9_ = bf16[384,384]{1,0:T(8,128)(2,1)S(1)} collective-permute-done((bf16[384,384]{1,0:T(8,128)(2,1)S(1)}, bf16[384,384]{1,0:T(8,128)(2,1)S(1)}, u32[]{:S(2)}, u32[]{:S(2)}) %collective-permute-start.7) | collective-permute-done | bytes 294944 | tf_op jit(solution)/shard_map/ppermute | solution.py:156
  16.4 0.4 shard_map.90
  16.9 3.7 %collective-permute-start.10 = (bf16[96,256]{1,0:T(8,128)(2,1)S(1)}, bf16[96,256]{1,0:T(8,128)(2,1)S(1)}, u32[]{:S(2)}, u32[]{:S(2)}) collective-permute-start(bf16[96,256]{1,0:T(8,128)(2,1)S(1)} %get-tuple-element.52), channel_id=1, source_target_pairs={{0,24},{4,28},{8,16},{12,20},{16,8},{20,12},{24,0},{28,4},{1,25},{... | collective-permute-start | bytes 147464 | tf_op jit(solution)/shard_map/ppermute | solution.py:161
  20.5 0.8 %collective-permute-start.9 = (bf16[96,256]{1,0:T(8,128)(2,1)S(1)}, bf16[96,256]{1,0:T(8,128)(2,1)S(1)}, u32[]{:S(2)}, u32[]{:S(2)}) collective-permute-start(bf16[96,256]{1,0:T(8,128)(2,1)S(1)} %get-tuple-element.51), channel_id=1, source_target_pairs={{0,16},{4,20},{8,24},{12,28},{16,0},{20,4},{24,8},{28,12},{1,17},{... | collective-permute-start | bytes 147464 | tf_op jit(solution)/shard_map/ppermute | solution.py:161
  21.3 2.1 %shard_map.91 = (bf16[512,96]{1,0:T(8,128)(2,1)S(1)}, bf16[512,1024]{1,0:T(8,128)(2,1)S(1)}, bf16[512,512]{1,0:T(8,128)(2,1)S(1)}) custom-call(bf16[512,1024]{1,0:T(8,128)(2,1)S(1)} %get-tuple-element.53.sel_ref, bf16[1024,512]{1,0:T(8,128)(2,1)S(1)} %get-tuple-element.48.token.wt_ref.refs_4_, bf16[1024,1024]{1,0:T(8,128)(2,1)S(1)} %copy-done.2, ...), custom_call_target="tpu_custom_call" | custom-call | flops 1711276032 | bytes 4489216 | tf_op jit(solution)/shard_map/pallas_call | solution.py:26
  23.4 1.2 %collective-permute-done.8.refs_1_ = bf16[96,256]{1,0:T(8,128)(2,1)S(1)} collective-permute-done((bf16[96,256]{1,0:T(8,128)(2,1)S(1)}, bf16[96,256]{1,0:T(8,128)(2,1)S(1)}, u32[]{:S(2)}, u32[]{:S(2)}) %collective-permute-start.8) | collective-permute-done | bytes 49184 | tf_op jit(solution)/shard_map/ppermute | solution.py:161
  24.6 0.9 %collective-permute-done.9.refs_2_ = bf16[96,256]{1,0:T(8,128)(2,1)S(1)} collective-permute-done((bf16[96,256]{1,0:T(8,128)(2,1)S(1)}, bf16[96,256]{1,0:T(8,128)(2,1)S(1)}, u32[]{:S(2)}, u32[]{:S(2)}) %collective-permute-start.9) | collective-permute-done | bytes 49184 | tf_op jit(solution)/shard_map/ppermute | solution.py:161
  25.8 1.6 %collective-permute-start.12 = (bf16[128,256]{1,0:T(8,128)(2,1)S(1)}, bf16[128,256]{1,0:T(8,128)(2,1)S(1)}, u32[]{:S(2)}, u32[]{:S(2)}) collective-permute-start(bf16[128,256]{1,0:T(8,128)(2,1)S(1)} %get-tuple-element.59), channel_id=1, source_target_pairs={{0,3},{1,2},{2,1},{3,0},{4,7},{5,6},{6,5},{7,4},{8,11},{9,10},{10,... | collective-permute-start | bytes 196616 | tf_op jit(solution)/shard_map/ppermute | solution.py:85
  27.4 1.9 %collective-permute-start.13 = (bf16[128,256]{1,0:T(8,128)(2,1)S(1)}, bf16[128,256]{1,0:T(8,128)(2,1)S(1)}, u32[]{:S(2)}, u32[]{:S(2)}) collective-permute-start(bf16[128,256]{1,0:T(8,128)(2,1)S(1)} %get-tuple-element.60), channel_id=1, source_target_pairs={{0,4},{1,5},{2,6},{3,7},{4,0},{5,1},{6,2},{7,3},{8,12},{9,13},{10,... | collective-permute-start | bytes 196616 | tf_op jit(solution)/shard_map/ppermute | solution.py:85
  29.3 1.3 %collective-permute-start.14 = (bf16[128,256]{1,0:T(8,128)(2,1)S(1)}, bf16[128,256]{1,0:T(8,128)(2,1)S(1)}, u32[]{:S(2)}, u32[]{:S(2)}) collective-permute-start(bf16[128,256]{1,0:T(8,128)(2,1)S(1)} %get-tuple-element.61), channel_id=1, source_target_pairs={{0,1},{1,0},{2,3},{3,2},{4,5},{5,4},{6,7},{7,6},{8,9},{9,8},{10,11... | collective-permute-start | bytes 196616 | tf_op jit(solution)/shard_map/ppermute | solution.py:85
  30.6 0.9 %shard_map.95.base_ref = f32[512,256]{1,0:T(8,128)S(1)} custom-call(bf16[96,256]{1,0:T(8,128)(2,1)S(1)} %get-tuple-element.55.token.refs_0_.y_ref, f32[1024,256]{1,0:T(8,128)S(1)} %copy-done, bf16[1024,96]{1,0:T(8,128)(2,1)S(1)} %shard_map.89.refs_10_.refs_2_.lb_ref, bf16[512,1024]{1,0:T(8,128)(2,1)S(1)} %get-tuple-element.64.si_ref, ...), custom_call_target="tpu_custom_call" | custom-call | flops 268435456 | bytes 2441216 | tf_op jit(solution)/shard_map/pallas_call | solution.py:26
  31.6 0.7 shard_map.93
  32.7 1.5 %collective-permute-start.16 = (bf16[128,256]{1,0:T(8,128)(2,1)S(1)}, bf16[128,256]{1,0:T(8,128)(2,1)S(1)}, u32[]{:S(2)}, u32[]{:S(2)}) collective-permute-start(bf16[128,256]{1,0:T(8,128)(2,1)S(1)} %get-tuple-element.67.refs_1_), channel_id=1, source_target_pairs={{0,3},{1,2},{2,1},{3,0},{4,7},{5,6},{6,5},{7,4},{8,11},{9,10},{10,... | collective-permute-start | bytes 196616 | tf_op jit(solution)/shard_map/ppermute | solution.py:85
  34.2 1.1 %collective-permute-start.17 = (bf16[128,256]{1,0:T(8,128)(2,1)S(1)}, bf16[128,256]{1,0:T(8,128)(2,1)S(1)}, u32[]{:S(2)}, u32[]{:S(2)}) collective-permute-start(bf16[128,256]{1,0:T(8,128)(2,1)S(1)} %get-tuple-element.68.refs_2_), channel_id=1, source_target_pairs={{0,4},{1,5},{2,6},{3,7},{4,0},{5,1},{6,2},{7,3},{8,12},{9,13},{10,... | collective-permute-start | bytes 196616 | tf_op jit(solution)/shard_map/ppermute | solution.py:85
  35.3 1.1 %collective-permute-start.18 = (bf16[128,256]{1,0:T(8,128)(2,1)S(1)}, bf16[128,256]{1,0:T(8,128)(2,1)S(1)}, u32[]{:S(2)}, u32[]{:S(2)}) collective-permute-start(bf16[128,256]{1,0:T(8,128)(2,1)S(1)} %get-tuple-element.69.refs_3_), channel_id=1, source_target_pairs={{0,1},{1,0},{2,3},{3,2},{4,5},{5,4},{6,7},{7,6},{8,9},{9,8},{10,11... | collective-permute-start | bytes 196616 | tf_op jit(solution)/shard_map/ppermute | solution.py:85
  36.4 2.0 %shard_map.94 = (f32[1024,256]{1,0:T(8,128)S(1)}, f32[96,256]{1,0:T(8,128)S(1)}) custom-call(bf16[96,256]{1,0:T(8,128)(2,1)S(1)} %get-tuple-element.55.token.refs_0_.y_ref, f32[1024,256]{1,0:T(8,128)S(1)} %copy-done, bf16[1024,96]{1,0:T(8,128)(2,1)S(1)} %shard_map.89.refs_10_.refs_2_.lb_ref, bf16[1024,96]{1,0:T(8,128)(2,1)S(1)} %get-tuple-element.47.bt_ref.refs_3_, ...), custom_call_target="tpu_custom_call" | custom-call | flops 1342177280 | bytes 5193728 | tf_op jit(solution)/shard_map/pallas_call | solution.py:26
  38.4 0.5 collective-permute-done.17.refs_2_
  39.1 1.8 %collective-permute-start.22 = (bf16[96,256]{1,0:T(8,128)(2,1)S(1)}, bf16[96,256]{1,0:T(8,128)(2,1)S(1)}, u32[]{:S(2)}, u32[]{:S(2)}) collective-permute-start(bf16[96,256]{1,0:T(8,128)(2,1)S(1)} %shard_map.97.refs_0_), channel_id=1, source_target_pairs={{0,4},{4,0},{8,12},{12,8},{16,20},{20,16},{24,28},{28,24},{1,5},{5... | collective-permute-start | bytes 147464 | tf_op jit(solution)/shard_map/ppermute | solution.py:156
  41.0 1.2 %collective-permute-start.20 = (bf16[96,256]{1,0:T(8,128)(2,1)S(1)}, bf16[96,256]{1,0:T(8,128)(2,1)S(1)}, u32[]{:S(2)}, u32[]{:S(2)}) collective-permute-start(bf16[96,256]{1,0:T(8,128)(2,1)S(1)} %shard_map.97.refs_0_), channel_id=1, source_target_pairs={{0,2},{1,3},{2,0},{3,1},{4,6},{5,7},{6,4},{7,5},{8,10},{9,11},{10,... | collective-permute-start | bytes 147464 | tf_op jit(solution)/shard_map/ppermute | solution.py:152
  42.1 0.7 collective-permute-start.21
  42.8 0.5 collective-permute-done.22.refs_4_
  43.3 1.0 %collective-permute-start.24 = (bf16[96,256]{1,0:T(8,128)(2,1)S(1)}, bf16[96,256]{1,0:T(8,128)(2,1)S(1)}, u32[]{:S(2)}, u32[]{:S(2)}) collective-permute-start(bf16[96,256]{1,0:T(8,128)(2,1)S(1)} %collective-permute-done.22.refs_4_), channel_id=1, source_target_pairs={{0,2},{1,3},{2,0},{3,1},{4,6},{5,7},{6,4},{7,5},{8,10},{9,11},{10,... | collective-permute-start | bytes 147464 | tf_op jit(solution)/shard_map/ppermute | solution.py:152
  44.3 0.9 %collective-permute-start.25 = (bf16[96,256]{1,0:T(8,128)(2,1)S(1)}, bf16[96,256]{1,0:T(8,128)(2,1)S(1)}, u32[]{:S(2)}, u32[]{:S(2)}) collective-permute-start(bf16[96,256]{1,0:T(8,128)(2,1)S(1)} %collective-permute-done.22.refs_4_), channel_id=1, source_target_pairs={{0,3},{1,2},{2,1},{3,0},{4,7},{5,6},{6,5},{7,4},{8,11},{9,10},{10,... | collective-permute-start | bytes 147464 | tf_op jit(solution)/shard_map/ppermute | solution.py:152
  45.2 1.2 %shard_map.98.refs_10_.refs_1_.base_ref = f32[1024,256]{1,0:T(8,128)S(1)} custom-call(f32[1024,256]{1,0:T(8,128)S(1)} %get-tuple-element.70.sol_ref.refs_12_, bf16[1024,1024]{1,0:T(8,128)(2,1)S(1)} %copy-done.1, f32[1024,256]{1,0:T(8,128)S(1)} %copy-done, bf16[1024,512]{1,0:T(8,128)(2,1)S(1)} %get-tuple-element.48.token.wt_ref.refs_4_, ...), custom_call_target="tpu_custom_call" | custom-call | flops 805306368 | bytes 5505024 | tf_op jit(solution)/shard_map/pallas_call | solution.py:26
  46.4 1.2 %collective-permute-done.24.refs_6_ = bf16[96,256]{1,0:T(8,128)(2,1)S(1)} collective-permute-done((bf16[96,256]{1,0:T(8,128)(2,1)S(1)}, bf16[96,256]{1,0:T(8,128)(2,1)S(1)}, u32[]{:S(2)}, u32[]{:S(2)}) %collective-permute-start.24) | collective-permute-done | bytes 49184 | tf_op jit(solution)/shard_map/ppermute | solution.py:152
  47.6 0.7 collective-permute-done.25.refs_7_
  48.8 2.1 %collective-permute-start.26 = (bf16[96,256]{1,0:T(8,128)(2,1)S(1)}, bf16[96,256]{1,0:T(8,128)(2,1)S(1)}, u32[]{:S(2)}, u32[]{:S(2)}) collective-permute-start(bf16[96,256]{1,0:T(8,128)(2,1)S(1)} %get-tuple-element.72), channel_id=1, source_target_pairs={{0,8},{4,12},{8,0},{12,4},{16,24},{20,28},{24,16},{28,20},{1,9},{5... | collective-permute-start | bytes 147464 | tf_op jit(solution)/shard_map/ppermute | solution.py:161
  50.9 0.7 %collective-permute-start.27 = (bf16[96,256]{1,0:T(8,128)(2,1)S(1)}, bf16[96,256]{1,0:T(8,128)(2,1)S(1)}, u32[]{:S(2)}, u32[]{:S(2)}) collective-permute-start(bf16[96,256]{1,0:T(8,128)(2,1)S(1)} %get-tuple-element.73), channel_id=1, source_target_pairs={{0,16},{4,20},{8,24},{12,28},{16,0},{20,4},{24,8},{28,12},{1,17},{... | collective-permute-start | bytes 147464 | tf_op jit(solution)/shard_map/ppermute | solution.py:161
  51.7 1.7 %collective-permute-start.28 = (bf16[96,256]{1,0:T(8,128)(2,1)S(1)}, bf16[96,256]{1,0:T(8,128)(2,1)S(1)}, u32[]{:S(2)}, u32[]{:S(2)}) collective-permute-start(bf16[96,256]{1,0:T(8,128)(2,1)S(1)} %get-tuple-element.74), channel_id=1, source_target_pairs={{0,24},{4,28},{8,16},{12,20},{16,8},{20,12},{24,0},{28,4},{1,25},{... | collective-permute-start | bytes 147464 | tf_op jit(solution)/shard_map/ppermute | solution.py:161
  53.4 3.7 %collective-permute-done.27.refs_2_ = bf16[96,256]{1,0:T(8,128)(2,1)S(1)} collective-permute-done((bf16[96,256]{1,0:T(8,128)(2,1)S(1)}, bf16[96,256]{1,0:T(8,128)(2,1)S(1)}, u32[]{:S(2)}, u32[]{:S(2)}) %collective-permute-start.27) | collective-permute-done | bytes 49184 | tf_op jit(solution)/shard_map/ppermute | solution.py:161
  57.1 0.6 collective-permute-done.28.refs_3_
  58.0 1.3 %collective-permute-start.30 = (bf16[128,256]{1,0:T(8,128)(2,1)S(1)}, bf16[128,256]{1,0:T(8,128)(2,1)S(1)}, u32[]{:S(2)}, u32[]{:S(2)}) collective-permute-start(bf16[128,256]{1,0:T(8,128)(2,1)S(1)} %get-tuple-element.77), channel_id=1, source_target_pairs={{0,3},{1,2},{2,1},{3,0},{4,7},{5,6},{6,5},{7,4},{8,11},{9,10},{10,... | collective-permute-start | bytes 196616 | tf_op jit(solution)/shard_map/ppermute | solution.py:85
  59.2 1.6 %collective-permute-start.31 = (bf16[128,256]{1,0:T(8,128)(2,1)S(1)}, bf16[128,256]{1,0:T(8,128)(2,1)S(1)}, u32[]{:S(2)}, u32[]{:S(2)}) collective-permute-start(bf16[128,256]{1,0:T(8,128)(2,1)S(1)} %get-tuple-element.78), channel_id=1, source_target_pairs={{0,4},{1,5},{2,6},{3,7},{4,0},{5,1},{6,2},{7,3},{8,12},{9,13},{10,... | collective-permute-start | bytes 196616 | tf_op jit(solution)/shard_map/ppermute | solution.py:85
  60.8 0.7 collective-permute-start.32
  61.5 0.9 %shard_map.102.base_ref = f32[512,256]{1,0:T(8,128)S(1)} custom-call(bf16[96,256]{1,0:T(8,128)(2,1)S(1)} %get-tuple-element.75.refs_0_.y_ref, f32[1024,256]{1,0:T(8,128)S(1)} %shard_map.98.refs_10_.refs_1_.base_ref, bf16[1024,96]{1,0:T(8,128)(2,1)S(1)} %shard_map.89.refs_10_.refs_2_.lb_ref, bf16[512,1024]{1,0:T(8,128)(2,1)S(1)} %get-tuple-element.64.si_ref, ...), custom_call_target="tpu_custom_call" | custom-call | flops 268435456 | bytes 2703360 | tf_op jit(solution)/shard_map/pallas_call | solution.py:26
  62.5 1.6 %collective-permute-done.31.refs_10_.refs_2_ = bf16[128,256]{1,0:T(8,128)(2,1)S(1)} collective-permute-done((bf16[128,256]{1,0:T(8,128)(2,1)S(1)}, bf16[128,256]{1,0:T(8,128)(2,1)S(1)}, u32[]{:S(2)}, u32[]{:S(2)}) %collective-permute-start.31) | collective-permute-done | bytes 65568 | tf_op jit(solution)/shard_map/ppermute | solution.py:85
  64.5 1.0 %collective-permute-start.34 = (bf16[128,256]{1,0:T(8,128)(2,1)S(1)}, bf16[128,256]{1,0:T(8,128)(2,1)S(1)}, u32[]{:S(2)}, u32[]{:S(2)}) collective-permute-start(bf16[128,256]{1,0:T(8,128)(2,1)S(1)} %get-tuple-element.83), channel_id=1, source_target_pairs={{0,3},{1,2},{2,1},{3,0},{4,7},{5,6},{6,5},{7,4},{8,11},{9,10},{10,... | collective-permute-start | bytes 196616 | tf_op jit(solution)/shard_map/ppermute | solution.py:85
  65.5 2.6 %collective-permute-start.35 = (bf16[128,256]{1,0:T(8,128)(2,1)S(1)}, bf16[128,256]{1,0:T(8,128)(2,1)S(1)}, u32[]{:S(2)}, u32[]{:S(2)}) collective-permute-start(bf16[128,256]{1,0:T(8,128)(2,1)S(1)} %get-tuple-element.84), channel_id=1, source_target_pairs={{0,4},{1,5},{2,6},{3,7},{4,0},{5,1},{6,2},{7,3},{8,12},{9,13},{10,... | collective-permute-start | bytes 196616 | tf_op jit(solution)/shard_map/ppermute | solution.py:85
  68.5 2.7 %shard_map.101 = (f32[1024,256]{1,0:T(8,128)}, f32[1024,256]{1,0:T(8,128)S(1)}) custom-call(bf16[96,256]{1,0:T(8,128)(2,1)S(1)} %get-tuple-element.75.refs_0_.y_ref, f32[1024,256]{1,0:T(8,128)S(1)} %shard_map.98.refs_10_.refs_1_.base_ref, bf16[1024,96]{1,0:T(8,128)(2,1)S(1)} %shard_map.89.refs_10_.refs_2_.lb_ref, ...), custom_call_target="tpu_custom_call" | custom-call | flops 1342177280 | bytes 9093120 | tf_op jit(solution)/shard_map/pallas_call | solution.py:26
  71.2 1.3 %shard_map.104 = f32[1024,256]{1,0:T(8,128)} custom-call(f32[1024,256]{1,0:T(8,128)S(1)} %get-tuple-element.81.res_ref, bf16[1024,512]{1,0:T(8,128)(2,1)S(1)} %get-tuple-element.48.token.wt_ref.refs_4_, bf16[128,256]{1,0:T(8,128)(2,1)S(1)} %collective-permute-done.33.refs_0_, bf16[128,256]{1,0:T(8,128)(2,1)S(1)} %collective-permute-done.34.refs_1_, ...), custom_call_target="tpu_custom_call" | custom-call | flops 268435456 | bytes 2359296 | tf_op jit(solution)/shard_map/pallas_call | solution.py:26
  (62 shorter events, 4.0 us)
Async XLA Ops:
  0.6 0.9 %copy-start.3 = (bf16[96,1024]{1,0:T(8,128)(2,1)S(1)}, bf16[96,1024]{1,0:T(8,128)(2,1)}, u32[]{:S(2)}) copy-start(bf16[96,1024]{1,0:T(8,128)(2,1)} %basis_ref.3) | copy-start | bytes 589828
  0.6 1.3 %copy-start = (f32[1024,256]{1,0:T(8,128)S(1)}, f32[1024,256]{1,0:T(8,128)}, u32[]{:S(2)}) copy-start(f32[1024,256]{1,0:T(8,128)} %refs_6_.1) | copy-start | bytes 3145732
  0.7 1.6 %copy-start.4 = (bf16[768,384]{1,0:T(8,128)(2,1)S(1)}, bf16[768,384]{1,0:T(8,128)(2,1)}, u32[]{:S(2)}) copy-start(bf16[768,384]{1,0:T(8,128)(2,1)} %inv_ref.2) | copy-start | bytes 1769476
  0.7 6.8 %copy-start.5 = (s32[1,4,128]{2,1,0:T(4,128)S(1)}, s32[1,4,128]{2,1,0:T(4,128)}, u32[]{:S(2)}) copy-start(s32[1,4,128]{2,1,0:T(4,128)} %param.13) | copy-start | bytes 6148
  0.7 9.6 %copy-start.6 = (f32[1,4,128]{2,1,0:T(4,128)S(1)}, f32[1,4,128]{2,1,0:T(4,128)}, u32[]{:S(2)}) copy-start(f32[1,4,128]{2,1,0:T(4,128)} %param.12) | copy-start | bytes 6148
  2.0 9.1 %copy-start.1 = (bf16[1024,1024]{1,0:T(8,128)(2,1)S(1)}, bf16[1024,1024]{1,0:T(8,128)(2,1)}, u32[]{:S(2)}) copy-start(bf16[1024,1024]{1,0:T(8,128)(2,1)} %refs_7_.1) | copy-start | bytes 6291460
  2.3 5.2 %collective-permute-start.3 = (bf16[96,256]{1,0:T(8,128)(2,1)S(1)}, bf16[96,256]{1,0:T(8,128)(2,1)S(1)}, u32[]{:S(2)}, u32[]{:S(2)}) collective-permute-start(bf16[96,256]{1,0:T(8,128)(2,1)S(1)} %get-tuple-element.44.token.refs_0_), channel_id=1, source_target_pairs={{0,4},{4,0},{8,12},{12,8},{16,20},{20,16},{24,28},{28,24},{1,5},{5... | collective-permute-start | bytes 147464 | tf_op jit(solution)/shard_map/ppermute | solution.py:156
  5.3 2.2 %collective-permute-start = (bf16[96,256]{1,0:T(8,128)(2,1)S(1)}, bf16[96,256]{1,0:T(8,128)(2,1)S(1)}, u32[]{:S(2)}, u32[]{:S(2)}) collective-permute-start(bf16[96,256]{1,0:T(8,128)(2,1)S(1)} %get-tuple-element.44.token.refs_0_), channel_id=1, source_target_pairs={{0,1},{1,0},{2,3},{3,2},{4,5},{5,4},{6,7},{7,6},{8,9},{9,8},{10,11... | collective-permute-start | bytes 147464 | tf_op jit(solution)/shard_map/ppermute | solution.py:152
  5.3 4.2 %collective-permute-start.1 = (bf16[96,256]{1,0:T(8,128)(2,1)S(1)}, bf16[96,256]{1,0:T(8,128)(2,1)S(1)}, u32[]{:S(2)}, u32[]{:S(2)}) collective-permute-start(bf16[96,256]{1,0:T(8,128)(2,1)S(1)} %get-tuple-element.44.token.refs_0_), channel_id=1, source_target_pairs={{0,2},{1,3},{2,0},{3,1},{4,6},{5,7},{6,4},{7,5},{8,10},{9,11},{10,... | collective-permute-start | bytes 147464 | tf_op jit(solution)/shard_map/ppermute | solution.py:152
  6.8 5.2 %collective-permute-start.2 = (bf16[96,256]{1,0:T(8,128)(2,1)S(1)}, bf16[96,256]{1,0:T(8,128)(2,1)S(1)}, u32[]{:S(2)}, u32[]{:S(2)}) collective-permute-start(bf16[96,256]{1,0:T(8,128)(2,1)S(1)} %get-tuple-element.44.token.refs_0_), channel_id=1, source_target_pairs={{0,3},{1,2},{2,1},{3,0},{4,7},{5,6},{6,5},{7,4},{8,11},{9,10},{10,... | collective-permute-start | bytes 147464 | tf_op jit(solution)/shard_map/ppermute | solution.py:152
  7.2 9.2 %collective-permute-start.7 = (bf16[384,384]{1,0:T(8,128)(2,1)S(1)}, bf16[384,384]{1,0:T(8,128)(2,1)S(1)}, u32[]{:S(2)}, u32[]{:S(2)}) collective-permute-start(bf16[384,384]{1,0:T(8,128)(2,1)S(1)} %get-tuple-element.46), channel_id=1, source_target_pairs={{0,4},{4,0},{8,12},{12,8},{16,20},{20,16},{24,28},{28,24},{1,5},{5... | collective-permute-start | bytes 884744 | tf_op jit(solution)/shard_map/ppermute | solution.py:156
  7.5 4.5 %collective-permute-start.4 = (bf16[96,256]{1,0:T(8,128)(2,1)S(1)}, bf16[96,256]{1,0:T(8,128)(2,1)S(1)}, u32[]{:S(2)}, u32[]{:S(2)}) collective-permute-start(bf16[96,256]{1,0:T(8,128)(2,1)S(1)} %collective-permute-done.3.refs_4_), channel_id=1, source_target_pairs={{0,1},{1,0},{2,3},{3,2},{4,5},{5,4},{6,7},{7,6},{8,9},{9,8},{10,11... | collective-permute-start | bytes 147464 | tf_op jit(solution)/shard_map/ppermute | solution.py:152
  7.6 4.4 %collective-permute-start.5 = (bf16[96,256]{1,0:T(8,128)(2,1)S(1)}, bf16[96,256]{1,0:T(8,128)(2,1)S(1)}, u32[]{:S(2)}, u32[]{:S(2)}) collective-permute-start(bf16[96,256]{1,0:T(8,128)(2,1)S(1)} %collective-permute-done.3.refs_4_), channel_id=1, source_target_pairs={{0,2},{1,3},{2,0},{3,1},{4,6},{5,7},{6,4},{7,5},{8,10},{9,11},{10,... | collective-permute-start | bytes 147464 | tf_op jit(solution)/shard_map/ppermute | solution.py:152
  9.5 3.5 %collective-permute-start.6 = (bf16[96,256]{1,0:T(8,128)(2,1)S(1)}, bf16[96,256]{1,0:T(8,128)(2,1)S(1)}, u32[]{:S(2)}, u32[]{:S(2)}) collective-permute-start(bf16[96,256]{1,0:T(8,128)(2,1)S(1)} %collective-permute-done.3.refs_4_), channel_id=1, source_target_pairs={{0,3},{1,2},{2,1},{3,0},{4,7},{5,6},{6,5},{7,4},{8,11},{9,10},{10,... | collective-permute-start | bytes 147464 | tf_op jit(solution)/shard_map/ppermute | solution.py:152
  11.1 10.2 %copy-start.2 = (bf16[1024,1024]{1,0:T(8,128)(2,1)S(1)}, bf16[1024,1024]{1,0:T(8,128)(2,1)}, u32[]{:S(2)}) copy-start(bf16[1024,1024]{1,0:T(8,128)(2,1)} %refs_5_.3) | copy-start | bytes 6291460
  16.9 6.5 %collective-permute-start.10 = (bf16[96,256]{1,0:T(8,128)(2,1)S(1)}, bf16[96,256]{1,0:T(8,128)(2,1)S(1)}, u32[]{:S(2)}, u32[]{:S(2)}) collective-permute-start(bf16[96,256]{1,0:T(8,128)(2,1)S(1)} %get-tuple-element.52), channel_id=1, source_target_pairs={{0,24},{4,28},{8,16},{12,20},{16,8},{20,12},{24,0},{28,4},{1,25},{... | collective-permute-start | bytes 147464 | tf_op jit(solution)/shard_map/ppermute | solution.py:161
  20.5 4.1 %collective-permute-start.8 = (bf16[96,256]{1,0:T(8,128)(2,1)S(1)}, bf16[96,256]{1,0:T(8,128)(2,1)S(1)}, u32[]{:S(2)}, u32[]{:S(2)}) collective-permute-start(bf16[96,256]{1,0:T(8,128)(2,1)S(1)} %get-tuple-element.50), channel_id=1, source_target_pairs={{0,8},{4,12},{8,0},{12,4},{16,24},{20,28},{24,16},{28,20},{1,9},{5... | collective-permute-start | bytes 147464 | tf_op jit(solution)/shard_map/ppermute | solution.py:161
  20.5 5.0 %collective-permute-start.9 = (bf16[96,256]{1,0:T(8,128)(2,1)S(1)}, bf16[96,256]{1,0:T(8,128)(2,1)S(1)}, u32[]{:S(2)}, u32[]{:S(2)}) collective-permute-start(bf16[96,256]{1,0:T(8,128)(2,1)S(1)} %get-tuple-element.51), channel_id=1, source_target_pairs={{0,16},{4,20},{8,24},{12,28},{16,0},{20,4},{24,8},{28,12},{1,17},{... | collective-permute-start | bytes 147464 | tf_op jit(solution)/shard_map/ppermute | solution.py:161
  25.7 6.6 %collective-permute-start.11 = (bf16[128,256]{1,0:T(8,128)(2,1)S(1)}, bf16[128,256]{1,0:T(8,128)(2,1)S(1)}, u32[]{:S(2)}, u32[]{:S(2)}) collective-permute-start(bf16[128,256]{1,0:T(8,128)(2,1)S(1)} %get-tuple-element.58), channel_id=1, source_target_pairs={{0,1},{1,0},{2,3},{3,2},{4,8},{5,9},{6,10},{7,11},{8,4},{9,5},{10,... | collective-permute-start | bytes 196616 | tf_op jit(solution)/shard_map/ppermute | solution.py:85
  25.8 6.5 %collective-permute-start.12 = (bf16[128,256]{1,0:T(8,128)(2,1)S(1)}, bf16[128,256]{1,0:T(8,128)(2,1)S(1)}, u32[]{:S(2)}, u32[]{:S(2)}) collective-permute-start(bf16[128,256]{1,0:T(8,128)(2,1)S(1)} %get-tuple-element.59), channel_id=1, source_target_pairs={{0,3},{1,2},{2,1},{3,0},{4,7},{5,6},{6,5},{7,4},{8,11},{9,10},{10,... | collective-permute-start | bytes 196616 | tf_op jit(solution)/shard_map/ppermute | solution.py:85
  27.4 4.9 %collective-permute-start.13 = (bf16[128,256]{1,0:T(8,128)(2,1)S(1)}, bf16[128,256]{1,0:T(8,128)(2,1)S(1)}, u32[]{:S(2)}, u32[]{:S(2)}) collective-permute-start(bf16[128,256]{1,0:T(8,128)(2,1)S(1)} %get-tuple-element.60), channel_id=1, source_target_pairs={{0,4},{1,5},{2,6},{3,7},{4,0},{5,1},{6,2},{7,3},{8,12},{9,13},{10,... | collective-permute-start | bytes 196616 | tf_op jit(solution)/shard_map/ppermute | solution.py:85
  29.3 3.0 %collective-permute-start.14 = (bf16[128,256]{1,0:T(8,128)(2,1)S(1)}, bf16[128,256]{1,0:T(8,128)(2,1)S(1)}, u32[]{:S(2)}, u32[]{:S(2)}) collective-permute-start(bf16[128,256]{1,0:T(8,128)(2,1)S(1)} %get-tuple-element.61), channel_id=1, source_target_pairs={{0,1},{1,0},{2,3},{3,2},{4,5},{5,4},{6,7},{7,6},{8,9},{9,8},{10,11... | collective-permute-start | bytes 196616 | tf_op jit(solution)/shard_map/ppermute | solution.py:85
  32.6 5.8 %collective-permute-start.15 = (bf16[128,256]{1,0:T(8,128)(2,1)S(1)}, bf16[128,256]{1,0:T(8,128)(2,1)S(1)}, u32[]{:S(2)}, u32[]{:S(2)}) collective-permute-start(bf16[128,256]{1,0:T(8,128)(2,1)S(1)} %get-tuple-element.66.refs_0_), channel_id=1, source_target_pairs={{0,1},{1,0},{2,3},{3,2},{4,8},{5,9},{6,10},{7,11},{8,4},{9,5},{10,... | collective-permute-start | bytes 196616 | tf_op jit(solution)/shard_map/ppermute | solution.py:85
  32.7 5.7 %collective-permute-start.16 = (bf16[128,256]{1,0:T(8,128)(2,1)S(1)}, bf16[128,256]{1,0:T(8,128)(2,1)S(1)}, u32[]{:S(2)}, u32[]{:S(2)}) collective-permute-start(bf16[128,256]{1,0:T(8,128)(2,1)S(1)} %get-tuple-element.67.refs_1_), channel_id=1, source_target_pairs={{0,3},{1,2},{2,1},{3,0},{4,7},{5,6},{6,5},{7,4},{8,11},{9,10},{10,... | collective-permute-start | bytes 196616 | tf_op jit(solution)/shard_map/ppermute | solution.py:85
  34.2 4.8 %collective-permute-start.17 = (bf16[128,256]{1,0:T(8,128)(2,1)S(1)}, bf16[128,256]{1,0:T(8,128)(2,1)S(1)}, u32[]{:S(2)}, u32[]{:S(2)}) collective-permute-start(bf16[128,256]{1,0:T(8,128)(2,1)S(1)} %get-tuple-element.68.refs_2_), channel_id=1, source_target_pairs={{0,4},{1,5},{2,6},{3,7},{4,0},{5,1},{6,2},{7,3},{8,12},{9,13},{10,... | collective-permute-start | bytes 196616 | tf_op jit(solution)/shard_map/ppermute | solution.py:85
  35.3 3.7 %collective-permute-start.18 = (bf16[128,256]{1,0:T(8,128)(2,1)S(1)}, bf16[128,256]{1,0:T(8,128)(2,1)S(1)}, u32[]{:S(2)}, u32[]{:S(2)}) collective-permute-start(bf16[128,256]{1,0:T(8,128)(2,1)S(1)} %get-tuple-element.69.refs_3_), channel_id=1, source_target_pairs={{0,1},{1,0},{2,3},{3,2},{4,5},{5,4},{6,7},{7,6},{8,9},{9,8},{10,11... | collective-permute-start | bytes 196616 | tf_op jit(solution)/shard_map/ppermute | solution.py:85
  39.1 4.2 %collective-permute-start.22 = (bf16[96,256]{1,0:T(8,128)(2,1)S(1)}, bf16[96,256]{1,0:T(8,128)(2,1)S(1)}, u32[]{:S(2)}, u32[]{:S(2)}) collective-permute-start(bf16[96,256]{1,0:T(8,128)(2,1)S(1)} %shard_map.97.refs_0_), channel_id=1, source_target_pairs={{0,4},{4,0},{8,12},{12,8},{16,20},{20,16},{24,28},{28,24},{1,5},{5... | collective-permute-start | bytes 147464 | tf_op jit(solution)/shard_map/ppermute | solution.py:156
  41.0 3.3 %collective-permute-start.19 = (bf16[96,256]{1,0:T(8,128)(2,1)S(1)}, bf16[96,256]{1,0:T(8,128)(2,1)S(1)}, u32[]{:S(2)}, u32[]{:S(2)}) collective-permute-start(bf16[96,256]{1,0:T(8,128)(2,1)S(1)} %shard_map.97.refs_0_), channel_id=1, source_target_pairs={{0,1},{1,0},{2,3},{3,2},{4,5},{5,4},{6,7},{7,6},{8,9},{9,8},{10,11... | collective-permute-start | bytes 147464 | tf_op jit(solution)/shard_map/ppermute | solution.py:152
  41.0 5.4 %collective-permute-start.20 = (bf16[96,256]{1,0:T(8,128)(2,1)S(1)}, bf16[96,256]{1,0:T(8,128)(2,1)S(1)}, u32[]{:S(2)}, u32[]{:S(2)}) collective-permute-start(bf16[96,256]{1,0:T(8,128)(2,1)S(1)} %shard_map.97.refs_0_), channel_id=1, source_target_pairs={{0,2},{1,3},{2,0},{3,1},{4,6},{5,7},{6,4},{7,5},{8,10},{9,11},{10,... | collective-permute-start | bytes 147464 | tf_op jit(solution)/shard_map/ppermute | solution.py:152
  42.1 4.3 %collective-permute-start.21 = (bf16[96,256]{1,0:T(8,128)(2,1)S(1)}, bf16[96,256]{1,0:T(8,128)(2,1)S(1)}, u32[]{:S(2)}, u32[]{:S(2)}) collective-permute-start(bf16[96,256]{1,0:T(8,128)(2,1)S(1)} %shard_map.97.refs_0_), channel_id=1, source_target_pairs={{0,3},{1,2},{2,1},{3,0},{4,7},{5,6},{6,5},{7,4},{8,11},{9,10},{10,... | collective-permute-start | bytes 147464 | tf_op jit(solution)/shard_map/ppermute | solution.py:152
  43.3 3.1 %collective-permute-start.23 = (bf16[96,256]{1,0:T(8,128)(2,1)S(1)}, bf16[96,256]{1,0:T(8,128)(2,1)S(1)}, u32[]{:S(2)}, u32[]{:S(2)}) collective-permute-start(bf16[96,256]{1,0:T(8,128)(2,1)S(1)} %collective-permute-done.22.refs_4_), channel_id=1, source_target_pairs={{0,1},{1,0},{2,3},{3,2},{4,5},{5,4},{6,7},{7,6},{8,9},{9,8},{10,11... | collective-permute-start | bytes 147464 | tf_op jit(solution)/shard_map/ppermute | solution.py:152
  43.3 4.3 %collective-permute-start.24 = (bf16[96,256]{1,0:T(8,128)(2,1)S(1)}, bf16[96,256]{1,0:T(8,128)(2,1)S(1)}, u32[]{:S(2)}, u32[]{:S(2)}) collective-permute-start(bf16[96,256]{1,0:T(8,128)(2,1)S(1)} %collective-permute-done.22.refs_4_), channel_id=1, source_target_pairs={{0,2},{1,3},{2,0},{3,1},{4,6},{5,7},{6,4},{7,5},{8,10},{9,11},{10,... | collective-permute-start | bytes 147464 | tf_op jit(solution)/shard_map/ppermute | solution.py:152
  44.3 4.0 %collective-permute-start.25 = (bf16[96,256]{1,0:T(8,128)(2,1)S(1)}, bf16[96,256]{1,0:T(8,128)(2,1)S(1)}, u32[]{:S(2)}, u32[]{:S(2)}) collective-permute-start(bf16[96,256]{1,0:T(8,128)(2,1)S(1)} %collective-permute-done.22.refs_4_), channel_id=1, source_target_pairs={{0,3},{1,2},{2,1},{3,0},{4,7},{5,6},{6,5},{7,4},{8,11},{9,10},{10,... | collective-permute-start | bytes 147464 | tf_op jit(solution)/shard_map/ppermute | solution.py:152
  48.8 4.6 %collective-permute-start.26 = (bf16[96,256]{1,0:T(8,128)(2,1)S(1)}, bf16[96,256]{1,0:T(8,128)(2,1)S(1)}, u32[]{:S(2)}, u32[]{:S(2)}) collective-permute-start(bf16[96,256]{1,0:T(8,128)(2,1)S(1)} %get-tuple-element.72), channel_id=1, source_target_pairs={{0,8},{4,12},{8,0},{12,4},{16,24},{20,28},{24,16},{28,20},{1,9},{5... | collective-permute-start | bytes 147464 | tf_op jit(solution)/shard_map/ppermute | solution.py:161
  50.9 6.2 %collective-permute-start.27 = (bf16[96,256]{1,0:T(8,128)(2,1)S(1)}, bf16[96,256]{1,0:T(8,128)(2,1)S(1)}, u32[]{:S(2)}, u32[]{:S(2)}) collective-permute-start(bf16[96,256]{1,0:T(8,128)(2,1)S(1)} %get-tuple-element.73), channel_id=1, source_target_pairs={{0,16},{4,20},{8,24},{12,28},{16,0},{20,4},{24,8},{28,12},{1,17},{... | collective-permute-start | bytes 147464 | tf_op jit(solution)/shard_map/ppermute | solution.py:161
  51.7 6.0 %collective-permute-start.28 = (bf16[96,256]{1,0:T(8,128)(2,1)S(1)}, bf16[96,256]{1,0:T(8,128)(2,1)S(1)}, u32[]{:S(2)}, u32[]{:S(2)}) collective-permute-start(bf16[96,256]{1,0:T(8,128)(2,1)S(1)} %get-tuple-element.74), channel_id=1, source_target_pairs={{0,24},{4,28},{8,16},{12,20},{16,8},{20,12},{24,0},{28,4},{1,25},{... | collective-permute-start | bytes 147464 | tf_op jit(solution)/shard_map/ppermute | solution.py:161
  57.9 4.6 %collective-permute-start.29 = (bf16[128,256]{1,0:T(8,128)(2,1)S(1)}, bf16[128,256]{1,0:T(8,128)(2,1)S(1)}, u32[]{:S(2)}, u32[]{:S(2)}) collective-permute-start(bf16[128,256]{1,0:T(8,128)(2,1)S(1)} %get-tuple-element.76), channel_id=1, source_target_pairs={{0,1},{1,0},{2,3},{3,2},{4,8},{5,9},{6,10},{7,11},{8,4},{9,5},{10,... | collective-permute-start | bytes 196616 | tf_op jit(solution)/shard_map/ppermute | solution.py:85
  58.0 4.5 %collective-permute-start.30 = (bf16[128,256]{1,0:T(8,128)(2,1)S(1)}, bf16[128,256]{1,0:T(8,128)(2,1)S(1)}, u32[]{:S(2)}, u32[]{:S(2)}) collective-permute-start(bf16[128,256]{1,0:T(8,128)(2,1)S(1)} %get-tuple-element.77), channel_id=1, source_target_pairs={{0,3},{1,2},{2,1},{3,0},{4,7},{5,6},{6,5},{7,4},{8,11},{9,10},{10,... | collective-permute-start | bytes 196616 | tf_op jit(solution)/shard_map/ppermute | solution.py:85
  59.2 4.8 %collective-permute-start.31 = (bf16[128,256]{1,0:T(8,128)(2,1)S(1)}, bf16[128,256]{1,0:T(8,128)(2,1)S(1)}, u32[]{:S(2)}, u32[]{:S(2)}) collective-permute-start(bf16[128,256]{1,0:T(8,128)(2,1)S(1)} %get-tuple-element.78), channel_id=1, source_target_pairs={{0,4},{1,5},{2,6},{3,7},{4,0},{5,1},{6,2},{7,3},{8,12},{9,13},{10,... | collective-permute-start | bytes 196616 | tf_op jit(solution)/shard_map/ppermute | solution.py:85
  60.8 3.2 %collective-permute-start.32 = (bf16[128,256]{1,0:T(8,128)(2,1)S(1)}, bf16[128,256]{1,0:T(8,128)(2,1)S(1)}, u32[]{:S(2)}, u32[]{:S(2)}) collective-permute-start(bf16[128,256]{1,0:T(8,128)(2,1)S(1)} %get-tuple-element.79), channel_id=1, source_target_pairs={{0,1},{1,0},{2,3},{3,2},{4,5},{5,4},{6,7},{7,6},{8,9},{9,8},{10,11... | collective-permute-start | bytes 196616 | tf_op jit(solution)/shard_map/ppermute | solution.py:85
  64.4 6.8 %collective-permute-start.33 = (bf16[128,256]{1,0:T(8,128)(2,1)S(1)}, bf16[128,256]{1,0:T(8,128)(2,1)S(1)}, u32[]{:S(2)}, u32[]{:S(2)}) collective-permute-start(bf16[128,256]{1,0:T(8,128)(2,1)S(1)} %get-tuple-element.82), channel_id=1, source_target_pairs={{0,1},{1,0},{2,3},{3,2},{4,8},{5,9},{6,10},{7,11},{8,4},{9,5},{10,... | collective-permute-start | bytes 196616 | tf_op jit(solution)/shard_map/ppermute | solution.py:85
  64.5 6.8 %collective-permute-start.34 = (bf16[128,256]{1,0:T(8,128)(2,1)S(1)}, bf16[128,256]{1,0:T(8,128)(2,1)S(1)}, u32[]{:S(2)}, u32[]{:S(2)}) collective-permute-start(bf16[128,256]{1,0:T(8,128)(2,1)S(1)} %get-tuple-element.83), channel_id=1, source_target_pairs={{0,3},{1,2},{2,1},{3,0},{4,7},{5,6},{6,5},{7,4},{8,11},{9,10},{10,... | collective-permute-start | bytes 196616 | tf_op jit(solution)/shard_map/ppermute | solution.py:85
  65.5 5.7 %collective-permute-start.35 = (bf16[128,256]{1,0:T(8,128)(2,1)S(1)}, bf16[128,256]{1,0:T(8,128)(2,1)S(1)}, u32[]{:S(2)}, u32[]{:S(2)}) collective-permute-start(bf16[128,256]{1,0:T(8,128)(2,1)S(1)} %get-tuple-element.84), channel_id=1, source_target_pairs={{0,4},{1,5},{2,6},{3,7},{4,0},{5,1},{6,2},{7,3},{8,12},{9,13},{10,... | collective-permute-start | bytes 196616 | tf_op jit(solution)/shard_map/ppermute | solution.py:85
  68.1 3.2 %collective-permute-start.36 = (bf16[128,256]{1,0:T(8,128)(2,1)S(1)}, bf16[128,256]{1,0:T(8,128)(2,1)S(1)}, u32[]{:S(2)}, u32[]{:S(2)}) collective-permute-start(bf16[128,256]{1,0:T(8,128)(2,1)S(1)} %get-tuple-element.85), channel_id=1, source_target_pairs={{0,1},{1,0},{2,3},{3,2},{4,5},{5,4},{6,7},{7,6},{8,9},{9,8},{10,11... | collective-permute-start | bytes 196616 | tf_op jit(solution)/shard_map/ppermute | solution.py:85

commit v7 on v6

--- a/solution.py
+++ b/solution.py
@@ -8,7 +8,6 @@
 from jax.sharding import PartitionSpec as P
 
 
-STEPS = 2
 BF = jnp.bfloat16
 F32 = jnp.float32
 VMEM = pl.BlockSpec(memory_space=pltpu.VMEM)
@@ -148,9 +147,10 @@
             ref[...] = (mm(same_ref[at, :], group[...]) + mm(other_ref[at, :], group_other[...])).astype(ref.dtype)
 
     def over_col(block):
-        return [block] + [
-            lax.ppermute(block, "col", [(i, i ^ k) for i in range(nc)]) for k in reversed(range(1, nc))
-        ][::-1]
+        out = [block]
+        for k in range(1, nc):
+            out.append(lax.ppermute(block, "col", [(i, i ^ k) for i in range(nc)]))
+        return out
 
     def over_pair(value):
         return lax.ppermute(value, "row", [(i, i ^ 1) for i in range(nr)])
@@ -164,7 +164,8 @@
     own_and_sends = [((cpd, nrhs), F32)] + [((cpd, nrhs), BF)] * (nz - 1)
 
     def k_coarse_faces(*refs):
-        parts, (bf_ref, y_ref), faces = refs[:nz], refs[nz : nz + 2], refs[nz + 2 :]
+        parts, bf_ref, refs = refs[:nz], refs[nz], refs[-5:]
+        y_ref, faces = refs[0], refs[1:]
         total = parts[0][...]
         for p in parts[1:]:
             total = total + p[...].astype(F32)
@@ -173,12 +174,15 @@
         for s, ref in enumerate(faces):
             ref[...] = mm(bf_ref[pl.ds(s * ovl, ovl), :], y).astype(BF)
 
-    def coarse_faces(parts):
-        y, *faces = call(k_coarse_faces, [((cpd, nrhs), BF)] + [((ovl, nrhs), BF)] * 4, *parts, bfac)
+    def coarse_faces(parts, *tokens):
+        y, *faces = call(
+            k_coarse_faces, [((cpd, nrhs), BF)] + [((ovl, nrhs), BF)] * 4, *parts, bfac, *tokens,
+            tokens=len(tokens),
+        )
         return y, faces
 
     def k_local(y_ref, base_ref, lb_ref, si_ref, bf_ref, *refs):
-        olds, face_ref, wb = refs[:-2], refs[-2], refs[-1]
+        face_ref, wb = refs[-2:] if len(refs) == 2 else (refs[7], refs[9])
         y = y_ref[...]
 
         def tile(at):
@@ -188,14 +192,22 @@
         for s in range(4):
             at = pl.ds(s * ovl, ovl)
             face = mm(bf_ref[at, :], y) + mm(si_ref[at, :], wb[...])
-            face_ref[at, :] = face + olds[s][...].astype(F32) if olds else face
-
-    def local(y, base, olds):
-        (face,) = call(
-            k_local, [((nf, nrhs), F32)], y, base, lbmat, simat, bfac, *olds,
+            face_ref[at, :] = face + refs[s][...].astype(F32) if len(refs) > 2 else face
+        if len(refs) > 2:
+            old_ref, bt_ref, inv_ref, pre_ref = refs[4:7] + refs[8:9]
+
+            def pre_tile(at):
+                pre_ref[at, :] = old_ref[at, :] + mm(bt_ref[at, :], y) + mm(inv_ref[at, :], wb[...])
+
+            row_loop(pre_tile)
+
+    def local(y, base, olds, old=None):
+        more = [] if old is None else [*olds, old, btmat, local_inv]
+        return call(
+            k_local, [((nf, nrhs), F32)] + ([((nloc, nrhs), F32)] if more else []),
+            y, base, lbmat, simat, bfac, *more,
             scratch=[pltpu.VMEM((nloc, nrhs), BF)], flops=2 * nf * nloc * nrhs,
         )
-        return face
 
     def k_faces(base_ref, f_ref, *refs):
         recvs, faces = refs[:4], refs[4:]
@@ -207,12 +219,8 @@
     def faces_after(base, recv):
         return call(k_faces, [((ovl, nrhs), BF)] * 4, base, fmat, *recv, flops=2 * nf * nf * nrhs)
 
-    def k_advance(first, last, *refs):
-        y_ref, base_ref, lb_ref, bt_ref, wt_ref, inv_ref, left_ref, right_ref = refs[:8]
-        recvs, refs = refs[8:12], refs[12:]
-        old_ref, refs = (None, refs) if first else (refs[0], refs[1:])
-        out_ref, res_ref, wb, vb, recv = refs[:5]
-        new_ref, sem = refs[5:] if last else (out_ref, None)
+    def k_advance(y_ref, base_ref, lb_ref, bt_ref, wt_ref, inv_ref, brhs_ref, z_ref, *refs):
+        recvs, (new_ref, res_ref, wb, vb, recv) = refs[:4], refs[4:]
         y = y_ref[...]
         for s, x in enumerate(recvs):
             recv[pl.ds(s * ovl, ovl), :] = x[...]
@@ -224,33 +232,48 @@
 
         def sol_tile(at):
             new = mm(bt_ref[at, :], y) + mm(inv_ref[at, :], wb[...])
-            if not first:
-                new = new + old_ref[at, :]
             new_ref[at, :] = new
             vb[at, :] = new.astype(BF)
 
         row_loop(sol_tile)
-        if last:
-            store = pltpu.make_async_copy(new_ref, out_ref, sem)
-            store.start()
-
-            def res_tile(at):
-                res_ref[at, :] = left_ref[at, :] - mm(right_ref[at, :], vb[...])
-
-            row_loop(res_tile)
-            store.wait()
-        else:
-            res_ref[...] = left_ref[...] - mm(right_ref[...], vb[...])
-
-    def advance(y, base, recv, old, last, left, right):
-        first = old is None
-        outs = [((nloc, nrhs), F32), (left.shape, F32)]
-        extra = [pltpu.VMEM((nloc, nrhs), F32), pltpu.SemaphoreType.DMA] if last else []
-        return call(
-            functools.partial(k_advance, first, last), outs,
-            y, base, lbmat, btmat, wt, local_inv, left, right, *recv, *([] if first else [old]),
-            scratch=[pltpu.VMEM((nloc, nrhs), BF)] * 2 + [pltpu.VMEM((nf, nrhs), BF)] + extra,
-            hbm_outs=1 if last else 0, flops=5 * nloc * nloc * nrhs,
+        res_ref[...] = brhs_ref[...] - mm(z_ref[...], vb[...])
+
+    def advance(y, base, recv, brhs, zmat):
+        return call(
+            k_advance, [((nloc, nrhs), F32), (brhs.shape, F32)],
+            y, base, lbmat, btmat, wt, local_inv, brhs, zmat, *recv,
+            scratch=[pltpu.VMEM((nloc, nrhs), BF)] * 2 + [pltpu.VMEM((nf, nrhs), BF)],
+            flops=5 * nloc * nloc * nrhs,
+        )
+
+    def k_finish(pre_ref, m_ref, rhs_ref, mat_ref, *refs):
+        recvs, (out_ref, res_ref, vb, recv, new_ref, sem) = refs[:4], refs[4:]
+        for s, x in enumerate(recvs):
+            recv[pl.ds(s * ovl, ovl), :] = x[...]
+
+        def sol_tile(at):
+            new = pre_ref[at, :] + mm(m_ref[at, :], recv[...])
+            new_ref[at, :] = new
+            vb[at, :] = new.astype(BF)
+
+        row_loop(sol_tile)
+        store = pltpu.make_async_copy(new_ref, out_ref, sem)
+        store.start()
+
+        def res_tile(at):
+            res_ref[at, :] = rhs_ref[at, :] - mm(mat_ref[at, :], vb[...])
+
+        row_loop(res_tile)
+        store.wait()
+
+    def finish(pre, steer, recv):
+        return call(
+            k_finish, [((nloc, nrhs), F32)] * 2, pre, steer, rhs, local_mat, *recv,
+            scratch=[
+                pltpu.VMEM((nloc, nrhs), BF), pltpu.VMEM((nf, nrhs), BF),
+                pltpu.VMEM((nloc, nrhs), F32), pltpu.SemaphoreType.DMA,
+            ],
+            hbm_outs=1, flops=2 * nloc * (nloc + nf) * nrhs,
         )
 
     def k_restrict_recv(base_ref, t_ref, *refs):
@@ -299,12 +322,18 @@
             hbm_outs=1, flops=2 * nloc * nf * nrhs,
         )[0]
 
-    def coarse_pair(mine, across, token):
-        return call(
-            k_coarse_pair, own_and_sends, *mine, *over_col(across), same, other, token,
+    def coarse_pair(gathered, token):
+        return call(
+            k_coarse_pair, own_and_sends, *gathered, same, other, token,
             scratch=[pltpu.VMEM((nc * cpd, nrhs), BF)] * 2, tokens=1,
             flops=4 * half * nc * cpd * nrhs,
         )
+
+    def k_steer(inv_ref, wt_ref, token, m_ref):
+        def tile(at):
+            m_ref[at, :] = mm(inv_ref[at, :], wt_ref[...]).astype(BF)
+
+        row_loop(tile)
 
     (lead,) = call(k_lead, [((8, 128), F32)], flops=8 * nloc * nloc * nrhs)
     restricted = mm(basis_t, rhs.astype(BF)).astype(BF)
@@ -314,7 +343,7 @@
     )
     across = over_pair(restricted)
     other = over_pair(cross)
-    mine = over_col(restricted)
+    gathered = over_col(restricted) + over_col(across)
     table = jnp.concatenate([margin_rows[0].astype(F32), couple[0]], axis=0)
     sel, wt, btmat = call(
         k_select, [((nf, nloc), BF), ((nloc, nf), BF), ((nloc, cpd), BF)], table, basis_t, restricted,
@@ -324,30 +353,34 @@
         k_mat_basis, [((nloc, cpd), BF)], local_mat, btmat, wt, tokens=1,
         flops=2 * nloc * nloc * cpd,
     )
-    own, *sends = coarse_pair(mine, across, lbmat)
+    own, *sends = coarse_pair(gathered, lbmat)
     bfac, simat, fmat = call(
         k_products, [((nf, cpd), BF), ((nf, nloc), BF), ((nf, nf), BF)],
         sel, wt, local_inv, btmat, own, tokens=1, flops=2 * nf * nloc * (nloc + nf + cpd),
     )
-    residual, solution, sent = rhs, None, []
-    for sweep in range(STEPS):
-        y, faces = coarse_faces(reduce_rows(own, sends))
-        recv = halo(faces)
-        if sweep == 0:
-            zmat, tmat, brhs = call(
-                k_restrictors, [((cpd, nloc), BF), ((cpd, nf), BF), ((cpd, nrhs), F32)],
-                basis_t, local_mat, wt, rhs, y, tokens=1, flops=2 * cpd * nloc * (nloc + nf + nrhs),
-            )
-        sent = faces_after(local(y, residual, sent), recv)
-        recv2 = halo(sent)
-        if sweep == STEPS - 1:
-            solution, res = advance(y, residual, recv, solution, True, rhs, local_mat)
-            residual = coupled(res, recv2)
-        else:
-            solution, restr = advance(y, residual, recv, solution, False, brhs, zmat)
-            (restricted,) = call(k_restrict_recv, [((cpd, nrhs), BF)], restr, tmat, *recv2)
-            residual = residual_of(solution, recv2)
-            own, *sends = coarse_pair(over_col(restricted), over_pair(restricted), residual)
+    y, faces = coarse_faces(reduce_rows(own, sends))
+    recv = halo(faces)
+    zmat, tmat, brhs = call(
+        k_restrictors, [((cpd, nloc), BF), ((cpd, nf), BF), ((cpd, nrhs), F32)],
+        basis_t, local_mat, wt, rhs, y, tokens=1, flops=2 * cpd * nloc * (nloc + nf + nrhs),
+    )
+    (face_base,) = local(y, rhs, [])
+    sent = faces_after(face_base, recv)
+    recv2 = halo(sent)
+    solution, restr = advance(y, rhs, recv, brhs, zmat)
+    (restricted,) = call(k_restrict_recv, [((cpd, nrhs), BF)], restr, tmat, *recv2)
+    across = over_pair(restricted)
+    gathered = over_col(restricted) + over_col(across)
+    residual = residual_of(solution, recv2)
+    own, *sends = coarse_pair(gathered, residual)
+    (steer,) = call(k_steer, [((nloc, nf), BF)], local_inv, wt, own, tokens=1, flops=2 * nloc * nloc * nf)
+    y, faces = coarse_faces(reduce_rows(own, sends), steer)
+    recv = halo(faces)
+    face_base, before = local(y, residual, sent, solution)
+    sent = faces_after(face_base, recv)
+    recv2 = halo(sent)
+    solution, res = finish(before, steer, recv)
+    residual = coupled(res, recv2)
     return (solution, residual)
 
 

time: 72.7 us -> 71.9 us (0.989)
  starting transfers between devices: 38.8 us -> 34.3 us
  waiting for transfers between devices: 15.4 us -> 18 us
  Pallas kernels: 15.8 us -> 17 us
    ppermute x16, starting transfers between devices: 16.4 us -> 12.4 us  [halo(): out.append(lax.ppermute(f, both, p))]
    ppermute x16, waiting for transfers between devices: 2.14 us -> 4.43 us  [halo(): out.append(lax.ppermute(f, both, p))]
    pallas_call x19 -> x20, Pallas kernels: 15.8 us -> 17 us  [call(): pl.pallas_call(kernel, out_shape=[jax.ShapeDtypeStruct(s, d) for s, d in...]
    ppermute x12, waiting for transfers between devices: 3.04 us -> 3.82 us  [over_col(): out.append(lax.ppermute(block, 'col', [(i, i ^ k) for i in range(nc)]))]
  transfers between devices with their start and end apart: 37 -> 37, of which waited for: 12 -> 15; matrix products, arithmetic and copies ran while one was open for 0% -> 0% of each run, Pallas kernels for 17% -> 19%
where the time goes in v7:
time: 71.9 us; the launch traced here: 71.7 us
  starting transfers between devices  34.3 us (48%)
  waiting for transfers between devices  18 us (25%)
  Pallas kernels  17 us (24%)
  local copies, waits for them, and re-layouts  1.21 us (2%)
  between operations  1 us (1%)
    pallas_call x20, Pallas kernels, call(): pl.pallas_call(kernel, out_shape=[jax.ShapeDtypeStruct(s, d) for s, d in...  17 us
    ppermute x16, starting transfers between devices, halo(): out.append(lax.ppermute(f, both, p))  12.4 us
    ppermute x6, starting transfers between devices, reduce_rows(): lax.ppermute(block, 'row', [(i, i ^ 2 * (k + 1)) for i in range(nr)])  8.9 us
    ppermute x12, starting transfers between devices, over_col(): out.append(lax.ppermute(block, 'col', [(i, i ^ k) for i in range(nc)]))  7.66 us
    ppermute x6, waiting for transfers between devices, reduce_rows(): lax.ppermute(block, 'row', [(i, i ^ 2 * (k + 1)) for i in range(nr)])  6.63 us
    ppermute x3, starting transfers between devices, over_pair(): return lax.ppermute(value, 'row', [(i, i ^ 1) for i in range(nr)])  5.27 us
    ppermute x16, waiting for transfers between devices, halo(): out.append(lax.ppermute(f, both, p))  4.43 us
    ppermute x12, waiting for transfers between devices, over_col(): out.append(lax.ppermute(block, 'col', [(i, i ^ k) for i in range(nc)]))  3.82 us
  transfers between devices with their start and end apart: 37, of which 15 were waited for; matrix products, arithmetic and copies ran while one was open for 0% of the time, Pallas kernels for 19%

profile of v7, /device:TPU:0, one launch (start us, length us, event | category | flops | bytes accessed | tf_op | source)
XLA Modules:
  0.0 71.7 jit_solution(2543616222769266179)
XLA Ops:
  0.7 1.2 %copy-done = f32[1024,256]{1,0:T(8,128)S(1)} copy-done((f32[1024,256]{1,0:T(8,128)S(1)}, f32[1024,256]{1,0:T(8,128)}, u32[]{:S(2)}) %copy-start) | copy-done | bytes 1048600
  2.2 3.1 %collective-permute-start.3 = (bf16[96,256]{1,0:T(8,128)(2,1)S(1)}, bf16[96,256]{1,0:T(8,128)(2,1)S(1)}, u32[]{:S(2)}, u32[]{:S(2)}) collective-permute-start(bf16[96,256]{1,0:T(8,128)(2,1)S(1)} %get-tuple-element.46.token.refs_0_), channel_id=1, source_target_pairs={{0,4},{4,0},{8,12},{12,8},{16,20},{20,16},{24,28},{28,24},{1,5},{5... | collective-permute-start | bytes 147464 | tf_op jit(solution)/shard_map/ppermute | solution.py:156
  5.2 0.7 collective-permute-start.2
  5.9 0.8 %collective-permute-start.1 = (bf16[96,256]{1,0:T(8,128)(2,1)S(1)}, bf16[96,256]{1,0:T(8,128)(2,1)S(1)}, u32[]{:S(2)}, u32[]{:S(2)}) collective-permute-start(bf16[96,256]{1,0:T(8,128)(2,1)S(1)} %get-tuple-element.46.token.refs_0_), channel_id=1, source_target_pairs={{0,2},{1,3},{2,0},{3,1},{4,6},{5,7},{6,4},{7,5},{8,10},{9,11},{10,... | collective-permute-start | bytes 147464 | tf_op jit(solution)/shard_map/ppermute | solution.py:152
  7.4 1.1 %collective-permute-start.6 = (bf16[96,256]{1,0:T(8,128)(2,1)S(1)}, bf16[96,256]{1,0:T(8,128)(2,1)S(1)}, u32[]{:S(2)}, u32[]{:S(2)}) collective-permute-start(bf16[96,256]{1,0:T(8,128)(2,1)S(1)} %collective-permute-done.3.refs_4_), channel_id=1, source_target_pairs={{0,3},{1,2},{2,1},{3,0},{4,7},{5,6},{6,5},{7,4},{8,11},{9,10},{10,... | collective-permute-start | bytes 147464 | tf_op jit(solution)/shard_map/ppermute | solution.py:152
  8.5 0.7 %collective-permute-done.2.refs_3_ = bf16[96,256]{1,0:T(8,128)(2,1)S(1)} collective-permute-done((bf16[96,256]{1,0:T(8,128)(2,1)S(1)}, bf16[96,256]{1,0:T(8,128)(2,1)S(1)}, u32[]{:S(2)}, u32[]{:S(2)}) %collective-permute-start.2) | collective-permute-done | bytes 49184 | tf_op jit(solution)/shard_map/ppermute | solution.py:152
  9.2 1.5 %collective-permute-start.5 = (bf16[96,256]{1,0:T(8,128)(2,1)S(1)}, bf16[96,256]{1,0:T(8,128)(2,1)S(1)}, u32[]{:S(2)}, u32[]{:S(2)}) collective-permute-start(bf16[96,256]{1,0:T(8,128)(2,1)S(1)} %collective-permute-done.3.refs_4_), channel_id=1, source_target_pairs={{0,2},{1,3},{2,0},{3,1},{4,6},{5,7},{6,4},{7,5},{8,10},{9,11},{10,... | collective-permute-start | bytes 147464 | tf_op jit(solution)/shard_map/ppermute | solution.py:152
  10.7 0.8 %shard_map.88 = (bf16[512,1024]{1,0:T(8,128)(2,1)S(1)}, bf16[1024,512]{1,0:T(8,128)(2,1)S(1)}, bf16[1024,96]{1,0:T(8,128)(2,1)S(1)}) custom-call(f32[8,128]{1,0:T(8,128)S(1)} %pad_maximum_fusion.table_ref, bf16[96,1024]{1,0:T(8,128)(2,1)S(1)} %copy-done.3, bf16[96,256]{1,0:T(8,128)(2,1)S(1)} %get-tuple-element.46.token.refs_0_), custom_call_target="tpu_custom_call" | custom-call | bytes 249856 | tf_op jit(solution)/shard_map/pallas_call | solution.py:25
  11.6 0.9 %shard_map.89.refs_10_.lb_ref = bf16[1024,96]{1,0:T(8,128)(2,1)S(1)} custom-call(bf16[1024,1024]{1,0:T(8,128)(2,1)S(1)} %copy-done.1, bf16[1024,96]{1,0:T(8,128)(2,1)S(1)} %get-tuple-element.49.bt_ref.refs_5_, bf16[1024,512]{1,0:T(8,128)(2,1)S(1)} %get-tuple-element.50.token.wt_ref), custom_call_target="tpu_custom_call" | custom-call | flops 201326592 | bytes 3342336 | tf_op jit(solution)/shard_map/pallas_call | solution.py:25
  12.5 0.8 %collective-permute-done.5.refs_6_ = bf16[96,256]{1,0:T(8,128)(2,1)S(1)} collective-permute-done((bf16[96,256]{1,0:T(8,128)(2,1)S(1)}, bf16[96,256]{1,0:T(8,128)(2,1)S(1)}, u32[]{:S(2)}, u32[]{:S(2)}) %collective-permute-start.5) | collective-permute-done | bytes 49184 | tf_op jit(solution)/shard_map/ppermute | solution.py:152
  13.3 2.8 %collective-permute-done.7.refs_9_ = bf16[384,384]{1,0:T(8,128)(2,1)S(1)} collective-permute-done((bf16[384,384]{1,0:T(8,128)(2,1)S(1)}, bf16[384,384]{1,0:T(8,128)(2,1)S(1)}, u32[]{:S(2)}, u32[]{:S(2)}) %collective-permute-start.7) | collective-permute-done | bytes 294944 | tf_op jit(solution)/shard_map/ppermute | solution.py:156
  16.6 1.6 %collective-permute-start.8 = (bf16[96,256]{1,0:T(8,128)(2,1)S(1)}, bf16[96,256]{1,0:T(8,128)(2,1)S(1)}, u32[]{:S(2)}, u32[]{:S(2)}) collective-permute-start(bf16[96,256]{1,0:T(8,128)(2,1)S(1)} %get-tuple-element.52), channel_id=1, source_target_pairs={{0,8},{4,12},{8,0},{12,4},{16,24},{20,28},{24,16},{28,20},{1,9},{5... | collective-permute-start | bytes 147464 | tf_op jit(solution)/shard_map/ppermute | solution.py:161
  18.3 2.6 %collective-permute-start.9 = (bf16[96,256]{1,0:T(8,128)(2,1)S(1)}, bf16[96,256]{1,0:T(8,128)(2,1)S(1)}, u32[]{:S(2)}, u32[]{:S(2)}) collective-permute-start(bf16[96,256]{1,0:T(8,128)(2,1)S(1)} %get-tuple-element.53), channel_id=1, source_target_pairs={{0,16},{4,20},{8,24},{12,28},{16,0},{20,4},{24,8},{28,12},{1,17},{... | collective-permute-start | bytes 147464 | tf_op jit(solution)/shard_map/ppermute | solution.py:161
  21.1 2.1 %shard_map.91 = (bf16[512,96]{1,0:T(8,128)(2,1)S(1)}, bf16[512,1024]{1,0:T(8,128)(2,1)S(1)}, bf16[512,512]{1,0:T(8,128)(2,1)S(1)}) custom-call(bf16[512,1024]{1,0:T(8,128)(2,1)S(1)} %get-tuple-element.55.sel_ref, bf16[1024,512]{1,0:T(8,128)(2,1)S(1)} %get-tuple-element.50.token.wt_ref, bf16[1024,1024]{1,0:T(8,128)(2,1)S(1)} %copy-done.2, ...), custom_call_target="tpu_custom_call" | custom-call | flops 1711276032 | bytes 4489216 | tf_op jit(solution)/shard_map/pallas_call | solution.py:25
  23.1 0.6 collective-permute-done.9.refs_2_
  23.8 3.3 %collective-permute-done.10.refs_3_ = bf16[96,256]{1,0:T(8,128)(2,1)S(1)} collective-permute-done((bf16[96,256]{1,0:T(8,128)(2,1)S(1)}, bf16[96,256]{1,0:T(8,128)(2,1)S(1)}, u32[]{:S(2)}, u32[]{:S(2)}) %collective-permute-start.10) | collective-permute-done | bytes 49184 | tf_op jit(solution)/shard_map/ppermute | solution.py:161
  27.4 1.6 %collective-permute-start.12 = (bf16[128,256]{1,0:T(8,128)(2,1)S(1)}, bf16[128,256]{1,0:T(8,128)(2,1)S(1)}, u32[]{:S(2)}, u32[]{:S(2)}) collective-permute-start(bf16[128,256]{1,0:T(8,128)(2,1)S(1)} %get-tuple-element.61), channel_id=1, source_target_pairs={{0,3},{1,2},{2,1},{3,0},{4,7},{5,6},{6,5},{7,4},{8,11},{9,10},{10,... | collective-permute-start | bytes 196616 | tf_op jit(solution)/shard_map/ppermute | solution.py:84
  29.1 0.9 %shard_map.95.base_ref = f32[512,256]{1,0:T(8,128)S(1)} custom-call(bf16[96,256]{1,0:T(8,128)(2,1)S(1)} %get-tuple-element.57.token.y_ref, f32[1024,256]{1,0:T(8,128)S(1)} %copy-done, bf16[1024,96]{1,0:T(8,128)(2,1)S(1)} %shard_map.89.refs_10_.lb_ref, bf16[512,1024]{1,0:T(8,128)(2,1)S(1)} %get-tuple-element.66.si_ref, ...), custom_call_target="tpu_custom_call" | custom-call | flops 268435456 | bytes 2441216 | tf_op jit(solution)/shard_map/pallas_call | solution.py:25
  30.0 0.7 %shard_map.93 = (bf16[96,1024]{1,0:T(8,128)(2,1)S(1)}, bf16[96,512]{1,0:T(8,128)(2,1)S(1)}, f32[96,256]{1,0:T(8,128)S(1)}) custom-call(bf16[96,1024]{1,0:T(8,128)(2,1)S(1)} %copy-done.3, bf16[1024,1024]{1,0:T(8,128)(2,1)S(1)} %copy-done.1, bf16[1024,512]{1,0:T(8,128)(2,1)S(1)} %get-tuple-element.50.token.wt_ref, f32[1024,256]{1,0:T(8,128)S(1)} %copy-done, ...), custom_call_target="tpu_custom_call" | custom-call | flops 352321536 | bytes 4440064 | tf_op jit(solution)/shard_map/pallas_call | solution.py:25
  30.8 0.5 collective-permute-done.12.refs_1_
  31.3 2.0 %collective-permute-done.13.refs_2_ = bf16[128,256]{1,0:T(8,128)(2,1)S(1)} collective-permute-done((bf16[128,256]{1,0:T(8,128)(2,1)S(1)}, bf16[128,256]{1,0:T(8,128)(2,1)S(1)}, u32[]{:S(2)}, u32[]{:S(2)}) %collective-permute-start.13) | collective-permute-done | bytes 65568 | tf_op jit(solution)/shard_map/ppermute | solution.py:84
  33.7 0.6 collective-permute-start.16
  34.3 1.9 %collective-permute-start.17 = (bf16[128,256]{1,0:T(8,128)(2,1)S(1)}, bf16[128,256]{1,0:T(8,128)(2,1)S(1)}, u32[]{:S(2)}, u32[]{:S(2)}) collective-permute-start(bf16[128,256]{1,0:T(8,128)(2,1)S(1)} %get-tuple-element.70.refs_2_), channel_id=1, source_target_pairs={{0,4},{1,5},{2,6},{3,7},{4,0},{5,1},{6,2},{7,3},{8,12},{9,13},{10,... | collective-permute-start | bytes 196616 | tf_op jit(solution)/shard_map/ppermute | solution.py:84
  36.2 0.6 collective-permute-start.18
  36.8 2.0 %shard_map.94 = (f32[1024,256]{1,0:T(8,128)S(1)}, f32[96,256]{1,0:T(8,128)S(1)}) custom-call(bf16[96,256]{1,0:T(8,128)(2,1)S(1)} %get-tuple-element.57.token.y_ref, f32[1024,256]{1,0:T(8,128)S(1)} %copy-done, bf16[1024,96]{1,0:T(8,128)(2,1)S(1)} %shard_map.89.refs_10_.lb_ref, bf16[1024,96]{1,0:T(8,128)(2,1)S(1)} %get-tuple-element.49.bt_ref.refs_5_, ...), custom_call_target="tpu_custom_call" | custom-call | flops 1342177280 | bytes 5193728 | tf_op jit(solution)/shard_map/pallas_call | solution.py:25
  39.4 2.0 %collective-permute-start.22 = (bf16[96,256]{1,0:T(8,128)(2,1)S(1)}, bf16[96,256]{1,0:T(8,128)(2,1)S(1)}, u32[]{:S(2)}, u32[]{:S(2)}) collective-permute-start(bf16[96,256]{1,0:T(8,128)(2,1)S(1)} %shard_map.97.refs_0_), channel_id=1, source_target_pairs={{0,4},{4,0},{8,12},{12,8},{16,20},{20,16},{24,28},{28,24},{1,5},{5... | collective-permute-start | bytes 147464 | tf_op jit(solution)/shard_map/ppermute | solution.py:156
  41.4 1.3 %collective-permute-start.20 = (bf16[96,256]{1,0:T(8,128)(2,1)S(1)}, bf16[96,256]{1,0:T(8,128)(2,1)S(1)}, u32[]{:S(2)}, u32[]{:S(2)}) collective-permute-start(bf16[96,256]{1,0:T(8,128)(2,1)S(1)} %shard_map.97.refs_0_), channel_id=1, source_target_pairs={{0,2},{1,3},{2,0},{3,1},{4,6},{5,7},{6,4},{7,5},{8,10},{9,11},{10,... | collective-permute-start | bytes 147464 | tf_op jit(solution)/shard_map/ppermute | solution.py:152
  42.7 0.5 collective-permute-start.19
  43.5 1.3 %collective-permute-start.24 = (bf16[96,256]{1,0:T(8,128)(2,1)S(1)}, bf16[96,256]{1,0:T(8,128)(2,1)S(1)}, u32[]{:S(2)}, u32[]{:S(2)}) collective-permute-start(bf16[96,256]{1,0:T(8,128)(2,1)S(1)} %collective-permute-done.22.refs_4_), channel_id=1, source_target_pairs={{0,2},{1,3},{2,0},{3,1},{4,6},{5,7},{6,4},{7,5},{8,10},{9,11},{10,... | collective-permute-start | bytes 147464 | tf_op jit(solution)/shard_map/ppermute | solution.py:152
  44.8 0.5 collective-permute-done.21.refs_3_
  45.4 1.2 %shard_map.98.refs_10_.base_ref = f32[1024,256]{1,0:T(8,128)S(1)} custom-call(f32[1024,256]{1,0:T(8,128)S(1)} %get-tuple-element.72.sol_ref.refs_4_, bf16[1024,1024]{1,0:T(8,128)(2,1)S(1)} %copy-done.1, f32[1024,256]{1,0:T(8,128)S(1)} %copy-done, bf16[1024,512]{1,0:T(8,128)(2,1)S(1)} %get-tuple-element.50.token.wt_ref, ...), custom_call_target="tpu_custom_call" | custom-call | flops 805306368 | bytes 5505024 | tf_op jit(solution)/shard_map/pallas_call | solution.py:25
  46.7 0.9 %collective-permute-done.25.refs_7_ = bf16[96,256]{1,0:T(8,128)(2,1)S(1)} collective-permute-done((bf16[96,256]{1,0:T(8,128)(2,1)S(1)}, bf16[96,256]{1,0:T(8,128)(2,1)S(1)}, u32[]{:S(2)}, u32[]{:S(2)}) %collective-permute-start.25) | collective-permute-done | bytes 49184 | tf_op jit(solution)/shard_map/ppermute | solution.py:152
  47.6 0.8 %collective-permute-done.24.refs_6_ = bf16[96,256]{1,0:T(8,128)(2,1)S(1)} collective-permute-done((bf16[96,256]{1,0:T(8,128)(2,1)S(1)}, bf16[96,256]{1,0:T(8,128)(2,1)S(1)}, u32[]{:S(2)}, u32[]{:S(2)}) %collective-permute-start.24) | collective-permute-done | bytes 49184 | tf_op jit(solution)/shard_map/ppermute | solution.py:152
  48.8 1.5 %collective-permute-start.26 = (bf16[96,256]{1,0:T(8,128)(2,1)S(1)}, bf16[96,256]{1,0:T(8,128)(2,1)S(1)}, u32[]{:S(2)}, u32[]{:S(2)}) collective-permute-start(bf16[96,256]{1,0:T(8,128)(2,1)S(1)} %get-tuple-element.74), channel_id=1, source_target_pairs={{0,8},{4,12},{8,0},{12,4},{16,24},{20,28},{24,16},{28,20},{1,9},{5... | collective-permute-start | bytes 147464 | tf_op jit(solution)/shard_map/ppermute | solution.py:161
  50.3 0.9 %collective-permute-start.27 = (bf16[96,256]{1,0:T(8,128)(2,1)S(1)}, bf16[96,256]{1,0:T(8,128)(2,1)S(1)}, u32[]{:S(2)}, u32[]{:S(2)}) collective-permute-start(bf16[96,256]{1,0:T(8,128)(2,1)S(1)} %get-tuple-element.75), channel_id=1, source_target_pairs={{0,16},{4,20},{8,24},{12,28},{16,0},{20,4},{24,8},{28,12},{1,17},{... | collective-permute-start | bytes 147464 | tf_op jit(solution)/shard_map/ppermute | solution.py:161
  51.2 2.0 %collective-permute-start.28 = (bf16[96,256]{1,0:T(8,128)(2,1)S(1)}, bf16[96,256]{1,0:T(8,128)(2,1)S(1)}, u32[]{:S(2)}, u32[]{:S(2)}) collective-permute-start(bf16[96,256]{1,0:T(8,128)(2,1)S(1)} %get-tuple-element.76), channel_id=1, source_target_pairs={{0,24},{4,28},{8,16},{12,20},{16,8},{20,12},{24,0},{28,4},{1,25},{... | collective-permute-start | bytes 147464 | tf_op jit(solution)/shard_map/ppermute | solution.py:161
  53.2 1.4 %shard_map.100.refs_5_.m_ref = bf16[1024,512]{1,0:T(8,128)(2,1)S(1)} custom-call(bf16[1024,1024]{1,0:T(8,128)(2,1)S(1)} %copy-done.2, bf16[1024,512]{1,0:T(8,128)(2,1)S(1)} %get-tuple-element.50.token.wt_ref, f32[96,256]{1,0:T(8,128)S(1)} %get-tuple-element.73.token.refs_0_), custom_call_target="tpu_custom_call" | custom-call | flops 1073741824 | bytes 3244032 | tf_op jit(solution)/shard_map/pallas_call | solution.py:25
  54.7 2.7 %collective-permute-done.27.refs_2_ = bf16[96,256]{1,0:T(8,128)(2,1)S(1)} collective-permute-done((bf16[96,256]{1,0:T(8,128)(2,1)S(1)}, bf16[96,256]{1,0:T(8,128)(2,1)S(1)}, u32[]{:S(2)}, u32[]{:S(2)}) %collective-permute-start.27) | collective-permute-done | bytes 49184 | tf_op jit(solution)/shard_map/ppermute | solution.py:161
  57.6 1.0 %collective-permute-start.30 = (bf16[128,256]{1,0:T(8,128)(2,1)S(1)}, bf16[128,256]{1,0:T(8,128)(2,1)S(1)}, u32[]{:S(2)}, u32[]{:S(2)}) collective-permute-start(bf16[128,256]{1,0:T(8,128)(2,1)S(1)} %get-tuple-element.80), channel_id=1, source_target_pairs={{0,3},{1,2},{2,1},{3,0},{4,7},{5,6},{6,5},{7,4},{8,11},{9,10},{10,... | collective-permute-start | bytes 196616 | tf_op jit(solution)/shard_map/ppermute | solution.py:84
  58.7 1.5 %collective-permute-start.31 = (bf16[128,256]{1,0:T(8,128)(2,1)S(1)}, bf16[128,256]{1,0:T(8,128)(2,1)S(1)}, u32[]{:S(2)}, u32[]{:S(2)}) collective-permute-start(bf16[128,256]{1,0:T(8,128)(2,1)S(1)} %get-tuple-element.81), channel_id=1, source_target_pairs={{0,4},{1,5},{2,6},{3,7},{4,0},{5,1},{6,2},{7,3},{8,12},{9,13},{10,... | collective-permute-start | bytes 196616 | tf_op jit(solution)/shard_map/ppermute | solution.py:84
  60.2 0.8 %collective-permute-start.32 = (bf16[128,256]{1,0:T(8,128)(2,1)S(1)}, bf16[128,256]{1,0:T(8,128)(2,1)S(1)}, u32[]{:S(2)}, u32[]{:S(2)}) collective-permute-start(bf16[128,256]{1,0:T(8,128)(2,1)S(1)} %get-tuple-element.82), channel_id=1, source_target_pairs={{0,1},{1,0},{2,3},{3,2},{4,5},{5,4},{6,7},{7,6},{8,9},{9,8},{10,11... | collective-permute-start | bytes 196616 | tf_op jit(solution)/shard_map/ppermute | solution.py:84
  60.9 1.9 %shard_map.102 = (f32[512,256]{1,0:T(8,128)S(1)}, f32[1024,256]{1,0:T(8,128)S(1)}) custom-call(bf16[96,256]{1,0:T(8,128)(2,1)S(1)} %get-tuple-element.77.y_ref, f32[1024,256]{1,0:T(8,128)S(1)} %shard_map.98.refs_10_.base_ref, bf16[1024,96]{1,0:T(8,128)(2,1)S(1)} %shard_map.89.refs_10_.lb_ref, bf16[512,1024]{1,0:T(8,128)(2,1)S(1)} %get-tuple-element.66.si_ref, ...), custom_call_target="tpu_custom_call" | custom-call | flops 268435456 | bytes 6045696 | tf_op jit(solution)/shard_map/pallas_call | solution.py:25
  62.9 0.6 collective-permute-done.31.refs_2_
  63.9 1.2 %collective-permute-start.34 = (bf16[128,256]{1,0:T(8,128)(2,1)S(1)}, bf16[128,256]{1,0:T(8,128)(2,1)S(1)}, u32[]{:S(2)}, u32[]{:S(2)}) collective-permute-start(bf16[128,256]{1,0:T(8,128)(2,1)S(1)} %get-tuple-element.87), channel_id=1, source_target_pairs={{0,3},{1,2},{2,1},{3,0},{4,7},{5,6},{6,5},{7,4},{8,11},{9,10},{10,... | collective-permute-start | bytes 196616 | tf_op jit(solution)/shard_map/ppermute | solution.py:84
  65.1 2.4 %collective-permute-start.35 = (bf16[128,256]{1,0:T(8,128)(2,1)S(1)}, bf16[128,256]{1,0:T(8,128)(2,1)S(1)}, u32[]{:S(2)}, u32[]{:S(2)}) collective-permute-start(bf16[128,256]{1,0:T(8,128)(2,1)S(1)} %get-tuple-element.88), channel_id=1, source_target_pairs={{0,4},{1,5},{2,6},{3,7},{4,0},{5,1},{6,2},{7,3},{8,12},{9,13},{10,... | collective-permute-start | bytes 196616 | tf_op jit(solution)/shard_map/ppermute | solution.py:84
  67.9 1.6 %shard_map.103 = (f32[1024,256]{1,0:T(8,128)}, f32[1024,256]{1,0:T(8,128)S(1)}) custom-call(f32[1024,256]{1,0:T(8,128)S(1)} %get-tuple-element.78.pre_ref, bf16[1024,512]{1,0:T(8,128)(2,1)S(1)} %shard_map.100.refs_5_.m_ref, f32[1024,256]{1,0:T(8,128)S(1)} %copy-done, bf16[1024,1024]{1,0:T(8,128)(2,1)S(1)} %copy-done.1, ...), custom_call_target="tpu_custom_call" | custom-call | flops 805306368 | bytes 5505024 | tf_op jit(solution)/shard_map/pallas_call | solution.py:25
  69.5 0.9 %collective-permute-done.35.refs_2_ = bf16[128,256]{1,0:T(8,128)(2,1)S(1)} collective-permute-done((bf16[128,256]{1,0:T(8,128)(2,1)S(1)}, bf16[128,256]{1,0:T(8,128)(2,1)S(1)}, u32[]{:S(2)}, u32[]{:S(2)}) %collective-permute-start.35) | collective-permute-done | bytes 65568 | tf_op jit(solution)/shard_map/ppermute | solution.py:84
  70.4 1.3 %shard_map.105 = f32[1024,256]{1,0:T(8,128)} custom-call(f32[1024,256]{1,0:T(8,128)S(1)} %get-tuple-element.84.res_ref, bf16[1024,512]{1,0:T(8,128)(2,1)S(1)} %get-tuple-element.50.token.wt_ref, bf16[128,256]{1,0:T(8,128)(2,1)S(1)} %collective-permute-done.33.refs_0_, bf16[128,256]{1,0:T(8,128)(2,1)S(1)} %collective-permute-done.34.refs_1_, ...), custom_call_target="tpu_custom_call" | custom-call | flops 268435456 | bytes 2359296 | tf_op jit(solution)/shard_map/pallas_call | solution.py:25
  (63 shorter events, 4.9 us)
Async XLA Ops:
  0.6 1.2 %copy-start = (f32[1024,256]{1,0:T(8,128)S(1)}, f32[1024,256]{1,0:T(8,128)}, u32[]{:S(2)}) copy-start(f32[1024,256]{1,0:T(8,128)} %rhs_ref.5) | copy-start | bytes 3145732
  0.6 1.2 %copy-start.3 = (bf16[96,1024]{1,0:T(8,128)(2,1)S(1)}, bf16[96,1024]{1,0:T(8,128)(2,1)}, u32[]{:S(2)}) copy-start(bf16[96,1024]{1,0:T(8,128)(2,1)} %basis_ref.3) | copy-start | bytes 589828
  0.7 1.5 %copy-start.4 = (bf16[768,384]{1,0:T(8,128)(2,1)S(1)}, bf16[768,384]{1,0:T(8,128)(2,1)}, u32[]{:S(2)}) copy-start(bf16[768,384]{1,0:T(8,128)(2,1)} %inv_ref.4) | copy-start | bytes 1769476
  0.7 6.7 %copy-start.5 = (s32[1,4,128]{2,1,0:T(4,128)S(1)}, s32[1,4,128]{2,1,0:T(4,128)}, u32[]{:S(2)}) copy-start(s32[1,4,128]{2,1,0:T(4,128)} %param.13) | copy-start | bytes 6148
  0.7 10.1 %copy-start.6 = (f32[1,4,128]{2,1,0:T(4,128)S(1)}, f32[1,4,128]{2,1,0:T(4,128)}, u32[]{:S(2)}) copy-start(f32[1,4,128]{2,1,0:T(4,128)} %param.12) | copy-start | bytes 6148
  1.9 9.7 %copy-start.1 = (bf16[1024,1024]{1,0:T(8,128)(2,1)S(1)}, bf16[1024,1024]{1,0:T(8,128)(2,1)}, u32[]{:S(2)}) copy-start(bf16[1024,1024]{1,0:T(8,128)(2,1)} %mat_ref.7) | copy-start | bytes 6291460
  2.2 5.2 %collective-permute-start.3 = (bf16[96,256]{1,0:T(8,128)(2,1)S(1)}, bf16[96,256]{1,0:T(8,128)(2,1)S(1)}, u32[]{:S(2)}, u32[]{:S(2)}) collective-permute-start(bf16[96,256]{1,0:T(8,128)(2,1)S(1)} %get-tuple-element.46.token.refs_0_), channel_id=1, source_target_pairs={{0,4},{4,0},{8,12},{12,8},{16,20},{20,16},{24,28},{28,24},{1,5},{5... | collective-permute-start | bytes 147464 | tf_op jit(solution)/shard_map/ppermute | solution.py:156
  5.2 4.0 %collective-permute-start.2 = (bf16[96,256]{1,0:T(8,128)(2,1)S(1)}, bf16[96,256]{1,0:T(8,128)(2,1)S(1)}, u32[]{:S(2)}, u32[]{:S(2)}) collective-permute-start(bf16[96,256]{1,0:T(8,128)(2,1)S(1)} %get-tuple-element.46.token.refs_0_), channel_id=1, source_target_pairs={{0,3},{1,2},{2,1},{3,0},{4,7},{5,6},{6,5},{7,4},{8,11},{9,10},{10,... | collective-permute-start | bytes 147464 | tf_op jit(solution)/shard_map/ppermute | solution.py:152
  5.9 4.8 %collective-permute-start.1 = (bf16[96,256]{1,0:T(8,128)(2,1)S(1)}, bf16[96,256]{1,0:T(8,128)(2,1)S(1)}, u32[]{:S(2)}, u32[]{:S(2)}) collective-permute-start(bf16[96,256]{1,0:T(8,128)(2,1)S(1)} %get-tuple-element.46.token.refs_0_), channel_id=1, source_target_pairs={{0,2},{1,3},{2,0},{3,1},{4,6},{5,7},{6,4},{7,5},{8,10},{9,11},{10,... | collective-permute-start | bytes 147464 | tf_op jit(solution)/shard_map/ppermute | solution.py:152
  6.7 5.7 %collective-permute-start = (bf16[96,256]{1,0:T(8,128)(2,1)S(1)}, bf16[96,256]{1,0:T(8,128)(2,1)S(1)}, u32[]{:S(2)}, u32[]{:S(2)}) collective-permute-start(bf16[96,256]{1,0:T(8,128)(2,1)S(1)} %get-tuple-element.46.token.refs_0_), channel_id=1, source_target_pairs={{0,1},{1,0},{2,3},{3,2},{4,5},{5,4},{6,7},{7,6},{8,9},{9,8},{10,11... | collective-permute-start | bytes 147464 | tf_op jit(solution)/shard_map/ppermute | solution.py:152
  7.1 9.1 %collective-permute-start.7 = (bf16[384,384]{1,0:T(8,128)(2,1)S(1)}, bf16[384,384]{1,0:T(8,128)(2,1)S(1)}, u32[]{:S(2)}, u32[]{:S(2)}) collective-permute-start(bf16[384,384]{1,0:T(8,128)(2,1)S(1)} %get-tuple-element.48), channel_id=1, source_target_pairs={{0,4},{4,0},{8,12},{12,8},{16,20},{20,16},{24,28},{28,24},{1,5},{5... | collective-permute-start | bytes 884744 | tf_op jit(solution)/shard_map/ppermute | solution.py:156
  7.4 5.1 %collective-permute-start.6 = (bf16[96,256]{1,0:T(8,128)(2,1)S(1)}, bf16[96,256]{1,0:T(8,128)(2,1)S(1)}, u32[]{:S(2)}, u32[]{:S(2)}) collective-permute-start(bf16[96,256]{1,0:T(8,128)(2,1)S(1)} %collective-permute-done.3.refs_4_), channel_id=1, source_target_pairs={{0,3},{1,2},{2,1},{3,0},{4,7},{5,6},{6,5},{7,4},{8,11},{9,10},{10,... | collective-permute-start | bytes 147464 | tf_op jit(solution)/shard_map/ppermute | solution.py:152
  9.2 4.1 %collective-permute-start.5 = (bf16[96,256]{1,0:T(8,128)(2,1)S(1)}, bf16[96,256]{1,0:T(8,128)(2,1)S(1)}, u32[]{:S(2)}, u32[]{:S(2)}) collective-permute-start(bf16[96,256]{1,0:T(8,128)(2,1)S(1)} %collective-permute-done.3.refs_4_), channel_id=1, source_target_pairs={{0,2},{1,3},{2,0},{3,1},{4,6},{5,7},{6,4},{7,5},{8,10},{9,11},{10,... | collective-permute-start | bytes 147464 | tf_op jit(solution)/shard_map/ppermute | solution.py:152
  10.7 2.6 %collective-permute-start.4 = (bf16[96,256]{1,0:T(8,128)(2,1)S(1)}, bf16[96,256]{1,0:T(8,128)(2,1)S(1)}, u32[]{:S(2)}, u32[]{:S(2)}) collective-permute-start(bf16[96,256]{1,0:T(8,128)(2,1)S(1)} %collective-permute-done.3.refs_4_), channel_id=1, source_target_pairs={{0,1},{1,0},{2,3},{3,2},{4,5},{5,4},{6,7},{7,6},{8,9},{9,8},{10,11... | collective-permute-start | bytes 147464 | tf_op jit(solution)/shard_map/ppermute | solution.py:152
  11.6 9.5 %copy-start.2 = (bf16[1024,1024]{1,0:T(8,128)(2,1)S(1)}, bf16[1024,1024]{1,0:T(8,128)(2,1)}, u32[]{:S(2)}) copy-start(bf16[1024,1024]{1,0:T(8,128)(2,1)} %refs_6_.1) | copy-start | bytes 6291460
  16.6 6.5 %collective-permute-start.8 = (bf16[96,256]{1,0:T(8,128)(2,1)S(1)}, bf16[96,256]{1,0:T(8,128)(2,1)S(1)}, u32[]{:S(2)}, u32[]{:S(2)}) collective-permute-start(bf16[96,256]{1,0:T(8,128)(2,1)S(1)} %get-tuple-element.52), channel_id=1, source_target_pairs={{0,8},{4,12},{8,0},{12,4},{16,24},{20,28},{24,16},{28,20},{1,9},{5... | collective-permute-start | bytes 147464 | tf_op jit(solution)/shard_map/ppermute | solution.py:161
  18.3 5.5 %collective-permute-start.9 = (bf16[96,256]{1,0:T(8,128)(2,1)S(1)}, bf16[96,256]{1,0:T(8,128)(2,1)S(1)}, u32[]{:S(2)}, u32[]{:S(2)}) collective-permute-start(bf16[96,256]{1,0:T(8,128)(2,1)S(1)} %get-tuple-element.53), channel_id=1, source_target_pairs={{0,16},{4,20},{8,24},{12,28},{16,0},{20,4},{24,8},{28,12},{1,17},{... | collective-permute-start | bytes 147464 | tf_op jit(solution)/shard_map/ppermute | solution.py:161
  20.8 6.3 %collective-permute-start.10 = (bf16[96,256]{1,0:T(8,128)(2,1)S(1)}, bf16[96,256]{1,0:T(8,128)(2,1)S(1)}, u32[]{:S(2)}, u32[]{:S(2)}) collective-permute-start(bf16[96,256]{1,0:T(8,128)(2,1)S(1)} %get-tuple-element.54), channel_id=1, source_target_pairs={{0,24},{4,28},{8,16},{12,20},{16,8},{20,12},{24,0},{28,4},{1,25},{... | collective-permute-start | bytes 147464 | tf_op jit(solution)/shard_map/ppermute | solution.py:161
  27.3 3.4 %collective-permute-start.11 = (bf16[128,256]{1,0:T(8,128)(2,1)S(1)}, bf16[128,256]{1,0:T(8,128)(2,1)S(1)}, u32[]{:S(2)}, u32[]{:S(2)}) collective-permute-start(bf16[128,256]{1,0:T(8,128)(2,1)S(1)} %get-tuple-element.60), channel_id=1, source_target_pairs={{0,1},{1,0},{2,3},{3,2},{4,8},{5,9},{6,10},{7,11},{8,4},{9,5},{10,... | collective-permute-start | bytes 196616 | tf_op jit(solution)/shard_map/ppermute | solution.py:84
  27.4 3.8 %collective-permute-start.12 = (bf16[128,256]{1,0:T(8,128)(2,1)S(1)}, bf16[128,256]{1,0:T(8,128)(2,1)S(1)}, u32[]{:S(2)}, u32[]{:S(2)}) collective-permute-start(bf16[128,256]{1,0:T(8,128)(2,1)S(1)} %get-tuple-element.61), channel_id=1, source_target_pairs={{0,3},{1,2},{2,1},{3,0},{4,7},{5,6},{6,5},{7,4},{8,11},{9,10},{10,... | collective-permute-start | bytes 196616 | tf_op jit(solution)/shard_map/ppermute | solution.py:84
  29.0 4.3 %collective-permute-start.13 = (bf16[128,256]{1,0:T(8,128)(2,1)S(1)}, bf16[128,256]{1,0:T(8,128)(2,1)S(1)}, u32[]{:S(2)}, u32[]{:S(2)}) collective-permute-start(bf16[128,256]{1,0:T(8,128)(2,1)S(1)} %get-tuple-element.62), channel_id=1, source_target_pairs={{0,4},{1,5},{2,6},{3,7},{4,0},{5,1},{6,2},{7,3},{8,12},{9,13},{10,... | collective-permute-start | bytes 196616 | tf_op jit(solution)/shard_map/ppermute | solution.py:84
  29.0 4.3 %collective-permute-start.14 = (bf16[128,256]{1,0:T(8,128)(2,1)S(1)}, bf16[128,256]{1,0:T(8,128)(2,1)S(1)}, u32[]{:S(2)}, u32[]{:S(2)}) collective-permute-start(bf16[128,256]{1,0:T(8,128)(2,1)S(1)} %get-tuple-element.63), channel_id=1, source_target_pairs={{0,1},{1,0},{2,3},{3,2},{4,5},{5,4},{6,7},{7,6},{8,9},{9,8},{10,11... | collective-permute-start | bytes 196616 | tf_op jit(solution)/shard_map/ppermute | solution.py:84
  33.6 5.2 %collective-permute-start.15 = (bf16[128,256]{1,0:T(8,128)(2,1)S(1)}, bf16[128,256]{1,0:T(8,128)(2,1)S(1)}, u32[]{:S(2)}, u32[]{:S(2)}) collective-permute-start(bf16[128,256]{1,0:T(8,128)(2,1)S(1)} %get-tuple-element.68.refs_0_), channel_id=1, source_target_pairs={{0,1},{1,0},{2,3},{3,2},{4,8},{5,9},{6,10},{7,11},{8,4},{9,5},{10,... | collective-permute-start | bytes 196616 | tf_op jit(solution)/shard_map/ppermute | solution.py:84
  33.7 5.1 %collective-permute-start.16 = (bf16[128,256]{1,0:T(8,128)(2,1)S(1)}, bf16[128,256]{1,0:T(8,128)(2,1)S(1)}, u32[]{:S(2)}, u32[]{:S(2)}) collective-permute-start(bf16[128,256]{1,0:T(8,128)(2,1)S(1)} %get-tuple-element.69.refs_1_), channel_id=1, source_target_pairs={{0,3},{1,2},{2,1},{3,0},{4,7},{5,6},{6,5},{7,4},{8,11},{9,10},{10,... | collective-permute-start | bytes 196616 | tf_op jit(solution)/shard_map/ppermute | solution.py:84
  34.3 4.9 %collective-permute-start.17 = (bf16[128,256]{1,0:T(8,128)(2,1)S(1)}, bf16[128,256]{1,0:T(8,128)(2,1)S(1)}, u32[]{:S(2)}, u32[]{:S(2)}) collective-permute-start(bf16[128,256]{1,0:T(8,128)(2,1)S(1)} %get-tuple-element.70.refs_2_), channel_id=1, source_target_pairs={{0,4},{1,5},{2,6},{3,7},{4,0},{5,1},{6,2},{7,3},{8,12},{9,13},{10,... | collective-permute-start | bytes 196616 | tf_op jit(solution)/shard_map/ppermute | solution.py:84
  36.2 3.0 %collective-permute-start.18 = (bf16[128,256]{1,0:T(8,128)(2,1)S(1)}, bf16[128,256]{1,0:T(8,128)(2,1)S(1)}, u32[]{:S(2)}, u32[]{:S(2)}) collective-permute-start(bf16[128,256]{1,0:T(8,128)(2,1)S(1)} %get-tuple-element.71.refs_3_), channel_id=1, source_target_pairs={{0,1},{1,0},{2,3},{3,2},{4,5},{5,4},{6,7},{7,6},{8,9},{9,8},{10,11... | collective-permute-start | bytes 196616 | tf_op jit(solution)/shard_map/ppermute | solution.py:84
  39.4 4.2 %collective-permute-start.22 = (bf16[96,256]{1,0:T(8,128)(2,1)S(1)}, bf16[96,256]{1,0:T(8,128)(2,1)S(1)}, u32[]{:S(2)}, u32[]{:S(2)}) collective-permute-start(bf16[96,256]{1,0:T(8,128)(2,1)S(1)} %shard_map.97.refs_0_), channel_id=1, source_target_pairs={{0,4},{4,0},{8,12},{12,8},{16,20},{20,16},{24,28},{28,24},{1,5},{5... | collective-permute-start | bytes 147464 | tf_op jit(solution)/shard_map/ppermute | solution.py:156
  41.3 4.0 %collective-permute-start.21 = (bf16[96,256]{1,0:T(8,128)(2,1)S(1)}, bf16[96,256]{1,0:T(8,128)(2,1)S(1)}, u32[]{:S(2)}, u32[]{:S(2)}) collective-permute-start(bf16[96,256]{1,0:T(8,128)(2,1)S(1)} %shard_map.97.refs_0_), channel_id=1, source_target_pairs={{0,3},{1,2},{2,1},{3,0},{4,7},{5,6},{6,5},{7,4},{8,11},{9,10},{10,... | collective-permute-start | bytes 147464 | tf_op jit(solution)/shard_map/ppermute | solution.py:152
  41.4 5.3 %collective-permute-start.20 = (bf16[96,256]{1,0:T(8,128)(2,1)S(1)}, bf16[96,256]{1,0:T(8,128)(2,1)S(1)}, u32[]{:S(2)}, u32[]{:S(2)}) collective-permute-start(bf16[96,256]{1,0:T(8,128)(2,1)S(1)} %shard_map.97.refs_0_), channel_id=1, source_target_pairs={{0,2},{1,3},{2,0},{3,1},{4,6},{5,7},{6,4},{7,5},{8,10},{9,11},{10,... | collective-permute-start | bytes 147464 | tf_op jit(solution)/shard_map/ppermute | solution.py:152
  42.7 4.0 %collective-permute-start.19 = (bf16[96,256]{1,0:T(8,128)(2,1)S(1)}, bf16[96,256]{1,0:T(8,128)(2,1)S(1)}, u32[]{:S(2)}, u32[]{:S(2)}) collective-permute-start(bf16[96,256]{1,0:T(8,128)(2,1)S(1)} %shard_map.97.refs_0_), channel_id=1, source_target_pairs={{0,1},{1,0},{2,3},{3,2},{4,5},{5,4},{6,7},{7,6},{8,9},{9,8},{10,11... | collective-permute-start | bytes 147464 | tf_op jit(solution)/shard_map/ppermute | solution.py:152
  43.5 4.0 %collective-permute-start.25 = (bf16[96,256]{1,0:T(8,128)(2,1)S(1)}, bf16[96,256]{1,0:T(8,128)(2,1)S(1)}, u32[]{:S(2)}, u32[]{:S(2)}) collective-permute-start(bf16[96,256]{1,0:T(8,128)(2,1)S(1)} %collective-permute-done.22.refs_4_), channel_id=1, source_target_pairs={{0,3},{1,2},{2,1},{3,0},{4,7},{5,6},{6,5},{7,4},{8,11},{9,10},{10,... | collective-permute-start | bytes 147464 | tf_op jit(solution)/shard_map/ppermute | solution.py:152
  43.5 4.8 %collective-permute-start.24 = (bf16[96,256]{1,0:T(8,128)(2,1)S(1)}, bf16[96,256]{1,0:T(8,128)(2,1)S(1)}, u32[]{:S(2)}, u32[]{:S(2)}) collective-permute-start(bf16[96,256]{1,0:T(8,128)(2,1)S(1)} %collective-permute-done.22.refs_4_), channel_id=1, source_target_pairs={{0,2},{1,3},{2,0},{3,1},{4,6},{5,7},{6,4},{7,5},{8,10},{9,11},{10,... | collective-permute-start | bytes 147464 | tf_op jit(solution)/shard_map/ppermute | solution.py:152
  45.4 3.0 %collective-permute-start.23 = (bf16[96,256]{1,0:T(8,128)(2,1)S(1)}, bf16[96,256]{1,0:T(8,128)(2,1)S(1)}, u32[]{:S(2)}, u32[]{:S(2)}) collective-permute-start(bf16[96,256]{1,0:T(8,128)(2,1)S(1)} %collective-permute-done.22.refs_4_), channel_id=1, source_target_pairs={{0,1},{1,0},{2,3},{3,2},{4,5},{5,4},{6,7},{7,6},{8,9},{9,8},{10,11... | collective-permute-start | bytes 147464 | tf_op jit(solution)/shard_map/ppermute | solution.py:152
  48.8 5.9 %collective-permute-start.26 = (bf16[96,256]{1,0:T(8,128)(2,1)S(1)}, bf16[96,256]{1,0:T(8,128)(2,1)S(1)}, u32[]{:S(2)}, u32[]{:S(2)}) collective-permute-start(bf16[96,256]{1,0:T(8,128)(2,1)S(1)} %get-tuple-element.74), channel_id=1, source_target_pairs={{0,8},{4,12},{8,0},{12,4},{16,24},{20,28},{24,16},{28,20},{1,9},{5... | collective-permute-start | bytes 147464 | tf_op jit(solution)/shard_map/ppermute | solution.py:161
  50.3 7.0 %collective-permute-start.27 = (bf16[96,256]{1,0:T(8,128)(2,1)S(1)}, bf16[96,256]{1,0:T(8,128)(2,1)S(1)}, u32[]{:S(2)}, u32[]{:S(2)}) collective-permute-start(bf16[96,256]{1,0:T(8,128)(2,1)S(1)} %get-tuple-element.75), channel_id=1, source_target_pairs={{0,16},{4,20},{8,24},{12,28},{16,0},{20,4},{24,8},{28,12},{1,17},{... | collective-permute-start | bytes 147464 | tf_op jit(solution)/shard_map/ppermute | solution.py:161
  51.2 6.1 %collective-permute-start.28 = (bf16[96,256]{1,0:T(8,128)(2,1)S(1)}, bf16[96,256]{1,0:T(8,128)(2,1)S(1)}, u32[]{:S(2)}, u32[]{:S(2)}) collective-permute-start(bf16[96,256]{1,0:T(8,128)(2,1)S(1)} %get-tuple-element.76), channel_id=1, source_target_pairs={{0,24},{4,28},{8,16},{12,20},{16,8},{20,12},{24,0},{28,4},{1,25},{... | collective-permute-start | bytes 147464 | tf_op jit(solution)/shard_map/ppermute | solution.py:161
  57.6 5.3 %collective-permute-start.29 = (bf16[128,256]{1,0:T(8,128)(2,1)S(1)}, bf16[128,256]{1,0:T(8,128)(2,1)S(1)}, u32[]{:S(2)}, u32[]{:S(2)}) collective-permute-start(bf16[128,256]{1,0:T(8,128)(2,1)S(1)} %get-tuple-element.79), channel_id=1, source_target_pairs={{0,1},{1,0},{2,3},{3,2},{4,8},{5,9},{6,10},{7,11},{8,4},{9,5},{10,... | collective-permute-start | bytes 196616 | tf_op jit(solution)/shard_map/ppermute | solution.py:84
  57.6 5.2 %collective-permute-start.30 = (bf16[128,256]{1,0:T(8,128)(2,1)S(1)}, bf16[128,256]{1,0:T(8,128)(2,1)S(1)}, u32[]{:S(2)}, u32[]{:S(2)}) collective-permute-start(bf16[128,256]{1,0:T(8,128)(2,1)S(1)} %get-tuple-element.80), channel_id=1, source_target_pairs={{0,3},{1,2},{2,1},{3,0},{4,7},{5,6},{6,5},{7,4},{8,11},{9,10},{10,... | collective-permute-start | bytes 196616 | tf_op jit(solution)/shard_map/ppermute | solution.py:84
  58.7 4.8 %collective-permute-start.31 = (bf16[128,256]{1,0:T(8,128)(2,1)S(1)}, bf16[128,256]{1,0:T(8,128)(2,1)S(1)}, u32[]{:S(2)}, u32[]{:S(2)}) collective-permute-start(bf16[128,256]{1,0:T(8,128)(2,1)S(1)} %get-tuple-element.81), channel_id=1, source_target_pairs={{0,4},{1,5},{2,6},{3,7},{4,0},{5,1},{6,2},{7,3},{8,12},{9,13},{10,... | collective-permute-start | bytes 196616 | tf_op jit(solution)/shard_map/ppermute | solution.py:84
  60.2 3.3 %collective-permute-start.32 = (bf16[128,256]{1,0:T(8,128)(2,1)S(1)}, bf16[128,256]{1,0:T(8,128)(2,1)S(1)}, u32[]{:S(2)}, u32[]{:S(2)}) collective-permute-start(bf16[128,256]{1,0:T(8,128)(2,1)S(1)} %get-tuple-element.82), channel_id=1, source_target_pairs={{0,1},{1,0},{2,3},{3,2},{4,5},{5,4},{6,7},{7,6},{8,9},{9,8},{10,11... | collective-permute-start | bytes 196616 | tf_op jit(solution)/shard_map/ppermute | solution.py:84
  63.8 5.7 %collective-permute-start.33 = (bf16[128,256]{1,0:T(8,128)(2,1)S(1)}, bf16[128,256]{1,0:T(8,128)(2,1)S(1)}, u32[]{:S(2)}, u32[]{:S(2)}) collective-permute-start(bf16[128,256]{1,0:T(8,128)(2,1)S(1)} %get-tuple-element.86), channel_id=1, source_target_pairs={{0,1},{1,0},{2,3},{3,2},{4,8},{5,9},{6,10},{7,11},{8,4},{9,5},{10,... | collective-permute-start | bytes 196616 | tf_op jit(solution)/shard_map/ppermute | solution.py:84
  63.9 5.6 %collective-permute-start.34 = (bf16[128,256]{1,0:T(8,128)(2,1)S(1)}, bf16[128,256]{1,0:T(8,128)(2,1)S(1)}, u32[]{:S(2)}, u32[]{:S(2)}) collective-permute-start(bf16[128,256]{1,0:T(8,128)(2,1)S(1)} %get-tuple-element.87), channel_id=1, source_target_pairs={{0,3},{1,2},{2,1},{3,0},{4,7},{5,6},{6,5},{7,4},{8,11},{9,10},{10,... | collective-permute-start | bytes 196616 | tf_op jit(solution)/shard_map/ppermute | solution.py:84
  65.1 5.4 %collective-permute-start.35 = (bf16[128,256]{1,0:T(8,128)(2,1)S(1)}, bf16[128,256]{1,0:T(8,128)(2,1)S(1)}, u32[]{:S(2)}, u32[]{:S(2)}) collective-permute-start(bf16[128,256]{1,0:T(8,128)(2,1)S(1)} %get-tuple-element.88), channel_id=1, source_target_pairs={{0,4},{1,5},{2,6},{3,7},{4,0},{5,1},{6,2},{7,3},{8,12},{9,13},{10,... | collective-permute-start | bytes 196616 | tf_op jit(solution)/shard_map/ppermute | solution.py:84
  67.5 2.9 %collective-permute-start.36 = (bf16[128,256]{1,0:T(8,128)(2,1)S(1)}, bf16[128,256]{1,0:T(8,128)(2,1)S(1)}, u32[]{:S(2)}, u32[]{:S(2)}) collective-permute-start(bf16[128,256]{1,0:T(8,128)(2,1)S(1)} %get-tuple-element.89), channel_id=1, source_target_pairs={{0,1},{1,0},{2,3},{3,2},{4,5},{5,4},{6,7},{7,6},{8,9},{9,8},{10,11... | collective-permute-start | bytes 196616 | tf_op jit(solution)/shard_map/ppermute | solution.py:84

commit v8 on v7

--- a/solution.py
+++ b/solution.py
@@ -142,9 +142,9 @@
         sends, (group, group_other) = refs[4:-2], refs[-2:]
         place(group, mine)
         place(group_other, theirs)
+        total = mm(same_ref[...], group[...]) + mm(other_ref[...], group_other[...])
         for i, ref in enumerate((own_ref,) + tuple(sends)):
-            at = pl.ds(i * cpd, cpd)
-            ref[...] = (mm(same_ref[at, :], group[...]) + mm(other_ref[at, :], group_other[...])).astype(ref.dtype)
+            ref[...] = total[i * cpd : (i + 1) * cpd].astype(ref.dtype)
 
     def over_col(block):
         out = [block]
@@ -171,8 +171,9 @@
             total = total + p[...].astype(F32)
         y = total.astype(BF)
         y_ref[...] = y
+        total = mm(bf_ref[...], y)
         for s, ref in enumerate(faces):
-            ref[...] = mm(bf_ref[pl.ds(s * ovl, ovl), :], y).astype(BF)
+            ref[...] = total[s * ovl : (s + 1) * ovl].astype(BF)
 
     def coarse_faces(parts, *tokens):
         y, *faces = call(
@@ -189,10 +190,11 @@
             wb[at, :] = (base_ref[at, :] - mm(lb_ref[at, :], y)).astype(BF)
 
         row_loop(tile)
+        face = mm(bf_ref[...], y) + mm(si_ref[...], wb[...])
         for s in range(4):
             at = pl.ds(s * ovl, ovl)
-            face = mm(bf_ref[at, :], y) + mm(si_ref[at, :], wb[...])
-            face_ref[at, :] = face + refs[s][...].astype(F32) if len(refs) > 2 else face
+            part = face[s * ovl : (s + 1) * ovl]
+            face_ref[at, :] = part + refs[s][...].astype(F32) if len(refs) > 2 else part
         if len(refs) > 2:
             old_ref, bt_ref, inv_ref, pre_ref = refs[4:7] + refs[8:9]
 
@@ -212,9 +214,9 @@
     def k_faces(base_ref, f_ref, *refs):
         recvs, faces = refs[:4], refs[4:]
         recv = jnp.concatenate([x[...] for x in recvs], axis=0)
+        total = base_ref[...] + mm(f_ref[...], recv)
         for s, ref in enumerate(faces):
-            at = pl.ds(s * ovl, ovl)
-            ref[...] = (base_ref[at, :] + mm(f_ref[at, :], recv)).astype(BF)
+            ref[...] = total[s * ovl : (s + 1) * ovl].astype(BF)
 
     def faces_after(base, recv):
         return call(k_faces, [((ovl, nrhs), BF)] * 4, base, fmat, *recv, flops=2 * nf * nf * nrhs)
@@ -228,7 +230,7 @@
         def base_tile(at):
             wb[at, :] = (base_ref[at, :] - mm(lb_ref[at, :], y) + mm(wt_ref[at, :], recv[...])).astype(BF)
 
-        row_loop(base_tile)
+        base_tile(pl.ds(0, nloc))
 
         def sol_tile(at):
             new = mm(bt_ref[at, :], y) + mm(inv_ref[at, :], wb[...])

time: 71.9 us -> 71.7 us (level)
  no operation moved by 1% of the time
where the time goes in v8:
time: 71.7 us; the launch traced here: 71.6 us
  starting transfers between devices  34.2 us (48%)
  waiting for transfers between devices  18.2 us (25%)
  Pallas kernels  16.7 us (23%)
  local copies, waits for them, and re-layouts  1.21 us (2%)
  between operations  1.01 us (1%)
    pallas_call x20, Pallas kernels, call(): pl.pallas_call(kernel, out_shape=[jax.ShapeDtypeStruct(s, d) for s, d in...  16.7 us
    ppermute x16, starting transfers between devices, halo(): out.append(lax.ppermute(f, both, p))  12.4 us
    ppermute x6, starting transfers between devices, reduce_rows(): lax.ppermute(block, 'row', [(i, i ^ 2 * (k + 1)) for i in range(nr)])  8.9 us
    ppermute x12, starting transfers between devices, over_col(): out.append(lax.ppermute(block, 'col', [(i, i ^ k) for i in range(nc)]))  7.67 us
    ppermute x6, waiting for transfers between devices, reduce_rows(): lax.ppermute(block, 'row', [(i, i ^ 2 * (k + 1)) for i in range(nr)])  6.62 us
    ppermute x3, starting transfers between devices, over_pair(): return lax.ppermute(value, 'row', [(i, i ^ 1) for i in range(nr)])  5.28 us
    ppermute x16, waiting for transfers between devices, halo(): out.append(lax.ppermute(f, both, p))  4.62 us
    ppermute x12, waiting for transfers between devices, over_col(): out.append(lax.ppermute(block, 'col', [(i, i ^ k) for i in range(nc)]))  3.83 us
  transfers between devices with their start and end apart: 37, of which 15 were waited for; matrix products, arithmetic and copies ran while one was open for 0% of the time, Pallas kernels for 19%

profile of v8, /device:TPU:0, one launch (start us, length us, event | category | flops | bytes accessed | tf_op | source)
XLA Modules:
  0.0 71.6 jit_solution(1018893220313142870)
XLA Ops:
  0.7 1.2 %copy-done = f32[1024,256]{1,0:T(8,128)S(1)} copy-done((f32[1024,256]{1,0:T(8,128)S(1)}, f32[1024,256]{1,0:T(8,128)}, u32[]{:S(2)}) %copy-start) | copy-done | bytes 1048600
  2.2 3.1 %collective-permute-start.3 = (bf16[96,256]{1,0:T(8,128)(2,1)S(1)}, bf16[96,256]{1,0:T(8,128)(2,1)S(1)}, u32[]{:S(2)}, u32[]{:S(2)}) collective-permute-start(bf16[96,256]{1,0:T(8,128)(2,1)S(1)} %get-tuple-element.46.token.refs_0_), channel_id=1, source_target_pairs={{0,4},{4,0},{8,12},{12,8},{16,20},{20,16},{24,28},{28,24},{1,5},{5... | collective-permute-start | bytes 147464 | tf_op jit(solution)/shard_map/ppermute | solution.py:156
  5.2 0.7 collective-permute-start.2
  5.9 0.8 %collective-permute-start.1 = (bf16[96,256]{1,0:T(8,128)(2,1)S(1)}, bf16[96,256]{1,0:T(8,128)(2,1)S(1)}, u32[]{:S(2)}, u32[]{:S(2)}) collective-permute-start(bf16[96,256]{1,0:T(8,128)(2,1)S(1)} %get-tuple-element.46.token.refs_0_), channel_id=1, source_target_pairs={{0,2},{1,3},{2,0},{3,1},{4,6},{5,7},{6,4},{7,5},{8,10},{9,11},{10,... | collective-permute-start | bytes 147464 | tf_op jit(solution)/shard_map/ppermute | solution.py:152
  7.4 1.1 %collective-permute-start.6 = (bf16[96,256]{1,0:T(8,128)(2,1)S(1)}, bf16[96,256]{1,0:T(8,128)(2,1)S(1)}, u32[]{:S(2)}, u32[]{:S(2)}) collective-permute-start(bf16[96,256]{1,0:T(8,128)(2,1)S(1)} %collective-permute-done.3.refs_4_), channel_id=1, source_target_pairs={{0,3},{1,2},{2,1},{3,0},{4,7},{5,6},{6,5},{7,4},{8,11},{9,10},{10,... | collective-permute-start | bytes 147464 | tf_op jit(solution)/shard_map/ppermute | solution.py:152
  8.5 0.7 %collective-permute-done.2.refs_3_ = bf16[96,256]{1,0:T(8,128)(2,1)S(1)} collective-permute-done((bf16[96,256]{1,0:T(8,128)(2,1)S(1)}, bf16[96,256]{1,0:T(8,128)(2,1)S(1)}, u32[]{:S(2)}, u32[]{:S(2)}) %collective-permute-start.2) | collective-permute-done | bytes 49184 | tf_op jit(solution)/shard_map/ppermute | solution.py:152
  9.2 1.5 %collective-permute-start.5 = (bf16[96,256]{1,0:T(8,128)(2,1)S(1)}, bf16[96,256]{1,0:T(8,128)(2,1)S(1)}, u32[]{:S(2)}, u32[]{:S(2)}) collective-permute-start(bf16[96,256]{1,0:T(8,128)(2,1)S(1)} %collective-permute-done.3.refs_4_), channel_id=1, source_target_pairs={{0,2},{1,3},{2,0},{3,1},{4,6},{5,7},{6,4},{7,5},{8,10},{9,11},{10,... | collective-permute-start | bytes 147464 | tf_op jit(solution)/shard_map/ppermute | solution.py:152
  10.7 0.8 %shard_map.88 = (bf16[512,1024]{1,0:T(8,128)(2,1)S(1)}, bf16[1024,512]{1,0:T(8,128)(2,1)S(1)}, bf16[1024,96]{1,0:T(8,128)(2,1)S(1)}) custom-call(f32[8,128]{1,0:T(8,128)S(1)} %pad_maximum_fusion.table_ref, bf16[96,1024]{1,0:T(8,128)(2,1)S(1)} %copy-done.3, bf16[96,256]{1,0:T(8,128)(2,1)S(1)} %get-tuple-element.46.token.refs_0_), custom_call_target="tpu_custom_call" | custom-call | bytes 249856 | tf_op jit(solution)/shard_map/pallas_call | solution.py:25
  11.6 0.9 %shard_map.89.refs_10_.lb_ref = bf16[1024,96]{1,0:T(8,128)(2,1)S(1)} custom-call(bf16[1024,1024]{1,0:T(8,128)(2,1)S(1)} %copy-done.1, bf16[1024,96]{1,0:T(8,128)(2,1)S(1)} %get-tuple-element.49.bt_ref.refs_5_, bf16[1024,512]{1,0:T(8,128)(2,1)S(1)} %get-tuple-element.50.token.wt_ref), custom_call_target="tpu_custom_call" | custom-call | flops 201326592 | bytes 3342336 | tf_op jit(solution)/shard_map/pallas_call | solution.py:25
  12.5 0.8 %collective-permute-done.5.refs_6_ = bf16[96,256]{1,0:T(8,128)(2,1)S(1)} collective-permute-done((bf16[96,256]{1,0:T(8,128)(2,1)S(1)}, bf16[96,256]{1,0:T(8,128)(2,1)S(1)}, u32[]{:S(2)}, u32[]{:S(2)}) %collective-permute-start.5) | collective-permute-done | bytes 49184 | tf_op jit(solution)/shard_map/ppermute | solution.py:152
  13.3 2.8 %collective-permute-done.7.refs_9_ = bf16[384,384]{1,0:T(8,128)(2,1)S(1)} collective-permute-done((bf16[384,384]{1,0:T(8,128)(2,1)S(1)}, bf16[384,384]{1,0:T(8,128)(2,1)S(1)}, u32[]{:S(2)}, u32[]{:S(2)}) %collective-permute-start.7) | collective-permute-done | bytes 294944 | tf_op jit(solution)/shard_map/ppermute | solution.py:156
  16.6 1.6 %collective-permute-start.8 = (bf16[96,256]{1,0:T(8,128)(2,1)S(1)}, bf16[96,256]{1,0:T(8,128)(2,1)S(1)}, u32[]{:S(2)}, u32[]{:S(2)}) collective-permute-start(bf16[96,256]{1,0:T(8,128)(2,1)S(1)} %get-tuple-element.52), channel_id=1, source_target_pairs={{0,8},{4,12},{8,0},{12,4},{16,24},{20,28},{24,16},{28,20},{1,9},{5... | collective-permute-start | bytes 147464 | tf_op jit(solution)/shard_map/ppermute | solution.py:161
  18.2 2.6 %collective-permute-start.9 = (bf16[96,256]{1,0:T(8,128)(2,1)S(1)}, bf16[96,256]{1,0:T(8,128)(2,1)S(1)}, u32[]{:S(2)}, u32[]{:S(2)}) collective-permute-start(bf16[96,256]{1,0:T(8,128)(2,1)S(1)} %get-tuple-element.53), channel_id=1, source_target_pairs={{0,16},{4,20},{8,24},{12,28},{16,0},{20,4},{24,8},{28,12},{1,17},{... | collective-permute-start | bytes 147464 | tf_op jit(solution)/shard_map/ppermute | solution.py:161
  21.0 2.1 %shard_map.91 = (bf16[512,96]{1,0:T(8,128)(2,1)S(1)}, bf16[512,1024]{1,0:T(8,128)(2,1)S(1)}, bf16[512,512]{1,0:T(8,128)(2,1)S(1)}) custom-call(bf16[512,1024]{1,0:T(8,128)(2,1)S(1)} %get-tuple-element.55.sel_ref, bf16[1024,512]{1,0:T(8,128)(2,1)S(1)} %get-tuple-element.50.token.wt_ref, bf16[1024,1024]{1,0:T(8,128)(2,1)S(1)} %copy-done.2, ...), custom_call_target="tpu_custom_call" | custom-call | flops 1711276032 | bytes 4489216 | tf_op jit(solution)/shard_map/pallas_call | solution.py:25
  23.1 0.6 collective-permute-done.9.refs_2_
  23.7 3.3 %collective-permute-done.10.refs_3_ = bf16[96,256]{1,0:T(8,128)(2,1)S(1)} collective-permute-done((bf16[96,256]{1,0:T(8,128)(2,1)S(1)}, bf16[96,256]{1,0:T(8,128)(2,1)S(1)}, u32[]{:S(2)}, u32[]{:S(2)}) %collective-permute-start.10) | collective-permute-done | bytes 49184 | tf_op jit(solution)/shard_map/ppermute | solution.py:161
  27.4 1.6 %collective-permute-start.12 = (bf16[128,256]{1,0:T(8,128)(2,1)S(1)}, bf16[128,256]{1,0:T(8,128)(2,1)S(1)}, u32[]{:S(2)}, u32[]{:S(2)}) collective-permute-start(bf16[128,256]{1,0:T(8,128)(2,1)S(1)} %get-tuple-element.61), channel_id=1, source_target_pairs={{0,3},{1,2},{2,1},{3,0},{4,7},{5,6},{6,5},{7,4},{8,11},{9,10},{10,... | collective-permute-start | bytes 196616 | tf_op jit(solution)/shard_map/ppermute | solution.py:84
  29.0 0.9 %shard_map.95.base_ref = f32[512,256]{1,0:T(8,128)S(1)} custom-call(bf16[96,256]{1,0:T(8,128)(2,1)S(1)} %get-tuple-element.57.token.y_ref, f32[1024,256]{1,0:T(8,128)S(1)} %copy-done, bf16[1024,96]{1,0:T(8,128)(2,1)S(1)} %shard_map.89.refs_10_.lb_ref, bf16[512,1024]{1,0:T(8,128)(2,1)S(1)} %get-tuple-element.66.si_ref, ...), custom_call_target="tpu_custom_call" | custom-call | flops 268435456 | bytes 2441216 | tf_op jit(solution)/shard_map/pallas_call | solution.py:25
  30.0 0.7 %shard_map.93 = (bf16[96,1024]{1,0:T(8,128)(2,1)S(1)}, bf16[96,512]{1,0:T(8,128)(2,1)S(1)}, f32[96,256]{1,0:T(8,128)S(1)}) custom-call(bf16[96,1024]{1,0:T(8,128)(2,1)S(1)} %copy-done.3, bf16[1024,1024]{1,0:T(8,128)(2,1)S(1)} %copy-done.1, bf16[1024,512]{1,0:T(8,128)(2,1)S(1)} %get-tuple-element.50.token.wt_ref, f32[1024,256]{1,0:T(8,128)S(1)} %copy-done, ...), custom_call_target="tpu_custom_call" | custom-call | flops 352321536 | bytes 4440064 | tf_op jit(solution)/shard_map/pallas_call | solution.py:25
  30.7 0.5 collective-permute-done.12.refs_1_
  31.2 2.0 %collective-permute-done.13.refs_2_ = bf16[128,256]{1,0:T(8,128)(2,1)S(1)} collective-permute-done((bf16[128,256]{1,0:T(8,128)(2,1)S(1)}, bf16[128,256]{1,0:T(8,128)(2,1)S(1)}, u32[]{:S(2)}, u32[]{:S(2)}) %collective-permute-start.13) | collective-permute-done | bytes 65568 | tf_op jit(solution)/shard_map/ppermute | solution.py:84
  33.6 0.6 collective-permute-start.16
  34.2 1.9 %collective-permute-start.17 = (bf16[128,256]{1,0:T(8,128)(2,1)S(1)}, bf16[128,256]{1,0:T(8,128)(2,1)S(1)}, u32[]{:S(2)}, u32[]{:S(2)}) collective-permute-start(bf16[128,256]{1,0:T(8,128)(2,1)S(1)} %get-tuple-element.70.refs_2_), channel_id=1, source_target_pairs={{0,4},{1,5},{2,6},{3,7},{4,0},{5,1},{6,2},{7,3},{8,12},{9,13},{10,... | collective-permute-start | bytes 196616 | tf_op jit(solution)/shard_map/ppermute | solution.py:84
  36.2 0.6 collective-permute-start.18
  36.7 1.8 %shard_map.94 = (f32[1024,256]{1,0:T(8,128)S(1)}, f32[96,256]{1,0:T(8,128)S(1)}) custom-call(bf16[96,256]{1,0:T(8,128)(2,1)S(1)} %get-tuple-element.57.token.y_ref, f32[1024,256]{1,0:T(8,128)S(1)} %copy-done, bf16[1024,96]{1,0:T(8,128)(2,1)S(1)} %shard_map.89.refs_10_.lb_ref, bf16[1024,96]{1,0:T(8,128)(2,1)S(1)} %get-tuple-element.49.bt_ref.refs_5_, ...), custom_call_target="tpu_custom_call" | custom-call | flops 1342177280 | bytes 5193728 | tf_op jit(solution)/shard_map/pallas_call | solution.py:25
  38.6 0.6 collective-permute-done.17.refs_2_
  39.3 2.0 %collective-permute-start.22 = (bf16[96,256]{1,0:T(8,128)(2,1)S(1)}, bf16[96,256]{1,0:T(8,128)(2,1)S(1)}, u32[]{:S(2)}, u32[]{:S(2)}) collective-permute-start(bf16[96,256]{1,0:T(8,128)(2,1)S(1)} %shard_map.97.refs_0_), channel_id=1, source_target_pairs={{0,4},{4,0},{8,12},{12,8},{16,20},{20,16},{24,28},{28,24},{1,5},{5... | collective-permute-start | bytes 147464 | tf_op jit(solution)/shard_map/ppermute | solution.py:156
  41.3 1.4 %collective-permute-start.20 = (bf16[96,256]{1,0:T(8,128)(2,1)S(1)}, bf16[96,256]{1,0:T(8,128)(2,1)S(1)}, u32[]{:S(2)}, u32[]{:S(2)}) collective-permute-start(bf16[96,256]{1,0:T(8,128)(2,1)S(1)} %shard_map.97.refs_0_), channel_id=1, source_target_pairs={{0,2},{1,3},{2,0},{3,1},{4,6},{5,7},{6,4},{7,5},{8,10},{9,11},{10,... | collective-permute-start | bytes 147464 | tf_op jit(solution)/shard_map/ppermute | solution.py:152
  43.5 1.3 %collective-permute-start.24 = (bf16[96,256]{1,0:T(8,128)(2,1)S(1)}, bf16[96,256]{1,0:T(8,128)(2,1)S(1)}, u32[]{:S(2)}, u32[]{:S(2)}) collective-permute-start(bf16[96,256]{1,0:T(8,128)(2,1)S(1)} %collective-permute-done.22.refs_4_), channel_id=1, source_target_pairs={{0,2},{1,3},{2,0},{3,1},{4,6},{5,7},{6,4},{7,5},{8,10},{9,11},{10,... | collective-permute-start | bytes 147464 | tf_op jit(solution)/shard_map/ppermute | solution.py:152
  44.8 0.5 collective-permute-done.21.refs_3_
  45.3 1.2 %shard_map.98.refs_10_.base_ref = f32[1024,256]{1,0:T(8,128)S(1)} custom-call(f32[1024,256]{1,0:T(8,128)S(1)} %get-tuple-element.72.sol_ref.refs_4_, bf16[1024,1024]{1,0:T(8,128)(2,1)S(1)} %copy-done.1, f32[1024,256]{1,0:T(8,128)S(1)} %copy-done, bf16[1024,512]{1,0:T(8,128)(2,1)S(1)} %get-tuple-element.50.token.wt_ref, ...), custom_call_target="tpu_custom_call" | custom-call | flops 805306368 | bytes 5505024 | tf_op jit(solution)/shard_map/pallas_call | solution.py:25
  46.6 0.9 %collective-permute-done.25.refs_7_ = bf16[96,256]{1,0:T(8,128)(2,1)S(1)} collective-permute-done((bf16[96,256]{1,0:T(8,128)(2,1)S(1)}, bf16[96,256]{1,0:T(8,128)(2,1)S(1)}, u32[]{:S(2)}, u32[]{:S(2)}) %collective-permute-start.25) | collective-permute-done | bytes 49184 | tf_op jit(solution)/shard_map/ppermute | solution.py:152
  47.5 0.8 %collective-permute-done.24.refs_6_ = bf16[96,256]{1,0:T(8,128)(2,1)S(1)} collective-permute-done((bf16[96,256]{1,0:T(8,128)(2,1)S(1)}, bf16[96,256]{1,0:T(8,128)(2,1)S(1)}, u32[]{:S(2)}, u32[]{:S(2)}) %collective-permute-start.24) | collective-permute-done | bytes 49184 | tf_op jit(solution)/shard_map/ppermute | solution.py:152
  48.7 1.5 %collective-permute-start.26 = (bf16[96,256]{1,0:T(8,128)(2,1)S(1)}, bf16[96,256]{1,0:T(8,128)(2,1)S(1)}, u32[]{:S(2)}, u32[]{:S(2)}) collective-permute-start(bf16[96,256]{1,0:T(8,128)(2,1)S(1)} %get-tuple-element.74), channel_id=1, source_target_pairs={{0,8},{4,12},{8,0},{12,4},{16,24},{20,28},{24,16},{28,20},{1,9},{5... | collective-permute-start | bytes 147464 | tf_op jit(solution)/shard_map/ppermute | solution.py:161
  50.2 0.9 %collective-permute-start.27 = (bf16[96,256]{1,0:T(8,128)(2,1)S(1)}, bf16[96,256]{1,0:T(8,128)(2,1)S(1)}, u32[]{:S(2)}, u32[]{:S(2)}) collective-permute-start(bf16[96,256]{1,0:T(8,128)(2,1)S(1)} %get-tuple-element.75), channel_id=1, source_target_pairs={{0,16},{4,20},{8,24},{12,28},{16,0},{20,4},{24,8},{28,12},{1,17},{... | collective-permute-start | bytes 147464 | tf_op jit(solution)/shard_map/ppermute | solution.py:161
  51.1 2.1 %collective-permute-start.28 = (bf16[96,256]{1,0:T(8,128)(2,1)S(1)}, bf16[96,256]{1,0:T(8,128)(2,1)S(1)}, u32[]{:S(2)}, u32[]{:S(2)}) collective-permute-start(bf16[96,256]{1,0:T(8,128)(2,1)S(1)} %get-tuple-element.76), channel_id=1, source_target_pairs={{0,24},{4,28},{8,16},{12,20},{16,8},{20,12},{24,0},{28,4},{1,25},{... | collective-permute-start | bytes 147464 | tf_op jit(solution)/shard_map/ppermute | solution.py:161
  53.1 1.4 %shard_map.100.refs_5_.m_ref = bf16[1024,512]{1,0:T(8,128)(2,1)S(1)} custom-call(bf16[1024,1024]{1,0:T(8,128)(2,1)S(1)} %copy-done.2, bf16[1024,512]{1,0:T(8,128)(2,1)S(1)} %get-tuple-element.50.token.wt_ref, f32[96,256]{1,0:T(8,128)S(1)} %get-tuple-element.73.token.refs_0_), custom_call_target="tpu_custom_call" | custom-call | flops 1073741824 | bytes 3244032 | tf_op jit(solution)/shard_map/pallas_call | solution.py:25
  54.6 2.7 %collective-permute-done.27.refs_2_ = bf16[96,256]{1,0:T(8,128)(2,1)S(1)} collective-permute-done((bf16[96,256]{1,0:T(8,128)(2,1)S(1)}, bf16[96,256]{1,0:T(8,128)(2,1)S(1)}, u32[]{:S(2)}, u32[]{:S(2)}) %collective-permute-start.27) | collective-permute-done | bytes 49184 | tf_op jit(solution)/shard_map/ppermute | solution.py:161
  57.5 1.0 %collective-permute-start.30 = (bf16[128,256]{1,0:T(8,128)(2,1)S(1)}, bf16[128,256]{1,0:T(8,128)(2,1)S(1)}, u32[]{:S(2)}, u32[]{:S(2)}) collective-permute-start(bf16[128,256]{1,0:T(8,128)(2,1)S(1)} %get-tuple-element.80), channel_id=1, source_target_pairs={{0,3},{1,2},{2,1},{3,0},{4,7},{5,6},{6,5},{7,4},{8,11},{9,10},{10,... | collective-permute-start | bytes 196616 | tf_op jit(solution)/shard_map/ppermute | solution.py:84
  58.6 1.5 %collective-permute-start.31 = (bf16[128,256]{1,0:T(8,128)(2,1)S(1)}, bf16[128,256]{1,0:T(8,128)(2,1)S(1)}, u32[]{:S(2)}, u32[]{:S(2)}) collective-permute-start(bf16[128,256]{1,0:T(8,128)(2,1)S(1)} %get-tuple-element.81), channel_id=1, source_target_pairs={{0,4},{1,5},{2,6},{3,7},{4,0},{5,1},{6,2},{7,3},{8,12},{9,13},{10,... | collective-permute-start | bytes 196616 | tf_op jit(solution)/shard_map/ppermute | solution.py:84
  60.1 0.7 %collective-permute-start.32 = (bf16[128,256]{1,0:T(8,128)(2,1)S(1)}, bf16[128,256]{1,0:T(8,128)(2,1)S(1)}, u32[]{:S(2)}, u32[]{:S(2)}) collective-permute-start(bf16[128,256]{1,0:T(8,128)(2,1)S(1)} %get-tuple-element.82), channel_id=1, source_target_pairs={{0,1},{1,0},{2,3},{3,2},{4,5},{5,4},{6,7},{7,6},{8,9},{9,8},{10,11... | collective-permute-start | bytes 196616 | tf_op jit(solution)/shard_map/ppermute | solution.py:84
  60.8 1.9 %shard_map.102 = (f32[512,256]{1,0:T(8,128)S(1)}, f32[1024,256]{1,0:T(8,128)S(1)}) custom-call(bf16[96,256]{1,0:T(8,128)(2,1)S(1)} %get-tuple-element.77.y_ref, f32[1024,256]{1,0:T(8,128)S(1)} %shard_map.98.refs_10_.base_ref, bf16[1024,96]{1,0:T(8,128)(2,1)S(1)} %shard_map.89.refs_10_.lb_ref, bf16[512,1024]{1,0:T(8,128)(2,1)S(1)} %get-tuple-element.66.si_ref, ...), custom_call_target="tpu_custom_call" | custom-call | flops 268435456 | bytes 6045696 | tf_op jit(solution)/shard_map/pallas_call | solution.py:25
  62.7 0.6 collective-permute-done.31.refs_2_
  63.7 1.2 %collective-permute-start.34 = (bf16[128,256]{1,0:T(8,128)(2,1)S(1)}, bf16[128,256]{1,0:T(8,128)(2,1)S(1)}, u32[]{:S(2)}, u32[]{:S(2)}) collective-permute-start(bf16[128,256]{1,0:T(8,128)(2,1)S(1)} %get-tuple-element.87), channel_id=1, source_target_pairs={{0,3},{1,2},{2,1},{3,0},{4,7},{5,6},{6,5},{7,4},{8,11},{9,10},{10,... | collective-permute-start | bytes 196616 | tf_op jit(solution)/shard_map/ppermute | solution.py:84
  64.9 2.4 %collective-permute-start.35 = (bf16[128,256]{1,0:T(8,128)(2,1)S(1)}, bf16[128,256]{1,0:T(8,128)(2,1)S(1)}, u32[]{:S(2)}, u32[]{:S(2)}) collective-permute-start(bf16[128,256]{1,0:T(8,128)(2,1)S(1)} %get-tuple-element.88), channel_id=1, source_target_pairs={{0,4},{1,5},{2,6},{3,7},{4,0},{5,1},{6,2},{7,3},{8,12},{9,13},{10,... | collective-permute-start | bytes 196616 | tf_op jit(solution)/shard_map/ppermute | solution.py:84
  67.7 1.6 %shard_map.103 = (f32[1024,256]{1,0:T(8,128)}, f32[1024,256]{1,0:T(8,128)S(1)}) custom-call(f32[1024,256]{1,0:T(8,128)S(1)} %get-tuple-element.78.pre_ref, bf16[1024,512]{1,0:T(8,128)(2,1)S(1)} %shard_map.100.refs_5_.m_ref, f32[1024,256]{1,0:T(8,128)S(1)} %copy-done, bf16[1024,1024]{1,0:T(8,128)(2,1)S(1)} %copy-done.1, ...), custom_call_target="tpu_custom_call" | custom-call | flops 805306368 | bytes 5505024 | tf_op jit(solution)/shard_map/pallas_call | solution.py:25
  69.4 0.9 %collective-permute-done.35.refs_2_ = bf16[128,256]{1,0:T(8,128)(2,1)S(1)} collective-permute-done((bf16[128,256]{1,0:T(8,128)(2,1)S(1)}, bf16[128,256]{1,0:T(8,128)(2,1)S(1)}, u32[]{:S(2)}, u32[]{:S(2)}) %collective-permute-start.35) | collective-permute-done | bytes 65568 | tf_op jit(solution)/shard_map/ppermute | solution.py:84
  70.3 1.3 %shard_map.105 = f32[1024,256]{1,0:T(8,128)} custom-call(f32[1024,256]{1,0:T(8,128)S(1)} %get-tuple-element.84.res_ref, bf16[1024,512]{1,0:T(8,128)(2,1)S(1)} %get-tuple-element.50.token.wt_ref, bf16[128,256]{1,0:T(8,128)(2,1)S(1)} %collective-permute-done.33.refs_0_, bf16[128,256]{1,0:T(8,128)(2,1)S(1)} %collective-permute-done.34.refs_1_, ...), custom_call_target="tpu_custom_call" | custom-call | flops 268435456 | bytes 2359296 | tf_op jit(solution)/shard_map/pallas_call | solution.py:25
  (63 shorter events, 4.8 us)
Async XLA Ops:
  0.6 1.2 %copy-start = (f32[1024,256]{1,0:T(8,128)S(1)}, f32[1024,256]{1,0:T(8,128)}, u32[]{:S(2)}) copy-start(f32[1024,256]{1,0:T(8,128)} %rhs_ref.5) | copy-start | bytes 3145732
  0.6 1.2 %copy-start.3 = (bf16[96,1024]{1,0:T(8,128)(2,1)S(1)}, bf16[96,1024]{1,0:T(8,128)(2,1)}, u32[]{:S(2)}) copy-start(bf16[96,1024]{1,0:T(8,128)(2,1)} %basis_ref.3) | copy-start | bytes 589828
  0.7 1.5 %copy-start.4 = (bf16[768,384]{1,0:T(8,128)(2,1)S(1)}, bf16[768,384]{1,0:T(8,128)(2,1)}, u32[]{:S(2)}) copy-start(bf16[768,384]{1,0:T(8,128)(2,1)} %inv_ref.4) | copy-start | bytes 1769476
  0.7 6.7 %copy-start.5 = (s32[1,4,128]{2,1,0:T(4,128)S(1)}, s32[1,4,128]{2,1,0:T(4,128)}, u32[]{:S(2)}) copy-start(s32[1,4,128]{2,1,0:T(4,128)} %param.13) | copy-start | bytes 6148
  0.7 10.1 %copy-start.6 = (f32[1,4,128]{2,1,0:T(4,128)S(1)}, f32[1,4,128]{2,1,0:T(4,128)}, u32[]{:S(2)}) copy-start(f32[1,4,128]{2,1,0:T(4,128)} %param.12) | copy-start | bytes 6148
  1.9 9.7 %copy-start.1 = (bf16[1024,1024]{1,0:T(8,128)(2,1)S(1)}, bf16[1024,1024]{1,0:T(8,128)(2,1)}, u32[]{:S(2)}) copy-start(bf16[1024,1024]{1,0:T(8,128)(2,1)} %mat_ref.7) | copy-start | bytes 6291460
  2.2 5.2 %collective-permute-start.3 = (bf16[96,256]{1,0:T(8,128)(2,1)S(1)}, bf16[96,256]{1,0:T(8,128)(2,1)S(1)}, u32[]{:S(2)}, u32[]{:S(2)}) collective-permute-start(bf16[96,256]{1,0:T(8,128)(2,1)S(1)} %get-tuple-element.46.token.refs_0_), channel_id=1, source_target_pairs={{0,4},{4,0},{8,12},{12,8},{16,20},{20,16},{24,28},{28,24},{1,5},{5... | collective-permute-start | bytes 147464 | tf_op jit(solution)/shard_map/ppermute | solution.py:156
  5.2 4.0 %collective-permute-start.2 = (bf16[96,256]{1,0:T(8,128)(2,1)S(1)}, bf16[96,256]{1,0:T(8,128)(2,1)S(1)}, u32[]{:S(2)}, u32[]{:S(2)}) collective-permute-start(bf16[96,256]{1,0:T(8,128)(2,1)S(1)} %get-tuple-element.46.token.refs_0_), channel_id=1, source_target_pairs={{0,3},{1,2},{2,1},{3,0},{4,7},{5,6},{6,5},{7,4},{8,11},{9,10},{10,... | collective-permute-start | bytes 147464 | tf_op jit(solution)/shard_map/ppermute | solution.py:152
  5.9 4.8 %collective-permute-start.1 = (bf16[96,256]{1,0:T(8,128)(2,1)S(1)}, bf16[96,256]{1,0:T(8,128)(2,1)S(1)}, u32[]{:S(2)}, u32[]{:S(2)}) collective-permute-start(bf16[96,256]{1,0:T(8,128)(2,1)S(1)} %get-tuple-element.46.token.refs_0_), channel_id=1, source_target_pairs={{0,2},{1,3},{2,0},{3,1},{4,6},{5,7},{6,4},{7,5},{8,10},{9,11},{10,... | collective-permute-start | bytes 147464 | tf_op jit(solution)/shard_map/ppermute | solution.py:152
  6.7 5.7 %collective-permute-start = (bf16[96,256]{1,0:T(8,128)(2,1)S(1)}, bf16[96,256]{1,0:T(8,128)(2,1)S(1)}, u32[]{:S(2)}, u32[]{:S(2)}) collective-permute-start(bf16[96,256]{1,0:T(8,128)(2,1)S(1)} %get-tuple-element.46.token.refs_0_), channel_id=1, source_target_pairs={{0,1},{1,0},{2,3},{3,2},{4,5},{5,4},{6,7},{7,6},{8,9},{9,8},{10,11... | collective-permute-start | bytes 147464 | tf_op jit(solution)/shard_map/ppermute | solution.py:152
  7.1 9.1 %collective-permute-start.7 = (bf16[384,384]{1,0:T(8,128)(2,1)S(1)}, bf16[384,384]{1,0:T(8,128)(2,1)S(1)}, u32[]{:S(2)}, u32[]{:S(2)}) collective-permute-start(bf16[384,384]{1,0:T(8,128)(2,1)S(1)} %get-tuple-element.48), channel_id=1, source_target_pairs={{0,4},{4,0},{8,12},{12,8},{16,20},{20,16},{24,28},{28,24},{1,5},{5... | collective-permute-start | bytes 884744 | tf_op jit(solution)/shard_map/ppermute | solution.py:156
  7.4 5.1 %collective-permute-start.6 = (bf16[96,256]{1,0:T(8,128)(2,1)S(1)}, bf16[96,256]{1,0:T(8,128)(2,1)S(1)}, u32[]{:S(2)}, u32[]{:S(2)}) collective-permute-start(bf16[96,256]{1,0:T(8,128)(2,1)S(1)} %collective-permute-done.3.refs_4_), channel_id=1, source_target_pairs={{0,3},{1,2},{2,1},{3,0},{4,7},{5,6},{6,5},{7,4},{8,11},{9,10},{10,... | collective-permute-start | bytes 147464 | tf_op jit(solution)/shard_map/ppermute | solution.py:152
  9.2 4.1 %collective-permute-start.5 = (bf16[96,256]{1,0:T(8,128)(2,1)S(1)}, bf16[96,256]{1,0:T(8,128)(2,1)S(1)}, u32[]{:S(2)}, u32[]{:S(2)}) collective-permute-start(bf16[96,256]{1,0:T(8,128)(2,1)S(1)} %collective-permute-done.3.refs_4_), channel_id=1, source_target_pairs={{0,2},{1,3},{2,0},{3,1},{4,6},{5,7},{6,4},{7,5},{8,10},{9,11},{10,... | collective-permute-start | bytes 147464 | tf_op jit(solution)/shard_map/ppermute | solution.py:152
  10.7 2.6 %collective-permute-start.4 = (bf16[96,256]{1,0:T(8,128)(2,1)S(1)}, bf16[96,256]{1,0:T(8,128)(2,1)S(1)}, u32[]{:S(2)}, u32[]{:S(2)}) collective-permute-start(bf16[96,256]{1,0:T(8,128)(2,1)S(1)} %collective-permute-done.3.refs_4_), channel_id=1, source_target_pairs={{0,1},{1,0},{2,3},{3,2},{4,5},{5,4},{6,7},{7,6},{8,9},{9,8},{10,11... | collective-permute-start | bytes 147464 | tf_op jit(solution)/shard_map/ppermute | solution.py:152
  11.6 9.4 %copy-start.2 = (bf16[1024,1024]{1,0:T(8,128)(2,1)S(1)}, bf16[1024,1024]{1,0:T(8,128)(2,1)}, u32[]{:S(2)}) copy-start(bf16[1024,1024]{1,0:T(8,128)(2,1)} %refs_6_.1) | copy-start | bytes 6291460
  16.6 6.5 %collective-permute-start.8 = (bf16[96,256]{1,0:T(8,128)(2,1)S(1)}, bf16[96,256]{1,0:T(8,128)(2,1)S(1)}, u32[]{:S(2)}, u32[]{:S(2)}) collective-permute-start(bf16[96,256]{1,0:T(8,128)(2,1)S(1)} %get-tuple-element.52), channel_id=1, source_target_pairs={{0,8},{4,12},{8,0},{12,4},{16,24},{20,28},{24,16},{28,20},{1,9},{5... | collective-permute-start | bytes 147464 | tf_op jit(solution)/shard_map/ppermute | solution.py:161
  18.2 5.5 %collective-permute-start.9 = (bf16[96,256]{1,0:T(8,128)(2,1)S(1)}, bf16[96,256]{1,0:T(8,128)(2,1)S(1)}, u32[]{:S(2)}, u32[]{:S(2)}) collective-permute-start(bf16[96,256]{1,0:T(8,128)(2,1)S(1)} %get-tuple-element.53), channel_id=1, source_target_pairs={{0,16},{4,20},{8,24},{12,28},{16,0},{20,4},{24,8},{28,12},{1,17},{... | collective-permute-start | bytes 147464 | tf_op jit(solution)/shard_map/ppermute | solution.py:161
  20.8 6.3 %collective-permute-start.10 = (bf16[96,256]{1,0:T(8,128)(2,1)S(1)}, bf16[96,256]{1,0:T(8,128)(2,1)S(1)}, u32[]{:S(2)}, u32[]{:S(2)}) collective-permute-start(bf16[96,256]{1,0:T(8,128)(2,1)S(1)} %get-tuple-element.54), channel_id=1, source_target_pairs={{0,24},{4,28},{8,16},{12,20},{16,8},{20,12},{24,0},{28,4},{1,25},{... | collective-permute-start | bytes 147464 | tf_op jit(solution)/shard_map/ppermute | solution.py:161
  27.3 3.4 %collective-permute-start.11 = (bf16[128,256]{1,0:T(8,128)(2,1)S(1)}, bf16[128,256]{1,0:T(8,128)(2,1)S(1)}, u32[]{:S(2)}, u32[]{:S(2)}) collective-permute-start(bf16[128,256]{1,0:T(8,128)(2,1)S(1)} %get-tuple-element.60), channel_id=1, source_target_pairs={{0,1},{1,0},{2,3},{3,2},{4,8},{5,9},{6,10},{7,11},{8,4},{9,5},{10,... | collective-permute-start | bytes 196616 | tf_op jit(solution)/shard_map/ppermute | solution.py:84
  27.4 3.8 %collective-permute-start.12 = (bf16[128,256]{1,0:T(8,128)(2,1)S(1)}, bf16[128,256]{1,0:T(8,128)(2,1)S(1)}, u32[]{:S(2)}, u32[]{:S(2)}) collective-permute-start(bf16[128,256]{1,0:T(8,128)(2,1)S(1)} %get-tuple-element.61), channel_id=1, source_target_pairs={{0,3},{1,2},{2,1},{3,0},{4,7},{5,6},{6,5},{7,4},{8,11},{9,10},{10,... | collective-permute-start | bytes 196616 | tf_op jit(solution)/shard_map/ppermute | solution.py:84
  28.9 4.3 %collective-permute-start.13 = (bf16[128,256]{1,0:T(8,128)(2,1)S(1)}, bf16[128,256]{1,0:T(8,128)(2,1)S(1)}, u32[]{:S(2)}, u32[]{:S(2)}) collective-permute-start(bf16[128,256]{1,0:T(8,128)(2,1)S(1)} %get-tuple-element.62), channel_id=1, source_target_pairs={{0,4},{1,5},{2,6},{3,7},{4,0},{5,1},{6,2},{7,3},{8,12},{9,13},{10,... | collective-permute-start | bytes 196616 | tf_op jit(solution)/shard_map/ppermute | solution.py:84
  28.9 4.3 %collective-permute-start.14 = (bf16[128,256]{1,0:T(8,128)(2,1)S(1)}, bf16[128,256]{1,0:T(8,128)(2,1)S(1)}, u32[]{:S(2)}, u32[]{:S(2)}) collective-permute-start(bf16[128,256]{1,0:T(8,128)(2,1)S(1)} %get-tuple-element.63), channel_id=1, source_target_pairs={{0,1},{1,0},{2,3},{3,2},{4,5},{5,4},{6,7},{7,6},{8,9},{9,8},{10,11... | collective-permute-start | bytes 196616 | tf_op jit(solution)/shard_map/ppermute | solution.py:84
  33.5 5.0 %collective-permute-start.15 = (bf16[128,256]{1,0:T(8,128)(2,1)S(1)}, bf16[128,256]{1,0:T(8,128)(2,1)S(1)}, u32[]{:S(2)}, u32[]{:S(2)}) collective-permute-start(bf16[128,256]{1,0:T(8,128)(2,1)S(1)} %get-tuple-element.68.refs_0_), channel_id=1, source_target_pairs={{0,1},{1,0},{2,3},{3,2},{4,8},{5,9},{6,10},{7,11},{8,4},{9,5},{10,... | collective-permute-start | bytes 196616 | tf_op jit(solution)/shard_map/ppermute | solution.py:84
  33.6 5.0 %collective-permute-start.16 = (bf16[128,256]{1,0:T(8,128)(2,1)S(1)}, bf16[128,256]{1,0:T(8,128)(2,1)S(1)}, u32[]{:S(2)}, u32[]{:S(2)}) collective-permute-start(bf16[128,256]{1,0:T(8,128)(2,1)S(1)} %get-tuple-element.69.refs_1_), channel_id=1, source_target_pairs={{0,3},{1,2},{2,1},{3,0},{4,7},{5,6},{6,5},{7,4},{8,11},{9,10},{10,... | collective-permute-start | bytes 196616 | tf_op jit(solution)/shard_map/ppermute | solution.py:84
  34.2 4.9 %collective-permute-start.17 = (bf16[128,256]{1,0:T(8,128)(2,1)S(1)}, bf16[128,256]{1,0:T(8,128)(2,1)S(1)}, u32[]{:S(2)}, u32[]{:S(2)}) collective-permute-start(bf16[128,256]{1,0:T(8,128)(2,1)S(1)} %get-tuple-element.70.refs_2_), channel_id=1, source_target_pairs={{0,4},{1,5},{2,6},{3,7},{4,0},{5,1},{6,2},{7,3},{8,12},{9,13},{10,... | collective-permute-start | bytes 196616 | tf_op jit(solution)/shard_map/ppermute | solution.py:84
  36.2 3.0 %collective-permute-start.18 = (bf16[128,256]{1,0:T(8,128)(2,1)S(1)}, bf16[128,256]{1,0:T(8,128)(2,1)S(1)}, u32[]{:S(2)}, u32[]{:S(2)}) collective-permute-start(bf16[128,256]{1,0:T(8,128)(2,1)S(1)} %get-tuple-element.71.refs_3_), channel_id=1, source_target_pairs={{0,1},{1,0},{2,3},{3,2},{4,5},{5,4},{6,7},{7,6},{8,9},{9,8},{10,11... | collective-permute-start | bytes 196616 | tf_op jit(solution)/shard_map/ppermute | solution.py:84
  39.3 4.2 %collective-permute-start.22 = (bf16[96,256]{1,0:T(8,128)(2,1)S(1)}, bf16[96,256]{1,0:T(8,128)(2,1)S(1)}, u32[]{:S(2)}, u32[]{:S(2)}) collective-permute-start(bf16[96,256]{1,0:T(8,128)(2,1)S(1)} %shard_map.97.refs_0_), channel_id=1, source_target_pairs={{0,4},{4,0},{8,12},{12,8},{16,20},{20,16},{24,28},{28,24},{1,5},{5... | collective-permute-start | bytes 147464 | tf_op jit(solution)/shard_map/ppermute | solution.py:156
  41.3 4.0 %collective-permute-start.21 = (bf16[96,256]{1,0:T(8,128)(2,1)S(1)}, bf16[96,256]{1,0:T(8,128)(2,1)S(1)}, u32[]{:S(2)}, u32[]{:S(2)}) collective-permute-start(bf16[96,256]{1,0:T(8,128)(2,1)S(1)} %shard_map.97.refs_0_), channel_id=1, source_target_pairs={{0,3},{1,2},{2,1},{3,0},{4,7},{5,6},{6,5},{7,4},{8,11},{9,10},{10,... | collective-permute-start | bytes 147464 | tf_op jit(solution)/shard_map/ppermute | solution.py:152
  41.3 5.3 %collective-permute-start.20 = (bf16[96,256]{1,0:T(8,128)(2,1)S(1)}, bf16[96,256]{1,0:T(8,128)(2,1)S(1)}, u32[]{:S(2)}, u32[]{:S(2)}) collective-permute-start(bf16[96,256]{1,0:T(8,128)(2,1)S(1)} %shard_map.97.refs_0_), channel_id=1, source_target_pairs={{0,2},{1,3},{2,0},{3,1},{4,6},{5,7},{6,4},{7,5},{8,10},{9,11},{10,... | collective-permute-start | bytes 147464 | tf_op jit(solution)/shard_map/ppermute | solution.py:152
  42.6 3.9 %collective-permute-start.19 = (bf16[96,256]{1,0:T(8,128)(2,1)S(1)}, bf16[96,256]{1,0:T(8,128)(2,1)S(1)}, u32[]{:S(2)}, u32[]{:S(2)}) collective-permute-start(bf16[96,256]{1,0:T(8,128)(2,1)S(1)} %shard_map.97.refs_0_), channel_id=1, source_target_pairs={{0,1},{1,0},{2,3},{3,2},{4,5},{5,4},{6,7},{7,6},{8,9},{9,8},{10,11... | collective-permute-start | bytes 147464 | tf_op jit(solution)/shard_map/ppermute | solution.py:152
  43.5 4.0 %collective-permute-start.25 = (bf16[96,256]{1,0:T(8,128)(2,1)S(1)}, bf16[96,256]{1,0:T(8,128)(2,1)S(1)}, u32[]{:S(2)}, u32[]{:S(2)}) collective-permute-start(bf16[96,256]{1,0:T(8,128)(2,1)S(1)} %collective-permute-done.22.refs_4_), channel_id=1, source_target_pairs={{0,3},{1,2},{2,1},{3,0},{4,7},{5,6},{6,5},{7,4},{8,11},{9,10},{10,... | collective-permute-start | bytes 147464 | tf_op jit(solution)/shard_map/ppermute | solution.py:152
  43.5 4.8 %collective-permute-start.24 = (bf16[96,256]{1,0:T(8,128)(2,1)S(1)}, bf16[96,256]{1,0:T(8,128)(2,1)S(1)}, u32[]{:S(2)}, u32[]{:S(2)}) collective-permute-start(bf16[96,256]{1,0:T(8,128)(2,1)S(1)} %collective-permute-done.22.refs_4_), channel_id=1, source_target_pairs={{0,2},{1,3},{2,0},{3,1},{4,6},{5,7},{6,4},{7,5},{8,10},{9,11},{10,... | collective-permute-start | bytes 147464 | tf_op jit(solution)/shard_map/ppermute | solution.py:152
  45.3 3.0 %collective-permute-start.23 = (bf16[96,256]{1,0:T(8,128)(2,1)S(1)}, bf16[96,256]{1,0:T(8,128)(2,1)S(1)}, u32[]{:S(2)}, u32[]{:S(2)}) collective-permute-start(bf16[96,256]{1,0:T(8,128)(2,1)S(1)} %collective-permute-done.22.refs_4_), channel_id=1, source_target_pairs={{0,1},{1,0},{2,3},{3,2},{4,5},{5,4},{6,7},{7,6},{8,9},{9,8},{10,11... | collective-permute-start | bytes 147464 | tf_op jit(solution)/shard_map/ppermute | solution.py:152
  48.7 5.9 %collective-permute-start.26 = (bf16[96,256]{1,0:T(8,128)(2,1)S(1)}, bf16[96,256]{1,0:T(8,128)(2,1)S(1)}, u32[]{:S(2)}, u32[]{:S(2)}) collective-permute-start(bf16[96,256]{1,0:T(8,128)(2,1)S(1)} %get-tuple-element.74), channel_id=1, source_target_pairs={{0,8},{4,12},{8,0},{12,4},{16,24},{20,28},{24,16},{28,20},{1,9},{5... | collective-permute-start | bytes 147464 | tf_op jit(solution)/shard_map/ppermute | solution.py:161
  50.2 7.0 %collective-permute-start.27 = (bf16[96,256]{1,0:T(8,128)(2,1)S(1)}, bf16[96,256]{1,0:T(8,128)(2,1)S(1)}, u32[]{:S(2)}, u32[]{:S(2)}) collective-permute-start(bf16[96,256]{1,0:T(8,128)(2,1)S(1)} %get-tuple-element.75), channel_id=1, source_target_pairs={{0,16},{4,20},{8,24},{12,28},{16,0},{20,4},{24,8},{28,12},{1,17},{... | collective-permute-start | bytes 147464 | tf_op jit(solution)/shard_map/ppermute | solution.py:161
  51.1 6.1 %collective-permute-start.28 = (bf16[96,256]{1,0:T(8,128)(2,1)S(1)}, bf16[96,256]{1,0:T(8,128)(2,1)S(1)}, u32[]{:S(2)}, u32[]{:S(2)}) collective-permute-start(bf16[96,256]{1,0:T(8,128)(2,1)S(1)} %get-tuple-element.76), channel_id=1, source_target_pairs={{0,24},{4,28},{8,16},{12,20},{16,8},{20,12},{24,0},{28,4},{1,25},{... | collective-permute-start | bytes 147464 | tf_op jit(solution)/shard_map/ppermute | solution.py:161
  57.5 5.3 %collective-permute-start.29 = (bf16[128,256]{1,0:T(8,128)(2,1)S(1)}, bf16[128,256]{1,0:T(8,128)(2,1)S(1)}, u32[]{:S(2)}, u32[]{:S(2)}) collective-permute-start(bf16[128,256]{1,0:T(8,128)(2,1)S(1)} %get-tuple-element.79), channel_id=1, source_target_pairs={{0,1},{1,0},{2,3},{3,2},{4,8},{5,9},{6,10},{7,11},{8,4},{9,5},{10,... | collective-permute-start | bytes 196616 | tf_op jit(solution)/shard_map/ppermute | solution.py:84
  57.5 5.2 %collective-permute-start.30 = (bf16[128,256]{1,0:T(8,128)(2,1)S(1)}, bf16[128,256]{1,0:T(8,128)(2,1)S(1)}, u32[]{:S(2)}, u32[]{:S(2)}) collective-permute-start(bf16[128,256]{1,0:T(8,128)(2,1)S(1)} %get-tuple-element.80), channel_id=1, source_target_pairs={{0,3},{1,2},{2,1},{3,0},{4,7},{5,6},{6,5},{7,4},{8,11},{9,10},{10,... | collective-permute-start | bytes 196616 | tf_op jit(solution)/shard_map/ppermute | solution.py:84
  58.6 4.8 %collective-permute-start.31 = (bf16[128,256]{1,0:T(8,128)(2,1)S(1)}, bf16[128,256]{1,0:T(8,128)(2,1)S(1)}, u32[]{:S(2)}, u32[]{:S(2)}) collective-permute-start(bf16[128,256]{1,0:T(8,128)(2,1)S(1)} %get-tuple-element.81), channel_id=1, source_target_pairs={{0,4},{1,5},{2,6},{3,7},{4,0},{5,1},{6,2},{7,3},{8,12},{9,13},{10,... | collective-permute-start | bytes 196616 | tf_op jit(solution)/shard_map/ppermute | solution.py:84
  60.1 3.3 %collective-permute-start.32 = (bf16[128,256]{1,0:T(8,128)(2,1)S(1)}, bf16[128,256]{1,0:T(8,128)(2,1)S(1)}, u32[]{:S(2)}, u32[]{:S(2)}) collective-permute-start(bf16[128,256]{1,0:T(8,128)(2,1)S(1)} %get-tuple-element.82), channel_id=1, source_target_pairs={{0,1},{1,0},{2,3},{3,2},{4,5},{5,4},{6,7},{7,6},{8,9},{9,8},{10,11... | collective-permute-start | bytes 196616 | tf_op jit(solution)/shard_map/ppermute | solution.py:84
  63.7 5.7 %collective-permute-start.33 = (bf16[128,256]{1,0:T(8,128)(2,1)S(1)}, bf16[128,256]{1,0:T(8,128)(2,1)S(1)}, u32[]{:S(2)}, u32[]{:S(2)}) collective-permute-start(bf16[128,256]{1,0:T(8,128)(2,1)S(1)} %get-tuple-element.86), channel_id=1, source_target_pairs={{0,1},{1,0},{2,3},{3,2},{4,8},{5,9},{6,10},{7,11},{8,4},{9,5},{10,... | collective-permute-start | bytes 196616 | tf_op jit(solution)/shard_map/ppermute | solution.py:84
  63.7 5.6 %collective-permute-start.34 = (bf16[128,256]{1,0:T(8,128)(2,1)S(1)}, bf16[128,256]{1,0:T(8,128)(2,1)S(1)}, u32[]{:S(2)}, u32[]{:S(2)}) collective-permute-start(bf16[128,256]{1,0:T(8,128)(2,1)S(1)} %get-tuple-element.87), channel_id=1, source_target_pairs={{0,3},{1,2},{2,1},{3,0},{4,7},{5,6},{6,5},{7,4},{8,11},{9,10},{10,... | collective-permute-start | bytes 196616 | tf_op jit(solution)/shard_map/ppermute | solution.py:84
  64.9 5.3 %collective-permute-start.35 = (bf16[128,256]{1,0:T(8,128)(2,1)S(1)}, bf16[128,256]{1,0:T(8,128)(2,1)S(1)}, u32[]{:S(2)}, u32[]{:S(2)}) collective-permute-start(bf16[128,256]{1,0:T(8,128)(2,1)S(1)} %get-tuple-element.88), channel_id=1, source_target_pairs={{0,4},{1,5},{2,6},{3,7},{4,0},{5,1},{6,2},{7,3},{8,12},{9,13},{10,... | collective-permute-start | bytes 196616 | tf_op jit(solution)/shard_map/ppermute | solution.py:84
  67.3 2.9 %collective-permute-start.36 = (bf16[128,256]{1,0:T(8,128)(2,1)S(1)}, bf16[128,256]{1,0:T(8,128)(2,1)S(1)}, u32[]{:S(2)}, u32[]{:S(2)}) collective-permute-start(bf16[128,256]{1,0:T(8,128)(2,1)S(1)} %get-tuple-element.89), channel_id=1, source_target_pairs={{0,1},{1,0},{2,3},{3,2},{4,5},{5,4},{6,7},{7,6},{8,9},{9,8},{10,11... | collective-permute-start | bytes 196616 | tf_op jit(solution)/shard_map/ppermute | solution.py:84
